TPU v7x, 512 devices: a whole 4x4x16 slice. The times are simulated.
512 devices in a mesh: gz: 32 (over y, z_hi, core), gy: 16 (over z_lo, x).
Axes of the slice: x: 4, y: 4, z: 16 (z_hi: 4, z_lo: 4; z = z_hi * 4 + z_lo), core: 2. Of those that a mesh axis runs over, the one named last changes fastest.
Arguments:
- features: bfloat16 [16, 128, 128, 128], P(None, 'gz', 'gy'), may hold values from -6 to 6
- labels: int32 [128, 128, 128], P('gz', 'gy'), may hold values from 0 to 1
- sign_map: int32 [128, 128, 128], P('gz', 'gy'), may hold values from 0 to 1
- conv_first: bfloat16 [16, 16, 3, 3, 3], replicated, may hold values from -0.3125 to 0.3125
- conv_second: bfloat16 [16, 16, 3, 3, 3], replicated, may hold values from -0.3125 to 0.3125
- speed_weight: float32 [16], replicated, may hold values from -1.5 to 1.5
Outputs:
- d_features: bfloat16 [16, 128, 128, 128], P(None, 'gz', 'gy')
- grad_first: float32 [16, 16, 3, 3, 3], replicated
- grad_second: float32 [16, 16, 3, 3, 3], replicated
- grad_speed: float32 [16], replicated
All inputs are finite; a program needn't handle non-finite values.
Results may differ from a plain program's by a relative error of at most 0.01.
Values may be sent and summed in bfloat16 or wider, within the bound.
No kernel may reach another device: no remote copies, remote signals or barrier semaphores. Data moves between devices by JAX's collectives and lax.ppermute only.
A program may use at most 128 MiB of HBM per device.

v0:
```python
import jax
import jax.numpy as jnp
from jax import lax
from jax.sharding import PartitionSpec as P

C = 16
STEPS = 4


time_step = 0.25
spread_rate = 0.5
slope_floor = 0.1
layout = ("NCDHW", "OIDHW", "NCDHW")


def extended(value, sides, width):
    for axis, dim in sides:
        size, length = (lax.axis_size(axis), value.shape[dim])
        up = [(i, (i + 1) % size) for i in range(size - 1)]
        down = [(j, i) for i, j in up]
        last = lax.slice_in_dim(value, length - width, length, axis=dim)
        initial = lax.slice_in_dim(value, 0, width, axis=dim)
        before = lax.ppermute(last, axis, up)
        after = lax.ppermute(initial, axis, down)
        value = jnp.concatenate([before, value, after], axis=dim)
    return value


def for_sending(value):
    return jax.tree.map(lambda a: a.astype(jnp.bfloat16) if a.dtype == jnp.float32 else a, value)


def from_behind(block, axis, distance):
    devices = range(lax.axis_size(axis))
    route = [(i - distance, i) for i in devices if i - distance in devices]
    return lax.ppermute(block, axis, route)


def front(padded, speed):
    grid = jnp.pad(padded, ((0, 0), (0, 0), (1, 1)))
    centre = grid[1:-1, 1:-1, 1:-1]
    up_z = grid[2:, 1:-1, 1:-1]
    low_z = grid[:-2, 1:-1, 1:-1]
    up_y = grid[1:-1, 2:, 1:-1]
    low_y = grid[1:-1, :-2, 1:-1]
    up_x = grid[1:-1, 1:-1, 2:]
    low_x = grid[1:-1, 1:-1, :-2]
    dif_z = (up_z - low_z) * 0.5
    dif_y = (up_y - low_y) * 0.5
    dif_x = (up_x - low_x) * 0.5
    slope = jnp.sqrt(dif_z * dif_z + dif_y * dif_y + dif_x * dif_x + slope_floor)
    laplace = up_z + low_z + up_y + low_y + up_x + low_x - 6.0 * centre
    return centre + time_step * (speed * slope + spread_rate * laplace)


def silu_slope(value):
    sig = jax.nn.sigmoid(value)
    return sig * (1.0 + value * (1.0 - sig))


def conv_halo(field):
    return extended(field, (("gz", 1), ("gy", 2)), 1)


def conv_local(padded, weight):
    grid = jnp.pad(padded, ((0, 0), (0, 0), (0, 0), (1, 1)))
    return lax.conv_general_dilated(
        grid[None],
        weight,
        (1, 1, 1),
        "VALID",
        dimension_numbers=layout,
        preferred_element_type=jnp.float32,
    )[0]


def flip_weight(weight):
    return jnp.flip(weight, (2, 3, 4)).transpose(1, 0, 2, 3, 4)


def weight_grad(padded, d_out):
    grid = jnp.pad(padded, ((0, 0), (0, 0), (0, 0), (1, 1)))
    d_weight = lax.conv_general_dilated(
        grid[:, None],
        d_out[:, None],
        (1, 1, 1),
        "VALID",
        dimension_numbers=layout,
        preferred_element_type=jnp.float32,
    )
    return d_weight.transpose(1, 0, 2, 3, 4)


def conv_back(weight, d_out):
    d_grid = lax.conv_general_dilated(
        d_out[None],
        flip_weight(weight),
        (1, 1, 1),
        ((2, 2), (2, 2), (2, 2)),
        dimension_numbers=layout,
        preferred_element_type=jnp.float32,
    )[0]
    return d_grid[..., 1:-1]


def fold_axis(grad, width, dim, which):
    inner = grad.shape[dim] - 2 * width
    lower = lax.slice_in_dim(grad, 0, width, axis=dim)
    upper = lax.slice_in_dim(grad, inner + width, inner + 2 * width, axis=dim)
    core = lax.slice_in_dim(grad, width, inner + width, axis=dim)
    if which == 0:
        from_below = from_behind(for_sending(upper), "gz", 1).astype(upper.dtype)
        from_above = from_behind(for_sending(lower), "gz", -1).astype(lower.dtype)
    else:
        from_below = from_behind(for_sending(upper), "gy", 1).astype(upper.dtype)
        from_above = from_behind(for_sending(lower), "gy", -1).astype(lower.dtype)
    head = [(0, 0)] * grad.ndim
    tail = [(0, 0)] * grad.ndim
    head[dim] = (0, inner - width)
    tail[dim] = (inner - width, 0)
    return core + jnp.pad(from_below, head) + jnp.pad(from_above, tail)


def fold_rims(grad, width, zdim):
    return fold_axis(fold_axis(grad, width, zdim, 0), width, zdim + 1, 1)


def input_grad(weight, d_out):
    return fold_rims(conv_back(weight, d_out), 1, 1)


def on_device(features, labels, sign_map, conv_first, conv_second, speed_weight):
    high = lax.Precision.HIGHEST
    feat_pad = conv_halo(features)
    act_first = conv_local(feat_pad, conv_first)
    hidden = jax.nn.silu(act_first).astype(jnp.bfloat16)
    hidden_pad = conv_halo(hidden)
    act_second = conv_local(hidden_pad, conv_second)
    top = jax.nn.silu(act_second)
    speed = jnp.tanh(jnp.einsum("c,czyx->zyx", speed_weight, top, precision=high))
    phi_start = 2.0 * sign_map.astype(jnp.float32) - 1.0
    target = labels.astype(jnp.float32)
    stored = []
    phi = phi_start
    for step in range(STEPS):
        padded = extended(phi, (("gz", 0), ("gy", 1)), 1)
        stored.append(padded)
        phi = front(padded, speed)
    d_phi = jax.nn.sigmoid(phi) - target
    d_speed = jnp.zeros_like(speed)
    for padded in reversed(stored):
        back = jax.vjp(front, padded, speed)[1]
        d_padded, d_part = back(d_phi)
        d_speed = d_speed + d_part
        d_phi = fold_rims(d_padded, 1, 0)
    d_pre = d_speed * (1.0 - speed * speed)
    raw_speed = jnp.einsum("zyx,czyx->c", d_pre, top, precision=high)
    d_second = (speed_weight[:, None, None, None] * d_pre[None] * silu_slope(act_second)).astype(
        jnp.bfloat16
    )
    raw_second = weight_grad(hidden_pad, d_second)
    d_hidden = input_grad(conv_second, d_second)
    d_first = (d_hidden * silu_slope(act_first)).astype(jnp.bfloat16)
    raw_first = weight_grad(feat_pad, d_first)
    d_feat = input_grad(conv_first, d_first)
    raw_first, raw_second, raw_speed = lax.psum((raw_first, raw_second, raw_speed), ("gz", "gy"))
    total = (
        jnp.sum(raw_first * raw_first)
        + jnp.sum(raw_second * raw_second)
        + jnp.sum(raw_speed * raw_speed)
    )
    count = 54.0 * C * C + C
    factor = 1.0 / jnp.maximum(jnp.sqrt(total) / jnp.sqrt(jnp.float32(count)), 1.0)
    return (
        d_feat.astype(jnp.bfloat16),
        raw_first * factor,
        raw_second * factor,
        raw_speed * factor,
    )


def solution(mesh):
    in_specs = (P(None, "gz", "gy", None), P("gz", "gy", None), P("gz", "gy", None), P(), P(), P())
    out_specs = (P(None, "gz", "gy", None), P(), P(), P())
    return jax.shard_map(
        on_device, mesh=mesh, in_specs=in_specs, out_specs=out_specs, check_vma=False
    )
```

profile of v0, /device:TPU:1, one launch (start us, length us, event | category | flops | bytes accessed | tf_op | source)
XLA Modules:
  0.0 513.7 jit_solution(8016700852686420210)
XLA Ops:
  1.5 10.2 %collective-permute-start = (bf16[16,1,8,128]{3,0,2,1:T(8,128)(2,1)S(1)}, bf16[16,1,8,128]{3,0,2,1:T(8,128)(2,1)S(1)}, u32[]{:S(2)}, u32[]{:S(2)}) collective-permute-start(bf16[16,1,8,128]{3,0,2,1:T(8,128)(2,1)S(1)} %copy.83), channel_id=1, source_target_pairs={{0,16},{16,32},{32,48},{48,64},{64,80},{80,96},{96,112},{112,128},... | collective-permute-start | bytes 98312 | tf_op jit(solution)/shard_map/ppermute | solution.py:23
  15.3 5.5 %collective-permute-done.1 = bf16[16,1,8,128]{3,0,2,1:T(8,128)(2,1)S(1)} collective-permute-done((bf16[16,1,8,128]{3,0,2,1:T(8,128)(2,1)S(1)}, bf16[16,1,8,128]{3,0,2,1:T(8,128)(2,1)S(1)}, u32[]{:S(2)}, u32[]{:S(2)}) %collective-permute-start.1) | collective-permute-done | bytes 32800 | tf_op jit(solution)/shard_map/ppermute | solution.py:24
  20.9 3.1 collective-permute-start.2
  27.2 7.5 %collective-permute-start.9 = (f32[1,8,128]{2,1,0:T(8,128)S(1)}, f32[1,8,128]{2,1,0:T(8,128)S(1)}, u32[]{:S(2)}, u32[]{:S(2)}) collective-permute-start(f32[1,8,128]{2,1,0:T(8,128)S(1)} %get-tuple-element.113), channel_id=1, source_target_pairs={{0,16},{16,32},{32,48},{48,64},{64,80},{80,96},{96,112},{112,128},... | collective-permute-start | bytes 12296 | tf_op jit(solution)/shard_map/ppermute | solution.py:23
  37.4 4.2 copy.46
  42.7 5.8 %fusion.6 = f32[4,8,8,17,16]{4,2,3,1,0:T(8,128)} fusion(bf16[16,16,3,3,3]{1,0,4,3,2:T(8,128)(2,1)S(1)} %copy-done.23, bf16[16,6,10,1,7,2]{0,4,5,2,1,3:T(8,128)(2,1)S(1)} %slice.441, bf16[16,6,10,1,8,17]{0,4,5,2,1,3:T(8,128)(2,1)} %copy.46), kind=kOutput, calls=%fused_computation.8 | convolution fusion | flops 61037568 | bytes 580352 | tf_op jit(solution)/shard_map/conv_general_dilated | solution.py:67
  48.5 2.9 copy.47
  53.1 3.6 collective-permute-start.4
  60.0 4.6 collective-permute-start.11
  65.8 4.0 collective-permute-start.6
  71.5 2.9 collective-permute-done.7
  77.1 4.2 copy.50
  82.3 5.8 %fusion.10 = f32[4,8,8,17,16]{4,2,3,1,0:T(8,128)} fusion(bf16[16,16,3,3,3]{1,0,4,3,2:T(8,128)(2,1)S(1)} %copy-done, bf16[16,6,10,1,7,2]{0,4,5,2,1,3:T(8,128)(2,1)S(1)} %slice.445, bf16[16,6,10,1,8,17]{0,4,5,2,1,3:T(8,128)(2,1)} %copy.50), kind=kOutput, calls=%fused_computation.11 | convolution fusion | flops 61037568 | bytes 580352 | tf_op jit(solution)/shard_map/conv_general_dilated | solution.py:67
  88.1 2.9 copy.51
  97.0 7.9 %collective-permute-start.13 = (f32[1,8,128]{2,1,0:T(8,128)S(1)}, f32[1,8,128]{2,1,0:T(8,128)S(1)}, u32[]{:S(2)}, u32[]{:S(2)}) collective-permute-start(f32[1,8,128]{2,1,0:T(8,128)S(1)} %get-tuple-element.111), channel_id=1, source_target_pairs={{0,16},{16,32},{32,48},{48,64},{64,80},{80,96},{96,112},{112,128},... | collective-permute-start | bytes 12296 | tf_op jit(solution)/shard_map/ppermute | solution.py:23
  107.0 4.8 collective-permute-start.15
  114.7 8.9 %collective-permute-start.17 = (f32[1,8,128]{2,1,0:T(8,128)S(1)}, f32[1,8,128]{2,1,0:T(8,128)S(1)}, u32[]{:S(2)}, u32[]{:S(2)}) collective-permute-start(f32[1,8,128]{2,1,0:T(8,128)S(1)} %get-tuple-element.109), channel_id=1, source_target_pairs={{0,16},{16,32},{32,48},{48,64},{64,80},{80,96},{96,112},{112,128},... | collective-permute-start | bytes 12296 | tf_op jit(solution)/shard_map/ppermute | solution.py:23
  125.7 4.5 collective-permute-start.19
  133.1 8.9 %collective-permute-start.21 = (f32[1,8,128]{2,1,0:T(8,128)S(1)}, f32[1,8,128]{2,1,0:T(8,128)S(1)}, u32[]{:S(2)}, u32[]{:S(2)}) collective-permute-start(f32[1,8,128]{2,1,0:T(8,128)S(1)} %get-tuple-element.107), channel_id=1, source_target_pairs={{0,16},{16,32},{32,48},{48,64},{64,80},{80,96},{96,112},{112,128},... | collective-permute-start | bytes 12296 | tf_op jit(solution)/shard_map/ppermute | solution.py:23
  144.1 5.2 %collective-permute-start.23 = (f32[6,1,128]{2,1,0:T(1,128)S(1)}, f32[6,1,128]{2,1,0:T(1,128)S(1)}, u32[]{:S(2)}, u32[]{:S(2)}) collective-permute-start(f32[6,1,128]{2,1,0:T(1,128)S(1)} %get-tuple-element.92), channel_id=1, source_target_pairs={{0,1},{1,2},{2,3},{3,4},{4,5},{5,6},{6,7},{7,8},{8,9},{9,10},{10,1... | collective-permute-start | bytes 9224 | tf_op jit(solution)/shard_map/ppermute | solution.py:23
  151.3 8.9 %collective-permute-start.24 = (bf16[1,10,128]{2,1,0:T(8,128)(2,1)S(1)}, bf16[1,10,128]{2,1,0:T(8,128)(2,1)S(1)}, u32[]{:S(2)}, u32[]{:S(2)}) collective-permute-start(bf16[1,10,128]{2,1,0:T(8,128)(2,1)S(1)} %get-tuple-element.85), channel_id=1, source_target_pairs={{0,16},{16,32},{32,48},{48,64},{64,80},{80,96},{96,112},{112,128},... | collective-permute-start | bytes 7688 | tf_op jit(solution)/shard_map/ppermute | solution.py:36
  162.2 6.9 %collective-permute-done.25 = bf16[1,10,128]{2,1,0:T(8,128)(2,1)S(1)} collective-permute-done((bf16[1,10,128]{2,1,0:T(8,128)(2,1)S(1)}, bf16[1,10,128]{2,1,0:T(8,128)(2,1)S(1)}, u32[]{:S(2)}, u32[]{:S(2)}) %collective-permute-start.25) | collective-permute-done | bytes 2592 | tf_op jit(solution)/shard_map/ppermute | solution.py:36
  169.2 5.7 %collective-permute-start.26 = (bf16[4,1,128]{2,1,0:T(2,128)(2,1)S(1)}, bf16[4,1,128]{2,1,0:T(2,128)(2,1)S(1)}, u32[]{:S(2)}, u32[]{:S(2)}) collective-permute-start(bf16[4,1,128]{2,1,0:T(2,128)(2,1)S(1)} %get-tuple-element.104), channel_id=1, source_target_pairs={{0,1},{1,2},{2,3},{3,4},{4,5},{5,6},{6,7},{7,8},{8,9},{9,10},{10,1... | collective-permute-start | bytes 3080 | tf_op jit(solution)/shard_map/ppermute | solution.py:36
  176.2 5.7 %collective-permute-done.27 = bf16[4,1,128]{2,1,0:T(2,128)(2,1)S(1)} collective-permute-done((bf16[4,1,128]{2,1,0:T(2,128)(2,1)S(1)}, bf16[4,1,128]{2,1,0:T(2,128)(2,1)S(1)}, u32[]{:S(2)}, u32[]{:S(2)}) %collective-permute-start.27) | collective-permute-done | bytes 1056 | tf_op jit(solution)/shard_map/ppermute | solution.py:36
  182.7 3.1 collective-permute-start.28
  187.7 6.9 %collective-permute-done.29 = bf16[1,10,128]{2,1,0:T(8,128)(2,1)S(1)} collective-permute-done((bf16[1,10,128]{2,1,0:T(8,128)(2,1)S(1)}, bf16[1,10,128]{2,1,0:T(8,128)(2,1)S(1)}, u32[]{:S(2)}, u32[]{:S(2)}) %collective-permute-start.29) | collective-permute-done | bytes 2592 | tf_op jit(solution)/shard_map/ppermute | solution.py:36
  194.7 6.0 %collective-permute-start.30 = (bf16[4,1,128]{2,1,0:T(2,128)(2,1)S(1)}, bf16[4,1,128]{2,1,0:T(2,128)(2,1)S(1)}, u32[]{:S(2)}, u32[]{:S(2)}) collective-permute-start(bf16[4,1,128]{2,1,0:T(2,128)(2,1)S(1)} %get-tuple-element.102), channel_id=1, source_target_pairs={{0,1},{1,2},{2,3},{3,4},{4,5},{5,6},{6,7},{7,8},{8,9},{9,10},{10,1... | collective-permute-start | bytes 3080 | tf_op jit(solution)/shard_map/ppermute | solution.py:36
  202.1 5.7 %collective-permute-done.31 = bf16[4,1,128]{2,1,0:T(2,128)(2,1)S(1)} collective-permute-done((bf16[4,1,128]{2,1,0:T(2,128)(2,1)S(1)}, bf16[4,1,128]{2,1,0:T(2,128)(2,1)S(1)}, u32[]{:S(2)}, u32[]{:S(2)}) %collective-permute-start.31) | collective-permute-done | bytes 1056 | tf_op jit(solution)/shard_map/ppermute | solution.py:36
  208.6 3.1 collective-permute-start.32
  213.6 6.9 %collective-permute-done.33 = bf16[1,10,128]{2,1,0:T(8,128)(2,1)S(1)} collective-permute-done((bf16[1,10,128]{2,1,0:T(8,128)(2,1)S(1)}, bf16[1,10,128]{2,1,0:T(8,128)(2,1)S(1)}, u32[]{:S(2)}, u32[]{:S(2)}) %collective-permute-start.33) | collective-permute-done | bytes 2592 | tf_op jit(solution)/shard_map/ppermute | solution.py:36
  221.8 6.3 %collective-permute-start.34 = (bf16[4,1,128]{2,1,0:T(2,128)(2,1)}, bf16[4,1,128]{2,1,0:T(2,128)(2,1)}, u32[]{:S(2)}, u32[]{:S(2)}) collective-permute-start(bf16[4,1,128]{2,1,0:T(2,128)(2,1)} %get-tuple-element.100), channel_id=1, source_target_pairs={{0,1},{1,2},{2,3},{3,4},{4,5},{5,6},{6,7},{7,8},{8,9},{9,10},{10,1... | collective-permute-start | bytes 3080 | tf_op jit(solution)/shard_map/ppermute | solution.py:36
  229.6 6.7 %copy.62 = bf16[16,1,6,10,130]{0,1,4,3,2:T(2,128)(2,1)} copy(bf16[16,1,6,10,130]{4,0,3,2,1:T(8,128)(2,1)S(1)} %copy-done.4) | data formatting | bytes 499200 | tf_op jit(solution)/shard_map/broadcast_in_dim | solution.py:84
  236.4 6.7 %copy.64 = bf16[16,1,6,10,130]{0,1,4,3,2:T(2,128)(2,1)} copy(bf16[16,1,6,10,130]{4,0,3,2,1:T(8,128)(2,1)S(1)} %copy-done.5) | data formatting | bytes 499200 | tf_op jit(solution)/shard_map/broadcast_in_dim | solution.py:84
  248.0 3.8 copy.65
  256.4 8.0 %convolution_select_fusion.1 = f32[6,10,8,17,16]{4,2,3,1,0:T(8,128)} fusion(bf16[16,16,3,3,3]{1,0,4,3,2:T(8,128)(2,1)S(1)} %copy-done, pred[8,17]{0,1:T(8,128)(4,1)S(1)} %copy-done.25, bf16[16,4,8,1,7,2]{0,4,5,2,1,3:T(8,128)(2,1)S(1)} %slice.482, bf16[16,4,8,1,8,17]{0,4,5,2,1,3:T(8,128)(2,1)} %copy.56), kind=kOutput, calls=%fused_computation.19 | convolution fusion | flops 60759552 | bytes 689800 | tf_op jit(solution)/shard_map/conv_general_dilated | solution.py:95
  264.4 6.2 %copy.57 = f32[6,10,8,17,16]{3,2,4,1,0:T(8,128)} copy(f32[6,10,8,17,16]{4,2,3,1,0:T(8,128)} %convolution_select_fusion.1) | data formatting | bytes 1044480 | tf_op jit(solution)/shard_map/conv_general_dilated | solution.py:95
  270.6 3.2 reshape.79
  278.7 29.5 %fusion.120 = f32[16,16,3,3,3]{0,1,4,3,2:T(8,128)S(1)} fusion(bf16[16,1,6,10,130]{0,1,4,3,2:T(2,128)(2,1)} %copy.64, bf16[16,1,4,8,128]{0,1,4,3,2:T(2,128)(2,1)} %copy.65), kind=kOutput, calls=%fused_computation.275 | convolution fusion | flops 56623104 | bytes 408320 | tf_op jit(solution)/shard_map/transpose | solution.py:91
  308.5 4.1 collective-permute-start.38
  314.3 3.2 collective-permute-done.39
  320.5 6.7 %convolution_select_fusion = f32[6,10,8,17,16]{4,2,3,1,0:T(8,128)} fusion(bf16[16,16,3,3,3]{1,0,4,3,2:T(8,128)(2,1)S(1)} %copy-done.24, pred[8,17]{0,1:T(8,128)(4,1)S(1)} %copy-done.25, bf16[16,4,8,1,7,2]{0,4,5,2,1,3:T(8,128)(2,1)S(1)} %slice.490, bf16[16,4,8,1,8,17]{0,4,5,2,1,3:T(8,128)(2,1)S(1)} %copy.60), kind=kOutput, calls=%fused_computation.18 | convolution fusion | flops 60759552 | bytes 689800 | tf_op jit(solution)/shard_map/conv_general_dilated | solution.py:95
  327.3 6.3 %copy.61 = f32[6,10,8,17,16]{3,2,4,1,0:T(8,128)} copy(f32[6,10,8,17,16]{4,2,3,1,0:T(8,128)} %convolution_select_fusion) | data formatting | bytes 1044480 | tf_op jit(solution)/shard_map/conv_general_dilated | solution.py:95
  333.6 3.2 reshape.86
  339.6 29.8 %fusion.119 = f32[16,16,3,3,3]{0,1,4,3,2:T(8,128)} fusion(bf16[16,1,6,10,130]{0,1,4,3,2:T(2,128)(2,1)} %copy.62, bf16[16,1,4,8,128]{0,1,4,3,2:T(2,128)(2,1)S(1)} %copy.63), kind=kOutput, calls=%fused_computation.274 | convolution fusion | flops 56623104 | bytes 408320 | tf_op jit(solution)/shard_map/transpose | solution.py:91
  369.4 119.2 %all-reduce.47 = (f32[16,16,3,3,3]{0,1,4,3,2:T(8,128)S(1)}, f32[16,16,3,3,3]{0,1,4,3,2:T(8,128)S(1)}, f32[16]{0:T(128)S(1)}) all-reduce(f32[16,16,3,3,3]{0,1,4,3,2:T(8,128)} %fusion.119, f32[16,16,3,3,3]{0,1,4,3,2:T(8,128)S(1)} %fusion.120, f32[16]{0:T(128)S(1)} %convolution_bitcast_fusion), channel_id=1, replica_groups=mesh['gz'=32,'gy'=16] {'gz','gy'}, use_global_device_ids=true, to_apply=%region_0.1 | all-reduce | flops 13840 | bytes 110720 | tf_op jit(solution)/shard_map/psum | solution.py:166
  492.9 2.9 collective-permute-start.40
  497.9 7.4 %collective-permute-done.41 = bf16[16,1,10,128]{3,0,2,1:T(8,128)(2,1)S(1)} collective-permute-done((bf16[16,1,10,128]{3,0,2,1:T(8,128)(2,1)S(1)}, bf16[16,1,10,128]{3,0,2,1:T(8,128)(2,1)S(1)}, u32[]{:S(2)}, u32[]{:S(2)}) %collective-permute-start.41) | collective-permute-done | bytes 40992 | tf_op jit(solution)/shard_map/ppermute | solution.py:36
  505.4 2.9 collective-permute-start.42
  (210 shorter events, 86.8 us)
Async XLA Ops:
  1.5 12.9 %collective-permute-start = (bf16[16,1,8,128]{3,0,2,1:T(8,128)(2,1)S(1)}, bf16[16,1,8,128]{3,0,2,1:T(8,128)(2,1)S(1)}, u32[]{:S(2)}, u32[]{:S(2)}) collective-permute-start(bf16[16,1,8,128]{3,0,2,1:T(8,128)(2,1)S(1)} %copy.83), channel_id=1, source_target_pairs={{0,16},{16,32},{32,48},{48,64},{64,80},{80,96},{96,112},{112,128},... | collective-permute-start | bytes 98312 | tf_op jit(solution)/shard_map/ppermute | solution.py:23
  11.7 9.1 %collective-permute-start.1 = (bf16[16,1,8,128]{3,0,2,1:T(8,128)(2,1)S(1)}, bf16[16,1,8,128]{3,0,2,1:T(8,128)(2,1)S(1)}, u32[]{:S(2)}, u32[]{:S(2)}) collective-permute-start(bf16[16,1,8,128]{3,0,2,1:T(8,128)(2,1)S(1)} %copy.84), channel_id=1, source_target_pairs={{16,0},{32,16},{48,32},{64,48},{80,64},{96,80},{112,96},{128,112},... | collective-permute-start | bytes 98312 | tf_op jit(solution)/shard_map/ppermute | solution.py:24
  20.9 13.9 %collective-permute-start.2 = (bf16[16,6,1,128]{3,0,2,1:T(8,128)(2,1)S(1)}, bf16[16,6,1,128]{3,0,2,1:T(8,128)(2,1)S(1)}, u32[]{:S(2)}, u32[]{:S(2)}) collective-permute-start(bf16[16,6,1,128]{3,0,2,1:T(8,128)(2,1)S(1)} %get-tuple-element.59), channel_id=1, source_target_pairs={{0,1},{1,2},{2,3},{3,4},{4,5},{5,6},{6,7},{7,8},{8,9},{9,10},{10,1... | collective-permute-start | bytes 73736 | tf_op jit(solution)/shard_map/ppermute | solution.py:23
  24.0 10.8 %collective-permute-start.3 = (bf16[16,6,1,128]{3,0,2,1:T(8,128)(2,1)S(1)}, bf16[16,6,1,128]{3,0,2,1:T(8,128)(2,1)S(1)}, u32[]{:S(2)}, u32[]{:S(2)}) collective-permute-start(bf16[16,6,1,128]{3,0,2,1:T(8,128)(2,1)S(1)} %get-tuple-element.60), channel_id=1, source_target_pairs={{1,0},{2,1},{3,2},{4,3},{5,4},{6,5},{7,6},{8,7},{9,8},{10,9},{11,1... | collective-permute-start | bytes 73736 | tf_op jit(solution)/shard_map/ppermute | solution.py:24
  25.3 33.3 %collective-permute-start.8 = (f32[1,8,128]{2,1,0:T(8,128)S(1)}, f32[1,8,128]{2,1,0:T(8,128)S(1)}, u32[]{:S(2)}, u32[]{:S(2)}) collective-permute-start(f32[1,8,128]{2,1,0:T(8,128)S(1)} %get-tuple-element.114), channel_id=1, source_target_pairs={{16,0},{32,16},{48,32},{64,48},{80,64},{96,80},{112,96},{128,112},... | collective-permute-start | bytes 12296 | tf_op jit(solution)/shard_map/ppermute | solution.py:24
  27.2 31.4 %collective-permute-start.9 = (f32[1,8,128]{2,1,0:T(8,128)S(1)}, f32[1,8,128]{2,1,0:T(8,128)S(1)}, u32[]{:S(2)}, u32[]{:S(2)}) collective-permute-start(f32[1,8,128]{2,1,0:T(8,128)S(1)} %get-tuple-element.113), channel_id=1, source_target_pairs={{0,16},{16,32},{32,48},{48,64},{64,80},{80,96},{96,112},{112,128},... | collective-permute-start | bytes 12296 | tf_op jit(solution)/shard_map/ppermute | solution.py:23
  53.1 11.5 %collective-permute-start.4 = (bf16[16,1,8,128]{3,0,2,1:T(8,128)(2,1)S(1)}, bf16[16,1,8,128]{3,0,2,1:T(8,128)(2,1)S(1)}, u32[]{:S(2)}, u32[]{:S(2)}) collective-permute-start(bf16[16,1,8,128]{3,0,2,1:T(8,128)(2,1)S(1)} %get-tuple-element.65), channel_id=1, source_target_pairs={{0,16},{16,32},{32,48},{48,64},{64,80},{80,96},{96,112},{112,128},... | collective-permute-start | bytes 98312 | tf_op jit(solution)/shard_map/ppermute | solution.py:23
  56.7 9.1 %collective-permute-start.5 = (bf16[16,1,8,128]{3,0,2,1:T(8,128)(2,1)S(1)}, bf16[16,1,8,128]{3,0,2,1:T(8,128)(2,1)S(1)}, u32[]{:S(2)}, u32[]{:S(2)}) collective-permute-start(bf16[16,1,8,128]{3,0,2,1:T(8,128)(2,1)S(1)} %get-tuple-element.66), channel_id=1, source_target_pairs={{16,0},{32,16},{48,32},{64,48},{80,64},{96,80},{112,96},{128,112},... | collective-permute-start | bytes 98312 | tf_op jit(solution)/shard_map/ppermute | solution.py:24
  58.7 12.6 %collective-permute-start.10 = (f32[6,1,128]{2,1,0:T(1,128)S(1)}, f32[6,1,128]{2,1,0:T(1,128)S(1)}, u32[]{:S(2)}, u32[]{:S(2)}) collective-permute-start(f32[6,1,128]{2,1,0:T(1,128)S(1)} %get-tuple-element.99), channel_id=1, source_target_pairs={{1,0},{2,1},{3,2},{4,3},{5,4},{6,5},{7,6},{8,7},{9,8},{10,9},{11,1... | collective-permute-start | bytes 9224 | tf_op jit(solution)/shard_map/ppermute | solution.py:24
  60.0 11.4 %collective-permute-start.11 = (f32[6,1,128]{2,1,0:T(1,128)S(1)}, f32[6,1,128]{2,1,0:T(1,128)S(1)}, u32[]{:S(2)}, u32[]{:S(2)}) collective-permute-start(f32[6,1,128]{2,1,0:T(1,128)S(1)} %get-tuple-element.98), channel_id=1, source_target_pairs={{0,1},{1,2},{2,3},{3,4},{4,5},{5,6},{6,7},{7,8},{8,9},{9,10},{10,1... | collective-permute-start | bytes 9224 | tf_op jit(solution)/shard_map/ppermute | solution.py:23
  65.8 5.7 %collective-permute-start.6 = (bf16[16,6,1,128]{3,0,2,1:T(8,128)(2,1)S(1)}, bf16[16,6,1,128]{3,0,2,1:T(8,128)(2,1)S(1)}, u32[]{:S(2)}, u32[]{:S(2)}) collective-permute-start(bf16[16,6,1,128]{3,0,2,1:T(8,128)(2,1)S(1)} %get-tuple-element.57), channel_id=1, source_target_pairs={{0,1},{1,2},{2,3},{3,4},{4,5},{5,6},{6,7},{7,8},{8,9},{9,10},{10,1... | collective-permute-start | bytes 73736 | tf_op jit(solution)/shard_map/ppermute | solution.py:23
  69.8 4.6 collective-permute-start.7
  94.6 135.0 %copy-start.4 = (bf16[16,1,6,10,130]{4,0,3,2,1:T(8,128)(2,1)S(1)}, bf16[16,1,6,10,130]{4,0,3,2,1:T(8,128)(2,1)}, u32[]{:S(2)}) copy-start(bf16[16,1,6,10,130]{4,0,3,2,1:T(8,128)(2,1)} %get-tuple-element.55) | copy-start | bytes 748804
  95.1 9.9 %collective-permute-start.12 = (f32[1,8,128]{2,1,0:T(8,128)S(1)}, f32[1,8,128]{2,1,0:T(8,128)S(1)}, u32[]{:S(2)}, u32[]{:S(2)}) collective-permute-start(f32[1,8,128]{2,1,0:T(8,128)S(1)} %get-tuple-element.112), channel_id=1, source_target_pairs={{16,0},{32,16},{48,32},{64,48},{80,64},{96,80},{112,96},{128,112},... | collective-permute-start | bytes 12296 | tf_op jit(solution)/shard_map/ppermute | solution.py:24
  97.0 8.7 %collective-permute-start.13 = (f32[1,8,128]{2,1,0:T(8,128)S(1)}, f32[1,8,128]{2,1,0:T(8,128)S(1)}, u32[]{:S(2)}, u32[]{:S(2)}) collective-permute-start(f32[1,8,128]{2,1,0:T(8,128)S(1)} %get-tuple-element.111), channel_id=1, source_target_pairs={{0,16},{16,32},{32,48},{48,64},{64,80},{80,96},{96,112},{112,128},... | collective-permute-start | bytes 12296 | tf_op jit(solution)/shard_map/ppermute | solution.py:23
  105.7 6.1 %collective-permute-start.14 = (f32[6,1,128]{2,1,0:T(1,128)S(1)}, f32[6,1,128]{2,1,0:T(1,128)S(1)}, u32[]{:S(2)}, u32[]{:S(2)}) collective-permute-start(f32[6,1,128]{2,1,0:T(1,128)S(1)} %get-tuple-element.97), channel_id=1, source_target_pairs={{1,0},{2,1},{3,2},{4,3},{5,4},{6,5},{7,6},{8,7},{9,8},{10,9},{11,1... | collective-permute-start | bytes 9224 | tf_op jit(solution)/shard_map/ppermute | solution.py:24
  107.0 5.6 %collective-permute-start.15 = (f32[6,1,128]{2,1,0:T(1,128)S(1)}, f32[6,1,128]{2,1,0:T(1,128)S(1)}, u32[]{:S(2)}, u32[]{:S(2)}) collective-permute-start(f32[6,1,128]{2,1,0:T(1,128)S(1)} %get-tuple-element.96), channel_id=1, source_target_pairs={{0,1},{1,2},{2,3},{3,4},{4,5},{5,6},{6,7},{7,8},{8,9},{9,10},{10,1... | collective-permute-start | bytes 9224 | tf_op jit(solution)/shard_map/ppermute | solution.py:23
  112.8 123.6 %copy-start.10 = (f32[4,8,128]{2,1,0:T(8,128)}, f32[4,8,128]{2,1,0:T(8,128)S(1)}, u32[]{:S(2)}) copy-start(f32[4,8,128]{2,1,0:T(8,128)S(1)} %get-tuple-element.46) | copy-start | bytes 49156
  112.8 10.9 %collective-permute-start.16 = (f32[1,8,128]{2,1,0:T(8,128)S(1)}, f32[1,8,128]{2,1,0:T(8,128)S(1)}, u32[]{:S(2)}, u32[]{:S(2)}) collective-permute-start(f32[1,8,128]{2,1,0:T(8,128)S(1)} %get-tuple-element.110), channel_id=1, source_target_pairs={{16,0},{32,16},{48,32},{64,48},{80,64},{96,80},{112,96},{128,112},... | collective-permute-start | bytes 12296 | tf_op jit(solution)/shard_map/ppermute | solution.py:24
  114.7 9.7 %collective-permute-start.17 = (f32[1,8,128]{2,1,0:T(8,128)S(1)}, f32[1,8,128]{2,1,0:T(8,128)S(1)}, u32[]{:S(2)}, u32[]{:S(2)}) collective-permute-start(f32[1,8,128]{2,1,0:T(8,128)S(1)} %get-tuple-element.109), channel_id=1, source_target_pairs={{0,16},{16,32},{32,48},{48,64},{64,80},{80,96},{96,112},{112,128},... | collective-permute-start | bytes 12296 | tf_op jit(solution)/shard_map/ppermute | solution.py:23
  124.4 5.8 %collective-permute-start.18 = (f32[6,1,128]{2,1,0:T(1,128)S(1)}, f32[6,1,128]{2,1,0:T(1,128)S(1)}, u32[]{:S(2)}, u32[]{:S(2)}) collective-permute-start(f32[6,1,128]{2,1,0:T(1,128)S(1)} %get-tuple-element.95), channel_id=1, source_target_pairs={{1,0},{2,1},{3,2},{4,3},{5,4},{6,5},{7,6},{8,7},{9,8},{10,9},{11,1... | collective-permute-start | bytes 9224 | tf_op jit(solution)/shard_map/ppermute | solution.py:24
  125.7 5.3 %collective-permute-start.19 = (f32[6,1,128]{2,1,0:T(1,128)S(1)}, f32[6,1,128]{2,1,0:T(1,128)S(1)}, u32[]{:S(2)}, u32[]{:S(2)}) collective-permute-start(f32[6,1,128]{2,1,0:T(1,128)S(1)} %get-tuple-element.94), channel_id=1, source_target_pairs={{0,1},{1,2},{2,3},{3,4},{4,5},{5,6},{6,7},{7,8},{8,9},{9,10},{10,1... | collective-permute-start | bytes 9224 | tf_op jit(solution)/shard_map/ppermute | solution.py:23
  131.2 105.2 %copy-start.11 = (f32[4,8,128]{2,1,0:T(8,128)}, f32[4,8,128]{2,1,0:T(8,128)S(1)}, u32[]{:S(2)}) copy-start(f32[4,8,128]{2,1,0:T(8,128)S(1)} %get-tuple-element.44) | copy-start | bytes 49156
  131.2 10.9 %collective-permute-start.20 = (f32[1,8,128]{2,1,0:T(8,128)S(1)}, f32[1,8,128]{2,1,0:T(8,128)S(1)}, u32[]{:S(2)}, u32[]{:S(2)}) collective-permute-start(f32[1,8,128]{2,1,0:T(8,128)S(1)} %get-tuple-element.108), channel_id=1, source_target_pairs={{16,0},{32,16},{48,32},{64,48},{80,64},{96,80},{112,96},{128,112},... | collective-permute-start | bytes 12296 | tf_op jit(solution)/shard_map/ppermute | solution.py:24
  133.1 9.7 %collective-permute-start.21 = (f32[1,8,128]{2,1,0:T(8,128)S(1)}, f32[1,8,128]{2,1,0:T(8,128)S(1)}, u32[]{:S(2)}, u32[]{:S(2)}) collective-permute-start(f32[1,8,128]{2,1,0:T(8,128)S(1)} %get-tuple-element.107), channel_id=1, source_target_pairs={{0,16},{16,32},{32,48},{48,64},{64,80},{80,96},{96,112},{112,128},... | collective-permute-start | bytes 12296 | tf_op jit(solution)/shard_map/ppermute | solution.py:23
  142.8 6.5 %collective-permute-start.22 = (f32[6,1,128]{2,1,0:T(1,128)S(1)}, f32[6,1,128]{2,1,0:T(1,128)S(1)}, u32[]{:S(2)}, u32[]{:S(2)}) collective-permute-start(f32[6,1,128]{2,1,0:T(1,128)S(1)} %get-tuple-element.93), channel_id=1, source_target_pairs={{1,0},{2,1},{3,2},{4,3},{5,4},{6,5},{7,6},{8,7},{9,8},{10,9},{11,1... | collective-permute-start | bytes 9224 | tf_op jit(solution)/shard_map/ppermute | solution.py:24
  144.1 6.0 %collective-permute-start.23 = (f32[6,1,128]{2,1,0:T(1,128)S(1)}, f32[6,1,128]{2,1,0:T(1,128)S(1)}, u32[]{:S(2)}, u32[]{:S(2)}) collective-permute-start(f32[6,1,128]{2,1,0:T(1,128)S(1)} %get-tuple-element.92), channel_id=1, source_target_pairs={{0,1},{1,2},{2,3},{3,4},{4,5},{5,6},{6,7},{7,8},{8,9},{9,10},{10,1... | collective-permute-start | bytes 9224 | tf_op jit(solution)/shard_map/ppermute | solution.py:23
  151.3 10.9 %collective-permute-start.24 = (bf16[1,10,128]{2,1,0:T(8,128)(2,1)S(1)}, bf16[1,10,128]{2,1,0:T(8,128)(2,1)S(1)}, u32[]{:S(2)}, u32[]{:S(2)}) collective-permute-start(bf16[1,10,128]{2,1,0:T(8,128)(2,1)S(1)} %get-tuple-element.85), channel_id=1, source_target_pairs={{0,16},{16,32},{32,48},{48,64},{64,80},{80,96},{96,112},{112,128},... | collective-permute-start | bytes 7688 | tf_op jit(solution)/shard_map/ppermute | solution.py:36
  160.2 8.8 %collective-permute-start.25 = (bf16[1,10,128]{2,1,0:T(8,128)(2,1)S(1)}, bf16[1,10,128]{2,1,0:T(8,128)(2,1)S(1)}, u32[]{:S(2)}, u32[]{:S(2)}) collective-permute-start(bf16[1,10,128]{2,1,0:T(8,128)(2,1)S(1)} %get-tuple-element.86), channel_id=1, source_target_pairs={{16,0},{32,16},{48,32},{64,48},{80,64},{96,80},{112,96},{128,112},... | collective-permute-start | bytes 7688 | tf_op jit(solution)/shard_map/ppermute | solution.py:36
  169.2 7.1 %collective-permute-start.26 = (bf16[4,1,128]{2,1,0:T(2,128)(2,1)S(1)}, bf16[4,1,128]{2,1,0:T(2,128)(2,1)S(1)}, u32[]{:S(2)}, u32[]{:S(2)}) collective-permute-start(bf16[4,1,128]{2,1,0:T(2,128)(2,1)S(1)} %get-tuple-element.104), channel_id=1, source_target_pairs={{0,1},{1,2},{2,3},{3,4},{4,5},{5,6},{6,7},{7,8},{8,9},{9,10},{10,1... | collective-permute-start | bytes 3080 | tf_op jit(solution)/shard_map/ppermute | solution.py:36
  174.9 7.0 %collective-permute-start.27 = (bf16[4,1,128]{2,1,0:T(2,128)(2,1)S(1)}, bf16[4,1,128]{2,1,0:T(2,128)(2,1)S(1)}, u32[]{:S(2)}, u32[]{:S(2)}) collective-permute-start(bf16[4,1,128]{2,1,0:T(2,128)(2,1)S(1)} %get-tuple-element.105), channel_id=1, source_target_pairs={{1,0},{2,1},{3,2},{4,3},{5,4},{6,5},{7,6},{8,7},{9,8},{10,9},{11,1... | collective-permute-start | bytes 3080 | tf_op jit(solution)/shard_map/ppermute | solution.py:36
  182.7 5.0 collective-permute-start.28
  185.8 8.8 %collective-permute-start.29 = (bf16[1,10,128]{2,1,0:T(8,128)(2,1)S(1)}, bf16[1,10,128]{2,1,0:T(8,128)(2,1)S(1)}, u32[]{:S(2)}, u32[]{:S(2)}) collective-permute-start(bf16[1,10,128]{2,1,0:T(8,128)(2,1)S(1)} %get-tuple-element.84), channel_id=1, source_target_pairs={{16,0},{32,16},{48,32},{64,48},{80,64},{96,80},{112,96},{128,112},... | collective-permute-start | bytes 7688 | tf_op jit(solution)/shard_map/ppermute | solution.py:36
  194.7 7.3 %collective-permute-start.30 = (bf16[4,1,128]{2,1,0:T(2,128)(2,1)S(1)}, bf16[4,1,128]{2,1,0:T(2,128)(2,1)S(1)}, u32[]{:S(2)}, u32[]{:S(2)}) collective-permute-start(bf16[4,1,128]{2,1,0:T(2,128)(2,1)S(1)} %get-tuple-element.102), channel_id=1, source_target_pairs={{0,1},{1,2},{2,3},{3,4},{4,5},{5,6},{6,7},{7,8},{8,9},{9,10},{10,1... | collective-permute-start | bytes 3080 | tf_op jit(solution)/shard_map/ppermute | solution.py:36
  200.7 7.0 %collective-permute-start.31 = (bf16[4,1,128]{2,1,0:T(2,128)(2,1)S(1)}, bf16[4,1,128]{2,1,0:T(2,128)(2,1)S(1)}, u32[]{:S(2)}, u32[]{:S(2)}) collective-permute-start(bf16[4,1,128]{2,1,0:T(2,128)(2,1)S(1)} %get-tuple-element.103), channel_id=1, source_target_pairs={{1,0},{2,1},{3,2},{4,3},{5,4},{6,5},{7,6},{8,7},{9,8},{10,9},{11,1... | collective-permute-start | bytes 3080 | tf_op jit(solution)/shard_map/ppermute | solution.py:36
  208.6 5.0 collective-permute-start.32
  211.7 8.8 %collective-permute-start.33 = (bf16[1,10,128]{2,1,0:T(8,128)(2,1)S(1)}, bf16[1,10,128]{2,1,0:T(8,128)(2,1)S(1)}, u32[]{:S(2)}, u32[]{:S(2)}) collective-permute-start(bf16[1,10,128]{2,1,0:T(8,128)(2,1)S(1)} %get-tuple-element.82), channel_id=1, source_target_pairs={{16,0},{32,16},{48,32},{64,48},{80,64},{96,80},{112,96},{128,112},... | collective-permute-start | bytes 7688 | tf_op jit(solution)/shard_map/ppermute | solution.py:36
  221.8 24.4 %collective-permute-start.34 = (bf16[4,1,128]{2,1,0:T(2,128)(2,1)}, bf16[4,1,128]{2,1,0:T(2,128)(2,1)}, u32[]{:S(2)}, u32[]{:S(2)}) collective-permute-start(bf16[4,1,128]{2,1,0:T(2,128)(2,1)} %get-tuple-element.100), channel_id=1, source_target_pairs={{0,1},{1,2},{2,3},{3,4},{4,5},{5,6},{6,7},{7,8},{8,9},{9,10},{10,1... | collective-permute-start | bytes 3080 | tf_op jit(solution)/shard_map/ppermute | solution.py:36
  228.1 18.1 %collective-permute-start.35 = (bf16[4,1,128]{2,1,0:T(2,128)(2,1)}, bf16[4,1,128]{2,1,0:T(2,128)(2,1)}, u32[]{:S(2)}, u32[]{:S(2)}) collective-permute-start(bf16[4,1,128]{2,1,0:T(2,128)(2,1)} %get-tuple-element.101), channel_id=1, source_target_pairs={{1,0},{2,1},{3,2},{4,3},{5,4},{6,5},{7,6},{8,7},{9,8},{10,9},{11,1... | collective-permute-start | bytes 3080 | tf_op jit(solution)/shard_map/ppermute | solution.py:36
  273.9 34.4 %collective-permute-start.36 = (bf16[16,1,10,128]{3,0,2,1:T(8,128)(2,1)S(1)}, bf16[16,1,10,128]{3,0,2,1:T(8,128)(2,1)S(1)}, u32[]{:S(2)}, u32[]{:S(2)}) collective-permute-start(bf16[16,1,10,128]{3,0,2,1:T(8,128)(2,1)S(1)} %get-tuple-element.51), channel_id=1, source_target_pairs={{0,16},{16,32},{32,48},{48,64},{64,80},{80,96},{96,112},{112,128},... | collective-permute-start | bytes 122888 | tf_op jit(solution)/shard_map/ppermute | solution.py:36
  276.2 32.1 %collective-permute-start.37 = (bf16[16,1,10,128]{3,0,2,1:T(8,128)(2,1)S(1)}, bf16[16,1,10,128]{3,0,2,1:T(8,128)(2,1)S(1)}, u32[]{:S(2)}, u32[]{:S(2)}) collective-permute-start(bf16[16,1,10,128]{3,0,2,1:T(8,128)(2,1)S(1)} %get-tuple-element.52), channel_id=1, source_target_pairs={{16,0},{32,16},{48,32},{64,48},{80,64},{96,80},{112,96},{128,112},... | collective-permute-start | bytes 122888 | tf_op jit(solution)/shard_map/ppermute | solution.py:36
  308.5 5.8 %collective-permute-start.38 = (bf16[16,4,1,128]{3,0,2,1:T(8,128)(2,1)S(1)}, bf16[16,4,1,128]{3,0,2,1:T(8,128)(2,1)S(1)}, u32[]{:S(2)}, u32[]{:S(2)}) collective-permute-start(bf16[16,4,1,128]{3,0,2,1:T(8,128)(2,1)S(1)} %get-tuple-element.63), channel_id=1, source_target_pairs={{0,1},{1,2},{2,3},{3,4},{4,5},{5,6},{6,7},{7,8},{8,9},{9,10},{10,1... | collective-permute-start | bytes 49160 | tf_op jit(solution)/shard_map/ppermute | solution.py:36
  312.6 5.0 collective-permute-start.39
  369.4 144.2 %copy-start.1 = (bf16[16,16,3,3,3]{1,0,4,3,2:T(8,128)(2,1)S(1)}, bf16[16,16,3,3,3]{1,0,4,3,2:T(8,128)(2,1)}, u32[]{:S(2)}) copy-start(bf16[16,16,3,3,3]{1,0,4,3,2:T(8,128)(2,1)} %param.10) | copy-start | bytes 41476
  492.9 4.9 collective-permute-start.40
  495.9 9.4 %collective-permute-start.41 = (bf16[16,1,10,128]{3,0,2,1:T(8,128)(2,1)S(1)}, bf16[16,1,10,128]{3,0,2,1:T(8,128)(2,1)S(1)}, u32[]{:S(2)}, u32[]{:S(2)}) collective-permute-start(bf16[16,1,10,128]{3,0,2,1:T(8,128)(2,1)S(1)} %get-tuple-element.50), channel_id=1, source_target_pairs={{16,0},{32,16},{48,32},{64,48},{80,64},{96,80},{112,96},{128,112},... | collective-permute-start | bytes 122888 | tf_op jit(solution)/shard_map/ppermute | solution.py:36
  505.4 6.4 %collective-permute-start.42 = (bf16[16,4,1,128]{3,0,2,1:T(8,128)(2,1)S(1)}, bf16[16,4,1,128]{3,0,2,1:T(8,128)(2,1)S(1)}, u32[]{:S(2)}, u32[]{:S(2)}) collective-permute-start(bf16[16,4,1,128]{3,0,2,1:T(8,128)(2,1)S(1)} %get-tuple-element.61), channel_id=1, source_target_pairs={{0,1},{1,2},{2,3},{3,4},{4,5},{5,6},{6,7},{7,8},{8,9},{9,10},{10,1... | collective-permute-start | bytes 49160 | tf_op jit(solution)/shard_map/ppermute | solution.py:36
  508.4 4.5 collective-permute-start.43
  (22 other events, 447.1 us)
where the time goes:
time: 524 us; the launch traced here: 514 us
  starting transfers between devices  155 us (30%)
  blocking collectives  119 us (23%)
  matrix products  86.3 us (16%)
  local copies, waits for them, and re-layouts  78.4 us (15%)
  waiting for transfers between devices  57.7 us (11%)
  other arithmetic  12.8 us (2%)
    psum x1, blocking collectives, on_device(): lax.psum((raw_first, raw_second, raw_speed), ('gz', 'gy'))  119 us
    ppermute x12, starting transfers between devices, extended(): before = lax.ppermute(last, axis, up)  73.4 us
    ppermute x20, starting transfers between devices, from_behind(): return lax.ppermute(block, axis, route)  62.2 us
    transpose x2, matrix products, weight_grad(): return d_weight.transpose(1, 0, 2, 3, 4)  59.3 us
    ppermute x20, waiting for transfers between devices, from_behind(): return lax.ppermute(block, axis, route)  43.7 us
    conv_general_dilated x10, local copies, waits for them, and re-layouts, conv_back(): lax.conv_general_dilated(d_out[None], flip_weight(weight), (1, 1, 1), ((2...  25.9 us
    conv_general_dilated x12, local copies, waits for them, and re-layouts, conv_local(): lax.conv_general_dilated(grid[None], weight, (1, 1, 1), 'VALID', dimensio...  22 us
    ppermute x12, starting transfers between devices, extended(): after = lax.ppermute(initial, axis, down)  19.4 us
  transfers between devices with their start and end apart: 44, of which 17 were waited for; matrix products, arithmetic and copies ran while one was open for 13% of the time, Pallas kernels for 0%

commit v1 on v0

v1 whole, which is shorter than its diff:
```python
import jax
import jax.numpy as jnp
from jax import lax
from jax.experimental import pallas as pl
from jax.experimental.pallas import tpu as pltpu
from jax.sharding import PartitionSpec as P

C = 16
BZ = 4
BY = 8
X = 128
TAPS = 27 * C
A = 0.25
FLOOR = 0.1
SENT = jnp.bfloat16
f32 = jnp.float32
bf16 = jnp.bfloat16


def sides(v):
    axis = v.ndim - 1
    lane = lax.broadcasted_iota(jnp.int32, v.shape, axis)
    low = jnp.where(lane == 0, 0.0, pltpu.roll(v, 1, axis))
    up = jnp.where(lane == X - 1, 0.0, pltpu.roll(v, X - 1, axis))
    return low, up


def put_taps(ref, index, v):
    low, up = sides(v)
    ref[index, :, 0] = low.astype(bf16)
    ref[index, :, 1] = v.astype(bf16)
    ref[index, :, 2] = up.astype(bf16)


def two_rows(weight, taps_ref, z, y):
    patch = taps_ref[pl.ds(z, 3), y : y + 4].reshape(4 * 9 * C, X)
    out = jnp.dot(weight, patch, preferred_element_type=f32)
    return out[:C], out[C:]


def inside(start, shape, limit):
    row = start + lax.broadcasted_iota(jnp.int32, shape, 0)
    return (row >= 0) & (row < limit)


def prepare(at, f_ref, s_ref, ft_ref, me_ref, mo_ref):
    py = at[3]
    row = lax.broadcasted_iota(jnp.int32, (BY, X), 0)
    for z in range(BZ):
        ft_ref[z] = jnp.transpose(f_ref[:, z].astype(f32), (1, 0, 2)).astype(bf16)
    for ref, start, high in ((me_ref, 6 - 6 * py, py == 0), (mo_ref, 6 * py, py == 1)):
        for z in range(BZ):
            ref[2 * z : 2 * z + 2] = ft_ref[z, pl.ds(start, 2)]
        parts = []
        for z in range(BZ):
            own = s_ref[z].astype(f32)
            parts.append(jnp.where(high, pltpu.roll(own, 4, 0), own))
        halves = [jnp.where(row < 4, parts[i], pltpu.roll(parts[i + 1], 4, 0)) for i in (0, 2)]
        ref[2 * BZ] = jnp.concatenate(halves, axis=0).astype(bf16)


def extend(at, ft_ref, s_ref, re_ref, ro_ref, fy_ref, sy_ref, ma_ref, mb_ref):
    pz, py = at[2], at[3]
    row = lax.broadcasted_iota(jnp.int32, (BY, X), 0)
    te = re_ref[2 * BZ].astype(f32)
    to = ro_ref[2 * BZ].astype(f32)
    before = jnp.where(py == 0, to, te)
    after = jnp.where(py == 0, te, to)
    for z in range(BZ):
        fy_ref[z, 2 : 2 + BY] = ft_ref[z]
        fy_ref[z, pl.ds(10 - 10 * py, 2)] = re_ref[2 * z : 2 * z + 2]
        fy_ref[z, pl.ds(10 * py, 2)] = ro_ref[2 * z : 2 * z + 2]
        half, low = (z // 2) * 8, (z % 2) * 4
        own = pltpu.roll(s_ref[z].astype(f32), 4, 0)
        b = before[half : half + 8]
        a = after[half : half + 8]
        b = pltpu.roll(b, 4, 0) if low else b
        a = a if low else pltpu.roll(a, 4, 0)
        sy_ref[z] = jnp.concatenate([jnp.where(row < 4, b, own), jnp.where(row < 4, own, a)], axis=0)
    for ref, start, sign in ((ma_ref, 2 - 2 * pz, 1 - pz), (mb_ref, 2 * pz, pz)):
        for k in range(2):
            ref[12 * k : 12 * k + 12] = fy_ref[start + k]
        for k in range(3):
            ref[24 + k] = sy_ref[sign + k].astype(bf16)


def forward(nz, ny, at, fy_ref, sy_ref, ma_ref, mb_ref, lab_ref, w1_ref, w2_ref, sw_ref,
            fx_ref, hx_ref, slope1_ref, slope2_ref, top_ref, fields_ref, own_ref, g0_ref, p_ref):
    iz, iy, pz = at[0], at[1], at[2]
    for k in range(BZ):
        put_taps(fx_ref, 2 + k, fy_ref[k].astype(f32))
    for k in range(2):
        put_taps(fx_ref, 6 - 6 * pz + k, ma_ref[12 * k : 12 * k + 12].astype(f32))
        put_taps(fx_ref, 6 * pz + k, mb_ref[12 * k : 12 * k + 12].astype(f32))
    w1 = w1_ref[...]
    w2 = w2_ref[...]

    def first(z, carry):
        zg = iz * BZ - 1 + z
        zin = (zg >= 0) & (zg < nz)
        for y in range(0, BY + 2, 2):
            acts = two_rows(w1, fx_ref, z, y)
            hid = []
            for j, act in enumerate(acts):
                yg = iy * BY - 1 + y + j
                keep = jnp.where(zin & (yg >= 0) & (yg < ny), 1.0, 0.0)
                sig = jax.nn.sigmoid(act)
                slope1_ref[z, y + j] = sig * (1.0 + act * (1.0 - sig)) * keep
                hid.append((act * sig * keep)[None])
            hid = jnp.concatenate(hid, axis=0)
            low, up = sides(hid)
            hx_ref[z, y : y + 2, 0] = low.astype(bf16)
            hx_ref[z, y : y + 2, 1] = hid.astype(bf16)
            hx_ref[z, y : y + 2, 2] = up.astype(bf16)
        return carry

    lax.fori_loop(0, BZ + 2, first, 0)
    sw = sw_ref[...]

    def second(z, carry):
        rows = []
        for y in range(0, BY, 2):
            for j, act in enumerate(two_rows(w2, hx_ref, z, y)):
                sig = jax.nn.sigmoid(act)
                top = act * sig
                top_ref[z, y + j] = top
                slope2_ref[z, y + j] = sig * (1.0 + act * (1.0 - sig))
                rows.append(jnp.sum(top * sw, axis=0, keepdims=True))
        own_ref[0, z] = jnp.tanh(jnp.concatenate(rows, axis=0))
        return carry

    lax.fori_loop(0, BZ, second, 0)

    for k in range(BZ):
        p_ref[3 + k] = sy_ref[k]
    for k in range(3):
        p_ref[7 - 7 * pz + k] = ma_ref[24 + k].astype(f32)
        p_ref[7 * pz + k] = mb_ref[24 + k].astype(f32)
    rows_in = inside(iy * BY - 4, (16, X), ny)
    for k in range(10):
        zg = iz * BZ - 3 + k
        p_ref[k] = jnp.where(rows_in & (zg >= 0) & (zg < nz), 2.0 * p_ref[k] - 1.0, 0.0)
    for k in range(8):
        centre, uz, lz = p_ref[k + 1], p_ref[k + 2], p_ref[k]
        ly, uy = pltpu.roll(centre, 1, 0), pltpu.roll(centre, 15, 0)
        lx, ux = sides(centre)
        dz, dy, dx = (uz - lz) * 0.5, (uy - ly) * 0.5, (ux - lx) * 0.5
        g = jnp.sqrt(dz * dz + dy * dy + dx * dx + FLOOR)
        g0_ref[k] = g
        if 2 <= k < 6:
            lap = uz + lz + uy + ly + ux + lx - 6.0 * centre
            base = pltpu.roll(centre + (A * 0.5) * lap, 12, 0)[:8]
            own_ref[1, k - 2] = base + A * own_ref[0, k - 2] * pltpu.roll(g, 12, 0)[:8]
    for z in range(BZ):
        own_ref[2, z] = lab_ref[z].astype(f32)
    fields_ref[...] = own_ref[...].astype(fields_ref.dtype)


def march(nz, ny, at, own_ref, ye_ref, mate_ref, far_ref, far2_ref, g0_ref, dpre_ref,
          sp, lab, ph, w_s, dz_s, dy_s, dx_s, ag_s, ds, dd):
    iz, iy, pz, py = at[0], at[1], at[2], at[3]
    base = 4 * pz

    def place(start, block):
        for k in range(BZ):
            for ref, f in ((sp, 0), (ph, 1), (lab, 2)):
                plane = jnp.concatenate([block(i, f, k).astype(f32) for i in range(3)], axis=0)
                if f == 1:
                    ph[0, start + k] = plane
                else:
                    ref[start + k] = plane

    def mine(i, f, k):
        return own_ref[f, k] if i == 1 else ye_ref[i, f, k]

    place(8 + 4 * pz, mine)
    place(12 - 4 * pz, lambda i, f, k: mate_ref[i, f, k])
    place(16 * pz + 4 - 4 * pz, lambda i, f, k: far_ref[0, i, f, k])
    place(16 * pz + 4 * pz, lambda i, f, k: far_ref[1, i, f, k])
    place(16 - 16 * pz + 4 * pz, lambda i, f, k: far2_ref[0, i, f, k])
    place(16 - 16 * pz + 4 - 4 * pz, lambda i, f, k: far2_ref[1, i, f, k])

    dd[0, 0] = jnp.zeros((24, X), f32)
    rows_in = inside(iy * BY - 8, (24, X), ny)
    first_plane = (iz - pz) * BZ - 8

    def within(z):
        zg = first_plane + z
        return rows_in & (zg >= 0) & (zg < nz)

    for t in (1, 2, 3):

        def step(i, carry, t=t):
            z = base + i
            centre, uz, lz = ph[t - 1, z], ph[t - 1, z + 1], ph[t - 1, z - 1]
            ly, uy = pltpu.roll(centre, 1, 0), pltpu.roll(centre, 23, 0)
            lx, ux = sides(centre)
            dz, dy, dx = (uz - lz) * 0.5, (uy - ly) * 0.5, (ux - lx) * 0.5
            g = jnp.sqrt(dz * dz + dy * dy + dx * dx + FLOOR)
            lap = uz + lz + uy + ly + ux + lx - 6.0 * centre
            speed = sp[z]
            ag = A * g
            new = jnp.where(within(z), centre + speed * ag + (A * 0.5) * lap, 0.0)
            w_s[t - 1, z] = (A * 0.5) * speed / g
            dz_s[t - 1, z] = dz
            dy_s[t - 1, z] = dy
            dx_s[t - 1, z] = dx
            ag_s[t - 1, z] = ag
            if t < 3:
                ph[t, z] = new
            else:
                dd[0, z] = jnp.where(within(z), jax.nn.sigmoid(new) - lab[z], 0.0)
            return carry

        lax.fori_loop(t, 20 - t, step, 0)

    for n, t in enumerate((3, 2, 1)):
        src, dst = n % 2, (n + 1) % 2

        def back(i, carry, t=t, n=n, src=src, dst=dst):
            l1, a1, a2 = carry
            z = base + i
            d = dd[src, z]
            add = ag_s[t - 1, z] * d
            ds[z] = add if n == 0 else ds[z] + add
            w = w_s[t - 1, z] * d
            e = (A * 0.5) * d
            qz, qy, qx = w * dz_s[t - 1, z], w * dy_s[t - 1, z], w * dx_s[t - 1, z]
            local = (1.0 - 3.0 * A) * d
            local = local + pltpu.roll(e + qy, 1, 0) + pltpu.roll(e - qy, 23, 0)
            local = local + sides(e + qx)[0] + sides(e - qx)[1]
            dd[dst, z - 1] = jnp.where(within(z - 1), l1 + a2 + (e - qz), 0.0)
            return local, e + qz, a1

        zero = dd[0, 0]
        lax.fori_loop(2 + n + 1, 18 - n - 1, back, (zero, zero, zero))

    for k in range(8):
        z = base + 6 + k
        speed = sp[z]
        left = 1.0 - speed * speed
        one = pltpu.roll(ds[z] * left, 20, 0)[:16]
        two = pltpu.roll(dd[1, z] * left, 20, 0)[:16]
        dpre_ref[k] = one + A * two * g0_ref[k]


def backward(at, dpre_ref, slope2_ref, s2y_ref, sa_ref, sb_ref, sw_ref, hx_ref, fx_ref, slope1_ref,
             top_ref, w1_ref, w2_ref, df_ref, grad_ref, dx_ref, ex_ref):
    pz = at[2]
    sw = sw_ref[...]

    def second(z, k, slope):
        for y in range(BY + 4):
            d = dpre_ref[z, 2 + y : 3 + y, :]
            value = (sw * d * slope(y))[None]
            low, up = sides(value)
            dx_ref[z, y : y + 1, 0] = low.astype(bf16)
            dx_ref[z, y : y + 1, 1] = value.astype(bf16)
            dx_ref[z, y : y + 1, 2] = up.astype(bf16)

    for k in range(BZ):
        def own(y, k=k):
            if 2 <= y < 2 + BY:
                return slope2_ref[k, y - 2]
            return s2y_ref[k, y].astype(f32)
        second(2 + k, k, own)
    for k in range(2):
        second(6 - 6 * pz + k, k, lambda y, k=k: sa_ref[k, y].astype(f32))
        second(6 * pz + k, k, lambda y, k=k: sb_ref[k, y].astype(f32))

    w2 = w2_ref[...]
    w1 = w1_ref[...]

    def hidden(z, carry):
        for y in range(0, BY + 2, 2):
            both = two_rows(w2, dx_ref, z, y)
            d = jnp.concatenate([(v * slope1_ref[z, y + j])[None] for j, v in enumerate(both)], axis=0)
            low, up = sides(d)
            ex_ref[z, y : y + 2, 0] = low.astype(bf16)
            ex_ref[z, y : y + 2, 1] = d.astype(bf16)
            ex_ref[z, y : y + 2, 2] = up.astype(bf16)
        return carry

    lax.fori_loop(0, BZ + 2, hidden, 0)

    def features(z, carry):
        rows = []
        for y in range(0, BY, 2):
            a, b = two_rows(w1, ex_ref, z, y)
            rows += [a[None], b[None]]
        plane = jnp.concatenate(rows, axis=0)
        df_ref[:, z] = jnp.transpose(plane, (1, 0, 2)).astype(bf16)
        return carry

    lax.fori_loop(0, BZ, features, 0)

    nt = (((1,), (1,)), ((), ()))

    def weights(z, carry):
        g1, g2, gs = carry
        for y in range(BY):
            d2 = dx_ref[z + 2, y + 2, 1]
            d1 = ex_ref[z + 1, y + 1, 1]
            p2 = hx_ref[pl.ds(z, 3), y : y + 3].reshape(TAPS, X)
            p1 = fx_ref[pl.ds(z + 1, 3), y + 1 : y + 4].reshape(TAPS, X)
            g2 = g2 + lax.dot_general(d2, p2, nt, preferred_element_type=f32)
            g1 = g1 + lax.dot_general(d1, p1, nt, preferred_element_type=f32)
            gs = gs + dpre_ref[z + 2, 4 + y : 5 + y, :] * top_ref[z, y]
        return g1, g2, gs

    zero = jnp.zeros((C, TAPS), f32)
    g1, g2, gs = lax.fori_loop(0, BZ, weights, (zero, zero, jnp.zeros((C, X), f32)))
    grad_ref[...] = jnp.zeros_like(grad_ref)
    grad_ref[0, :, :TAPS] = g1
    grad_ref[1, :, :TAPS] = g2
    grad_ref[0, :, TAPS : TAPS + 1] = jnp.sum(gs, axis=1, keepdims=True)


def finish(a_ref, b_ref, out_ref):
    a, b = a_ref[...], b_ref[...]
    total = jnp.sum(a * a) + jnp.sum(b * b)
    count = 54.0 * C * C + C
    factor = 1.0 / jnp.maximum(jnp.sqrt(jnp.full((1, 1), total)) / jnp.sqrt(f32(count)), 1.0)
    out_ref[0] = a * factor
    out_ref[1] = b * factor


def call(kernel, outs, scratch=(), flops=0):
    smem = pl.BlockSpec(memory_space=pltpu.SMEM)
    vmem = pl.BlockSpec(memory_space=pltpu.VMEM)

    def run(at, *args):
        args = ((at,) if at is not None else ()) + args
        specs = [smem if (i == 0 and at is not None) else vmem for i in range(len(args))]
        many = isinstance(outs, (list, tuple))
        size = sum(a.size * a.dtype.itemsize for a in args)
        return pl.pallas_call(
            kernel,
            out_shape=outs,
            in_specs=specs,
            out_specs=[vmem] * len(outs) if many else vmem,
            scratch_shapes=list(scratch),
            cost_estimate=pl.CostEstimate(flops=flops, bytes_accessed=size, transcendentals=0),
            compiler_params=pltpu.CompilerParams(vmem_limit_bytes=40 * 1024 * 1024),
        )(*args)

    return run


def shape(dims, dtype=bf16):
    return jax.ShapeDtypeStruct(dims, dtype)


def even(value, axis):
    n = lax.axis_size(axis)
    return lax.ppermute(value, axis, [(i, i ^ 1) for i in range(n)])


def odd(value, axis):
    n = lax.axis_size(axis)
    pairs = [(i, i + 1) for i in range(1, n - 1, 2)]
    return lax.ppermute(value, axis, pairs + [(j, i) for i, j in pairs])


def row_weights(taps_last):
    first = jnp.pad(taps_last, ((0, 0), (0, 0), (0, 1), (0, 0)))
    second = jnp.pad(taps_last, ((0, 0), (0, 0), (1, 0), (0, 0)))
    return jnp.concatenate([first, second], axis=0).reshape(2 * C, 36 * C)


def taps_of(weight):
    return weight.transpose(0, 2, 3, 4, 1).reshape(C, 3, 3, 3 * C)


def taps_back(weight):
    return jnp.flip(weight, (2, 3, 4)).transpose(1, 2, 3, 4, 0).reshape(C, 3, 3, 3 * C)


def total_of(grad, iz):
    core = iz % 2
    keep = lax.dynamic_index_in_dim(grad, core, 0, keepdims=False)
    give = lax.dynamic_index_in_dim(grad, 1 - core, 0, keepdims=False)
    part = keep + even(give, "gz")
    for axis, masks in (("gy", (1, 3, 4, 8)), ("gz", (8, 24, 2, 6))):
        n = lax.axis_size(axis)
        for mask in masks:
            if mask < n:
                part = part + lax.ppermute(part, axis, [(i, i ^ mask) for i in range(n)])
    other = even(part, "gz")
    return jnp.where(core == 0, part, other), jnp.where(core == 0, other, part)


def on_device(features, labels, sign_map, conv_first, conv_second, speed_weight):
    nz, ny = BZ * lax.axis_size("gz"), BY * lax.axis_size("gy")
    iz, iy = lax.axis_index("gz"), lax.axis_index("gy")
    pz, py = iz % 2, iy % 2
    at = jnp.stack([iz, iy, pz, py]).astype(jnp.int32)
    sw = jnp.broadcast_to(speed_weight[:, None], (C, X))
    w1, w2 = row_weights(taps_of(conv_first)), row_weights(taps_of(conv_second))
    w1b, w2b = row_weights(taps_back(conv_first)), row_weights(taps_back(conv_second))

    ft, me, mo = call(prepare, [shape((BZ, BY, C, X)), shape((9, C, X)), shape((9, C, X))])(
        at, features, sign_map
    )
    re, ro = even(me, "gy"), odd(mo, "gy")
    fy, sy, ma, mb = call(
        extend,
        [shape((BZ, 12, C, X)), shape((BZ, 16, X), f32), shape((27, C, X)), shape((27, C, X))],
    )(at, ft, sign_map, re, ro)
    ra, rb = even(ma, "gz"), odd(mb, "gz")

    fx, hx, slope1, slope2, top, fields, own, g0 = call(
        lambda *refs: forward(nz, ny, *refs),
        [
            shape((8, 12, 3, C, X)),
            shape((6, 10, 3, C, X)),
            shape((6, 10, C, X), f32),
            shape((BZ, BY, C, X), f32),
            shape((BZ, BY, C, X), f32),
            shape((3, BZ, BY, X), SENT),
            shape((3, BZ, BY, X), f32),
            shape((8, 16, X), f32),
        ],
        [pltpu.VMEM((10, 16, X), f32)],
    )(at, fy, sy, ra, rb, labels, w1, w2, sw)

    fe, fo = even(fields, "gy"), odd(fields, "gy")
    before, after = jnp.where(py == 0, fo, fe), jnp.where(py == 0, fe, fo)
    ye = jnp.stack([before, fields, after])
    mate = even(ye, "gz")
    far = odd(jnp.stack([ye, mate]), "gz")
    far2 = even(far, "gz")

    s2 = slope2.astype(bf16)
    se = even(lax.dynamic_slice_in_dim(s2, 6 - 6 * py, 2, 1), "gy")
    so = odd(lax.dynamic_slice_in_dim(s2, 6 * py, 2, 1), "gy")
    s2y = jnp.concatenate([jnp.where(py == 0, so, se), s2, jnp.where(py == 0, se, so)], axis=1)
    sa = even(lax.dynamic_slice_in_dim(s2y, 2 - 2 * pz, 2, 0), "gz")
    sb = odd(lax.dynamic_slice_in_dim(s2y, 2 * pz, 2, 0), "gz")

    plane = (24, 24, X)
    dpre = call(
        lambda *refs: march(nz, ny, *refs),
        shape((8, 16, X), f32),
        [
            pltpu.VMEM(plane, f32),
            pltpu.VMEM(plane, f32),
            pltpu.VMEM((3,) + plane, f32),
            pltpu.VMEM((3,) + plane, f32),
            pltpu.VMEM((3,) + plane, f32),
            pltpu.VMEM((3,) + plane, f32),
            pltpu.VMEM((3,) + plane, f32),
            pltpu.VMEM((3,) + plane, f32),
            pltpu.VMEM(plane, f32),
            pltpu.VMEM((2,) + plane, f32),
        ],
    )(at, own, ye, mate, far, far2, g0)

    d_features, grad = call(
        backward,
        [shape((C, BZ, BY, X)), shape((2, C, 512), f32)],
        [pltpu.VMEM((8, 12, 3, C, X), bf16), pltpu.VMEM((6, 10, 3, C, X), bf16)],
    )(at, dpre, slope2, s2y, sa, sb, sw, hx, fx, slope1, top, w1b, w2b)

    a, b = total_of(grad, iz)
    out = call(finish, shape((2, C, 512), f32))(None, a, b)
    first, second = (
        out[i, :, :TAPS].reshape(C, 3, 3, 3, C).transpose(0, 4, 1, 2, 3) for i in range(2)
    )
    return d_features, first, second, out[0, :, TAPS]


def solution(mesh):
    in_specs = (P(None, "gz", "gy", None), P("gz", "gy", None), P("gz", "gy", None), P(), P(), P())
    out_specs = (P(None, "gz", "gy", None), P(), P(), P())
    return jax.shard_map(
        on_device, mesh=mesh, in_specs=in_specs, out_specs=out_specs, check_vma=False
    )
```

time: 524 us -> 175 us (0.33); the launches traced: 514 us -> 174 us
  blocking collectives: 119 us -> 0 us
  matrix products: 86.3 us -> 0 us
  local copies, waits for them, and re-layouts: 78.4 us -> 13.9 us
  starting transfers between devices: 155 us -> 97.1 us
  Pallas kernels: 0 us -> 21.6 us
  waiting for transfers between devices: 57.7 us -> 37.7 us
  other arithmetic: 12.8 us -> 2.66 us
    psum x1 -> x0, blocking collectives: 119 us -> none  [on_device(): lax.psum((raw_first, raw_second, raw_speed), ('gz', 'gy'))]
    transpose x2 -> x0, matrix products: 59.3 us -> none  [weight_grad(): return d_weight.transpose(1, 0, 2, 3, 4)]
    ppermute x44 -> x23, starting transfers between devices: 155 us -> 97.1 us  [the longest x9 46.3 us: even(): return lax.ppermute(value, axis, [(i, i ^ 1) for i in range(n)])]
    conv_general_dilated x22 -> x0, local copies, waits for them, and re-layouts: 47.9 us -> none  [the longest x10 25.9 us: conv_back(): lax.conv_general_dilated(d_out[None], flip_weight(weight), (1, 1, 1), ((2...]
    conv_general_dilated x4 -> x0, matrix products: 26.3 us -> none  [the longest x2 14.7 us: conv_back(): lax.conv_general_dilated(d_out[None], flip_weight(weight), (1, 1, 1), ((2...]
    pallas_call x0 -> x6, Pallas kernels: none -> 21.6 us  [run(): pl.pallas_call(kernel, out_shape=outs, in_specs=specs, out_specs=[vmem] *...]
    ppermute x44 -> x23, waiting for transfers between devices: 57.7 us -> 37.7 us  [the longest x8 23.4 us: total_of(): part = part + lax.ppermute(part, axis, [(i, i ^ mask) for i in range(n)])]
    broadcast_in_dim x6 -> x1, local copies, waits for them, and re-layouts: 15.6 us -> 0.07 us  [on_device(): sw = jnp.broadcast_to(speed_weight[:, None], (C, X))]
  transfers between devices with their start and end apart: 44 -> 23, of which waited for: 17 -> 12; matrix products, arithmetic and copies ran while one was open for 13% -> 5% of each run, Pallas kernels for 0% -> 5%
where the time goes in v1:
time: 175 us; the launch traced here: 174 us
  starting transfers between devices  97.1 us (55%)
  waiting for transfers between devices  37.7 us (22%)
  Pallas kernels  21.6 us (12%)
  local copies, waits for them, and re-layouts  13.9 us (8%)
  other arithmetic  2.66 us (2%)
    ppermute x9, starting transfers between devices, even(): return lax.ppermute(value, axis, [(i, i ^ 1) for i in range(n)])  46.3 us
    ppermute x8, starting transfers between devices, total_of(): part = part + lax.ppermute(part, axis, [(i, i ^ mask) for i in range(n)])  29.4 us
    ppermute x8, waiting for transfers between devices, total_of(): part = part + lax.ppermute(part, axis, [(i, i ^ mask) for i in range(n)])  23.4 us
    pallas_call x6, Pallas kernels, run(): pl.pallas_call(kernel, out_shape=outs, in_specs=specs, out_specs=[vmem] *...  21.6 us
    ppermute x6, starting transfers between devices, odd(): return lax.ppermute(value, axis, pairs + [(j, i) for i, j in pairs])  21.5 us
    ppermute x6, waiting for transfers between devices, odd(): return lax.ppermute(value, axis, pairs + [(j, i) for i, j in pairs])  12.3 us
    unnamed x24, local copies, waits for them, and re-layouts  6.01 us
  transfers between devices with their start and end apart: 23, of which 12 were waited for; matrix products, arithmetic and copies ran while one was open for 5% of the time, Pallas kernels for 5%

profile of v1, /device:TPU:1, one launch (start us, length us, event | category | flops | bytes accessed | tf_op | source)
XLA Modules:
  0.0 174.2 jit_solution(9700589891920798766)
XLA Ops:
  0.7 0.9 copy-done
  1.6 0.7 copy-done.1
  3.0 3.9 %collective-permute-start = (bf16[9,16,128]{2,1,0:T(8,128)(2,1)S(1)}, bf16[9,16,128]{2,1,0:T(8,128)(2,1)S(1)}, u32[]{:S(2)}, u32[]{:S(2)}) collective-permute-start(bf16[9,16,128]{2,1,0:T(8,128)(2,1)S(1)} %get-tuple-element.22), channel_id=1, source_target_pairs={{0,1},{1,0},{2,3},{3,2},{4,5},{5,4},{6,7},{7,6},{8,9},{9,8},{10,11... | collective-permute-start | bytes 110600 | tf_op jit(solution)/shard_map/ppermute | solution.py:356
  7.6 1.0 copy.16
  8.7 0.9 rev.7
  10.6 7.5 %collective-permute-start.2 = (bf16[27,16,128]{2,1,0:T(8,128)(2,1)S(1)}, bf16[27,16,128]{2,1,0:T(8,128)(2,1)S(1)}, u32[]{:S(2)}, u32[]{:S(2)}) collective-permute-start(bf16[27,16,128]{2,1,0:T(8,128)(2,1)S(1)} %get-tuple-element.26), channel_id=1, source_target_pairs={{0,16},{16,0},{32,48},{48,32},{64,80},{80,64},{96,112},{112,96},{1... | collective-permute-start | bytes 331784 | tf_op jit(solution)/shard_map/ppermute | solution.py:356
  18.2 4.0 %collective-permute-start.3 = (bf16[27,16,128]{2,1,0:T(8,128)(2,1)S(1)}, bf16[27,16,128]{2,1,0:T(8,128)(2,1)S(1)}, u32[]{:S(2)}, u32[]{:S(2)}) collective-permute-start(bf16[27,16,128]{2,1,0:T(8,128)(2,1)S(1)} %get-tuple-element.27), channel_id=1, source_target_pairs={{16,32},{48,64},{80,96},{112,128},{144,160},{176,192},{208,224},{2... | collective-permute-start | bytes 331784 | tf_op jit(solution)/shard_map/ppermute | solution.py:362
  22.4 0.7 copy.20
  23.2 5.0 %collective-permute-done.3.refs_4_ = bf16[27,16,128]{2,1,0:T(8,128)(2,1)S(1)} collective-permute-done((bf16[27,16,128]{2,1,0:T(8,128)(2,1)S(1)}, bf16[27,16,128]{2,1,0:T(8,128)(2,1)S(1)}, u32[]{:S(2)}, u32[]{:S(2)}) %collective-permute-start.3) | collective-permute-done | bytes 110624 | tf_op jit(solution)/shard_map/ppermute | solution.py:362
  28.2 0.7 copy-done.7
  28.9 4.5 %shard_map.95 = (bf16[8,12,3,16,128]{4,3,2,1,0:T(8,128)(2,1)S(1)}, bf16[6,10,3,16,128]{4,3,2,1,0:T(8,128)(2,1)S(1)}, f32[6,10,16,128]{3,2,1,0:T(8,128)S(1)}, f32...) custom-call(s32[4]{0:T(128)S(1)} %pad_add_fusion.at.refs_0_, ...), custom_call_target="tpu_custom_call" | custom-call | bytes 548880 | tf_op jit(solution)/shard_map/pallas_call | solution.py:337
  34.8 9.4 %collective-permute-start.5 = (bf16[3,4,8,128]{3,2,1,0:T(8,128)(2,1)}, bf16[3,4,8,128]{3,2,1,0:T(8,128)(2,1)S(1)}, u32[]{:S(2)}, u32[]{:S(2)}) collective-permute-start(bf16[3,4,8,128]{3,2,1,0:T(8,128)(2,1)} %get-tuple-element.29), channel_id=1, source_target_pairs={{0,1},{1,0},{2,3},{3,2},{4,5},{5,4},{6,7},{7,6},{8,9},{9,8},{10,11... | collective-permute-start | bytes 73736 | tf_op jit(solution)/shard_map/ppermute | solution.py:356
  44.2 0.9 fusion.10
  45.2 0.9 rev.8
  46.2 0.7 copy.22
  47.0 0.8 fusion.12
  47.8 1.9 %collective-permute-start.6 = (bf16[3,3,4,8,128]{4,3,2,1,0:T(8,128)(2,1)S(1)}, bf16[3,3,4,8,128]{4,3,2,1,0:T(8,128)(2,1)S(1)}, u32[]{:S(2)}, u32[]{:S(2)}) collective-permute-start(bf16[3,3,4,8,128]{4,3,2,1,0:T(8,128)(2,1)S(1)} %get-tuple-element.47.refs_2_), channel_id=1, source_target_pairs={{0,16},{16,0},{32,48},{48,32},{64,80},{80,64},{96,112},{112,96},{1... | collective-permute-start | bytes 221192 | tf_op jit(solution)/shard_map/ppermute | solution.py:356
  50.4 6.7 %collective-permute-start.10 = (bf16[4,2,16,128]{3,2,1,0:T(8,128)(2,1)S(1)}, bf16[4,2,16,128]{3,2,1,0:T(8,128)(2,1)S(1)}, u32[]{:S(2)}, u32[]{:S(2)}) collective-permute-start(bf16[4,2,16,128]{3,2,1,0:T(8,128)(2,1)S(1)} %get-tuple-element.45), channel_id=1, source_target_pairs={{0,1},{1,0},{2,3},{3,2},{4,5},{5,4},{6,7},{7,6},{8,9},{9,8},{10,11... | collective-permute-start | bytes 98312 | tf_op jit(solution)/shard_map/ppermute | solution.py:356
  57.1 8.8 %collective-permute-start.7 = (bf16[2,3,3,4,8,128]{5,4,3,2,1,0:T(8,128)(2,1)S(1)}, bf16[2,3,3,4,8,128]{5,4,3,2,1,0:T(8,128)(2,1)S(1)}, u32[]{:S(2)}, u32[]{:S(2)}) collective-permute-start(bf16[2,3,3,4,8,128]{5,4,3,2,1,0:T(8,128)(2,1)S(1)} %pad_maximum_fusion.1), channel_id=1, source_target_pairs={{16,32},{48,64},{80,96},{112,128},{144,160},{176,192},{208,224},{2... | collective-permute-start | bytes 442376 | tf_op jit(solution)/shard_map/ppermute | solution.py:362
  66.0 7.3 %collective-permute-done.7.refs_4_ = bf16[2,3,3,4,8,128]{5,4,3,2,1,0:T(8,128)(2,1)S(1)} collective-permute-done((bf16[2,3,3,4,8,128]{5,4,3,2,1,0:T(8,128)(2,1)S(1)}, bf16[2,3,3,4,8,128]{5,4,3,2,1,0:T(8,128)(2,1)S(1)}, u32[]{:S(2)}, u32[]{:S(2)}) %collective-permute-start.7) | collective-permute-done | bytes 147488 | tf_op jit(solution)/shard_map/ppermute | solution.py:362
  73.3 1.9 %collective-permute-start.8 = (bf16[2,3,3,4,8,128]{5,4,3,2,1,0:T(8,128)(2,1)S(1)}, bf16[2,3,3,4,8,128]{5,4,3,2,1,0:T(8,128)(2,1)}, u32[]{:S(2)}, u32[]{:S(2)}) collective-permute-start(bf16[2,3,3,4,8,128]{5,4,3,2,1,0:T(8,128)(2,1)S(1)} %collective-permute-done.7.refs_4_), channel_id=1, source_target_pairs={{0,16},{16,0},{32,48},{48,32},{64,80},{80,64},{96,112},{112,96},{1... | collective-permute-start | bytes 442376 | tf_op jit(solution)/shard_map/ppermute | solution.py:356
  76.0 2.4 %collective-permute-start.11 = (bf16[2,12,16,128]{3,2,1,0:T(8,128)(2,1)}, bf16[2,12,16,128]{3,2,1,0:T(8,128)(2,1)}, u32[]{:S(2)}, u32[]{:S(2)}) collective-permute-start(bf16[2,12,16,128]{3,2,1,0:T(8,128)(2,1)} %get-tuple-element.43), channel_id=1, source_target_pairs={{0,16},{16,0},{32,48},{48,32},{64,80},{80,64},{96,112},{112,96},{1... | collective-permute-start | bytes 294920 | tf_op jit(solution)/shard_map/ppermute | solution.py:356
  78.4 6.7 %collective-permute-start.12 = (bf16[2,12,16,128]{3,2,1,0:T(8,128)(2,1)}, bf16[2,12,16,128]{3,2,1,0:T(8,128)(2,1)}, u32[]{:S(2)}, u32[]{:S(2)}) collective-permute-start(bf16[2,12,16,128]{3,2,1,0:T(8,128)(2,1)} %get-tuple-element.42), channel_id=1, source_target_pairs={{16,32},{48,64},{80,96},{112,128},{144,160},{176,192},{208,224},{2... | collective-permute-start | bytes 294920 | tf_op jit(solution)/shard_map/ppermute | solution.py:362
  85.7 1.0 reshape.40.w2_ref
  86.8 0.8 copy-done.4
  87.6 0.8 copy-done.6
  88.4 8.5 %shard_map.96.dpre_ref = f32[8,16,128]{2,1,0:T(8,128)S(1)} custom-call(s32[4]{0:T(128)S(1)} %pad_add_fusion.at.refs_0_, f32[3,4,8,128]{3,2,1,0:T(8,128)S(1)} %copy-done.6, bf16[3,3,4,8,128]{4,3,2,1,0:T(8,128)(2,1)S(1)} %get-tuple-element.47.refs_2_, bf16[3,3,4,8,128]{4,3,2,1,0:T(8,128)(2,1)S(1)} %collective-permute-done.6.refs_3_, ...), custom_call_target="tpu_custom_call" | custom-call | bytes 557072 | tf_op jit(solution)/shard_map/pallas_call | solution.py:337
  97.0 7.2 %shard_map.97 = (bf16[16,4,8,128]{3,2,1,0:T(8,128)(2,1)}, f32[2,16,512]{2,1,0:T(8,128)S(1)}) custom-call(s32[4]{0:T(128)S(1)} %pad_add_fusion.at.refs_0_, f32[8,16,128]{2,1,0:T(8,128)S(1)} %shard_map.96.dpre_ref, f32[4,8,16,128]{3,2,1,0:T(8,128)S(1)} %get-tuple-element.31.slope2_ref, bf16[4,12,16,128]{3,2,1,0:T(8,128)(2,1)S(1)} %pad_maximum_fusion.s2y_ref, ...), custom_call_target="tpu_custom_call" | custom-call | bytes 3473424 | tf_op jit(solution)/shard_map/pallas_call | solution.py:337
  104.2 1.9 %collective-permute-start.13 = (f32[16,512]{1,0:T(8,128)S(1)}, f32[16,512]{1,0:T(8,128)S(1)}, u32[]{:S(2)}, u32[]{:S(2)}) collective-permute-start(f32[16,512]{1,0:T(8,128)S(1)} %dynamic-slice_bitcast_fusion), channel_id=1, source_target_pairs={{0,16},{16,0},{32,48},{48,32},{64,80},{80,64},{96,112},{112,96},{1... | collective-permute-start | bytes 98312 | tf_op jit(solution)/shard_map/ppermute | solution.py:356
  106.1 1.2 collective-permute-done.13
  107.3 1.9 %collective-permute-start.14 = (f32[16,512]{1,0:T(8,128)S(1)}, f32[16,512]{1,0:T(8,128)S(1)}, u32[]{:S(2)}, u32[]{:S(2)}) collective-permute-start(f32[16,512]{1,0:T(8,128)S(1)} %bitcast_add_fusion), channel_id=1, source_target_pairs={{0,1},{1,0},{2,3},{3,2},{4,5},{5,4},{6,7},{7,6},{8,9},{9,8},{10,11... | collective-permute-start | bytes 98312 | tf_op jit(solution)/shard_map/ppermute | solution.py:388
  109.2 2.7 %collective-permute-done.14 = f32[16,512]{1,0:T(8,128)S(1)} collective-permute-done((f32[16,512]{1,0:T(8,128)S(1)}, f32[16,512]{1,0:T(8,128)S(1)}, u32[]{:S(2)}, u32[]{:S(2)}) %collective-permute-start.14) | collective-permute-done | bytes 32800 | tf_op jit(solution)/shard_map/ppermute | solution.py:388
  112.0 3.4 %collective-permute-start.15 = (f32[16,512]{1,0:T(8,128)S(1)}, f32[16,512]{1,0:T(8,128)S(1)}, u32[]{:S(2)}, u32[]{:S(2)}) collective-permute-start(f32[16,512]{1,0:T(8,128)S(1)} %add.82), channel_id=1, source_target_pairs={{0,3},{1,2},{2,1},{3,0},{4,7},{5,6},{6,5},{7,4},{8,11},{9,10},{10,... | collective-permute-start | bytes 98312 | tf_op jit(solution)/shard_map/ppermute | solution.py:388
  115.4 2.4 %collective-permute-done.15 = f32[16,512]{1,0:T(8,128)S(1)} collective-permute-done((f32[16,512]{1,0:T(8,128)S(1)}, f32[16,512]{1,0:T(8,128)S(1)}, u32[]{:S(2)}, u32[]{:S(2)}) %collective-permute-start.15) | collective-permute-done | bytes 32800 | tf_op jit(solution)/shard_map/ppermute | solution.py:388
  117.8 2.9 %collective-permute-start.16 = (f32[16,512]{1,0:T(8,128)S(1)}, f32[16,512]{1,0:T(8,128)S(1)}, u32[]{:S(2)}, u32[]{:S(2)}) collective-permute-start(f32[16,512]{1,0:T(8,128)S(1)} %add.83), channel_id=1, source_target_pairs={{0,4},{1,5},{2,6},{3,7},{4,0},{5,1},{6,2},{7,3},{8,12},{9,13},{10,... | collective-permute-start | bytes 98312 | tf_op jit(solution)/shard_map/ppermute | solution.py:388
  120.7 1.8 %collective-permute-done.16 = f32[16,512]{1,0:T(8,128)S(1)} collective-permute-done((f32[16,512]{1,0:T(8,128)S(1)}, f32[16,512]{1,0:T(8,128)S(1)}, u32[]{:S(2)}, u32[]{:S(2)}) %collective-permute-start.16) | collective-permute-done | bytes 32800 | tf_op jit(solution)/shard_map/ppermute | solution.py:388
  122.5 3.2 %collective-permute-start.17 = (f32[16,512]{1,0:T(8,128)S(1)}, f32[16,512]{1,0:T(8,128)S(1)}, u32[]{:S(2)}, u32[]{:S(2)}) collective-permute-start(f32[16,512]{1,0:T(8,128)S(1)} %add.84), channel_id=1, source_target_pairs={{0,8},{1,9},{2,10},{3,11},{4,12},{5,13},{6,14},{7,15},{8,0},{9,1},... | collective-permute-start | bytes 98312 | tf_op jit(solution)/shard_map/ppermute | solution.py:388
  125.7 2.3 %collective-permute-done.17 = f32[16,512]{1,0:T(8,128)S(1)} collective-permute-done((f32[16,512]{1,0:T(8,128)S(1)}, f32[16,512]{1,0:T(8,128)S(1)}, u32[]{:S(2)}, u32[]{:S(2)}) %collective-permute-start.17) | collective-permute-done | bytes 32800 | tf_op jit(solution)/shard_map/ppermute | solution.py:388
  128.0 6.3 %collective-permute-start.18 = (f32[16,512]{1,0:T(8,128)S(1)}, f32[16,512]{1,0:T(8,128)S(1)}, u32[]{:S(2)}, u32[]{:S(2)}) collective-permute-start(f32[16,512]{1,0:T(8,128)S(1)} %add.85), channel_id=1, source_target_pairs={{0,128},{16,144},{32,160},{48,176},{64,192},{80,208},{96,224},{112... | collective-permute-start | bytes 98312 | tf_op jit(solution)/shard_map/ppermute | solution.py:388
  134.4 1.3 collective-permute-done.18
  135.7 5.4 %collective-permute-start.19 = (f32[16,512]{1,0:T(8,128)S(1)}, f32[16,512]{1,0:T(8,128)S(1)}, u32[]{:S(2)}, u32[]{:S(2)}) collective-permute-start(f32[16,512]{1,0:T(8,128)S(1)} %add.86), channel_id=1, source_target_pairs={{0,384},{16,400},{32,416},{48,432},{64,448},{80,464},{96,480},{112... | collective-permute-start | bytes 98312 | tf_op jit(solution)/shard_map/ppermute | solution.py:388
  141.1 1.3 collective-permute-done.19
  142.4 3.2 %collective-permute-start.20 = (f32[16,512]{1,0:T(8,128)S(1)}, f32[16,512]{1,0:T(8,128)S(1)}, u32[]{:S(2)}, u32[]{:S(2)}) collective-permute-start(f32[16,512]{1,0:T(8,128)S(1)} %add.87), channel_id=1, source_target_pairs={{0,32},{16,48},{32,0},{48,16},{64,96},{80,112},{96,64},{112,80},{1... | collective-permute-start | bytes 98312 | tf_op jit(solution)/shard_map/ppermute | solution.py:388
  145.6 6.0 %collective-permute-done.20 = f32[16,512]{1,0:T(8,128)S(1)} collective-permute-done((f32[16,512]{1,0:T(8,128)S(1)}, f32[16,512]{1,0:T(8,128)S(1)}, u32[]{:S(2)}, u32[]{:S(2)}) %collective-permute-start.20) | collective-permute-done | bytes 32800 | tf_op jit(solution)/shard_map/ppermute | solution.py:388
  151.6 3.0 %collective-permute-start.21 = (f32[16,512]{1,0:T(8,128)S(1)}, f32[16,512]{1,0:T(8,128)S(1)}, u32[]{:S(2)}, u32[]{:S(2)}) collective-permute-start(f32[16,512]{1,0:T(8,128)S(1)} %add.88), channel_id=1, source_target_pairs={{0,96},{16,112},{32,64},{48,80},{64,32},{80,48},{96,0},{112,16},{1... | collective-permute-start | bytes 98312 | tf_op jit(solution)/shard_map/ppermute | solution.py:388
  154.7 5.5 %collective-permute-done.21 = f32[16,512]{1,0:T(8,128)S(1)} collective-permute-done((f32[16,512]{1,0:T(8,128)S(1)}, f32[16,512]{1,0:T(8,128)S(1)}, u32[]{:S(2)}, u32[]{:S(2)}) %collective-permute-start.21) | collective-permute-done | bytes 32800 | tf_op jit(solution)/shard_map/ppermute | solution.py:388
  160.2 10.5 %collective-permute-start.22 = (f32[16,512]{1,0:T(8,128)S(1)}, f32[16,512]{1,0:T(8,128)S(1)}, u32[]{:S(2)}, u32[]{:S(2)}) collective-permute-start(f32[16,512]{1,0:T(8,128)S(1)} %add.89), channel_id=1, source_target_pairs={{0,16},{16,0},{32,48},{48,32},{64,80},{80,64},{96,112},{112,96},{1... | collective-permute-start | bytes 98312 | tf_op jit(solution)/shard_map/ppermute | solution.py:356
  170.7 0.8 collective-permute-done.22
  (71 shorter events, 9.0 us)
Async XLA Ops:
  0.6 9.4 %copy-start.2 = (s32[4,8,128]{2,1,0:T(8,128)S(1)}, s32[4,8,128]{2,1,0:T(8,128)}, u32[]{:S(2)}) copy-start(s32[4,8,128]{2,1,0:T(8,128)} %s_ref.3) | copy-start | bytes 49156
  0.7 0.9 copy-start
  1.6 0.7 copy-start.1
  2.4 7.4 %copy-start.8 = (bf16[16,16,3,3,3]{1,0,4,3,2:T(8,128)(2,1)S(1)}, bf16[16,16,3,3,3]{1,0,4,3,2:T(8,128)(2,1)}, u32[]{:S(2)}) copy-start(bf16[16,16,3,3,3]{1,0,4,3,2:T(8,128)(2,1)} %param.10) | copy-start | bytes 41476
  3.0 7.0 %collective-permute-start = (bf16[9,16,128]{2,1,0:T(8,128)(2,1)S(1)}, bf16[9,16,128]{2,1,0:T(8,128)(2,1)S(1)}, u32[]{:S(2)}, u32[]{:S(2)}) collective-permute-start(bf16[9,16,128]{2,1,0:T(8,128)(2,1)S(1)} %get-tuple-element.22), channel_id=1, source_target_pairs={{0,1},{1,0},{2,3},{3,2},{4,5},{5,4},{6,7},{7,6},{8,9},{9,8},{10,11... | collective-permute-start | bytes 110600 | tf_op jit(solution)/shard_map/ppermute | solution.py:356
  6.9 3.1 %collective-permute-start.1 = (bf16[9,16,128]{2,1,0:T(8,128)(2,1)S(1)}, bf16[9,16,128]{2,1,0:T(8,128)(2,1)S(1)}, u32[]{:S(2)}, u32[]{:S(2)}) collective-permute-start(bf16[9,16,128]{2,1,0:T(8,128)(2,1)S(1)} %get-tuple-element.23), channel_id=1, source_target_pairs={{1,2},{3,4},{5,6},{7,8},{9,10},{11,12},{13,14},{2,1},{4,3},{6,5},{... | collective-permute-start | bytes 110600 | tf_op jit(solution)/shard_map/ppermute | solution.py:362
  7.6 20.6 %copy-start.10 = (f32[16]{0:T(128)S(1)}, f32[16]{0:T(128)}, u32[]{:S(2)}) copy-start(f32[16]{0:T(128)} %param.11) | copy-start | bytes 196
  10.6 12.5 %collective-permute-start.2 = (bf16[27,16,128]{2,1,0:T(8,128)(2,1)S(1)}, bf16[27,16,128]{2,1,0:T(8,128)(2,1)S(1)}, u32[]{:S(2)}, u32[]{:S(2)}) collective-permute-start(bf16[27,16,128]{2,1,0:T(8,128)(2,1)S(1)} %get-tuple-element.26), channel_id=1, source_target_pairs={{0,16},{16,0},{32,48},{48,32},{64,80},{80,64},{96,112},{112,96},{1... | collective-permute-start | bytes 331784 | tf_op jit(solution)/shard_map/ppermute | solution.py:356
  18.2 10.0 %collective-permute-start.3 = (bf16[27,16,128]{2,1,0:T(8,128)(2,1)S(1)}, bf16[27,16,128]{2,1,0:T(8,128)(2,1)S(1)}, u32[]{:S(2)}, u32[]{:S(2)}) collective-permute-start(bf16[27,16,128]{2,1,0:T(8,128)(2,1)S(1)} %get-tuple-element.27), channel_id=1, source_target_pairs={{16,32},{48,64},{80,96},{112,128},{144,160},{176,192},{208,224},{2... | collective-permute-start | bytes 331784 | tf_op jit(solution)/shard_map/ppermute | solution.py:362
  28.2 0.7 copy-start.7
  33.5 0.6 copy-start.5
  34.1 13.7 %copy-start.3 = (f32[8,16,128]{2,1,0:T(8,128)}, f32[8,16,128]{2,1,0:T(8,128)S(1)}, u32[]{:S(2)}) copy-start(f32[8,16,128]{2,1,0:T(8,128)S(1)} %get-tuple-element.30.refs_6_) | copy-start | bytes 196612
  34.1 12.9 %collective-permute-start.4 = (bf16[3,4,8,128]{3,2,1,0:T(8,128)(2,1)}, bf16[3,4,8,128]{3,2,1,0:T(8,128)(2,1)S(1)}, u32[]{:S(2)}, u32[]{:S(2)}) collective-permute-start(bf16[3,4,8,128]{3,2,1,0:T(8,128)(2,1)} %get-tuple-element.29), channel_id=1, source_target_pairs={{1,2},{3,4},{5,6},{7,8},{9,10},{11,12},{13,14},{2,1},{4,3},{6,5},{... | collective-permute-start | bytes 73736 | tf_op jit(solution)/shard_map/ppermute | solution.py:362
  34.8 12.2 %collective-permute-start.5 = (bf16[3,4,8,128]{3,2,1,0:T(8,128)(2,1)}, bf16[3,4,8,128]{3,2,1,0:T(8,128)(2,1)S(1)}, u32[]{:S(2)}, u32[]{:S(2)}) collective-permute-start(bf16[3,4,8,128]{3,2,1,0:T(8,128)(2,1)} %get-tuple-element.29), channel_id=1, source_target_pairs={{0,1},{1,0},{2,3},{3,2},{4,5},{5,4},{6,7},{7,6},{8,9},{9,8},{10,11... | collective-permute-start | bytes 73736 | tf_op jit(solution)/shard_map/ppermute | solution.py:356
  46.9 38.1 %copy-start.9 = (bf16[16,3,3,48]{3,2,1,0:T(4,128)(2,1)S(1)}, bf16[16,3,3,48]{3,2,1,0:T(4,128)(2,1)}, u32[]{:S(2)}) copy-start(bf16[16,3,3,48]{3,2,1,0:T(4,128)(2,1)} %copy.22) | copy-start | bytes 41476
  47.8 9.3 %collective-permute-start.6 = (bf16[3,3,4,8,128]{4,3,2,1,0:T(8,128)(2,1)S(1)}, bf16[3,3,4,8,128]{4,3,2,1,0:T(8,128)(2,1)S(1)}, u32[]{:S(2)}, u32[]{:S(2)}) collective-permute-start(bf16[3,3,4,8,128]{4,3,2,1,0:T(8,128)(2,1)S(1)} %get-tuple-element.47.refs_2_), channel_id=1, source_target_pairs={{0,16},{16,0},{32,48},{48,32},{64,80},{80,64},{96,112},{112,96},{1... | collective-permute-start | bytes 221192 | tf_op jit(solution)/shard_map/ppermute | solution.py:356
  49.7 16.2 %collective-permute-start.9 = (bf16[4,2,16,128]{3,2,1,0:T(8,128)(2,1)S(1)}, bf16[4,2,16,128]{3,2,1,0:T(8,128)(2,1)S(1)}, u32[]{:S(2)}, u32[]{:S(2)}) collective-permute-start(bf16[4,2,16,128]{3,2,1,0:T(8,128)(2,1)S(1)} %get-tuple-element.44), channel_id=1, source_target_pairs={{1,2},{3,4},{5,6},{7,8},{9,10},{11,12},{13,14},{2,1},{4,3},{6,5},{... | collective-permute-start | bytes 98312 | tf_op jit(solution)/shard_map/ppermute | solution.py:362
  50.4 15.6 %collective-permute-start.10 = (bf16[4,2,16,128]{3,2,1,0:T(8,128)(2,1)S(1)}, bf16[4,2,16,128]{3,2,1,0:T(8,128)(2,1)S(1)}, u32[]{:S(2)}, u32[]{:S(2)}) collective-permute-start(bf16[4,2,16,128]{3,2,1,0:T(8,128)(2,1)S(1)} %get-tuple-element.45), channel_id=1, source_target_pairs={{0,1},{1,0},{2,3},{3,2},{4,5},{5,4},{6,7},{7,6},{8,9},{9,8},{10,11... | collective-permute-start | bytes 98312 | tf_op jit(solution)/shard_map/ppermute | solution.py:356
  57.1 16.2 %collective-permute-start.7 = (bf16[2,3,3,4,8,128]{5,4,3,2,1,0:T(8,128)(2,1)S(1)}, bf16[2,3,3,4,8,128]{5,4,3,2,1,0:T(8,128)(2,1)S(1)}, u32[]{:S(2)}, u32[]{:S(2)}) collective-permute-start(bf16[2,3,3,4,8,128]{5,4,3,2,1,0:T(8,128)(2,1)S(1)} %pad_maximum_fusion.1), channel_id=1, source_target_pairs={{16,32},{48,64},{80,96},{112,128},{144,160},{176,192},{208,224},{2... | collective-permute-start | bytes 442376 | tf_op jit(solution)/shard_map/ppermute | solution.py:362
  73.3 13.4 %collective-permute-start.8 = (bf16[2,3,3,4,8,128]{5,4,3,2,1,0:T(8,128)(2,1)S(1)}, bf16[2,3,3,4,8,128]{5,4,3,2,1,0:T(8,128)(2,1)}, u32[]{:S(2)}, u32[]{:S(2)}) collective-permute-start(bf16[2,3,3,4,8,128]{5,4,3,2,1,0:T(8,128)(2,1)S(1)} %collective-permute-done.7.refs_4_), channel_id=1, source_target_pairs={{0,16},{16,0},{32,48},{48,32},{64,80},{80,64},{96,112},{112,96},{1... | collective-permute-start | bytes 442376 | tf_op jit(solution)/shard_map/ppermute | solution.py:356
  76.0 21.0 %collective-permute-start.11 = (bf16[2,12,16,128]{3,2,1,0:T(8,128)(2,1)}, bf16[2,12,16,128]{3,2,1,0:T(8,128)(2,1)}, u32[]{:S(2)}, u32[]{:S(2)}) collective-permute-start(bf16[2,12,16,128]{3,2,1,0:T(8,128)(2,1)} %get-tuple-element.43), channel_id=1, source_target_pairs={{0,16},{16,0},{32,48},{48,32},{64,80},{80,64},{96,112},{112,96},{1... | collective-permute-start | bytes 294920 | tf_op jit(solution)/shard_map/ppermute | solution.py:356
  78.4 18.6 %collective-permute-start.12 = (bf16[2,12,16,128]{3,2,1,0:T(8,128)(2,1)}, bf16[2,12,16,128]{3,2,1,0:T(8,128)(2,1)}, u32[]{:S(2)}, u32[]{:S(2)}) collective-permute-start(bf16[2,12,16,128]{3,2,1,0:T(8,128)(2,1)} %get-tuple-element.42), channel_id=1, source_target_pairs={{16,32},{48,64},{80,96},{112,128},{144,160},{176,192},{208,224},{2... | collective-permute-start | bytes 294920 | tf_op jit(solution)/shard_map/ppermute | solution.py:362
  86.8 0.8 copy-start.4
  87.6 0.8 copy-start.6
  104.2 3.1 %collective-permute-start.13 = (f32[16,512]{1,0:T(8,128)S(1)}, f32[16,512]{1,0:T(8,128)S(1)}, u32[]{:S(2)}, u32[]{:S(2)}) collective-permute-start(f32[16,512]{1,0:T(8,128)S(1)} %dynamic-slice_bitcast_fusion), channel_id=1, source_target_pairs={{0,16},{16,0},{32,48},{48,32},{64,80},{80,64},{96,112},{112,96},{1... | collective-permute-start | bytes 98312 | tf_op jit(solution)/shard_map/ppermute | solution.py:356
  107.3 4.6 %collective-permute-start.14 = (f32[16,512]{1,0:T(8,128)S(1)}, f32[16,512]{1,0:T(8,128)S(1)}, u32[]{:S(2)}, u32[]{:S(2)}) collective-permute-start(f32[16,512]{1,0:T(8,128)S(1)} %bitcast_add_fusion), channel_id=1, source_target_pairs={{0,1},{1,0},{2,3},{3,2},{4,5},{5,4},{6,7},{7,6},{8,9},{9,8},{10,11... | collective-permute-start | bytes 98312 | tf_op jit(solution)/shard_map/ppermute | solution.py:388
  112.0 5.9 %collective-permute-start.15 = (f32[16,512]{1,0:T(8,128)S(1)}, f32[16,512]{1,0:T(8,128)S(1)}, u32[]{:S(2)}, u32[]{:S(2)}) collective-permute-start(f32[16,512]{1,0:T(8,128)S(1)} %add.82), channel_id=1, source_target_pairs={{0,3},{1,2},{2,1},{3,0},{4,7},{5,6},{6,5},{7,4},{8,11},{9,10},{10,... | collective-permute-start | bytes 98312 | tf_op jit(solution)/shard_map/ppermute | solution.py:388
  117.8 4.6 %collective-permute-start.16 = (f32[16,512]{1,0:T(8,128)S(1)}, f32[16,512]{1,0:T(8,128)S(1)}, u32[]{:S(2)}, u32[]{:S(2)}) collective-permute-start(f32[16,512]{1,0:T(8,128)S(1)} %add.83), channel_id=1, source_target_pairs={{0,4},{1,5},{2,6},{3,7},{4,0},{5,1},{6,2},{7,3},{8,12},{9,13},{10,... | collective-permute-start | bytes 98312 | tf_op jit(solution)/shard_map/ppermute | solution.py:388
  122.5 5.5 %collective-permute-start.17 = (f32[16,512]{1,0:T(8,128)S(1)}, f32[16,512]{1,0:T(8,128)S(1)}, u32[]{:S(2)}, u32[]{:S(2)}) collective-permute-start(f32[16,512]{1,0:T(8,128)S(1)} %add.84), channel_id=1, source_target_pairs={{0,8},{1,9},{2,10},{3,11},{4,12},{5,13},{6,14},{7,15},{8,0},{9,1},... | collective-permute-start | bytes 98312 | tf_op jit(solution)/shard_map/ppermute | solution.py:388
  128.0 7.6 %collective-permute-start.18 = (f32[16,512]{1,0:T(8,128)S(1)}, f32[16,512]{1,0:T(8,128)S(1)}, u32[]{:S(2)}, u32[]{:S(2)}) collective-permute-start(f32[16,512]{1,0:T(8,128)S(1)} %add.85), channel_id=1, source_target_pairs={{0,128},{16,144},{32,160},{48,176},{64,192},{80,208},{96,224},{112... | collective-permute-start | bytes 98312 | tf_op jit(solution)/shard_map/ppermute | solution.py:388
  135.7 6.7 %collective-permute-start.19 = (f32[16,512]{1,0:T(8,128)S(1)}, f32[16,512]{1,0:T(8,128)S(1)}, u32[]{:S(2)}, u32[]{:S(2)}) collective-permute-start(f32[16,512]{1,0:T(8,128)S(1)} %add.86), channel_id=1, source_target_pairs={{0,384},{16,400},{32,416},{48,432},{64,448},{80,464},{96,480},{112... | collective-permute-start | bytes 98312 | tf_op jit(solution)/shard_map/ppermute | solution.py:388
  142.4 9.2 %collective-permute-start.20 = (f32[16,512]{1,0:T(8,128)S(1)}, f32[16,512]{1,0:T(8,128)S(1)}, u32[]{:S(2)}, u32[]{:S(2)}) collective-permute-start(f32[16,512]{1,0:T(8,128)S(1)} %add.87), channel_id=1, source_target_pairs={{0,32},{16,48},{32,0},{48,16},{64,96},{80,112},{96,64},{112,80},{1... | collective-permute-start | bytes 98312 | tf_op jit(solution)/shard_map/ppermute | solution.py:388
  151.6 8.6 %collective-permute-start.21 = (f32[16,512]{1,0:T(8,128)S(1)}, f32[16,512]{1,0:T(8,128)S(1)}, u32[]{:S(2)}, u32[]{:S(2)}) collective-permute-start(f32[16,512]{1,0:T(8,128)S(1)} %add.88), channel_id=1, source_target_pairs={{0,96},{16,112},{32,64},{48,80},{64,32},{80,48},{96,0},{112,16},{1... | collective-permute-start | bytes 98312 | tf_op jit(solution)/shard_map/ppermute | solution.py:388
  160.2 11.4 %collective-permute-start.22 = (f32[16,512]{1,0:T(8,128)S(1)}, f32[16,512]{1,0:T(8,128)S(1)}, u32[]{:S(2)}, u32[]{:S(2)}) collective-permute-start(f32[16,512]{1,0:T(8,128)S(1)} %add.89), channel_id=1, source_target_pairs={{0,16},{16,0},{32,48},{48,32},{64,80},{80,64},{96,112},{112,96},{1... | collective-permute-start | bytes 98312 | tf_op jit(solution)/shard_map/ppermute | solution.py:356

commit v2 on v1

--- a/solution.py
+++ b/solution.py
@@ -85,8 +85,8 @@
 
 
 def forward(nz, ny, at, fy_ref, sy_ref, ma_ref, mb_ref, lab_ref, w1_ref, w2_ref, sw_ref,
-            fx_ref, hx_ref, slope1_ref, slope2_ref, top_ref, fields_ref, own_ref, g0_ref, p_ref):
-    iz, iy, pz = at[0], at[1], at[2]
+            fx_ref, hx_ref, slope1_ref, slope2_ref, top_ref, me_ref, mo_ref, own_ref, g0_ref, p_ref):
+    iz, iy, pz, py = at[0], at[1], at[2], at[3]
     for k in range(BZ):
         put_taps(fx_ref, 2 + k, fy_ref[k].astype(f32))
     for k in range(2):
@@ -153,7 +153,34 @@
             own_ref[1, k - 2] = base + A * own_ref[0, k - 2] * pltpu.roll(g, 12, 0)[:8]
     for z in range(BZ):
         own_ref[2, z] = lab_ref[z].astype(f32)
-    fields_ref[...] = own_ref[...].astype(fields_ref.dtype)
+    for ref, start in ((me_ref, 6 - 6 * py), (mo_ref, 6 * py)):
+        ref[:12] = own_ref[...].reshape(12, BY, X).astype(SENT)
+        for z in range(BZ):
+            ref[12 + 4 * z : 16 + 4 * z] = slope2_ref[z, pl.ds(start, 2)].reshape(4, 8, X).astype(SENT)
+
+
+def widen(at, me_ref, slope2_ref, re_ref, ro_ref, ma_ref, s2y_ref):
+    pz, py = at[2], at[3]
+    ma_ref[12:24] = me_ref[:12]
+    ma_ref[pl.ds(24 - 24 * py, 12)] = re_ref[:12]
+    ma_ref[pl.ds(24 * py, 12)] = ro_ref[:12]
+    for z in range(BZ):
+        s2y_ref[z, 2 : 2 + BY] = slope2_ref[z].astype(bf16)
+        for ref, start in ((re_ref, 10 - 10 * py), (ro_ref, 10 * py)):
+            rows = ref[12 + 4 * z : 16 + 4 * z].astype(f32).reshape(2, C, X)
+            s2y_ref[z, pl.ds(start, 2)] = rows.astype(bf16)
+    for k in range(2):
+        rows = s2y_ref[2 - 2 * pz + k].astype(f32).reshape(24, 8, X)
+        ma_ref[36 + 24 * k : 60 + 24 * k] = rows.astype(SENT)
+
+
+def relay(at, ma_ref, ra_ref, s2y_ref, mb_ref):
+    pz = at[2]
+    mb_ref[:36] = ma_ref[:36]
+    mb_ref[36:72] = ra_ref[:36]
+    for k in range(2):
+        rows = s2y_ref[2 * pz + k].astype(f32).reshape(24, 8, X)
+        mb_ref[72 + 24 * k : 96 + 24 * k] = rows.astype(SENT)
 
 
 def march(nz, ny, at, own_ref, ye_ref, mate_ref, far_ref, far2_ref, g0_ref, dpre_ref,
@@ -170,15 +197,18 @@
                 else:
                     ref[start + k] = plane
 
+    def piece(ref, first):
+        return lambda i, f, k: ref[first + 12 * i + 4 * f + k]
+
     def mine(i, f, k):
-        return own_ref[f, k] if i == 1 else ye_ref[i, f, k]
+        return own_ref[f, k] if i == 1 else ye_ref[12 * i + 4 * f + k]
 
     place(8 + 4 * pz, mine)
-    place(12 - 4 * pz, lambda i, f, k: mate_ref[i, f, k])
-    place(16 * pz + 4 - 4 * pz, lambda i, f, k: far_ref[0, i, f, k])
-    place(16 * pz + 4 * pz, lambda i, f, k: far_ref[1, i, f, k])
-    place(16 - 16 * pz + 4 * pz, lambda i, f, k: far2_ref[0, i, f, k])
-    place(16 - 16 * pz + 4 - 4 * pz, lambda i, f, k: far2_ref[1, i, f, k])
+    place(12 - 4 * pz, piece(mate_ref, 0))
+    place(16 * pz + 4 - 4 * pz, piece(far_ref, 0))
+    place(16 * pz + 4 * pz, piece(far_ref, 36))
+    place(16 - 16 * pz + 4 * pz, piece(far2_ref, 0))
+    place(16 - 16 * pz + 4 - 4 * pz, piece(far2_ref, 36))
 
     dd[0, 0] = jnp.zeros((24, X), f32)
     rows_in = inside(iy * BY - 8, (24, X), ny)
@@ -212,7 +242,7 @@
                 dd[0, z] = jnp.where(within(z), jax.nn.sigmoid(new) - lab[z], 0.0)
             return carry
 
-        lax.fori_loop(t, 20 - t, step, 0)
+        lax.fori_loop(t, 20 - t, step, 0, unroll=2)
 
     for n, t in enumerate((3, 2, 1)):
         src, dst = n % 2, (n + 1) % 2
@@ -233,7 +263,7 @@
             return local, e + qz, a1
 
         zero = dd[0, 0]
-        lax.fori_loop(2 + n + 1, 18 - n - 1, back, (zero, zero, zero))
+        lax.fori_loop(3 + n, 17 - n, back, (zero, zero, zero), unroll=2)
 
     for k in range(8):
         z = base + 6 + k
@@ -244,7 +274,7 @@
         dpre_ref[k] = one + A * two * g0_ref[k]
 
 
-def backward(at, dpre_ref, slope2_ref, s2y_ref, sa_ref, sb_ref, sw_ref, hx_ref, fx_ref, slope1_ref,
+def backward(at, dpre_ref, slope2_ref, s2y_ref, ra_ref, rb_ref, sw_ref, hx_ref, fx_ref, slope1_ref,
              top_ref, w1_ref, w2_ref, df_ref, grad_ref, dx_ref, ex_ref):
     pz = at[2]
     sw = sw_ref[...]
@@ -265,8 +295,10 @@
             return s2y_ref[k, y].astype(f32)
         second(2 + k, k, own)
     for k in range(2):
-        second(6 - 6 * pz + k, k, lambda y, k=k: sa_ref[k, y].astype(f32))
-        second(6 * pz + k, k, lambda y, k=k: sb_ref[k, y].astype(f32))
+        for ref, first, z in ((ra_ref, 36, 6 - 6 * pz), (rb_ref, 72, 6 * pz)):
+            def far(y, ref=ref, first=first + 24 * k):
+                return ref[first + 2 * y : first + 2 * y + 2].astype(f32).reshape(C, X)
+            second(z + k, k, far)
 
     w2 = w2_ref[...]
     w1 = w1_ref[...]
@@ -298,13 +330,13 @@
 
     def weights(z, carry):
         g1, g2, gs = carry
+        d2 = jnp.concatenate([dx_ref[z + 2, y + 2, 1] for y in range(BY)], axis=1)
+        d1 = jnp.concatenate([ex_ref[z + 1, y + 1, 1] for y in range(BY)], axis=1)
+        p2 = [hx_ref[pl.ds(z, 3), y : y + 3].reshape(TAPS, X) for y in range(BY)]
+        p1 = [fx_ref[pl.ds(z + 1, 3), y + 1 : y + 4].reshape(TAPS, X) for y in range(BY)]
+        g2 = g2 + lax.dot_general(d2, jnp.concatenate(p2, axis=1), nt, preferred_element_type=f32)
+        g1 = g1 + lax.dot_general(d1, jnp.concatenate(p1, axis=1), nt, preferred_element_type=f32)
         for y in range(BY):
-            d2 = dx_ref[z + 2, y + 2, 1]
-            d1 = ex_ref[z + 1, y + 1, 1]
-            p2 = hx_ref[pl.ds(z, 3), y : y + 3].reshape(TAPS, X)
-            p1 = fx_ref[pl.ds(z + 1, 3), y + 1 : y + 4].reshape(TAPS, X)
-            g2 = g2 + lax.dot_general(d2, p2, nt, preferred_element_type=f32)
-            g1 = g1 + lax.dot_general(d1, p1, nt, preferred_element_type=f32)
             gs = gs + dpre_ref[z + 2, 4 + y : 5 + y, :] * top_ref[z, y]
         return g1, g2, gs
 
@@ -341,7 +373,7 @@
             out_specs=[vmem] * len(outs) if many else vmem,
             scratch_shapes=list(scratch),
             cost_estimate=pl.CostEstimate(flops=flops, bytes_accessed=size, transcendentals=0),
-            compiler_params=pltpu.CompilerParams(vmem_limit_bytes=40 * 1024 * 1024),
+            compiler_params=pltpu.CompilerParams(vmem_limit_bytes=16 * 1024 * 1024),
         )(*args)
 
     return run
@@ -381,11 +413,14 @@
     keep = lax.dynamic_index_in_dim(grad, core, 0, keepdims=False)
     give = lax.dynamic_index_in_dim(grad, 1 - core, 0, keepdims=False)
     part = keep + even(give, "gz")
-    for axis, masks in (("gy", (1, 3, 4, 8)), ("gz", (8, 24, 2, 6))):
+    for axis, unit in (("gy", 1), ("gy", 4), ("gz", 8), ("gz", 2)):
         n = lax.axis_size(axis)
-        for mask in masks:
-            if mask < n:
-                part = part + lax.ppermute(part, axis, [(i, i ^ mask) for i in range(n)])
+        masks = [m * unit for m in (1, 2, 3) if m * unit < n]
+        got = [lax.ppermute(part, axis, [(i, i ^ m) for i in range(n)]) for m in masks]
+        if len(got) == 3:
+            part = (part + got[0]) + (got[1] + got[2])
+        elif got:
+            part = part + got[0]
     other = even(part, "gz")
     return jnp.where(core == 0, part, other), jnp.where(core == 0, other, part)
 
@@ -409,7 +444,7 @@
     )(at, ft, sign_map, re, ro)
     ra, rb = even(ma, "gz"), odd(mb, "gz")
 
-    fx, hx, slope1, slope2, top, fields, own, g0 = call(
+    fx, hx, slope1, slope2, top, fe, fo, own, g0 = call(
         lambda *refs: forward(nz, ny, *refs),
         [
             shape((8, 12, 3, C, X)),
@@ -417,26 +452,20 @@
             shape((6, 10, C, X), f32),
             shape((BZ, BY, C, X), f32),
             shape((BZ, BY, C, X), f32),
-            shape((3, BZ, BY, X), SENT),
+            shape((28, 8, X), SENT),
+            shape((28, 8, X), SENT),
             shape((3, BZ, BY, X), f32),
             shape((8, 16, X), f32),
         ],
         [pltpu.VMEM((10, 16, X), f32)],
     )(at, fy, sy, ra, rb, labels, w1, w2, sw)
 
-    fe, fo = even(fields, "gy"), odd(fields, "gy")
-    before, after = jnp.where(py == 0, fo, fe), jnp.where(py == 0, fe, fo)
-    ye = jnp.stack([before, fields, after])
-    mate = even(ye, "gz")
-    far = odd(jnp.stack([ye, mate]), "gz")
-    far2 = even(far, "gz")
-
-    s2 = slope2.astype(bf16)
-    se = even(lax.dynamic_slice_in_dim(s2, 6 - 6 * py, 2, 1), "gy")
-    so = odd(lax.dynamic_slice_in_dim(s2, 6 * py, 2, 1), "gy")
-    s2y = jnp.concatenate([jnp.where(py == 0, so, se), s2, jnp.where(py == 0, se, so)], axis=1)
-    sa = even(lax.dynamic_slice_in_dim(s2y, 2 - 2 * pz, 2, 0), "gz")
-    sb = odd(lax.dynamic_slice_in_dim(s2y, 2 * pz, 2, 0), "gz")
+    ge, go = even(fe, "gy"), odd(fo, "gy")
+    fa, s2y = call(widen, [shape((84, 8, X), SENT), shape((BZ, 12, C, X))])(at, fe, slope2, ge, go)
+    ha = even(fa, "gz")
+    fb = call(relay, shape((120, 8, X), SENT))(at, fa, ha, s2y)
+    hb = odd(fb, "gz")
+    hc = even(hb[:72], "gz")
 
     plane = (24, 24, X)
     dpre = call(
@@ -454,13 +483,13 @@
             pltpu.VMEM(plane, f32),
             pltpu.VMEM((2,) + plane, f32),
         ],
-    )(at, own, ye, mate, far, far2, g0)
+    )(at, own, fa, ha, hb, hc, g0)
 
     d_features, grad = call(
         backward,
         [shape((C, BZ, BY, X)), shape((2, C, 512), f32)],
         [pltpu.VMEM((8, 12, 3, C, X), bf16), pltpu.VMEM((6, 10, 3, C, X), bf16)],
-    )(at, dpre, slope2, s2y, sa, sb, sw, hx, fx, slope1, top, w1b, w2b)
+    )(at, dpre, slope2, s2y, ha, hb, sw, hx, fx, slope1, top, w1b, w2b)
 
     a, b = total_of(grad, iz)
     out = call(finish, shape((2, C, 512), f32))(None, a, b)

time: 175 us -> 175 us (level)
  waiting for transfers between devices: 37.7 us -> 26.2 us
  starting transfers between devices: 97.1 us -> 105 us
  local copies, waits for them, and re-layouts: 13.9 us -> 18.9 us
  Pallas kernels: 21.6 us -> 18.6 us
    ppermute x8 -> x12, starting transfers between devices: 29.4 us -> 60.2 us  [total_of(): lax.ppermute(part, axis, [(i, i ^ m) for i in range(n)])]
    ppermute x9 -> x7, starting transfers between devices: 46.3 us -> 32.6 us  [even(): return lax.ppermute(value, axis, [(i, i ^ 1) for i in range(n)])]
    ppermute x6 -> x4, starting transfers between devices: 21.5 us -> 12.6 us  [odd(): return lax.ppermute(value, axis, pairs + [(j, i) for i, j in pairs])]
    ppermute x8 -> x12, waiting for transfers between devices: 23.4 us -> 15.4 us  [total_of(): lax.ppermute(part, axis, [(i, i ^ m) for i in range(n)])]
    ppermute x6 -> x4, waiting for transfers between devices: 12.3 us -> 6.88 us  [odd(): return lax.ppermute(value, axis, pairs + [(j, i) for i, j in pairs])]
    pallas_call x6 -> x8, Pallas kernels: 21.6 us -> 18.6 us  [run(): pl.pallas_call(kernel, out_shape=outs, in_specs=specs, out_specs=[vmem] *...]
    ppermute x9 -> x7, waiting for transfers between devices: 2.02 us -> 3.92 us  [even(): return lax.ppermute(value, axis, [(i, i ^ 1) for i in range(n)])]
    reshape x2, local copies, waits for them, and re-layouts: 1.47 us -> 3.24 us  [taps_back(): jnp.flip(weight, (2, 3, 4)).transpose(1, 2, 3, 4, 0).reshape(C, 3, 3, 3 * C)]
  transfers between devices with their start and end apart: 23 -> 23, of which waited for: 12 -> 11; matrix products, arithmetic and copies ran while one was open for 5% -> 8% of each run, Pallas kernels for 5% -> 0%
where the time goes in v2:
time: 175 us; the launch traced here: 174 us
  starting transfers between devices  105 us (60%)
  waiting for transfers between devices  26.2 us (15%)
  local copies, waits for them, and re-layouts  18.9 us (11%)
  Pallas kernels  18.6 us (11%)
  other arithmetic  3.33 us (2%)
    ppermute x12, starting transfers between devices, total_of(): lax.ppermute(part, axis, [(i, i ^ m) for i in range(n)])  60.2 us
    ppermute x7, starting transfers between devices, even(): return lax.ppermute(value, axis, [(i, i ^ 1) for i in range(n)])  32.6 us
    pallas_call x8, Pallas kernels, run(): pl.pallas_call(kernel, out_shape=outs, in_specs=specs, out_specs=[vmem] *...  18.6 us
    ppermute x12, waiting for transfers between devices, total_of(): lax.ppermute(part, axis, [(i, i ^ m) for i in range(n)])  15.4 us
    ppermute x4, starting transfers between devices, odd(): return lax.ppermute(value, axis, pairs + [(j, i) for i, j in pairs])  12.6 us
    ppermute x4, waiting for transfers between devices, odd(): return lax.ppermute(value, axis, pairs + [(j, i) for i, j in pairs])  6.88 us
    unnamed x24, local copies, waits for them, and re-layouts  6.23 us
    ppermute x7, waiting for transfers between devices, even(): return lax.ppermute(value, axis, [(i, i ^ 1) for i in range(n)])  3.92 us
  transfers between devices with their start and end apart: 23, of which 11 were waited for; matrix products, arithmetic and copies ran while one was open for 8% of the time, Pallas kernels for 0%

profile of v2, /device:TPU:1, one launch (start us, length us, event | category | flops | bytes accessed | tf_op | source)
XLA Modules:
  0.0 173.7 jit_solution(8042948451319816472)
XLA Ops:
  0.8 0.9 copy-done.2
  3.0 3.9 %collective-permute-start = (bf16[9,16,128]{2,1,0:T(8,128)(2,1)S(1)}, bf16[9,16,128]{2,1,0:T(8,128)(2,1)S(1)}, u32[]{:S(2)}, u32[]{:S(2)}) collective-permute-start(bf16[9,16,128]{2,1,0:T(8,128)(2,1)S(1)} %get-tuple-element.25), channel_id=1, source_target_pairs={{0,1},{1,0},{2,3},{3,2},{4,5},{5,4},{6,7},{7,6},{8,9},{9,8},{10,11... | collective-permute-start | bytes 110600 | tf_op jit(solution)/shard_map/ppermute | solution.py:388
  7.6 1.0 copy.16
  8.9 1.0 copy.18
  10.6 7.6 %collective-permute-start.2 = (bf16[27,16,128]{2,1,0:T(8,128)(2,1)S(1)}, bf16[27,16,128]{2,1,0:T(8,128)(2,1)S(1)}, u32[]{:S(2)}, u32[]{:S(2)}) collective-permute-start(bf16[27,16,128]{2,1,0:T(8,128)(2,1)S(1)} %get-tuple-element.29), channel_id=1, source_target_pairs={{0,16},{16,0},{32,48},{48,32},{64,80},{80,64},{96,112},{112,96},{1... | collective-permute-start | bytes 331784 | tf_op jit(solution)/shard_map/ppermute | solution.py:388
  18.2 4.0 %collective-permute-start.3 = (bf16[27,16,128]{2,1,0:T(8,128)(2,1)S(1)}, bf16[27,16,128]{2,1,0:T(8,128)(2,1)S(1)}, u32[]{:S(2)}, u32[]{:S(2)}) collective-permute-start(bf16[27,16,128]{2,1,0:T(8,128)(2,1)S(1)} %get-tuple-element.30), channel_id=1, source_target_pairs={{16,32},{48,64},{80,96},{112,128},{144,160},{176,192},{208,224},{2... | collective-permute-start | bytes 331784 | tf_op jit(solution)/shard_map/ppermute | solution.py:394
  22.4 5.7 %collective-permute-done.3.refs_4_ = bf16[27,16,128]{2,1,0:T(8,128)(2,1)S(1)} collective-permute-done((bf16[27,16,128]{2,1,0:T(8,128)(2,1)S(1)}, bf16[27,16,128]{2,1,0:T(8,128)(2,1)S(1)}, u32[]{:S(2)}, u32[]{:S(2)}) %collective-permute-start.3) | collective-permute-done | bytes 110624 | tf_op jit(solution)/shard_map/ppermute | solution.py:394
  28.2 3.9 %shard_map.95 = (bf16[8,12,3,16,128]{4,3,2,1,0:T(8,128)(2,1)S(1)}, bf16[6,10,3,16,128]{4,3,2,1,0:T(8,128)(2,1)S(1)}, f32[6,10,16,128]{3,2,1,0:T(8,128)S(1)}, f32...) custom-call(s32[4]{0:T(128)S(1)} %pad_add_fusion.at.refs_0_, ...), custom_call_target="tpu_custom_call" | custom-call | bytes 548880 | tf_op jit(solution)/shard_map/pallas_call | solution.py:369
  32.8 7.1 %collective-permute-start.4 = (bf16[28,8,128]{2,1,0:T(8,128)(2,1)S(1)}, bf16[28,8,128]{2,1,0:T(8,128)(2,1)S(1)}, u32[]{:S(2)}, u32[]{:S(2)}) collective-permute-start(bf16[28,8,128]{2,1,0:T(8,128)(2,1)S(1)} %get-tuple-element.32.me_ref), channel_id=1, source_target_pairs={{0,1},{1,0},{2,3},{3,2},{4,5},{5,4},{6,7},{7,6},{8,9},{9,8},{10,11... | collective-permute-start | bytes 172040 | tf_op jit(solution)/shard_map/ppermute | solution.py:388
  40.6 0.9 collective-permute-done.4.re_ref
  42.1 1.9 %collective-permute-start.6 = (bf16[84,8,128]{2,1,0:T(8,128)(2,1)S(1)}, bf16[84,8,128]{2,1,0:T(8,128)(2,1)S(1)}, u32[]{:S(2)}, u32[]{:S(2)}) collective-permute-start(bf16[84,8,128]{2,1,0:T(8,128)(2,1)S(1)} %get-tuple-element.35.ma_ref.refs_2_), channel_id=1, source_target_pairs={{0,16},{16,0},{32,48},{48,32},{64,80},{80,64},{96,112},{112,96},{1... | collective-permute-start | bytes 516104 | tf_op jit(solution)/shard_map/ppermute | solution.py:388
  44.0 1.4 collective-permute-done.6.ra_ref.refs_3_
  45.4 1.3 shard_map.97
  46.6 7.3 %collective-permute-start.7 = (bf16[120,8,128]{2,1,0:T(8,128)(2,1)}, bf16[120,8,128]{2,1,0:T(8,128)(2,1)S(1)}, u32[]{:S(2)}, u32[]{:S(2)}) collective-permute-start(bf16[120,8,128]{2,1,0:T(8,128)(2,1)} %shard_map.97), channel_id=1, source_target_pairs={{16,32},{48,64},{80,96},{112,128},{144,160},{176,192},{208,224},{2... | collective-permute-start | bytes 737288 | tf_op jit(solution)/shard_map/ppermute | solution.py:394
  53.9 1.6 rev.7
  55.5 1.6 copy.20
  57.1 1.1 collective-permute-done.7.refs_4_.rb_ref
  58.9 1.9 %collective-permute-start.8 = (bf16[72,8,128]{2,1,0:T(8,128)(2,1)}, bf16[72,8,128]{2,1,0:T(8,128)(2,1)}, u32[]{:S(2)}, u32[]{:S(2)}) collective-permute-start(bf16[72,8,128]{2,1,0:T(8,128)(2,1)} %slice.16), channel_id=1, source_target_pairs={{0,16},{16,0},{32,48},{48,32},{64,80},{80,64},{96,112},{112,96},{1... | collective-permute-start | bytes 442376 | tf_op jit(solution)/shard_map/ppermute | solution.py:388
  60.8 1.6 fusion.10
  62.4 1.5 rev.8
  64.0 1.0 reshape.38.w1_ref
  65.0 1.6 copy.22
  66.6 1.6 fusion.11
  68.2 1.0 reshape.40.w2_ref
  69.3 0.8 copy-done.4
  70.9 5.4 %shard_map.98.dpre_ref = f32[8,16,128]{2,1,0:T(8,128)S(1)} custom-call(s32[4]{0:T(128)S(1)} %pad_add_fusion.at.refs_0_, f32[3,4,8,128]{3,2,1,0:T(8,128)S(1)} %copy-done.8, bf16[84,8,128]{2,1,0:T(8,128)(2,1)S(1)} %get-tuple-element.35.ma_ref.refs_2_, bf16[84,8,128]{2,1,0:T(8,128)(2,1)S(1)} %collective-permute-done.6.ra_ref.refs_3_, ...), custom_call_target="tpu_custom_call" | custom-call | bytes 851984 | tf_op jit(solution)/shard_map/pallas_call | solution.py:369
  76.3 0.9 copy-done.1
  77.3 6.1 %shard_map.99 = (bf16[16,4,8,128]{3,2,1,0:T(8,128)(2,1)}, f32[2,16,512]{2,1,0:T(8,128)S(1)}) custom-call(s32[4]{0:T(128)S(1)} %pad_add_fusion.at.refs_0_, f32[8,16,128]{2,1,0:T(8,128)S(1)} %shard_map.98.dpre_ref, f32[4,8,16,128]{3,2,1,0:T(8,128)S(1)} %get-tuple-element.33.slope2_ref, bf16[4,12,16,128]{3,2,1,0:T(8,128)(2,1)S(1)} %get-tuple-element.36.s2y_ref, ...), custom_call_target="tpu_custom_call" | custom-call | bytes 3694608 | tf_op jit(solution)/shard_map/pallas_call | solution.py:369
  83.4 2.4 %collective-permute-start.9 = (f32[16,512]{1,0:T(8,128)S(1)}, f32[16,512]{1,0:T(8,128)S(1)}, u32[]{:S(2)}, u32[]{:S(2)}) collective-permute-start(f32[16,512]{1,0:T(8,128)S(1)} %dynamic-slice_bitcast_fusion), channel_id=1, source_target_pairs={{0,16},{16,0},{32,48},{48,32},{64,80},{80,64},{96,112},{112,96},{1... | collective-permute-start | bytes 98312 | tf_op jit(solution)/shard_map/ppermute | solution.py:388
  86.6 10.9 %collective-permute-start.10 = (f32[16,512]{1,0:T(8,128)S(1)}, f32[16,512]{1,0:T(8,128)S(1)}, u32[]{:S(2)}, u32[]{:S(2)}) collective-permute-start(f32[16,512]{1,0:T(8,128)S(1)} %bitcast_add_fusion), channel_id=1, source_target_pairs={{0,1},{1,0},{2,3},{3,2},{4,5},{5,4},{6,7},{7,6},{8,9},{9,8},{10,11... | collective-permute-start | bytes 98312 | tf_op jit(solution)/shard_map/ppermute | solution.py:419
  97.6 7.0 %collective-permute-start.11 = (f32[16,512]{1,0:T(8,128)S(1)}, f32[16,512]{1,0:T(8,128)S(1)}, u32[]{:S(2)}, u32[]{:S(2)}) collective-permute-start(f32[16,512]{1,0:T(8,128)S(1)} %bitcast_add_fusion), channel_id=1, source_target_pairs={{0,2},{1,3},{2,0},{3,1},{4,6},{5,7},{6,4},{7,5},{8,10},{9,11},{10,... | collective-permute-start | bytes 98312 | tf_op jit(solution)/shard_map/ppermute | solution.py:419
  104.5 2.2 %collective-permute-start.12 = (f32[16,512]{1,0:T(8,128)S(1)}, f32[16,512]{1,0:T(8,128)S(1)}, u32[]{:S(2)}, u32[]{:S(2)}) collective-permute-start(f32[16,512]{1,0:T(8,128)S(1)} %bitcast_add_fusion), channel_id=1, source_target_pairs={{0,3},{1,2},{2,1},{3,0},{4,7},{5,6},{6,5},{7,4},{8,11},{9,10},{10,... | collective-permute-start | bytes 98312 | tf_op jit(solution)/shard_map/ppermute | solution.py:419
  106.8 3.6 %collective-permute-done.12 = f32[16,512]{1,0:T(8,128)S(1)} collective-permute-done((f32[16,512]{1,0:T(8,128)S(1)}, f32[16,512]{1,0:T(8,128)S(1)}, u32[]{:S(2)}, u32[]{:S(2)}) %collective-permute-start.12) | collective-permute-done | bytes 32800 | tf_op jit(solution)/shard_map/ppermute | solution.py:419
  110.4 2.7 %collective-permute-start.13 = (f32[16,512]{1,0:T(8,128)S(1)}, f32[16,512]{1,0:T(8,128)S(1)}, u32[]{:S(2)}, u32[]{:S(2)}) collective-permute-start(f32[16,512]{1,0:T(8,128)S(1)} %add_add_fusion.3), channel_id=1, source_target_pairs={{0,4},{1,5},{2,6},{3,7},{4,0},{5,1},{6,2},{7,3},{8,12},{9,13},{10,... | collective-permute-start | bytes 98312 | tf_op jit(solution)/shard_map/ppermute | solution.py:419
  113.2 2.3 %collective-permute-start.14 = (f32[16,512]{1,0:T(8,128)S(1)}, f32[16,512]{1,0:T(8,128)S(1)}, u32[]{:S(2)}, u32[]{:S(2)}) collective-permute-start(f32[16,512]{1,0:T(8,128)S(1)} %add_add_fusion.3), channel_id=1, source_target_pairs={{0,8},{1,9},{2,10},{3,11},{4,12},{5,13},{6,14},{7,15},{8,0},{9,1},... | collective-permute-start | bytes 98312 | tf_op jit(solution)/shard_map/ppermute | solution.py:419
  115.5 4.2 %collective-permute-start.15 = (f32[16,512]{1,0:T(8,128)S(1)}, f32[16,512]{1,0:T(8,128)S(1)}, u32[]{:S(2)}, u32[]{:S(2)}) collective-permute-start(f32[16,512]{1,0:T(8,128)S(1)} %add_add_fusion.3), channel_id=1, source_target_pairs={{0,12},{1,13},{2,14},{3,15},{4,8},{5,9},{6,10},{7,11},{8,4},{9,5},... | collective-permute-start | bytes 98312 | tf_op jit(solution)/shard_map/ppermute | solution.py:419
  119.8 2.3 %collective-permute-done.15 = f32[16,512]{1,0:T(8,128)S(1)} collective-permute-done((f32[16,512]{1,0:T(8,128)S(1)}, f32[16,512]{1,0:T(8,128)S(1)}, u32[]{:S(2)}, u32[]{:S(2)}) %collective-permute-start.15) | collective-permute-done | bytes 32800 | tf_op jit(solution)/shard_map/ppermute | solution.py:419
  122.1 7.9 %collective-permute-start.16 = (f32[16,512]{1,0:T(8,128)S(1)}, f32[16,512]{1,0:T(8,128)S(1)}, u32[]{:S(2)}, u32[]{:S(2)}) collective-permute-start(f32[16,512]{1,0:T(8,128)S(1)} %add_add_fusion.2), channel_id=1, source_target_pairs={{0,128},{16,144},{32,160},{48,176},{64,192},{80,208},{96,224},{112... | collective-permute-start | bytes 98312 | tf_op jit(solution)/shard_map/ppermute | solution.py:419
  130.0 4.8 %collective-permute-start.17 = (f32[16,512]{1,0:T(8,128)S(1)}, f32[16,512]{1,0:T(8,128)S(1)}, u32[]{:S(2)}, u32[]{:S(2)}) collective-permute-start(f32[16,512]{1,0:T(8,128)S(1)} %add_add_fusion.2), channel_id=1, source_target_pairs={{0,256},{16,272},{32,288},{48,304},{64,320},{80,336},{96,352},{112... | collective-permute-start | bytes 98312 | tf_op jit(solution)/shard_map/ppermute | solution.py:419
  134.8 1.9 %collective-permute-start.18 = (f32[16,512]{1,0:T(8,128)S(1)}, f32[16,512]{1,0:T(8,128)S(1)}, u32[]{:S(2)}, u32[]{:S(2)}) collective-permute-start(f32[16,512]{1,0:T(8,128)S(1)} %add_add_fusion.2), channel_id=1, source_target_pairs={{0,384},{16,400},{32,416},{48,432},{64,448},{80,464},{96,480},{112... | collective-permute-start | bytes 98312 | tf_op jit(solution)/shard_map/ppermute | solution.py:419
  136.8 3.9 %collective-permute-done.18 = f32[16,512]{1,0:T(8,128)S(1)} collective-permute-done((f32[16,512]{1,0:T(8,128)S(1)}, f32[16,512]{1,0:T(8,128)S(1)}, u32[]{:S(2)}, u32[]{:S(2)}) %collective-permute-start.18) | collective-permute-done | bytes 32800 | tf_op jit(solution)/shard_map/ppermute | solution.py:419
  140.7 3.7 %collective-permute-start.19 = (f32[16,512]{1,0:T(8,128)S(1)}, f32[16,512]{1,0:T(8,128)S(1)}, u32[]{:S(2)}, u32[]{:S(2)}) collective-permute-start(f32[16,512]{1,0:T(8,128)S(1)} %add_add_fusion.1), channel_id=1, source_target_pairs={{0,32},{16,48},{32,0},{48,16},{64,96},{80,112},{96,64},{112,80},{1... | collective-permute-start | bytes 98312 | tf_op jit(solution)/shard_map/ppermute | solution.py:419
  144.5 8.9 %collective-permute-start.20 = (f32[16,512]{1,0:T(8,128)S(1)}, f32[16,512]{1,0:T(8,128)S(1)}, u32[]{:S(2)}, u32[]{:S(2)}) collective-permute-start(f32[16,512]{1,0:T(8,128)S(1)} %add_add_fusion.1), channel_id=1, source_target_pairs={{0,64},{16,80},{32,96},{48,112},{64,0},{80,16},{96,32},{112,48},{1... | collective-permute-start | bytes 98312 | tf_op jit(solution)/shard_map/ppermute | solution.py:419
  153.4 3.5 %collective-permute-start.21 = (f32[16,512]{1,0:T(8,128)S(1)}, f32[16,512]{1,0:T(8,128)S(1)}, u32[]{:S(2)}, u32[]{:S(2)}) collective-permute-start(f32[16,512]{1,0:T(8,128)S(1)} %add_add_fusion.1), channel_id=1, source_target_pairs={{0,96},{16,112},{32,64},{48,80},{64,32},{80,48},{96,0},{112,16},{1... | collective-permute-start | bytes 98312 | tf_op jit(solution)/shard_map/ppermute | solution.py:419
  156.9 1.2 collective-permute-done.20
  158.1 4.3 %collective-permute-done.21 = f32[16,512]{1,0:T(8,128)S(1)} collective-permute-done((f32[16,512]{1,0:T(8,128)S(1)}, f32[16,512]{1,0:T(8,128)S(1)}, u32[]{:S(2)}, u32[]{:S(2)}) %collective-permute-start.21) | collective-permute-done | bytes 32800 | tf_op jit(solution)/shard_map/ppermute | solution.py:419
  162.4 7.8 %collective-permute-start.22 = (f32[16,512]{1,0:T(8,128)S(1)}, f32[16,512]{1,0:T(8,128)S(1)}, u32[]{:S(2)}, u32[]{:S(2)}) collective-permute-start(f32[16,512]{1,0:T(8,128)S(1)} %add_add_fusion), channel_id=1, source_target_pairs={{0,16},{16,0},{32,48},{48,32},{64,80},{80,64},{96,112},{112,96},{1... | collective-permute-start | bytes 98312 | tf_op jit(solution)/shard_map/ppermute | solution.py:388
  170.3 0.8 collective-permute-done.22
  (62 shorter events, 10.2 us)
Async XLA Ops:
  0.6 9.4 %copy-start.6 = (s32[4,8,128]{2,1,0:T(8,128)S(1)}, s32[4,8,128]{2,1,0:T(8,128)}, u32[]{:S(2)}) copy-start(s32[4,8,128]{2,1,0:T(8,128)} %s_ref.3) | copy-start | bytes 49156
  0.6 27.5 %copy-start.10 = (f32[16]{0:T(128)S(1)}, f32[16]{0:T(128)}, u32[]{:S(2)}) copy-start(f32[16]{0:T(128)} %param.11) | copy-start | bytes 196
  0.7 27.6 %copy-start.9 = (s32[4,8,128]{2,1,0:T(8,128)S(1)}, s32[4,8,128]{2,1,0:T(8,128)}, u32[]{:S(2)}) copy-start(s32[4,8,128]{2,1,0:T(8,128)} %refs_5_.1) | copy-start | bytes 49156
  0.8 0.9 copy-start.2
  1.7 0.7 copy-start.5
  3.0 7.0 %collective-permute-start = (bf16[9,16,128]{2,1,0:T(8,128)(2,1)S(1)}, bf16[9,16,128]{2,1,0:T(8,128)(2,1)S(1)}, u32[]{:S(2)}, u32[]{:S(2)}) collective-permute-start(bf16[9,16,128]{2,1,0:T(8,128)(2,1)S(1)} %get-tuple-element.25), channel_id=1, source_target_pairs={{0,1},{1,0},{2,3},{3,2},{4,5},{5,4},{6,7},{7,6},{8,9},{9,8},{10,11... | collective-permute-start | bytes 110600 | tf_op jit(solution)/shard_map/ppermute | solution.py:388
  6.9 3.1 %collective-permute-start.1 = (bf16[9,16,128]{2,1,0:T(8,128)(2,1)S(1)}, bf16[9,16,128]{2,1,0:T(8,128)(2,1)S(1)}, u32[]{:S(2)}, u32[]{:S(2)}) collective-permute-start(bf16[9,16,128]{2,1,0:T(8,128)(2,1)S(1)} %get-tuple-element.26), channel_id=1, source_target_pairs={{1,2},{3,4},{5,6},{7,8},{9,10},{11,12},{13,14},{2,1},{4,3},{6,5},{... | collective-permute-start | bytes 110600 | tf_op jit(solution)/shard_map/ppermute | solution.py:394
  10.6 11.8 %collective-permute-start.2 = (bf16[27,16,128]{2,1,0:T(8,128)(2,1)S(1)}, bf16[27,16,128]{2,1,0:T(8,128)(2,1)S(1)}, u32[]{:S(2)}, u32[]{:S(2)}) collective-permute-start(bf16[27,16,128]{2,1,0:T(8,128)(2,1)S(1)} %get-tuple-element.29), channel_id=1, source_target_pairs={{0,16},{16,0},{32,48},{48,32},{64,80},{80,64},{96,112},{112,96},{1... | collective-permute-start | bytes 331784 | tf_op jit(solution)/shard_map/ppermute | solution.py:388
  18.2 10.0 %collective-permute-start.3 = (bf16[27,16,128]{2,1,0:T(8,128)(2,1)S(1)}, bf16[27,16,128]{2,1,0:T(8,128)(2,1)S(1)}, u32[]{:S(2)}, u32[]{:S(2)}) collective-permute-start(bf16[27,16,128]{2,1,0:T(8,128)(2,1)S(1)} %get-tuple-element.30), channel_id=1, source_target_pairs={{16,32},{48,64},{80,96},{112,128},{144,160},{176,192},{208,224},{2... | collective-permute-start | bytes 331784 | tf_op jit(solution)/shard_map/ppermute | solution.py:394
  32.2 0.6 copy-start.7
  32.8 12.6 %copy-start = (f32[4,8,16,128]{3,2,1,0:T(8,128)}, f32[4,8,16,128]{3,2,1,0:T(8,128)S(1)}, u32[]{:S(2)}) copy-start(f32[4,8,16,128]{3,2,1,0:T(8,128)S(1)} %get-tuple-element.41.top_ref) | copy-start | bytes 786436
  32.8 31.2 %copy-start.3 = (f32[8,16,128]{2,1,0:T(8,128)}, f32[8,16,128]{2,1,0:T(8,128)S(1)}, u32[]{:S(2)}) copy-start(f32[8,16,128]{2,1,0:T(8,128)S(1)} %get-tuple-element.37.refs_6_) | copy-start | bytes 196612
  32.8 8.6 %collective-permute-start.4 = (bf16[28,8,128]{2,1,0:T(8,128)(2,1)S(1)}, bf16[28,8,128]{2,1,0:T(8,128)(2,1)S(1)}, u32[]{:S(2)}, u32[]{:S(2)}) collective-permute-start(bf16[28,8,128]{2,1,0:T(8,128)(2,1)S(1)} %get-tuple-element.32.me_ref), channel_id=1, source_target_pairs={{0,1},{1,0},{2,3},{3,2},{4,5},{5,4},{6,7},{7,6},{8,9},{9,8},{10,11... | collective-permute-start | bytes 172040 | tf_op jit(solution)/shard_map/ppermute | solution.py:388
  39.9 1.6 collective-permute-start.5
  42.1 3.3 %collective-permute-start.6 = (bf16[84,8,128]{2,1,0:T(8,128)(2,1)S(1)}, bf16[84,8,128]{2,1,0:T(8,128)(2,1)S(1)}, u32[]{:S(2)}, u32[]{:S(2)}) collective-permute-start(bf16[84,8,128]{2,1,0:T(8,128)(2,1)S(1)} %get-tuple-element.35.ma_ref.refs_2_), channel_id=1, source_target_pairs={{0,16},{16,0},{32,48},{48,32},{64,80},{80,64},{96,112},{112,96},{1... | collective-permute-start | bytes 516104 | tf_op jit(solution)/shard_map/ppermute | solution.py:388
  46.6 11.6 %collective-permute-start.7 = (bf16[120,8,128]{2,1,0:T(8,128)(2,1)}, bf16[120,8,128]{2,1,0:T(8,128)(2,1)S(1)}, u32[]{:S(2)}, u32[]{:S(2)}) collective-permute-start(bf16[120,8,128]{2,1,0:T(8,128)(2,1)} %shard_map.97), channel_id=1, source_target_pairs={{16,32},{48,64},{80,96},{112,128},{144,160},{176,192},{208,224},{2... | collective-permute-start | bytes 737288 | tf_op jit(solution)/shard_map/ppermute | solution.py:394
  58.9 10.3 %collective-permute-start.8 = (bf16[72,8,128]{2,1,0:T(8,128)(2,1)}, bf16[72,8,128]{2,1,0:T(8,128)(2,1)}, u32[]{:S(2)}, u32[]{:S(2)}) collective-permute-start(bf16[72,8,128]{2,1,0:T(8,128)(2,1)} %slice.16), channel_id=1, source_target_pairs={{0,16},{16,0},{32,48},{48,32},{64,80},{80,64},{96,112},{112,96},{1... | collective-permute-start | bytes 442376 | tf_op jit(solution)/shard_map/ppermute | solution.py:388
  69.3 0.8 copy-start.4
  70.1 0.8 copy-start.8
  76.3 1.0 copy-start.1
  83.4 3.2 %collective-permute-start.9 = (f32[16,512]{1,0:T(8,128)S(1)}, f32[16,512]{1,0:T(8,128)S(1)}, u32[]{:S(2)}, u32[]{:S(2)}) collective-permute-start(f32[16,512]{1,0:T(8,128)S(1)} %dynamic-slice_bitcast_fusion), channel_id=1, source_target_pairs={{0,16},{16,0},{32,48},{48,32},{64,80},{80,64},{96,112},{112,96},{1... | collective-permute-start | bytes 98312 | tf_op jit(solution)/shard_map/ppermute | solution.py:388
  86.6 20.1 %collective-permute-start.10 = (f32[16,512]{1,0:T(8,128)S(1)}, f32[16,512]{1,0:T(8,128)S(1)}, u32[]{:S(2)}, u32[]{:S(2)}) collective-permute-start(f32[16,512]{1,0:T(8,128)S(1)} %bitcast_add_fusion), channel_id=1, source_target_pairs={{0,1},{1,0},{2,3},{3,2},{4,5},{5,4},{6,7},{7,6},{8,9},{9,8},{10,11... | collective-permute-start | bytes 98312 | tf_op jit(solution)/shard_map/ppermute | solution.py:419
  97.6 9.2 %collective-permute-start.11 = (f32[16,512]{1,0:T(8,128)S(1)}, f32[16,512]{1,0:T(8,128)S(1)}, u32[]{:S(2)}, u32[]{:S(2)}) collective-permute-start(f32[16,512]{1,0:T(8,128)S(1)} %bitcast_add_fusion), channel_id=1, source_target_pairs={{0,2},{1,3},{2,0},{3,1},{4,6},{5,7},{6,4},{7,5},{8,10},{9,11},{10,... | collective-permute-start | bytes 98312 | tf_op jit(solution)/shard_map/ppermute | solution.py:419
  104.5 5.9 %collective-permute-start.12 = (f32[16,512]{1,0:T(8,128)S(1)}, f32[16,512]{1,0:T(8,128)S(1)}, u32[]{:S(2)}, u32[]{:S(2)}) collective-permute-start(f32[16,512]{1,0:T(8,128)S(1)} %bitcast_add_fusion), channel_id=1, source_target_pairs={{0,3},{1,2},{2,1},{3,0},{4,7},{5,6},{6,5},{7,4},{8,11},{9,10},{10,... | collective-permute-start | bytes 98312 | tf_op jit(solution)/shard_map/ppermute | solution.py:419
  110.4 9.3 %collective-permute-start.13 = (f32[16,512]{1,0:T(8,128)S(1)}, f32[16,512]{1,0:T(8,128)S(1)}, u32[]{:S(2)}, u32[]{:S(2)}) collective-permute-start(f32[16,512]{1,0:T(8,128)S(1)} %add_add_fusion.3), channel_id=1, source_target_pairs={{0,4},{1,5},{2,6},{3,7},{4,0},{5,1},{6,2},{7,3},{8,12},{9,13},{10,... | collective-permute-start | bytes 98312 | tf_op jit(solution)/shard_map/ppermute | solution.py:419
  113.2 6.6 %collective-permute-start.14 = (f32[16,512]{1,0:T(8,128)S(1)}, f32[16,512]{1,0:T(8,128)S(1)}, u32[]{:S(2)}, u32[]{:S(2)}) collective-permute-start(f32[16,512]{1,0:T(8,128)S(1)} %add_add_fusion.3), channel_id=1, source_target_pairs={{0,8},{1,9},{2,10},{3,11},{4,12},{5,13},{6,14},{7,15},{8,0},{9,1},... | collective-permute-start | bytes 98312 | tf_op jit(solution)/shard_map/ppermute | solution.py:419
  115.5 6.6 %collective-permute-start.15 = (f32[16,512]{1,0:T(8,128)S(1)}, f32[16,512]{1,0:T(8,128)S(1)}, u32[]{:S(2)}, u32[]{:S(2)}) collective-permute-start(f32[16,512]{1,0:T(8,128)S(1)} %add_add_fusion.3), channel_id=1, source_target_pairs={{0,12},{1,13},{2,14},{3,15},{4,8},{5,9},{6,10},{7,11},{8,4},{9,5},... | collective-permute-start | bytes 98312 | tf_op jit(solution)/shard_map/ppermute | solution.py:419
  122.1 14.7 %collective-permute-start.16 = (f32[16,512]{1,0:T(8,128)S(1)}, f32[16,512]{1,0:T(8,128)S(1)}, u32[]{:S(2)}, u32[]{:S(2)}) collective-permute-start(f32[16,512]{1,0:T(8,128)S(1)} %add_add_fusion.2), channel_id=1, source_target_pairs={{0,128},{16,144},{32,160},{48,176},{64,192},{80,208},{96,224},{112... | collective-permute-start | bytes 98312 | tf_op jit(solution)/shard_map/ppermute | solution.py:419
  130.0 6.8 %collective-permute-start.17 = (f32[16,512]{1,0:T(8,128)S(1)}, f32[16,512]{1,0:T(8,128)S(1)}, u32[]{:S(2)}, u32[]{:S(2)}) collective-permute-start(f32[16,512]{1,0:T(8,128)S(1)} %add_add_fusion.2), channel_id=1, source_target_pairs={{0,256},{16,272},{32,288},{48,304},{64,320},{80,336},{96,352},{112... | collective-permute-start | bytes 98312 | tf_op jit(solution)/shard_map/ppermute | solution.py:419
  134.8 5.9 %collective-permute-start.18 = (f32[16,512]{1,0:T(8,128)S(1)}, f32[16,512]{1,0:T(8,128)S(1)}, u32[]{:S(2)}, u32[]{:S(2)}) collective-permute-start(f32[16,512]{1,0:T(8,128)S(1)} %add_add_fusion.2), channel_id=1, source_target_pairs={{0,384},{16,400},{32,416},{48,432},{64,448},{80,464},{96,480},{112... | collective-permute-start | bytes 98312 | tf_op jit(solution)/shard_map/ppermute | solution.py:419
  140.7 16.2 %collective-permute-start.19 = (f32[16,512]{1,0:T(8,128)S(1)}, f32[16,512]{1,0:T(8,128)S(1)}, u32[]{:S(2)}, u32[]{:S(2)}) collective-permute-start(f32[16,512]{1,0:T(8,128)S(1)} %add_add_fusion.1), channel_id=1, source_target_pairs={{0,32},{16,48},{32,0},{48,16},{64,96},{80,112},{96,64},{112,80},{1... | collective-permute-start | bytes 98312 | tf_op jit(solution)/shard_map/ppermute | solution.py:419
  144.5 13.7 %collective-permute-start.20 = (f32[16,512]{1,0:T(8,128)S(1)}, f32[16,512]{1,0:T(8,128)S(1)}, u32[]{:S(2)}, u32[]{:S(2)}) collective-permute-start(f32[16,512]{1,0:T(8,128)S(1)} %add_add_fusion.1), channel_id=1, source_target_pairs={{0,64},{16,80},{32,96},{48,112},{64,0},{80,16},{96,32},{112,48},{1... | collective-permute-start | bytes 98312 | tf_op jit(solution)/shard_map/ppermute | solution.py:419
  153.4 9.0 %collective-permute-start.21 = (f32[16,512]{1,0:T(8,128)S(1)}, f32[16,512]{1,0:T(8,128)S(1)}, u32[]{:S(2)}, u32[]{:S(2)}) collective-permute-start(f32[16,512]{1,0:T(8,128)S(1)} %add_add_fusion.1), channel_id=1, source_target_pairs={{0,96},{16,112},{32,64},{48,80},{64,32},{80,48},{96,0},{112,16},{1... | collective-permute-start | bytes 98312 | tf_op jit(solution)/shard_map/ppermute | solution.py:419
  162.4 8.7 %collective-permute-start.22 = (f32[16,512]{1,0:T(8,128)S(1)}, f32[16,512]{1,0:T(8,128)S(1)}, u32[]{:S(2)}, u32[]{:S(2)}) collective-permute-start(f32[16,512]{1,0:T(8,128)S(1)} %add_add_fusion), channel_id=1, source_target_pairs={{0,16},{16,0},{32,48},{48,32},{64,80},{80,64},{96,112},{112,96},{1... | collective-permute-start | bytes 98312 | tf_op jit(solution)/shard_map/ppermute | solution.py:388

commit v3 on v2

--- a/solution.py
+++ b/solution.py
@@ -41,6 +41,22 @@
 def inside(start, shape, limit):
     row = start + lax.broadcasted_iota(jnp.int32, shape, 0)
     return (row >= 0) & (row < limit)
+
+
+def build(c1_ref, c2_ref, w1_ref, w2_ref, w1b_ref, w2b_ref):
+    zero = jnp.zeros((C, C), f32)
+    for src, fwd, adj in ((c1_ref, w1_ref, w1b_ref), (c2_ref, w2_ref, w2b_ref)):
+        for j in range(2):
+            one, two = [], []
+            for a in range(3):
+                for b in range(4):
+                    for c in range(3):
+                        tap = (a * 3 + b - j) * 3 + c
+                        ok = 0 <= b - j < 3
+                        one.append(src[tap].astype(f32) if ok else zero)
+                        two.append(src[26 - tap].astype(f32).T if ok else zero)
+            fwd[C * j : C * j + C] = jnp.concatenate(one, axis=1).astype(bf16)
+            adj[C * j : C * j + C] = jnp.concatenate(two, axis=1).astype(bf16)
 
 
 def prepare(at, f_ref, s_ref, ft_ref, me_ref, mo_ref):
@@ -159,7 +175,7 @@
             ref[12 + 4 * z : 16 + 4 * z] = slope2_ref[z, pl.ds(start, 2)].reshape(4, 8, X).astype(SENT)
 
 
-def widen(at, me_ref, slope2_ref, re_ref, ro_ref, ma_ref, s2y_ref):
+def widen(at, me_ref, slope2_ref, re_ref, ro_ref, ma_ref, mb_ref, s2y_ref):
     pz, py = at[2], at[3]
     ma_ref[12:24] = me_ref[:12]
     ma_ref[pl.ds(24 - 24 * py, 12)] = re_ref[:12]
@@ -172,15 +188,13 @@
     for k in range(2):
         rows = s2y_ref[2 - 2 * pz + k].astype(f32).reshape(24, 8, X)
         ma_ref[36 + 24 * k : 60 + 24 * k] = rows.astype(SENT)
-
-
-def relay(at, ma_ref, ra_ref, s2y_ref, mb_ref):
-    pz = at[2]
+        rows = s2y_ref[2 * pz + k].astype(f32).reshape(24, 8, X)
+        mb_ref[24 * k : 24 + 24 * k] = rows.astype(SENT)
+
+
+def relay(ma_ref, ra_ref, mb_ref):
     mb_ref[:36] = ma_ref[:36]
-    mb_ref[36:72] = ra_ref[:36]
-    for k in range(2):
-        rows = s2y_ref[2 * pz + k].astype(f32).reshape(24, 8, X)
-        mb_ref[72 + 24 * k : 96 + 24 * k] = rows.astype(SENT)
+    mb_ref[36:] = ra_ref[:36]
 
 
 def march(nz, ny, at, own_ref, ye_ref, mate_ref, far_ref, far2_ref, g0_ref, dpre_ref,
@@ -295,7 +309,7 @@
             return s2y_ref[k, y].astype(f32)
         second(2 + k, k, own)
     for k in range(2):
-        for ref, first, z in ((ra_ref, 36, 6 - 6 * pz), (rb_ref, 72, 6 * pz)):
+        for ref, first, z in ((ra_ref, 36, 6 - 6 * pz), (rb_ref, 0, 6 * pz)):
             def far(y, ref=ref, first=first + 24 * k):
                 return ref[first + 2 * y : first + 2 * y + 2].astype(f32).reshape(C, X)
             second(z + k, k, far)
@@ -345,16 +359,19 @@
     grad_ref[...] = jnp.zeros_like(grad_ref)
     grad_ref[0, :, :TAPS] = g1
     grad_ref[1, :, :TAPS] = g2
-    grad_ref[0, :, TAPS : TAPS + 1] = jnp.sum(gs, axis=1, keepdims=True)
-
-
-def finish(a_ref, b_ref, out_ref):
+    grad_ref[0, :1, TAPS : TAPS + C] = jnp.sum(jnp.transpose(gs), axis=0, keepdims=True)
+
+
+def finish(a_ref, b_ref, first_ref, second_ref, speed_ref):
     a, b = a_ref[...], b_ref[...]
     total = jnp.sum(a * a) + jnp.sum(b * b)
     count = 54.0 * C * C + C
     factor = 1.0 / jnp.maximum(jnp.sqrt(jnp.full((1, 1), total)) / jnp.sqrt(f32(count)), 1.0)
-    out_ref[0] = a * factor
-    out_ref[1] = b * factor
+    a, b = a * factor, b * factor
+    for t in range(27):
+        first_ref[t] = a[:, C * t : C * t + C]
+        second_ref[t] = b[:, C * t : C * t + C]
+    speed_ref[...] = a[:1, TAPS : TAPS + C]
 
 
 def call(kernel, outs, scratch=(), flops=0):
@@ -394,20 +411,6 @@
     return lax.ppermute(value, axis, pairs + [(j, i) for i, j in pairs])
 
 
-def row_weights(taps_last):
-    first = jnp.pad(taps_last, ((0, 0), (0, 0), (0, 1), (0, 0)))
-    second = jnp.pad(taps_last, ((0, 0), (0, 0), (1, 0), (0, 0)))
-    return jnp.concatenate([first, second], axis=0).reshape(2 * C, 36 * C)
-
-
-def taps_of(weight):
-    return weight.transpose(0, 2, 3, 4, 1).reshape(C, 3, 3, 3 * C)
-
-
-def taps_back(weight):
-    return jnp.flip(weight, (2, 3, 4)).transpose(1, 2, 3, 4, 0).reshape(C, 3, 3, 3 * C)
-
-
 def total_of(grad, iz):
     core = iz % 2
     keep = lax.dynamic_index_in_dim(grad, core, 0, keepdims=False)
@@ -415,12 +418,12 @@
     part = keep + even(give, "gz")
     for axis, unit in (("gy", 1), ("gy", 4), ("gz", 8), ("gz", 2)):
         n = lax.axis_size(axis)
-        masks = [m * unit for m in (1, 2, 3) if m * unit < n]
-        got = [lax.ppermute(part, axis, [(i, i ^ m) for i in range(n)]) for m in masks]
-        if len(got) == 3:
-            part = (part + got[0]) + (got[1] + got[2])
-        elif got:
-            part = part + got[0]
+        size = min(4, n // unit)
+        if size > 1:
+            firsts = [i for i in range(n) if (i // unit) % size == 0]
+            groups = [[i + unit * k for k in range(size)] for i in firsts]
+            parts = lax.all_gather(part, axis, axis_index_groups=groups)
+            part = jnp.sum(parts, axis=0)
     other = even(part, "gz")
     return jnp.where(core == 0, part, other), jnp.where(core == 0, other, part)
 
@@ -431,8 +434,8 @@
     pz, py = iz % 2, iy % 2
     at = jnp.stack([iz, iy, pz, py]).astype(jnp.int32)
     sw = jnp.broadcast_to(speed_weight[:, None], (C, X))
-    w1, w2 = row_weights(taps_of(conv_first)), row_weights(taps_of(conv_second))
-    w1b, w2b = row_weights(taps_back(conv_first)), row_weights(taps_back(conv_second))
+    taps = [w.transpose(2, 3, 4, 0, 1).reshape(27, C, C) for w in (conv_first, conv_second)]
+    w1, w2, w1b, w2b = call(build, [shape((2 * C, 36 * C))] * 4)(None, *taps)
 
     ft, me, mo = call(prepare, [shape((BZ, BY, C, X)), shape((9, C, X)), shape((9, C, X))])(
         at, features, sign_map
@@ -461,11 +464,14 @@
     )(at, fy, sy, ra, rb, labels, w1, w2, sw)
 
     ge, go = even(fe, "gy"), odd(fo, "gy")
-    fa, s2y = call(widen, [shape((84, 8, X), SENT), shape((BZ, 12, C, X))])(at, fe, slope2, ge, go)
+    fa, fs, s2y = call(
+        widen, [shape((84, 8, X), SENT), shape((48, 8, X), SENT), shape((BZ, 12, C, X))]
+    )(at, fe, slope2, ge, go)
     ha = even(fa, "gz")
-    fb = call(relay, shape((120, 8, X), SENT))(at, fa, ha, s2y)
-    hb = odd(fb, "gz")
-    hc = even(hb[:72], "gz")
+    hb = odd(call(relay, shape((72, 8, X), SENT))(None, fa, ha), "gz")
+    hb, fs = lax.optimization_barrier((hb, fs))
+    hc = even(hb, "gz")
+    hs = odd(fs, "gz")
 
     plane = (24, 24, X)
     dpre = call(
@@ -489,14 +495,15 @@
         backward,
         [shape((C, BZ, BY, X)), shape((2, C, 512), f32)],
         [pltpu.VMEM((8, 12, 3, C, X), bf16), pltpu.VMEM((6, 10, 3, C, X), bf16)],
-    )(at, dpre, slope2, s2y, ha, hb, sw, hx, fx, slope1, top, w1b, w2b)
+    )(at, dpre, slope2, s2y, ha, hs, sw, hx, fx, slope1, top, w1b, w2b)
 
     a, b = total_of(grad, iz)
-    out = call(finish, shape((2, C, 512), f32))(None, a, b)
+    tap_major = shape((27, C, C), f32)
+    first, second, speed = call(finish, [tap_major, tap_major, shape((1, C), f32)])(None, a, b)
     first, second = (
-        out[i, :, :TAPS].reshape(C, 3, 3, 3, C).transpose(0, 4, 1, 2, 3) for i in range(2)
+        g.reshape(3, 3, 3, C, C).transpose(3, 4, 0, 1, 2) for g in (first, second)
     )
-    return d_features, first, second, out[0, :, TAPS]
+    return d_features, first, second, speed.reshape(C)
 
 
 def solution(mesh):

time: 175 us -> 158 us (0.903)
  blocking collectives: 0 us -> 57.4 us
  starting transfers between devices: 105 us -> 58.7 us
  waiting for transfers between devices: 26.2 us -> 11.4 us
  local copies, waits for them, and re-layouts: 18.9 us -> 9.03 us
  other arithmetic: 3.33 us -> 0.14 us
    ppermute x12 -> x0, starting transfers between devices: 60.2 us -> none  [total_of(): lax.ppermute(part, axis, [(i, i ^ m) for i in range(n)])]
    all_gather x0 -> x4, blocking collectives: none -> 57.4 us  [total_of(): parts = lax.all_gather(part, axis, axis_index_groups=groups)]
    ppermute x12 -> x0, waiting for transfers between devices: 15.4 us -> none  [total_of(): lax.ppermute(part, axis, [(i, i ^ m) for i in range(n)])]
    ppermute x4 -> x5, starting transfers between devices: 12.6 us -> 19.8 us  [odd(): return lax.ppermute(value, axis, pairs + [(j, i) for i, j in pairs])]
    ppermute x7, starting transfers between devices: 32.6 us -> 38.8 us  [even(): return lax.ppermute(value, axis, [(i, i ^ 1) for i in range(n)])]
    reshape x8 -> x0, local copies, waits for them, and re-layouts: 5.78 us -> none  [the longest x2 3.24 us: taps_back(): jnp.flip(weight, (2, 3, 4)).transpose(1, 2, 3, 4, 0).reshape(C, 3, 3, 3 * C)]
    concatenate x4 -> x0, other arithmetic: 3.19 us -> none  [row_weights(): return jnp.concatenate([first, second], axis=0).reshape(2 * C, 36 * C)]
    rev x2 -> x0, local copies, waits for them, and re-layouts: 3.1 us -> none  [taps_back(): jnp.flip(weight, (2, 3, 4)).transpose(1, 2, 3, 4, 0).reshape(C, 3, 3, 3 * C)]
  transfers between devices with their start and end apart: 23 -> 12, of which waited for: 11 -> 7; matrix products, arithmetic and copies ran while one was open for 8% -> 0% of each run, Pallas kernels for 0% -> 4%
where the time goes in v3:
time: 158 us; the launch traced here: 157 us
  starting transfers between devices  58.7 us (37%)
  blocking collectives  57.4 us (36%)
  Pallas kernels  19.8 us (13%)
  waiting for transfers between devices  11.4 us (7%)
  local copies, waits for them, and re-layouts  9.03 us (6%)
    all_gather x4, blocking collectives, total_of(): parts = lax.all_gather(part, axis, axis_index_groups=groups)  57.4 us
    ppermute x7, starting transfers between devices, even(): return lax.ppermute(value, axis, [(i, i ^ 1) for i in range(n)])  38.8 us
    ppermute x5, starting transfers between devices, odd(): return lax.ppermute(value, axis, pairs + [(j, i) for i, j in pairs])  19.8 us
    pallas_call x9, Pallas kernels, run(): pl.pallas_call(kernel, out_shape=outs, in_specs=specs, out_specs=[vmem] *...  19.8 us
    unnamed x22, local copies, waits for them, and re-layouts  8.3 us
    ppermute x5, waiting for transfers between devices, odd(): return lax.ppermute(value, axis, pairs + [(j, i) for i, j in pairs])  6.48 us
    ppermute x7, waiting for transfers between devices, even(): return lax.ppermute(value, axis, [(i, i ^ 1) for i in range(n)])  4.92 us
  transfers between devices with their start and end apart: 12, of which 7 were waited for; matrix products, arithmetic and copies ran while one was open for 0% of the time, Pallas kernels for 4%

profile of v3, /device:TPU:1, one launch (start us, length us, event | category | flops | bytes accessed | tf_op | source)
XLA Modules:
  0.0 157.4 jit_solution(4840983169353011828)
XLA Ops:
  0.6 0.1 pad_add_fusion.at.refs_0_
  0.7 0.9 copy-done
  1.6 0.7 copy-done.3
  2.4 0.6 shard_map.93
  3.0 3.9 %collective-permute-start = (bf16[9,16,128]{2,1,0:T(8,128)(2,1)S(1)}, bf16[9,16,128]{2,1,0:T(8,128)(2,1)S(1)}, u32[]{:S(2)}, u32[]{:S(2)}) collective-permute-start(bf16[9,16,128]{2,1,0:T(8,128)(2,1)S(1)} %get-tuple-element.35), channel_id=1, source_target_pairs={{0,1},{1,0},{2,3},{3,2},{4,5},{5,4},{6,7},{7,6},{8,9},{9,8},{10,11... | collective-permute-start | bytes 110600 | tf_op jit(solution)/shard_map/ppermute | solution.py:405
  6.9 0.7 collective-permute-start.1
  7.6 0.7 collective-permute-done.re_ref
  8.2 0.6 shard_map.94
  8.8 9.3 %collective-permute-start.2 = (bf16[27,16,128]{2,1,0:T(8,128)(2,1)S(1)}, bf16[27,16,128]{2,1,0:T(8,128)(2,1)S(1)}, u32[]{:S(2)}, u32[]{:S(2)}) collective-permute-start(bf16[27,16,128]{2,1,0:T(8,128)(2,1)S(1)} %get-tuple-element.39), channel_id=1, source_target_pairs={{0,16},{16,0},{32,48},{48,32},{64,80},{80,64},{96,112},{112,96},{1... | collective-permute-start | bytes 331784 | tf_op jit(solution)/shard_map/ppermute | solution.py:405
  18.2 3.4 %collective-permute-start.3 = (bf16[27,16,128]{2,1,0:T(8,128)(2,1)S(1)}, bf16[27,16,128]{2,1,0:T(8,128)(2,1)S(1)}, u32[]{:S(2)}, u32[]{:S(2)}) collective-permute-start(bf16[27,16,128]{2,1,0:T(8,128)(2,1)S(1)} %get-tuple-element.40), channel_id=1, source_target_pairs={{16,32},{48,64},{80,96},{112,128},{144,160},{176,192},{208,224},{2... | collective-permute-start | bytes 331784 | tf_op jit(solution)/shard_map/ppermute | solution.py:411
  21.5 0.0 copy-start.1
  21.5 0.9 copy-done.1
  22.4 0.9 copy-done.2
  23.3 0.4 shard_map.95
  23.7 0.0 copy-start.6
  23.7 0.6 copy-done.6
  24.4 0.6 copy-done.8
  25.0 3.2 %collective-permute-done.3.refs_4_ = bf16[27,16,128]{2,1,0:T(8,128)(2,1)S(1)} collective-permute-done((bf16[27,16,128]{2,1,0:T(8,128)(2,1)S(1)}, bf16[27,16,128]{2,1,0:T(8,128)(2,1)S(1)}, u32[]{:S(2)}, u32[]{:S(2)}) %collective-permute-start.3) | collective-permute-done | bytes 110624 | tf_op jit(solution)/shard_map/ppermute | solution.py:411
  28.1 0.7 broadcast_in_dim.2.refs_8_.sw_ref
  28.9 0.7 copy-done.10
  29.6 3.9 %shard_map.96 = (bf16[8,12,3,16,128]{4,3,2,1,0:T(8,128)(2,1)S(1)}, bf16[6,10,3,16,128]{4,3,2,1,0:T(8,128)(2,1)S(1)}, f32[6,10,16,128]{3,2,1,0:T(8,128)S(1)}, f32...) custom-call(s32[4]{0:T(128)S(1)} %pad_add_fusion.at.refs_0_, ...), custom_call_target="tpu_custom_call" | custom-call | bytes 548880 | tf_op jit(solution)/shard_map/pallas_call | solution.py:386
  33.5 0.0 copy-start.4
  33.5 0.6 copy-done.4
  34.1 6.7 %collective-permute-start.4 = (bf16[28,8,128]{2,1,0:T(8,128)(2,1)S(1)}, bf16[28,8,128]{2,1,0:T(8,128)(2,1)S(1)}, u32[]{:S(2)}, u32[]{:S(2)}) collective-permute-start(bf16[28,8,128]{2,1,0:T(8,128)(2,1)S(1)} %get-tuple-element.44.me_ref), channel_id=1, source_target_pairs={{0,1},{1,0},{2,3},{3,2},{4,5},{5,4},{6,7},{7,6},{8,9},{9,8},{10,11... | collective-permute-start | bytes 172040 | tf_op jit(solution)/shard_map/ppermute | solution.py:405
  40.9 0.7 collective-permute-start.5
  41.6 0.9 collective-permute-done.4.re_ref
  42.4 1.2 shard_map.97
  43.7 1.9 %collective-permute-start.6 = (bf16[84,8,128]{2,1,0:T(8,128)(2,1)S(1)}, bf16[84,8,128]{2,1,0:T(8,128)(2,1)S(1)}, u32[]{:S(2)}, u32[]{:S(2)}) collective-permute-start(bf16[84,8,128]{2,1,0:T(8,128)(2,1)S(1)} %get-tuple-element.47.ma_ref.refs_2_), channel_id=1, source_target_pairs={{0,16},{16,0},{32,48},{48,32},{64,80},{80,64},{96,112},{112,96},{1... | collective-permute-start | bytes 516104 | tf_op jit(solution)/shard_map/ppermute | solution.py:405
  45.6 1.4 collective-permute-done.6.ra_ref.refs_3_
  47.0 7.2 %collective-permute-start.7 = (bf16[72,8,128]{2,1,0:T(8,128)(2,1)S(1)}, bf16[72,8,128]{2,1,0:T(8,128)(2,1)}, u32[]{:S(2)}, u32[]{:S(2)}) collective-permute-start(bf16[72,8,128]{2,1,0:T(8,128)(2,1)S(1)} %shard_map.98), channel_id=1, source_target_pairs={{16,32},{48,64},{80,96},{112,128},{144,160},{176,192},{208,224},{2... | collective-permute-start | bytes 442376 | tf_op jit(solution)/shard_map/ppermute | solution.py:411
  54.2 3.3 %collective-permute-done.7.refs_4_ = bf16[72,8,128]{2,1,0:T(8,128)(2,1)} collective-permute-done((bf16[72,8,128]{2,1,0:T(8,128)(2,1)S(1)}, bf16[72,8,128]{2,1,0:T(8,128)(2,1)}, u32[]{:S(2)}, u32[]{:S(2)}) %collective-permute-start.7) | collective-permute-done | bytes 147488 | tf_op jit(solution)/shard_map/ppermute | solution.py:411
  57.5 1.9 %collective-permute-start.8 = (bf16[72,8,128]{2,1,0:T(8,128)(2,1)}, bf16[72,8,128]{2,1,0:T(8,128)(2,1)}, u32[]{:S(2)}, u32[]{:S(2)}) collective-permute-start(bf16[72,8,128]{2,1,0:T(8,128)(2,1)} %collective-permute-done.7.refs_4_), channel_id=1, source_target_pairs={{0,16},{16,0},{32,48},{48,32},{64,80},{80,64},{96,112},{112,96},{1... | collective-permute-start | bytes 442376 | tf_op jit(solution)/shard_map/ppermute | solution.py:405
  59.4 8.0 %collective-permute-start.9 = (bf16[48,8,128]{2,1,0:T(8,128)(2,1)}, bf16[48,8,128]{2,1,0:T(8,128)(2,1)}, u32[]{:S(2)}, u32[]{:S(2)}) collective-permute-start(bf16[48,8,128]{2,1,0:T(8,128)(2,1)} %get-tuple-element.52), channel_id=1, source_target_pairs={{16,32},{48,64},{80,96},{112,128},{144,160},{176,192},{208,224},{2... | collective-permute-start | bytes 294920 | tf_op jit(solution)/shard_map/ppermute | solution.py:411
  67.4 0.0 copy-start.5
  67.4 0.8 copy-done.5
  68.2 5.5 %shard_map.99.dpre_ref = f32[8,16,128]{2,1,0:T(8,128)S(1)} custom-call(s32[4]{0:T(128)S(1)} %pad_add_fusion.at.refs_0_, f32[3,4,8,128]{3,2,1,0:T(8,128)S(1)} %copy-done.5, bf16[84,8,128]{2,1,0:T(8,128)(2,1)S(1)} %get-tuple-element.47.ma_ref.refs_2_, bf16[84,8,128]{2,1,0:T(8,128)(2,1)S(1)} %collective-permute-done.6.ra_ref.refs_3_, ...), custom_call_target="tpu_custom_call" | custom-call | bytes 753680 | tf_op jit(solution)/shard_map/pallas_call | solution.py:386
  73.7 0.8 copy-done.7
  74.5 0.8 copy-done.9
  75.2 6.5 %shard_map.100 = (bf16[16,4,8,128]{3,2,1,0:T(8,128)(2,1)}, f32[2,16,512]{2,1,0:T(8,128)S(1)}) custom-call(s32[4]{0:T(128)S(1)} %pad_add_fusion.at.refs_0_, f32[8,16,128]{2,1,0:T(8,128)S(1)} %shard_map.99.dpre_ref, f32[4,8,16,128]{3,2,1,0:T(8,128)S(1)} %get-tuple-element.45.slope2_ref, bf16[4,12,16,128]{3,2,1,0:T(8,128)(2,1)S(1)} %get-tuple-element.51.s2y_ref, ...), custom_call_target="tpu_custom_call" | custom-call | bytes 3547152 | tf_op jit(solution)/shard_map/pallas_call | solution.py:386
  81.7 1.9 %collective-permute-start.10 = (f32[16,512]{1,0:T(8,128)S(1)}, f32[16,512]{1,0:T(8,128)S(1)}, u32[]{:S(2)}, u32[]{:S(2)}) collective-permute-start(f32[16,512]{1,0:T(8,128)S(1)} %dynamic-slice_bitcast_fusion), channel_id=1, source_target_pairs={{0,16},{16,0},{32,48},{48,32},{64,80},{80,64},{96,112},{112,96},{1... | collective-permute-start | bytes 98312 | tf_op jit(solution)/shard_map/ppermute | solution.py:405
  83.7 1.2 collective-permute-done.10
  84.8 19.2 %all-gather = f32[64,512]{1,0:T(8,128)S(1)} all-gather(f32[16,512]{1,0:T(8,128)S(1)} %bitcast_add_fusion), channel_id=2, replica_groups={{0,1,2,3},{4,5,6,7},{8,9,10,11},{12,13,14,15},{16,17,18,19},{20,21,22,2..., dimensions={0}, use_global_device_ids=true | all-gather | bytes 163840 | tf_op jit(solution)/shard_map/all_gather | solution.py:425
  104.1 10.8 %all-gather.1 = f32[64,512]{1,0:T(8,128)S(1)} all-gather(f32[16,512]{1,0:T(8,128)S(1)} %reduce_sum.36), channel_id=3, replica_groups={{0,4,8,12},{1,5,9,13},{2,6,10,14},{3,7,11,15},{16,20,24,28},{17,21,25,2..., dimensions={0}, use_global_device_ids=true | all-gather | bytes 163840 | tf_op jit(solution)/shard_map/all_gather | solution.py:425
  114.9 12.9 %all-gather.2 = f32[64,512]{1,0:T(8,128)S(1)} all-gather(f32[16,512]{1,0:T(8,128)S(1)} %reduce_sum.37), channel_id=4, replica_groups={{0,128,256,384},{16,144,272,400},{32,160,288,416},{48,176,304,432},{64,..., dimensions={0}, use_global_device_ids=true | all-gather | bytes 163840 | tf_op jit(solution)/shard_map/all_gather | solution.py:425
  127.8 14.5 %all-gather.3 = f32[64,512]{1,0:T(8,128)S(1)} all-gather(f32[16,512]{1,0:T(8,128)S(1)} %reduce_sum.38), channel_id=5, replica_groups={{0,32,64,96},{16,48,80,112},{128,160,192,224},{144,176,208,240},{256,28..., dimensions={0}, use_global_device_ids=true | all-gather | bytes 163840 | tf_op jit(solution)/shard_map/all_gather | solution.py:425
  142.3 13.1 %collective-permute-start.11 = (f32[16,512]{1,0:T(8,128)S(1)}, f32[16,512]{1,0:T(8,128)S(1)}, u32[]{:S(2)}, u32[]{:S(2)}) collective-permute-start(f32[16,512]{1,0:T(8,128)S(1)} %reduce_sum.39), channel_id=1, source_target_pairs={{0,16},{16,0},{32,48},{48,32},{64,80},{80,64},{96,112},{112,96},{1... | collective-permute-start | bytes 98312 | tf_op jit(solution)/shard_map/ppermute | solution.py:405
  155.5 0.8 collective-permute-done.11
  156.3 1.1 shard_map.101
  (20 shorter events, 0.1 us)
Async XLA Ops:
  0.7 0.9 copy-start
  1.6 0.7 copy-start.3
  3.0 5.3 %collective-permute-start = (bf16[9,16,128]{2,1,0:T(8,128)(2,1)S(1)}, bf16[9,16,128]{2,1,0:T(8,128)(2,1)S(1)}, u32[]{:S(2)}, u32[]{:S(2)}) collective-permute-start(bf16[9,16,128]{2,1,0:T(8,128)(2,1)S(1)} %get-tuple-element.35), channel_id=1, source_target_pairs={{0,1},{1,0},{2,3},{3,2},{4,5},{5,4},{6,7},{7,6},{8,9},{9,8},{10,11... | collective-permute-start | bytes 110600 | tf_op jit(solution)/shard_map/ppermute | solution.py:405
  6.9 1.3 collective-permute-start.1
  8.8 16.1 %collective-permute-start.2 = (bf16[27,16,128]{2,1,0:T(8,128)(2,1)S(1)}, bf16[27,16,128]{2,1,0:T(8,128)(2,1)S(1)}, u32[]{:S(2)}, u32[]{:S(2)}) collective-permute-start(bf16[27,16,128]{2,1,0:T(8,128)(2,1)S(1)} %get-tuple-element.39), channel_id=1, source_target_pairs={{0,16},{16,0},{32,48},{48,32},{64,80},{80,64},{96,112},{112,96},{1... | collective-permute-start | bytes 331784 | tf_op jit(solution)/shard_map/ppermute | solution.py:405
  18.2 10.0 %collective-permute-start.3 = (bf16[27,16,128]{2,1,0:T(8,128)(2,1)S(1)}, bf16[27,16,128]{2,1,0:T(8,128)(2,1)S(1)}, u32[]{:S(2)}, u32[]{:S(2)}) collective-permute-start(bf16[27,16,128]{2,1,0:T(8,128)(2,1)S(1)} %get-tuple-element.40), channel_id=1, source_target_pairs={{16,32},{48,64},{80,96},{112,128},{144,160},{176,192},{208,224},{2... | collective-permute-start | bytes 331784 | tf_op jit(solution)/shard_map/ppermute | solution.py:411
  21.5 0.9 copy-start.1
  22.4 0.9 copy-start.2
  23.7 0.6 copy-start.6
  24.4 0.6 copy-start.8
  28.9 0.7 copy-start.10
  33.5 0.6 copy-start.4
  34.1 8.3 %collective-permute-start.4 = (bf16[28,8,128]{2,1,0:T(8,128)(2,1)S(1)}, bf16[28,8,128]{2,1,0:T(8,128)(2,1)S(1)}, u32[]{:S(2)}, u32[]{:S(2)}) collective-permute-start(bf16[28,8,128]{2,1,0:T(8,128)(2,1)S(1)} %get-tuple-element.44.me_ref), channel_id=1, source_target_pairs={{0,1},{1,0},{2,3},{3,2},{4,5},{5,4},{6,7},{7,6},{8,9},{9,8},{10,11... | collective-permute-start | bytes 172040 | tf_op jit(solution)/shard_map/ppermute | solution.py:405
  40.9 1.6 collective-permute-start.5
  43.7 3.3 %collective-permute-start.6 = (bf16[84,8,128]{2,1,0:T(8,128)(2,1)S(1)}, bf16[84,8,128]{2,1,0:T(8,128)(2,1)S(1)}, u32[]{:S(2)}, u32[]{:S(2)}) collective-permute-start(bf16[84,8,128]{2,1,0:T(8,128)(2,1)S(1)} %get-tuple-element.47.ma_ref.refs_2_), channel_id=1, source_target_pairs={{0,16},{16,0},{32,48},{48,32},{64,80},{80,64},{96,112},{112,96},{1... | collective-permute-start | bytes 516104 | tf_op jit(solution)/shard_map/ppermute | solution.py:405
  47.0 10.5 %collective-permute-start.7 = (bf16[72,8,128]{2,1,0:T(8,128)(2,1)S(1)}, bf16[72,8,128]{2,1,0:T(8,128)(2,1)}, u32[]{:S(2)}, u32[]{:S(2)}) collective-permute-start(bf16[72,8,128]{2,1,0:T(8,128)(2,1)S(1)} %shard_map.98), channel_id=1, source_target_pairs={{16,32},{48,64},{80,96},{112,128},{144,160},{176,192},{208,224},{2... | collective-permute-start | bytes 442376 | tf_op jit(solution)/shard_map/ppermute | solution.py:411
  57.5 9.9 %collective-permute-start.8 = (bf16[72,8,128]{2,1,0:T(8,128)(2,1)}, bf16[72,8,128]{2,1,0:T(8,128)(2,1)}, u32[]{:S(2)}, u32[]{:S(2)}) collective-permute-start(bf16[72,8,128]{2,1,0:T(8,128)(2,1)} %collective-permute-done.7.refs_4_), channel_id=1, source_target_pairs={{0,16},{16,0},{32,48},{48,32},{64,80},{80,64},{96,112},{112,96},{1... | collective-permute-start | bytes 442376 | tf_op jit(solution)/shard_map/ppermute | solution.py:405
  59.4 14.3 %collective-permute-start.9 = (bf16[48,8,128]{2,1,0:T(8,128)(2,1)}, bf16[48,8,128]{2,1,0:T(8,128)(2,1)}, u32[]{:S(2)}, u32[]{:S(2)}) collective-permute-start(bf16[48,8,128]{2,1,0:T(8,128)(2,1)} %get-tuple-element.52), channel_id=1, source_target_pairs={{16,32},{48,64},{80,96},{112,128},{144,160},{176,192},{208,224},{2... | collective-permute-start | bytes 294920 | tf_op jit(solution)/shard_map/ppermute | solution.py:411
  67.4 0.8 copy-start.5
  73.7 0.8 copy-start.7
  74.5 0.8 copy-start.9
  81.7 3.1 %collective-permute-start.10 = (f32[16,512]{1,0:T(8,128)S(1)}, f32[16,512]{1,0:T(8,128)S(1)}, u32[]{:S(2)}, u32[]{:S(2)}) collective-permute-start(f32[16,512]{1,0:T(8,128)S(1)} %dynamic-slice_bitcast_fusion), channel_id=1, source_target_pairs={{0,16},{16,0},{32,48},{48,32},{64,80},{80,64},{96,112},{112,96},{1... | collective-permute-start | bytes 98312 | tf_op jit(solution)/shard_map/ppermute | solution.py:405
  142.3 14.0 %collective-permute-start.11 = (f32[16,512]{1,0:T(8,128)S(1)}, f32[16,512]{1,0:T(8,128)S(1)}, u32[]{:S(2)}, u32[]{:S(2)}) collective-permute-start(f32[16,512]{1,0:T(8,128)S(1)} %reduce_sum.39), channel_id=1, source_target_pairs={{0,16},{16,0},{32,48},{48,32},{64,80},{80,64},{96,112},{112,96},{1... | collective-permute-start | bytes 98312 | tf_op jit(solution)/shard_map/ppermute | solution.py:405

commit v4 on v3

--- a/solution.py
+++ b/solution.py
@@ -43,7 +43,9 @@
     return (row >= 0) & (row < limit)
 
 
-def build(c1_ref, c2_ref, w1_ref, w2_ref, w1b_ref, w2b_ref):
+def build(c1_ref, c2_ref, sp_ref, lab_ref, w1_ref, w2_ref, w1b_ref, w2b_ref, sw_ref, labf_ref):
+    sw_ref[...] = jnp.transpose(jnp.broadcast_to(sp_ref[...], (X, C)))
+    labf_ref[...] = lab_ref[...].astype(f32)
     zero = jnp.zeros((C, C), f32)
     for src, fwd, adj in ((c1_ref, w1_ref, w1b_ref), (c2_ref, w2_ref, w2b_ref)):
         for j in range(2):
@@ -101,13 +103,14 @@
 
 
 def forward(nz, ny, at, fy_ref, sy_ref, ma_ref, mb_ref, lab_ref, w1_ref, w2_ref, sw_ref,
-            fx_ref, hx_ref, slope1_ref, slope2_ref, top_ref, me_ref, mo_ref, own_ref, g0_ref, p_ref):
+            fc_ref, hx_ref, slope1_ref, slope2_ref, top_ref, me_ref, mo_ref, own_ref, g0_ref, p_ref, fx_ref):
     iz, iy, pz, py = at[0], at[1], at[2], at[3]
     for k in range(BZ):
         put_taps(fx_ref, 2 + k, fy_ref[k].astype(f32))
     for k in range(2):
         put_taps(fx_ref, 6 - 6 * pz + k, ma_ref[12 * k : 12 * k + 12].astype(f32))
         put_taps(fx_ref, 6 * pz + k, mb_ref[12 * k : 12 * k + 12].astype(f32))
+    fc_ref[...] = fx_ref[1:7, 1:11]
     w1 = w1_ref[...]
     w2 = w2_ref[...]
 
@@ -168,7 +171,7 @@
             base = pltpu.roll(centre + (A * 0.5) * lap, 12, 0)[:8]
             own_ref[1, k - 2] = base + A * own_ref[0, k - 2] * pltpu.roll(g, 12, 0)[:8]
     for z in range(BZ):
-        own_ref[2, z] = lab_ref[z].astype(f32)
+        own_ref[2, z] = lab_ref[z]
     for ref, start in ((me_ref, 6 - 6 * py), (mo_ref, 6 * py)):
         ref[:12] = own_ref[...].reshape(12, BY, X).astype(SENT)
         for z in range(BZ):
@@ -347,7 +350,7 @@
         d2 = jnp.concatenate([dx_ref[z + 2, y + 2, 1] for y in range(BY)], axis=1)
         d1 = jnp.concatenate([ex_ref[z + 1, y + 1, 1] for y in range(BY)], axis=1)
         p2 = [hx_ref[pl.ds(z, 3), y : y + 3].reshape(TAPS, X) for y in range(BY)]
-        p1 = [fx_ref[pl.ds(z + 1, 3), y + 1 : y + 4].reshape(TAPS, X) for y in range(BY)]
+        p1 = [fx_ref[pl.ds(z, 3), y : y + 3].reshape(TAPS, X) for y in range(BY)]
         g2 = g2 + lax.dot_general(d2, jnp.concatenate(p2, axis=1), nt, preferred_element_type=f32)
         g1 = g1 + lax.dot_general(d1, jnp.concatenate(p1, axis=1), nt, preferred_element_type=f32)
         for y in range(BY):
@@ -357,9 +360,10 @@
     zero = jnp.zeros((C, TAPS), f32)
     g1, g2, gs = lax.fori_loop(0, BZ, weights, (zero, zero, jnp.zeros((C, X), f32)))
     grad_ref[...] = jnp.zeros_like(grad_ref)
-    grad_ref[0, :, :TAPS] = g1
-    grad_ref[1, :, :TAPS] = g2
-    grad_ref[0, :1, TAPS : TAPS + C] = jnp.sum(jnp.transpose(gs), axis=0, keepdims=True)
+    for i, g in enumerate((g1, g2)):
+        grad_ref[i, :C] = g[:, :256]
+        grad_ref[i, C:, : TAPS - 256] = g[:, 256:]
+    grad_ref[0, C : C + 1, TAPS - 256 : TAPS - 240] = jnp.sum(jnp.transpose(gs), axis=0, keepdims=True)
 
 
 def finish(a_ref, b_ref, first_ref, second_ref, speed_ref):
@@ -369,9 +373,10 @@
     factor = 1.0 / jnp.maximum(jnp.sqrt(jnp.full((1, 1), total)) / jnp.sqrt(f32(count)), 1.0)
     a, b = a * factor, b * factor
     for t in range(27):
-        first_ref[t] = a[:, C * t : C * t + C]
-        second_ref[t] = b[:, C * t : C * t + C]
-    speed_ref[...] = a[:1, TAPS : TAPS + C]
+        row, lane = C * (t // 16), C * (t % 16)
+        first_ref[t] = a[row : row + C, lane : lane + C]
+        second_ref[t] = b[row : row + C, lane : lane + C]
+    speed_ref[...] = a[C : C + 1, TAPS - 256 : TAPS - 240]
 
 
 def call(kernel, outs, scratch=(), flops=0):
@@ -411,19 +416,26 @@
     return lax.ppermute(value, axis, pairs + [(j, i) for i, j in pairs])
 
 
+def groups(n, unit):
+    size = max(1, min(4, n // unit))
+    firsts = [i for i in range(n) if (i // unit) % size == 0]
+    return [[i + unit * k for k in range(size)] for i in firsts]
+
+
 def total_of(grad, iz):
     core = iz % 2
     keep = lax.dynamic_index_in_dim(grad, core, 0, keepdims=False)
     give = lax.dynamic_index_in_dim(grad, 1 - core, 0, keepdims=False)
     part = keep + even(give, "gz")
-    for axis, unit in (("gy", 1), ("gy", 4), ("gz", 8), ("gz", 2)):
-        n = lax.axis_size(axis)
-        size = min(4, n // unit)
-        if size > 1:
-            firsts = [i for i in range(n) if (i // unit) % size == 0]
-            groups = [[i + unit * k for k in range(size)] for i in firsts]
-            parts = lax.all_gather(part, axis, axis_index_groups=groups)
-            part = jnp.sum(parts, axis=0)
+    row = groups(lax.axis_size("gy"), 1)
+    size = len(row[0])
+    chunks = part.reshape(size, 2 * C // size, 256)
+    part = jnp.sum(lax.all_to_all(chunks, "gy", 0, 0, axis_index_groups=row), axis=0)
+    for axis, unit in (("gy", 4), ("gz", 8), ("gz", 2)):
+        sets = groups(lax.axis_size(axis), unit)
+        if len(sets[0]) > 1:
+            part = jnp.sum(lax.all_gather(part, axis, axis_index_groups=sets), axis=0)
+    part = lax.all_gather(part, "gy", axis_index_groups=row).reshape(2 * C, 256)
     other = even(part, "gz")
     return jnp.where(core == 0, part, other), jnp.where(core == 0, other, part)
 
@@ -433,24 +445,27 @@
     iz, iy = lax.axis_index("gz"), lax.axis_index("gy")
     pz, py = iz % 2, iy % 2
     at = jnp.stack([iz, iy, pz, py]).astype(jnp.int32)
-    sw = jnp.broadcast_to(speed_weight[:, None], (C, X))
     taps = [w.transpose(2, 3, 4, 0, 1).reshape(27, C, C) for w in (conv_first, conv_second)]
-    w1, w2, w1b, w2b = call(build, [shape((2 * C, 36 * C))] * 4)(None, *taps)
+    w1, w2, w1b, w2b, sw, target = call(
+        build, [shape((2 * C, 36 * C))] * 4 + [shape((C, X), f32), shape((BZ, BY, X), f32)]
+    )(None, *taps, speed_weight.reshape(1, C), labels)
 
     ft, me, mo = call(prepare, [shape((BZ, BY, C, X)), shape((9, C, X)), shape((9, C, X))])(
         at, features, sign_map
     )
-    re, ro = even(me, "gy"), odd(mo, "gy")
+    ro = odd(mo, "gy")
+    re = even(me, "gy")
     fy, sy, ma, mb = call(
         extend,
         [shape((BZ, 12, C, X)), shape((BZ, 16, X), f32), shape((27, C, X)), shape((27, C, X))],
     )(at, ft, sign_map, re, ro)
-    ra, rb = even(ma, "gz"), odd(mb, "gz")
+    rb = odd(mb, "gz")
+    ra = even(ma, "gz")
 
     fx, hx, slope1, slope2, top, fe, fo, own, g0 = call(
         lambda *refs: forward(nz, ny, *refs),
         [
-            shape((8, 12, 3, C, X)),
+            shape((6, 10, 3, C, X)),
             shape((6, 10, 3, C, X)),
             shape((6, 10, C, X), f32),
             shape((BZ, BY, C, X), f32),
@@ -460,10 +475,11 @@
             shape((3, BZ, BY, X), f32),
             shape((8, 16, X), f32),
         ],
-        [pltpu.VMEM((10, 16, X), f32)],
-    )(at, fy, sy, ra, rb, labels, w1, w2, sw)
-
-    ge, go = even(fe, "gy"), odd(fo, "gy")
+        [pltpu.VMEM((10, 16, X), f32), pltpu.VMEM((8, 12, 3, C, X), bf16)],
+    )(at, fy, sy, ra, rb, target, w1, w2, sw)
+
+    go = odd(fo, "gy")
+    ge = even(fe, "gy")
     fa, fs, s2y = call(
         widen, [shape((84, 8, X), SENT), shape((48, 8, X), SENT), shape((BZ, 12, C, X))]
     )(at, fe, slope2, ge, go)
@@ -493,7 +509,7 @@
 
     d_features, grad = call(
         backward,
-        [shape((C, BZ, BY, X)), shape((2, C, 512), f32)],
+        [shape((C, BZ, BY, X)), shape((2, 2 * C, 256), f32)],
         [pltpu.VMEM((8, 12, 3, C, X), bf16), pltpu.VMEM((6, 10, 3, C, X), bf16)],
     )(at, dpre, slope2, s2y, ha, hs, sw, hx, fx, slope1, top, w1b, w2b)
 

time: 158 us -> 161 us (1.019)
  blocking collectives: 57.4 us -> 64.9 us
  local copies, waits for them, and re-layouts: 9.03 us -> 2.79 us
    all_to_all x0 -> x1, blocking collectives: none -> 17.9 us  [total_of(): lax.all_to_all(chunks, 'gy', 0, 0, axis_index_groups=row)]
    all_gather x4, blocking collectives: 57.4 us -> 47 us  [the longest x3 37.9 us: total_of(): part = jnp.sum(lax.all_gather(part, axis, axis_index_groups=sets), axis=0)]
    unnamed x22 -> x20, local copies, waits for them, and re-layouts: 8.3 us -> 2.79 us
    ppermute x5, waiting for transfers between devices: 6.48 us -> 8.09 us  [odd(): return lax.ppermute(value, axis, pairs + [(j, i) for i, j in pairs])]
  transfers between devices with their start and end apart: 12 -> 12, of which waited for: 7 -> 7; matrix products, arithmetic and copies ran while one was open for 0% -> 0% of each run, Pallas kernels for 4% -> 3%
where the time goes in v4:
time: 161 us
  blocking collectives  64.9 us (40%)
  starting transfers between devices  59.8 us (37%)
  Pallas kernels  19.1 us (12%)
  waiting for transfers between devices  13 us (8%)
  local copies, waits for them, and re-layouts  2.79 us (2%)
    ppermute x7, starting transfers between devices, even(): return lax.ppermute(value, axis, [(i, i ^ 1) for i in range(n)])  40 us
    all_gather x3, blocking collectives, total_of(): part = jnp.sum(lax.all_gather(part, axis, axis_index_groups=sets), axis=0)  37.9 us
    ppermute x5, starting transfers between devices, odd(): return lax.ppermute(value, axis, pairs + [(j, i) for i, j in pairs])  19.8 us
    pallas_call x9, Pallas kernels, run(): pl.pallas_call(kernel, out_shape=outs, in_specs=specs, out_specs=[vmem] *...  19.1 us
    all_to_all x1, blocking collectives, total_of(): lax.all_to_all(chunks, 'gy', 0, 0, axis_index_groups=row)  17.9 us
    all_gather x1, blocking collectives, total_of(): part = lax.all_gather(part, 'gy', axis_index_groups=row).reshape(2 * C, 256)  9.11 us
    ppermute x5, waiting for transfers between devices, odd(): return lax.ppermute(value, axis, pairs + [(j, i) for i, j in pairs])  8.09 us
    ppermute x7, waiting for transfers between devices, even(): return lax.ppermute(value, axis, [(i, i ^ 1) for i in range(n)])  4.92 us
  transfers between devices with their start and end apart: 12, of which 7 were waited for; matrix products, arithmetic and copies ran while one was open for 0% of the time, Pallas kernels for 3%

profile of v4, /device:TPU:1, one launch (start us, length us, event | category | flops | bytes accessed | tf_op | source)
XLA Modules:
  0.0 160.6 jit_solution(17549179723319760166)
XLA Ops:
  0.6 0.0 copy-start.3
  0.7 0.1 pad_add_fusion.at.refs_0_
  0.7 0.6 copy-done.3
  1.4 0.9 copy-done
  2.3 0.6 shard_map.93
  2.9 3.9 %collective-permute-start = (bf16[9,16,128]{2,1,0:T(8,128)(2,1)S(1)}, bf16[9,16,128]{2,1,0:T(8,128)(2,1)S(1)}, u32[]{:S(2)}, u32[]{:S(2)}) collective-permute-start(bf16[9,16,128]{2,1,0:T(8,128)(2,1)S(1)} %get-tuple-element.37), channel_id=1, source_target_pairs={{0,1},{1,0},{2,3},{3,2},{4,5},{5,4},{6,7},{7,6},{8,9},{9,8},{10,11... | collective-permute-start | bytes 110600 | tf_op jit(solution)/shard_map/ppermute | solution.py:410
  6.8 0.7 collective-permute-start.1
  7.5 0.7 collective-permute-done.re_ref
  8.2 0.0 collective-permute-done.1.ro_ref
  8.2 0.6 shard_map.94
  8.7 9.3 %collective-permute-start.2 = (bf16[27,16,128]{2,1,0:T(8,128)(2,1)S(1)}, bf16[27,16,128]{2,1,0:T(8,128)(2,1)S(1)}, u32[]{:S(2)}, u32[]{:S(2)}) collective-permute-start(bf16[27,16,128]{2,1,0:T(8,128)(2,1)S(1)} %get-tuple-element.41), channel_id=1, source_target_pairs={{0,16},{16,0},{32,48},{48,32},{64,80},{80,64},{96,112},{112,96},{1... | collective-permute-start | bytes 331784 | tf_op jit(solution)/shard_map/ppermute | solution.py:410
  18.1 3.4 %collective-permute-start.3 = (bf16[27,16,128]{2,1,0:T(8,128)(2,1)S(1)}, bf16[27,16,128]{2,1,0:T(8,128)(2,1)S(1)}, u32[]{:S(2)}, u32[]{:S(2)}) collective-permute-start(bf16[27,16,128]{2,1,0:T(8,128)(2,1)S(1)} %get-tuple-element.42), channel_id=1, source_target_pairs={{16,32},{48,64},{80,96},{112,128},{144,160},{176,192},{208,224},{2... | collective-permute-start | bytes 331784 | tf_op jit(solution)/shard_map/ppermute | solution.py:416
  21.5 0.0 copy-start.9
  21.5 0.0 copy-done.8
  21.5 0.6 copy-done.9
  22.1 0.4 shard_map.95
  22.5 0.0 copy-start.4
  22.5 0.6 copy-done.4
  23.2 0.0 collective-permute-done.2.refs_3_
  23.2 4.9 %collective-permute-done.3.refs_4_ = bf16[27,16,128]{2,1,0:T(8,128)(2,1)S(1)} collective-permute-done((bf16[27,16,128]{2,1,0:T(8,128)(2,1)S(1)}, bf16[27,16,128]{2,1,0:T(8,128)(2,1)S(1)}, u32[]{:S(2)}, u32[]{:S(2)}) %collective-permute-start.3) | collective-permute-done | bytes 110624 | tf_op jit(solution)/shard_map/ppermute | solution.py:416
  28.1 4.0 %shard_map.96 = (bf16[6,10,3,16,128]{4,3,2,1,0:T(8,128)(2,1)S(1)}, bf16[6,10,3,16,128]{4,3,2,1,0:T(8,128)(2,1)S(1)}, f32[6,10,16,128]{3,2,1,0:T(8,128)S(1)}, f32...) custom-call(s32[4]{0:T(128)S(1)} %pad_add_fusion.at.refs_0_, ...), custom_call_target="tpu_custom_call" | custom-call | bytes 548880 | tf_op jit(solution)/shard_map/pallas_call | solution.py:391
  32.0 6.8 %collective-permute-start.4 = (bf16[28,8,128]{2,1,0:T(8,128)(2,1)S(1)}, bf16[28,8,128]{2,1,0:T(8,128)(2,1)S(1)}, u32[]{:S(2)}, u32[]{:S(2)}) collective-permute-start(bf16[28,8,128]{2,1,0:T(8,128)(2,1)S(1)} %get-tuple-element.48.me_ref), channel_id=1, source_target_pairs={{0,1},{1,0},{2,3},{3,2},{4,5},{5,4},{6,7},{7,6},{8,9},{9,8},{10,11... | collective-permute-start | bytes 172040 | tf_op jit(solution)/shard_map/ppermute | solution.py:410
  38.8 0.7 collective-permute-start.5
  39.5 0.9 collective-permute-done.4.re_ref
  40.4 0.0 collective-permute-done.5.ro_ref
  40.4 1.2 shard_map.97
  41.6 1.9 %collective-permute-start.6 = (bf16[84,8,128]{2,1,0:T(8,128)(2,1)S(1)}, bf16[84,8,128]{2,1,0:T(8,128)(2,1)S(1)}, u32[]{:S(2)}, u32[]{:S(2)}) collective-permute-start(bf16[84,8,128]{2,1,0:T(8,128)(2,1)S(1)} %get-tuple-element.51.ma_ref.refs_2_), channel_id=1, source_target_pairs={{0,16},{16,0},{32,48},{48,32},{64,80},{80,64},{96,112},{112,96},{1... | collective-permute-start | bytes 516104 | tf_op jit(solution)/shard_map/ppermute | solution.py:410
  43.5 1.4 collective-permute-done.6.ra_ref.refs_3_
  44.9 7.2 %collective-permute-start.7 = (bf16[72,8,128]{2,1,0:T(8,128)(2,1)S(1)}, bf16[72,8,128]{2,1,0:T(8,128)(2,1)S(1)}, u32[]{:S(2)}, u32[]{:S(2)}) collective-permute-start(bf16[72,8,128]{2,1,0:T(8,128)(2,1)S(1)} %shard_map.98), channel_id=1, source_target_pairs={{16,32},{48,64},{80,96},{112,128},{144,160},{176,192},{208,224},{2... | collective-permute-start | bytes 442376 | tf_op jit(solution)/shard_map/ppermute | solution.py:416
  52.1 3.2 %collective-permute-done.7.refs_4_ = bf16[72,8,128]{2,1,0:T(8,128)(2,1)S(1)} collective-permute-done((bf16[72,8,128]{2,1,0:T(8,128)(2,1)S(1)}, bf16[72,8,128]{2,1,0:T(8,128)(2,1)S(1)}, u32[]{:S(2)}, u32[]{:S(2)}) %collective-permute-start.7) | collective-permute-done | bytes 147488 | tf_op jit(solution)/shard_map/ppermute | solution.py:416
  55.3 1.9 %collective-permute-start.8 = (bf16[72,8,128]{2,1,0:T(8,128)(2,1)S(1)}, bf16[72,8,128]{2,1,0:T(8,128)(2,1)S(1)}, u32[]{:S(2)}, u32[]{:S(2)}) collective-permute-start(bf16[72,8,128]{2,1,0:T(8,128)(2,1)S(1)} %collective-permute-done.7.refs_4_), channel_id=1, source_target_pairs={{0,16},{16,0},{32,48},{48,32},{64,80},{80,64},{96,112},{112,96},{1... | collective-permute-start | bytes 442376 | tf_op jit(solution)/shard_map/ppermute | solution.py:410
  57.2 8.0 %collective-permute-start.9 = (bf16[48,8,128]{2,1,0:T(8,128)(2,1)}, bf16[48,8,128]{2,1,0:T(8,128)(2,1)S(1)}, u32[]{:S(2)}, u32[]{:S(2)}) collective-permute-start(bf16[48,8,128]{2,1,0:T(8,128)(2,1)} %get-tuple-element.56), channel_id=1, source_target_pairs={{16,32},{48,64},{80,96},{112,128},{144,160},{176,192},{208,224},{2... | collective-permute-start | bytes 294920 | tf_op jit(solution)/shard_map/ppermute | solution.py:416
  65.2 0.0 collective-permute-done.8.refs_5_
  65.2 0.0 copy-start.5
  65.2 0.0 copy-start.7
  65.2 5.0 %shard_map.99.dpre_ref = f32[8,16,128]{2,1,0:T(8,128)S(1)} custom-call(s32[4]{0:T(128)S(1)} %pad_add_fusion.at.refs_0_, f32[3,4,8,128]{3,2,1,0:T(8,128)S(1)} %get-tuple-element.47.refs_1_, bf16[84,8,128]{2,1,0:T(8,128)(2,1)S(1)} %get-tuple-element.51.ma_ref.refs_2_, bf16[84,8,128]{2,1,0:T(8,128)(2,1)S(1)} %collective-permute-done.6.ra_ref.refs_3_, ...), custom_call_target="tpu_custom_call" | custom-call | bytes 753680 | tf_op jit(solution)/shard_map/pallas_call | solution.py:391
  70.2 0.0 collective-permute-done.9.rb_ref
  70.3 6.1 %shard_map.100 = (bf16[16,4,8,128]{3,2,1,0:T(8,128)(2,1)}, f32[2,32,256]{2,1,0:T(8,128)S(1)}) custom-call(s32[4]{0:T(128)S(1)} %pad_add_fusion.at.refs_0_, f32[8,16,128]{2,1,0:T(8,128)S(1)} %shard_map.99.dpre_ref, f32[4,8,16,128]{3,2,1,0:T(8,128)S(1)} %get-tuple-element.49.slope2_ref, bf16[4,12,16,128]{3,2,1,0:T(8,128)(2,1)S(1)} %get-tuple-element.55.s2y_ref, ...), custom_call_target="tpu_custom_call" | custom-call | bytes 3104784 | tf_op jit(solution)/shard_map/pallas_call | solution.py:391
  76.4 1.9 %collective-permute-start.10 = (f32[32,256]{1,0:T(8,128)S(1)}, f32[32,256]{1,0:T(8,128)S(1)}, u32[]{:S(2)}, u32[]{:S(2)}) collective-permute-start(f32[32,256]{1,0:T(8,128)S(1)} %dynamic-slice_bitcast_fusion), channel_id=1, source_target_pairs={{0,16},{16,0},{32,48},{48,32},{64,80},{80,64},{96,112},{112,96},{1... | collective-permute-start | bytes 98312 | tf_op jit(solution)/shard_map/ppermute | solution.py:410
  78.4 1.2 collective-permute-done.10
  79.5 17.9 %all_to_all.5 = f32[4,8,256]{2,1,0:T(8,128)S(1)} all-to-all(f32[4,8,256]{2,1,0:T(8,128)S(1)} %fusion), channel_id=1, replica_groups={{0,1,2,3},{4,5,6,7},{8,9,10,11},{12,13,14,15},{16,17,18,19},{20,21,22,2..., dimensions={0} | all-to-all | bytes 65536 | tf_op jit(solution)/shard_map/all_to_all | solution.py:433
  97.4 10.2 %all-gather = f32[32,256]{1,0:T(8,128)S(1)} all-gather(f32[8,256]{1,0:T(8,128)S(1)} %reduce_sum.36), channel_id=2, replica_groups={{0,4,8,12},{1,5,9,13},{2,6,10,14},{3,7,11,15},{16,20,24,28},{17,21,25,2..., dimensions={0}, use_global_device_ids=true | all-gather | bytes 40960 | tf_op jit(solution)/shard_map/all_gather | solution.py:437
  107.6 12.0 %all-gather.1 = f32[32,256]{1,0:T(8,128)S(1)} all-gather(f32[8,256]{1,0:T(8,128)S(1)} %bitcast_reduce_fusion.2), channel_id=3, replica_groups={{0,128,256,384},{16,144,272,400},{32,160,288,416},{48,176,304,432},{64,..., dimensions={0}, use_global_device_ids=true | all-gather | bytes 40960 | tf_op jit(solution)/shard_map/all_gather | solution.py:437
  119.6 15.7 %all-gather.2 = f32[32,256]{1,0:T(8,128)S(1)} all-gather(f32[8,256]{1,0:T(8,128)S(1)} %bitcast_reduce_fusion.1), channel_id=4, replica_groups={{0,32,64,96},{16,48,80,112},{128,160,192,224},{144,176,208,240},{256,28..., dimensions={0}, use_global_device_ids=true | all-gather | bytes 40960 | tf_op jit(solution)/shard_map/all_gather | solution.py:437
  135.3 9.1 %all-gather.3 = f32[32,256]{1,0:T(8,128)S(1)} all-gather(f32[8,256]{1,0:T(8,128)S(1)} %bitcast_reduce_fusion), channel_id=5, replica_groups={{0,1,2,3},{4,5,6,7},{8,9,10,11},{12,13,14,15},{16,17,18,19},{20,21,22,2..., dimensions={0}, use_global_device_ids=true | all-gather | bytes 40960 | tf_op jit(solution)/shard_map/all_gather | solution.py:438
  144.4 14.2 %collective-permute-start.11 = (f32[32,256]{1,0:T(8,128)S(1)}, f32[32,256]{1,0:T(8,128)S(1)}, u32[]{:S(2)}, u32[]{:S(2)}) collective-permute-start(f32[32,256]{1,0:T(8,128)S(1)} %all-gather.3), channel_id=1, source_target_pairs={{0,16},{16,0},{32,48},{48,32},{64,80},{80,64},{96,112},{112,96},{1... | collective-permute-start | bytes 98312 | tf_op jit(solution)/shard_map/ppermute | solution.py:410
  158.7 0.8 collective-permute-done.11
  159.5 1.1 shard_map.101
  (18 shorter events, 0.1 us)
Async XLA Ops:
  0.6 0.7 copy-start.3
  1.4 0.9 copy-start
  2.3 19.2 %copy-start.8 = (s32[4,8,128]{2,1,0:T(8,128)S(1)}, s32[4,8,128]{2,1,0:T(8,128)}, u32[]{:S(2)}) copy-start(s32[4,8,128]{2,1,0:T(8,128)} %lab_ref.1) | copy-start | bytes 49156
  2.9 5.3 %collective-permute-start = (bf16[9,16,128]{2,1,0:T(8,128)(2,1)S(1)}, bf16[9,16,128]{2,1,0:T(8,128)(2,1)S(1)}, u32[]{:S(2)}, u32[]{:S(2)}) collective-permute-start(bf16[9,16,128]{2,1,0:T(8,128)(2,1)S(1)} %get-tuple-element.37), channel_id=1, source_target_pairs={{0,1},{1,0},{2,3},{3,2},{4,5},{5,4},{6,7},{7,6},{8,9},{9,8},{10,11... | collective-permute-start | bytes 110600 | tf_op jit(solution)/shard_map/ppermute | solution.py:410
  6.8 1.3 collective-permute-start.1
  8.2 13.3 %copy-start.1 = (bf16[16,16,3,3,3]{1,0,4,3,2:T(8,128)(2,1)S(1)}, bf16[16,16,3,3,3]{1,0,4,3,2:T(8,128)(2,1)}, u32[]{:S(2)}) copy-start(bf16[16,16,3,3,3]{1,0,4,3,2:T(8,128)(2,1)} %param.9) | copy-start | bytes 41476
  8.2 13.3 %copy-start.2 = (bf16[16,16,3,3,3]{1,0,4,3,2:T(8,128)(2,1)S(1)}, bf16[16,16,3,3,3]{1,0,4,3,2:T(8,128)(2,1)}, u32[]{:S(2)}) copy-start(bf16[16,16,3,3,3]{1,0,4,3,2:T(8,128)(2,1)} %param.10) | copy-start | bytes 41476
  8.7 14.4 %collective-permute-start.2 = (bf16[27,16,128]{2,1,0:T(8,128)(2,1)S(1)}, bf16[27,16,128]{2,1,0:T(8,128)(2,1)S(1)}, u32[]{:S(2)}, u32[]{:S(2)}) collective-permute-start(bf16[27,16,128]{2,1,0:T(8,128)(2,1)S(1)} %get-tuple-element.41), channel_id=1, source_target_pairs={{0,16},{16,0},{32,48},{48,32},{64,80},{80,64},{96,112},{112,96},{1... | collective-permute-start | bytes 331784 | tf_op jit(solution)/shard_map/ppermute | solution.py:410
  18.1 10.0 %collective-permute-start.3 = (bf16[27,16,128]{2,1,0:T(8,128)(2,1)S(1)}, bf16[27,16,128]{2,1,0:T(8,128)(2,1)S(1)}, u32[]{:S(2)}, u32[]{:S(2)}) collective-permute-start(bf16[27,16,128]{2,1,0:T(8,128)(2,1)S(1)} %get-tuple-element.42), channel_id=1, source_target_pairs={{16,32},{48,64},{80,96},{112,128},{144,160},{176,192},{208,224},{2... | collective-permute-start | bytes 331784 | tf_op jit(solution)/shard_map/ppermute | solution.py:416
  21.5 0.7 copy-start.9
  22.5 0.6 copy-start.4
  23.1 8.9 %copy-start.6 = (bf16[32,576]{1,0:T(8,128)(2,1)}, bf16[32,576]{1,0:T(8,128)(2,1)S(1)}, u32[]{:S(2)}) copy-start(bf16[32,576]{1,0:T(8,128)(2,1)S(1)} %get-tuple-element.62.w2_ref) | copy-start | bytes 110596
  32.0 8.3 %collective-permute-start.4 = (bf16[28,8,128]{2,1,0:T(8,128)(2,1)S(1)}, bf16[28,8,128]{2,1,0:T(8,128)(2,1)S(1)}, u32[]{:S(2)}, u32[]{:S(2)}) collective-permute-start(bf16[28,8,128]{2,1,0:T(8,128)(2,1)S(1)} %get-tuple-element.48.me_ref), channel_id=1, source_target_pairs={{0,1},{1,0},{2,3},{3,2},{4,5},{5,4},{6,7},{7,6},{8,9},{9,8},{10,11... | collective-permute-start | bytes 172040 | tf_op jit(solution)/shard_map/ppermute | solution.py:410
  38.8 1.6 collective-permute-start.5
  41.6 3.3 %collective-permute-start.6 = (bf16[84,8,128]{2,1,0:T(8,128)(2,1)S(1)}, bf16[84,8,128]{2,1,0:T(8,128)(2,1)S(1)}, u32[]{:S(2)}, u32[]{:S(2)}) collective-permute-start(bf16[84,8,128]{2,1,0:T(8,128)(2,1)S(1)} %get-tuple-element.51.ma_ref.refs_2_), channel_id=1, source_target_pairs={{0,16},{16,0},{32,48},{48,32},{64,80},{80,64},{96,112},{112,96},{1... | collective-permute-start | bytes 516104 | tf_op jit(solution)/shard_map/ppermute | solution.py:410
  44.9 10.4 %collective-permute-start.7 = (bf16[72,8,128]{2,1,0:T(8,128)(2,1)S(1)}, bf16[72,8,128]{2,1,0:T(8,128)(2,1)S(1)}, u32[]{:S(2)}, u32[]{:S(2)}) collective-permute-start(bf16[72,8,128]{2,1,0:T(8,128)(2,1)S(1)} %shard_map.98), channel_id=1, source_target_pairs={{16,32},{48,64},{80,96},{112,128},{144,160},{176,192},{208,224},{2... | collective-permute-start | bytes 442376 | tf_op jit(solution)/shard_map/ppermute | solution.py:416
  55.3 9.9 %collective-permute-start.8 = (bf16[72,8,128]{2,1,0:T(8,128)(2,1)S(1)}, bf16[72,8,128]{2,1,0:T(8,128)(2,1)S(1)}, u32[]{:S(2)}, u32[]{:S(2)}) collective-permute-start(bf16[72,8,128]{2,1,0:T(8,128)(2,1)S(1)} %collective-permute-done.7.refs_4_), channel_id=1, source_target_pairs={{0,16},{16,0},{32,48},{48,32},{64,80},{80,64},{96,112},{112,96},{1... | collective-permute-start | bytes 442376 | tf_op jit(solution)/shard_map/ppermute | solution.py:410
  57.2 13.1 %collective-permute-start.9 = (bf16[48,8,128]{2,1,0:T(8,128)(2,1)}, bf16[48,8,128]{2,1,0:T(8,128)(2,1)S(1)}, u32[]{:S(2)}, u32[]{:S(2)}) collective-permute-start(bf16[48,8,128]{2,1,0:T(8,128)(2,1)} %get-tuple-element.56), channel_id=1, source_target_pairs={{16,32},{48,64},{80,96},{112,128},{144,160},{176,192},{208,224},{2... | collective-permute-start | bytes 294920 | tf_op jit(solution)/shard_map/ppermute | solution.py:416
  65.2 5.1 %copy-start.5 = (bf16[32,576]{1,0:T(8,128)(2,1)S(1)}, bf16[32,576]{1,0:T(8,128)(2,1)}, u32[]{:S(2)}) copy-start(bf16[32,576]{1,0:T(8,128)(2,1)} %copy-done.4) | copy-start | bytes 110596
  65.2 5.1 %copy-start.7 = (bf16[32,576]{1,0:T(8,128)(2,1)S(1)}, bf16[32,576]{1,0:T(8,128)(2,1)}, u32[]{:S(2)}) copy-start(bf16[32,576]{1,0:T(8,128)(2,1)} %copy-done.6) | copy-start | bytes 110596
  76.4 3.1 %collective-permute-start.10 = (f32[32,256]{1,0:T(8,128)S(1)}, f32[32,256]{1,0:T(8,128)S(1)}, u32[]{:S(2)}, u32[]{:S(2)}) collective-permute-start(f32[32,256]{1,0:T(8,128)S(1)} %dynamic-slice_bitcast_fusion), channel_id=1, source_target_pairs={{0,16},{16,0},{32,48},{48,32},{64,80},{80,64},{96,112},{112,96},{1... | collective-permute-start | bytes 98312 | tf_op jit(solution)/shard_map/ppermute | solution.py:410
  144.4 15.1 %collective-permute-start.11 = (f32[32,256]{1,0:T(8,128)S(1)}, f32[32,256]{1,0:T(8,128)S(1)}, u32[]{:S(2)}, u32[]{:S(2)}) collective-permute-start(f32[32,256]{1,0:T(8,128)S(1)} %all-gather.3), channel_id=1, source_target_pairs={{0,16},{16,0},{32,48},{48,32},{64,80},{80,64},{96,112},{112,96},{1... | collective-permute-start | bytes 98312 | tf_op jit(solution)/shard_map/ppermute | solution.py:410

commit v5 on v4

--- a/solution.py
+++ b/solution.py
@@ -4,6 +4,7 @@
 from jax.experimental import pallas as pl
 from jax.experimental.pallas import tpu as pltpu
 from jax.sharding import PartitionSpec as P
+
 
 C = 16
 BZ = 4
@@ -202,7 +203,7 @@
 
 def march(nz, ny, at, own_ref, ye_ref, mate_ref, far_ref, far2_ref, g0_ref, dpre_ref,
           sp, lab, ph, w_s, dz_s, dy_s, dx_s, ag_s, ds, dd):
-    iz, iy, pz, py = at[0], at[1], at[2], at[3]
+    iz, iy, pz = at[0], at[1], at[2]
     base = 4 * pz
 
     def place(start, block):
@@ -296,7 +297,7 @@
     pz = at[2]
     sw = sw_ref[...]
 
-    def second(z, k, slope):
+    def second(z, slope):
         for y in range(BY + 4):
             d = dpre_ref[z, 2 + y : 3 + y, :]
             value = (sw * d * slope(y))[None]
@@ -310,12 +311,14 @@
             if 2 <= y < 2 + BY:
                 return slope2_ref[k, y - 2]
             return s2y_ref[k, y].astype(f32)
-        second(2 + k, k, own)
+
+        second(2 + k, own)
     for k in range(2):
         for ref, first, z in ((ra_ref, 36, 6 - 6 * pz), (rb_ref, 0, 6 * pz)):
             def far(y, ref=ref, first=first + 24 * k):
                 return ref[first + 2 * y : first + 2 * y + 2].astype(f32).reshape(C, X)
-            second(z + k, k, far)
+
+            second(z + k, far)
 
     w2 = w2_ref[...]
     w1 = w1_ref[...]
@@ -427,15 +430,13 @@
     keep = lax.dynamic_index_in_dim(grad, core, 0, keepdims=False)
     give = lax.dynamic_index_in_dim(grad, 1 - core, 0, keepdims=False)
     part = keep + even(give, "gz")
-    row = groups(lax.axis_size("gy"), 1)
-    size = len(row[0])
-    chunks = part.reshape(size, 2 * C // size, 256)
-    part = jnp.sum(lax.all_to_all(chunks, "gy", 0, 0, axis_index_groups=row), axis=0)
-    for axis, unit in (("gy", 4), ("gz", 8), ("gz", 2)):
+    for axis, unit in (("gy", 1), ("gy", 4), ("gz", 8), ("gz", 2)):
         sets = groups(lax.axis_size(axis), unit)
-        if len(sets[0]) > 1:
+        if len(sets[0]) > 1 and unit == 8:
+            copies = jnp.broadcast_to(part[None], (len(sets[0]),) + part.shape)
+            part = jnp.sum(lax.all_to_all(copies, axis, 0, 0, axis_index_groups=sets), axis=0)
+        elif len(sets[0]) > 1:
             part = jnp.sum(lax.all_gather(part, axis, axis_index_groups=sets), axis=0)
-    part = lax.all_gather(part, "gy", axis_index_groups=row).reshape(2 * C, 256)
     other = even(part, "gz")
     return jnp.where(core == 0, part, other), jnp.where(core == 0, other, part)
 
@@ -486,8 +487,8 @@
     ha = even(fa, "gz")
     hb = odd(call(relay, shape((72, 8, X), SENT))(None, fa, ha), "gz")
     hb, fs = lax.optimization_barrier((hb, fs))
+    hs = odd(fs, "gz")
     hc = even(hb, "gz")
-    hs = odd(fs, "gz")
 
     plane = (24, 24, X)
     dpre = call(
@@ -525,6 +526,7 @@
 def solution(mesh):
     in_specs = (P(None, "gz", "gy", None), P("gz", "gy", None), P("gz", "gy", None), P(), P(), P())
     out_specs = (P(None, "gz", "gy", None), P(), P(), P())
+
     return jax.shard_map(
         on_device, mesh=mesh, in_specs=in_specs, out_specs=out_specs, check_vma=False
     )

time: 161 us -> 151 us (0.938)
  blocking collectives: 64.9 us -> 57.6 us
  starting transfers between devices: 59.8 us -> 57.1 us
    all_gather x1 -> x0, blocking collectives: 9.11 us -> none  [total_of(): part = lax.all_gather(part, 'gy', axis_index_groups=row).reshape(2 * C, 256)]
    all_gather x3, blocking collectives: 37.9 us -> 46 us  [total_of(): part = jnp.sum(lax.all_gather(part, axis, axis_index_groups=sets), axis=0)]
    all_to_all x1, blocking collectives: 17.9 us -> 11.6 us  [total_of(): lax.all_to_all(copies, axis, 0, 0, axis_index_groups=sets)]
    ppermute x7, starting transfers between devices: 40 us -> 37.2 us  [even(): return lax.ppermute(value, axis, [(i, i ^ 1) for i in range(n)])]
  transfers between devices with their start and end apart: 12 -> 12, of which waited for: 7 -> 7; matrix products, arithmetic and copies ran while one was open for 0% -> 0% of each run, Pallas kernels for 3% -> 4%
where the time goes in v5:
time: 151 us
  blocking collectives  57.6 us (38%)
  starting transfers between devices  57.1 us (38%)
  Pallas kernels  19.1 us (13%)
  waiting for transfers between devices  13 us (9%)
  local copies, waits for them, and re-layouts  2.8 us (2%)
    all_gather x3, blocking collectives, total_of(): part = jnp.sum(lax.all_gather(part, axis, axis_index_groups=sets), axis=0)  46 us
    ppermute x7, starting transfers between devices, even(): return lax.ppermute(value, axis, [(i, i ^ 1) for i in range(n)])  37.2 us
    ppermute x5, starting transfers between devices, odd(): return lax.ppermute(value, axis, pairs + [(j, i) for i, j in pairs])  19.8 us
    pallas_call x9, Pallas kernels, run(): pl.pallas_call(kernel, out_shape=outs, in_specs=specs, out_specs=[vmem] *...  19.1 us
    all_to_all x1, blocking collectives, total_of(): lax.all_to_all(copies, axis, 0, 0, axis_index_groups=sets)  11.6 us
    ppermute x5, waiting for transfers between devices, odd(): return lax.ppermute(value, axis, pairs + [(j, i) for i, j in pairs])  8.09 us
    ppermute x7, waiting for transfers between devices, even(): return lax.ppermute(value, axis, [(i, i ^ 1) for i in range(n)])  4.92 us
  transfers between devices with their start and end apart: 12, of which 7 were waited for; matrix products, arithmetic and copies ran while one was open for 0% of the time, Pallas kernels for 4%

profile of v5, /device:TPU:1, one launch (start us, length us, event | category | flops | bytes accessed | tf_op | source)
XLA Modules:
  0.0 150.6 jit_solution(3306720164377194145)
XLA Ops:
  0.6 0.0 copy-start.3
  0.7 0.1 pad_add_fusion.at.refs_0_
  0.7 0.6 copy-done.3
  1.4 0.9 copy-done
  2.3 0.6 shard_map.93
  2.9 3.9 %collective-permute-start = (bf16[9,16,128]{2,1,0:T(8,128)(2,1)S(1)}, bf16[9,16,128]{2,1,0:T(8,128)(2,1)S(1)}, u32[]{:S(2)}, u32[]{:S(2)}) collective-permute-start(bf16[9,16,128]{2,1,0:T(8,128)(2,1)S(1)} %get-tuple-element.37), channel_id=1, source_target_pairs={{0,1},{1,0},{2,3},{3,2},{4,5},{5,4},{6,7},{7,6},{8,9},{9,8},{10,11... | collective-permute-start | bytes 110600 | tf_op jit(solution)/shard_map/ppermute | solution.py:413
  6.8 0.7 collective-permute-start.1
  7.5 0.7 collective-permute-done.re_ref
  8.2 0.0 collective-permute-done.1.ro_ref
  8.2 0.6 shard_map.94
  8.7 9.3 %collective-permute-start.2 = (bf16[27,16,128]{2,1,0:T(8,128)(2,1)S(1)}, bf16[27,16,128]{2,1,0:T(8,128)(2,1)S(1)}, u32[]{:S(2)}, u32[]{:S(2)}) collective-permute-start(bf16[27,16,128]{2,1,0:T(8,128)(2,1)S(1)} %get-tuple-element.41), channel_id=1, source_target_pairs={{0,16},{16,0},{32,48},{48,32},{64,80},{80,64},{96,112},{112,96},{1... | collective-permute-start | bytes 331784 | tf_op jit(solution)/shard_map/ppermute | solution.py:413
  18.1 3.4 %collective-permute-start.3 = (bf16[27,16,128]{2,1,0:T(8,128)(2,1)S(1)}, bf16[27,16,128]{2,1,0:T(8,128)(2,1)S(1)}, u32[]{:S(2)}, u32[]{:S(2)}) collective-permute-start(bf16[27,16,128]{2,1,0:T(8,128)(2,1)S(1)} %get-tuple-element.42), channel_id=1, source_target_pairs={{16,32},{48,64},{80,96},{112,128},{144,160},{176,192},{208,224},{2... | collective-permute-start | bytes 331784 | tf_op jit(solution)/shard_map/ppermute | solution.py:419
  21.5 0.0 copy-start.9
  21.5 0.0 copy-done.8
  21.5 0.0 copy-done.1
  21.5 0.6 copy-done.9
  22.1 0.4 shard_map.95
  22.5 0.0 copy-start.4
  22.5 0.6 copy-done.4
  23.2 0.0 collective-permute-done.2.refs_3_
  23.2 4.9 %collective-permute-done.3.refs_4_ = bf16[27,16,128]{2,1,0:T(8,128)(2,1)S(1)} collective-permute-done((bf16[27,16,128]{2,1,0:T(8,128)(2,1)S(1)}, bf16[27,16,128]{2,1,0:T(8,128)(2,1)S(1)}, u32[]{:S(2)}, u32[]{:S(2)}) %collective-permute-start.3) | collective-permute-done | bytes 110624 | tf_op jit(solution)/shard_map/ppermute | solution.py:419
  28.1 4.0 %shard_map.96 = (bf16[6,10,3,16,128]{4,3,2,1,0:T(8,128)(2,1)S(1)}, bf16[6,10,3,16,128]{4,3,2,1,0:T(8,128)(2,1)S(1)}, f32[6,10,16,128]{3,2,1,0:T(8,128)S(1)}, f32...) custom-call(s32[4]{0:T(128)S(1)} %pad_add_fusion.at.refs_0_, ...), custom_call_target="tpu_custom_call" | custom-call | bytes 548880 | tf_op jit(solution)/shard_map/pallas_call | solution.py:394
  32.0 6.8 %collective-permute-start.4 = (bf16[28,8,128]{2,1,0:T(8,128)(2,1)S(1)}, bf16[28,8,128]{2,1,0:T(8,128)(2,1)S(1)}, u32[]{:S(2)}, u32[]{:S(2)}) collective-permute-start(bf16[28,8,128]{2,1,0:T(8,128)(2,1)S(1)} %get-tuple-element.48.me_ref), channel_id=1, source_target_pairs={{0,1},{1,0},{2,3},{3,2},{4,5},{5,4},{6,7},{7,6},{8,9},{9,8},{10,11... | collective-permute-start | bytes 172040 | tf_op jit(solution)/shard_map/ppermute | solution.py:413
  38.8 0.7 collective-permute-start.5
  39.5 0.9 collective-permute-done.4.re_ref
  40.4 0.0 collective-permute-done.5.ro_ref
  40.4 1.2 shard_map.97
  41.6 1.9 %collective-permute-start.6 = (bf16[84,8,128]{2,1,0:T(8,128)(2,1)S(1)}, bf16[84,8,128]{2,1,0:T(8,128)(2,1)S(1)}, u32[]{:S(2)}, u32[]{:S(2)}) collective-permute-start(bf16[84,8,128]{2,1,0:T(8,128)(2,1)S(1)} %get-tuple-element.51.ma_ref.refs_2_), channel_id=1, source_target_pairs={{0,16},{16,0},{32,48},{48,32},{64,80},{80,64},{96,112},{112,96},{1... | collective-permute-start | bytes 516104 | tf_op jit(solution)/shard_map/ppermute | solution.py:413
  43.5 1.4 collective-permute-done.6.ra_ref.refs_3_
  44.9 7.2 %collective-permute-start.7 = (bf16[72,8,128]{2,1,0:T(8,128)(2,1)S(1)}, bf16[72,8,128]{2,1,0:T(8,128)(2,1)S(1)}, u32[]{:S(2)}, u32[]{:S(2)}) collective-permute-start(bf16[72,8,128]{2,1,0:T(8,128)(2,1)S(1)} %shard_map.98), channel_id=1, source_target_pairs={{16,32},{48,64},{80,96},{112,128},{144,160},{176,192},{208,224},{2... | collective-permute-start | bytes 442376 | tf_op jit(solution)/shard_map/ppermute | solution.py:419
  52.1 3.2 %collective-permute-done.7.refs_4_ = bf16[72,8,128]{2,1,0:T(8,128)(2,1)S(1)} collective-permute-done((bf16[72,8,128]{2,1,0:T(8,128)(2,1)S(1)}, bf16[72,8,128]{2,1,0:T(8,128)(2,1)S(1)}, u32[]{:S(2)}, u32[]{:S(2)}) %collective-permute-start.7) | collective-permute-done | bytes 147488 | tf_op jit(solution)/shard_map/ppermute | solution.py:419
  55.3 1.9 %collective-permute-start.8 = (bf16[72,8,128]{2,1,0:T(8,128)(2,1)S(1)}, bf16[72,8,128]{2,1,0:T(8,128)(2,1)S(1)}, u32[]{:S(2)}, u32[]{:S(2)}) collective-permute-start(bf16[72,8,128]{2,1,0:T(8,128)(2,1)S(1)} %collective-permute-done.7.refs_4_), channel_id=1, source_target_pairs={{0,16},{16,0},{32,48},{48,32},{64,80},{80,64},{96,112},{112,96},{1... | collective-permute-start | bytes 442376 | tf_op jit(solution)/shard_map/ppermute | solution.py:413
  57.2 8.0 %collective-permute-start.9 = (bf16[48,8,128]{2,1,0:T(8,128)(2,1)}, bf16[48,8,128]{2,1,0:T(8,128)(2,1)S(1)}, u32[]{:S(2)}, u32[]{:S(2)}) collective-permute-start(bf16[48,8,128]{2,1,0:T(8,128)(2,1)} %get-tuple-element.56), channel_id=1, source_target_pairs={{16,32},{48,64},{80,96},{112,128},{144,160},{176,192},{208,224},{2... | collective-permute-start | bytes 294920 | tf_op jit(solution)/shard_map/ppermute | solution.py:419
  65.2 0.0 collective-permute-done.8.refs_5_
  65.2 0.0 copy-start.5
  65.2 0.0 copy-start.7
  65.2 5.0 %shard_map.99.dpre_ref = f32[8,16,128]{2,1,0:T(8,128)S(1)} custom-call(s32[4]{0:T(128)S(1)} %pad_add_fusion.at.refs_0_, f32[3,4,8,128]{3,2,1,0:T(8,128)S(1)} %get-tuple-element.47.refs_1_, bf16[84,8,128]{2,1,0:T(8,128)(2,1)S(1)} %get-tuple-element.51.ma_ref.refs_2_, bf16[84,8,128]{2,1,0:T(8,128)(2,1)S(1)} %collective-permute-done.6.ra_ref.refs_3_, ...), custom_call_target="tpu_custom_call" | custom-call | bytes 753680 | tf_op jit(solution)/shard_map/pallas_call | solution.py:394
  70.2 0.0 collective-permute-done.9.rb_ref
  70.3 6.1 %shard_map.100 = (bf16[16,4,8,128]{3,2,1,0:T(8,128)(2,1)}, f32[2,32,256]{2,1,0:T(8,128)S(1)}) custom-call(s32[4]{0:T(128)S(1)} %pad_add_fusion.at.refs_0_, f32[8,16,128]{2,1,0:T(8,128)S(1)} %shard_map.99.dpre_ref, f32[4,8,16,128]{3,2,1,0:T(8,128)S(1)} %get-tuple-element.49.slope2_ref, bf16[4,12,16,128]{3,2,1,0:T(8,128)(2,1)S(1)} %get-tuple-element.55.s2y_ref, ...), custom_call_target="tpu_custom_call" | custom-call | bytes 3104784 | tf_op jit(solution)/shard_map/pallas_call | solution.py:394
  76.4 1.9 %collective-permute-start.10 = (f32[32,256]{1,0:T(8,128)S(1)}, f32[32,256]{1,0:T(8,128)S(1)}, u32[]{:S(2)}, u32[]{:S(2)}) collective-permute-start(f32[32,256]{1,0:T(8,128)S(1)} %dynamic-slice_bitcast_fusion), channel_id=1, source_target_pairs={{0,16},{16,0},{32,48},{48,32},{64,80},{80,64},{96,112},{112,96},{1... | collective-permute-start | bytes 98312 | tf_op jit(solution)/shard_map/ppermute | solution.py:413
  78.4 1.2 collective-permute-done.10
  79.5 19.2 %all-gather = f32[128,256]{1,0:T(8,128)S(1)} all-gather(f32[32,256]{1,0:T(8,128)S(1)} %bitcast_add_fusion), channel_id=2, replica_groups={{0,1,2,3},{4,5,6,7},{8,9,10,11},{12,13,14,15},{16,17,18,19},{20,21,22,2..., dimensions={0}, use_global_device_ids=true | all-gather | bytes 163840 | tf_op jit(solution)/shard_map/all_gather | solution.py:439
  98.7 10.8 %all-gather.1 = f32[128,256]{1,0:T(8,128)S(1)} all-gather(f32[32,256]{1,0:T(8,128)S(1)} %reduce_sum.36), channel_id=3, replica_groups={{0,4,8,12},{1,5,9,13},{2,6,10,14},{3,7,11,15},{16,20,24,28},{17,21,25,2..., dimensions={0}, use_global_device_ids=true | all-gather | bytes 163840 | tf_op jit(solution)/shard_map/all_gather | solution.py:439
  109.6 11.6 %all_to_all.5 = f32[4,32,256]{2,1,0:T(8,128)S(1)} all-to-all(f32[4,32,256]{2,1,0:T(8,128)S(1)} %broadcast_in_dim.2), channel_id=1, replica_groups={{0,128,256,384},{16,144,272,400},{32,160,288,416},{48,176,304,432},{64,..., dimensions={0} | all-to-all | bytes 262144 | tf_op jit(solution)/shard_map/all_to_all | solution.py:437
  121.2 15.9 %all-gather.2 = f32[128,256]{1,0:T(8,128)S(1)} all-gather(f32[32,256]{1,0:T(8,128)S(1)} %reduce_sum.38), channel_id=4, replica_groups={{0,32,64,96},{16,48,80,112},{128,160,192,224},{144,176,208,240},{256,28..., dimensions={0}, use_global_device_ids=true | all-gather | bytes 163840 | tf_op jit(solution)/shard_map/all_gather | solution.py:439
  137.2 11.5 %collective-permute-start.11 = (f32[32,256]{1,0:T(8,128)S(1)}, f32[32,256]{1,0:T(8,128)S(1)}, u32[]{:S(2)}, u32[]{:S(2)}) collective-permute-start(f32[32,256]{1,0:T(8,128)S(1)} %reduce_sum.39), channel_id=1, source_target_pairs={{0,16},{16,0},{32,48},{48,32},{64,80},{80,64},{96,112},{112,96},{1... | collective-permute-start | bytes 98312 | tf_op jit(solution)/shard_map/ppermute | solution.py:413
  148.7 0.8 collective-permute-done.11
  149.5 1.1 shard_map.101
  (18 shorter events, 0.1 us)
Async XLA Ops:
  0.6 0.7 copy-start.3
  1.4 0.9 copy-start
  2.3 19.2 %copy-start.8 = (s32[4,8,128]{2,1,0:T(8,128)S(1)}, s32[4,8,128]{2,1,0:T(8,128)}, u32[]{:S(2)}) copy-start(s32[4,8,128]{2,1,0:T(8,128)} %lab_ref.1) | copy-start | bytes 49156
  2.9 5.3 %collective-permute-start = (bf16[9,16,128]{2,1,0:T(8,128)(2,1)S(1)}, bf16[9,16,128]{2,1,0:T(8,128)(2,1)S(1)}, u32[]{:S(2)}, u32[]{:S(2)}) collective-permute-start(bf16[9,16,128]{2,1,0:T(8,128)(2,1)S(1)} %get-tuple-element.37), channel_id=1, source_target_pairs={{0,1},{1,0},{2,3},{3,2},{4,5},{5,4},{6,7},{7,6},{8,9},{9,8},{10,11... | collective-permute-start | bytes 110600 | tf_op jit(solution)/shard_map/ppermute | solution.py:413
  6.8 1.3 collective-permute-start.1
  8.2 13.3 %copy-start.1 = (bf16[16,16,3,3,3]{1,0,4,3,2:T(8,128)(2,1)S(1)}, bf16[16,16,3,3,3]{1,0,4,3,2:T(8,128)(2,1)}, u32[]{:S(2)}) copy-start(bf16[16,16,3,3,3]{1,0,4,3,2:T(8,128)(2,1)} %param.9) | copy-start | bytes 41476
  8.2 13.3 %copy-start.2 = (bf16[16,16,3,3,3]{1,0,4,3,2:T(8,128)(2,1)S(1)}, bf16[16,16,3,3,3]{1,0,4,3,2:T(8,128)(2,1)}, u32[]{:S(2)}) copy-start(bf16[16,16,3,3,3]{1,0,4,3,2:T(8,128)(2,1)} %param.10) | copy-start | bytes 41476
  8.7 14.4 %collective-permute-start.2 = (bf16[27,16,128]{2,1,0:T(8,128)(2,1)S(1)}, bf16[27,16,128]{2,1,0:T(8,128)(2,1)S(1)}, u32[]{:S(2)}, u32[]{:S(2)}) collective-permute-start(bf16[27,16,128]{2,1,0:T(8,128)(2,1)S(1)} %get-tuple-element.41), channel_id=1, source_target_pairs={{0,16},{16,0},{32,48},{48,32},{64,80},{80,64},{96,112},{112,96},{1... | collective-permute-start | bytes 331784 | tf_op jit(solution)/shard_map/ppermute | solution.py:413
  18.1 10.0 %collective-permute-start.3 = (bf16[27,16,128]{2,1,0:T(8,128)(2,1)S(1)}, bf16[27,16,128]{2,1,0:T(8,128)(2,1)S(1)}, u32[]{:S(2)}, u32[]{:S(2)}) collective-permute-start(bf16[27,16,128]{2,1,0:T(8,128)(2,1)S(1)} %get-tuple-element.42), channel_id=1, source_target_pairs={{16,32},{48,64},{80,96},{112,128},{144,160},{176,192},{208,224},{2... | collective-permute-start | bytes 331784 | tf_op jit(solution)/shard_map/ppermute | solution.py:419
  21.5 0.7 copy-start.9
  22.5 0.6 copy-start.4
  23.1 8.9 %copy-start.6 = (bf16[32,576]{1,0:T(8,128)(2,1)}, bf16[32,576]{1,0:T(8,128)(2,1)S(1)}, u32[]{:S(2)}) copy-start(bf16[32,576]{1,0:T(8,128)(2,1)S(1)} %get-tuple-element.62.w2_ref) | copy-start | bytes 110596
  32.0 8.3 %collective-permute-start.4 = (bf16[28,8,128]{2,1,0:T(8,128)(2,1)S(1)}, bf16[28,8,128]{2,1,0:T(8,128)(2,1)S(1)}, u32[]{:S(2)}, u32[]{:S(2)}) collective-permute-start(bf16[28,8,128]{2,1,0:T(8,128)(2,1)S(1)} %get-tuple-element.48.me_ref), channel_id=1, source_target_pairs={{0,1},{1,0},{2,3},{3,2},{4,5},{5,4},{6,7},{7,6},{8,9},{9,8},{10,11... | collective-permute-start | bytes 172040 | tf_op jit(solution)/shard_map/ppermute | solution.py:413
  38.8 1.6 %collective-permute-start.5 = (bf16[28,8,128]{2,1,0:T(8,128)(2,1)S(1)}, bf16[28,8,128]{2,1,0:T(8,128)(2,1)S(1)}, u32[]{:S(2)}, u32[]{:S(2)}) collective-permute-start(bf16[28,8,128]{2,1,0:T(8,128)(2,1)S(1)} %get-tuple-element.50), channel_id=1, source_target_pairs={{1,2},{3,4},{5,6},{7,8},{9,10},{11,12},{13,14},{2,1},{4,3},{6,5},{... | collective-permute-start | bytes 172040 | tf_op jit(solution)/shard_map/ppermute | solution.py:419
  41.6 3.3 %collective-permute-start.6 = (bf16[84,8,128]{2,1,0:T(8,128)(2,1)S(1)}, bf16[84,8,128]{2,1,0:T(8,128)(2,1)S(1)}, u32[]{:S(2)}, u32[]{:S(2)}) collective-permute-start(bf16[84,8,128]{2,1,0:T(8,128)(2,1)S(1)} %get-tuple-element.51.ma_ref.refs_2_), channel_id=1, source_target_pairs={{0,16},{16,0},{32,48},{48,32},{64,80},{80,64},{96,112},{112,96},{1... | collective-permute-start | bytes 516104 | tf_op jit(solution)/shard_map/ppermute | solution.py:413
  44.9 10.4 %collective-permute-start.7 = (bf16[72,8,128]{2,1,0:T(8,128)(2,1)S(1)}, bf16[72,8,128]{2,1,0:T(8,128)(2,1)S(1)}, u32[]{:S(2)}, u32[]{:S(2)}) collective-permute-start(bf16[72,8,128]{2,1,0:T(8,128)(2,1)S(1)} %shard_map.98), channel_id=1, source_target_pairs={{16,32},{48,64},{80,96},{112,128},{144,160},{176,192},{208,224},{2... | collective-permute-start | bytes 442376 | tf_op jit(solution)/shard_map/ppermute | solution.py:419
  55.3 9.9 %collective-permute-start.8 = (bf16[72,8,128]{2,1,0:T(8,128)(2,1)S(1)}, bf16[72,8,128]{2,1,0:T(8,128)(2,1)S(1)}, u32[]{:S(2)}, u32[]{:S(2)}) collective-permute-start(bf16[72,8,128]{2,1,0:T(8,128)(2,1)S(1)} %collective-permute-done.7.refs_4_), channel_id=1, source_target_pairs={{0,16},{16,0},{32,48},{48,32},{64,80},{80,64},{96,112},{112,96},{1... | collective-permute-start | bytes 442376 | tf_op jit(solution)/shard_map/ppermute | solution.py:413
  57.2 13.1 %collective-permute-start.9 = (bf16[48,8,128]{2,1,0:T(8,128)(2,1)}, bf16[48,8,128]{2,1,0:T(8,128)(2,1)S(1)}, u32[]{:S(2)}, u32[]{:S(2)}) collective-permute-start(bf16[48,8,128]{2,1,0:T(8,128)(2,1)} %get-tuple-element.56), channel_id=1, source_target_pairs={{16,32},{48,64},{80,96},{112,128},{144,160},{176,192},{208,224},{2... | collective-permute-start | bytes 294920 | tf_op jit(solution)/shard_map/ppermute | solution.py:419
  65.2 5.1 %copy-start.5 = (bf16[32,576]{1,0:T(8,128)(2,1)S(1)}, bf16[32,576]{1,0:T(8,128)(2,1)}, u32[]{:S(2)}) copy-start(bf16[32,576]{1,0:T(8,128)(2,1)} %copy-done.4) | copy-start | bytes 110596
  65.2 5.1 %copy-start.7 = (bf16[32,576]{1,0:T(8,128)(2,1)S(1)}, bf16[32,576]{1,0:T(8,128)(2,1)}, u32[]{:S(2)}) copy-start(bf16[32,576]{1,0:T(8,128)(2,1)} %copy-done.6) | copy-start | bytes 110596
  76.4 3.1 %collective-permute-start.10 = (f32[32,256]{1,0:T(8,128)S(1)}, f32[32,256]{1,0:T(8,128)S(1)}, u32[]{:S(2)}, u32[]{:S(2)}) collective-permute-start(f32[32,256]{1,0:T(8,128)S(1)} %dynamic-slice_bitcast_fusion), channel_id=1, source_target_pairs={{0,16},{16,0},{32,48},{48,32},{64,80},{80,64},{96,112},{112,96},{1... | collective-permute-start | bytes 98312 | tf_op jit(solution)/shard_map/ppermute | solution.py:413
  137.2 12.3 %collective-permute-start.11 = (f32[32,256]{1,0:T(8,128)S(1)}, f32[32,256]{1,0:T(8,128)S(1)}, u32[]{:S(2)}, u32[]{:S(2)}) collective-permute-start(f32[32,256]{1,0:T(8,128)S(1)} %reduce_sum.39), channel_id=1, source_target_pairs={{0,16},{16,0},{32,48},{48,32},{64,80},{80,64},{96,112},{112,96},{1... | collective-permute-start | bytes 98312 | tf_op jit(solution)/shard_map/ppermute | solution.py:413

commit v6 on v5

--- a/solution.py
+++ b/solution.py
@@ -196,9 +196,12 @@
         mb_ref[24 * k : 24 + 24 * k] = rows.astype(SENT)
 
 
-def relay(ma_ref, ra_ref, mb_ref):
+def relay(at, ma_ref, ra_ref, mb_ref):
+    pz = at[2]
     mb_ref[:36] = ma_ref[:36]
-    mb_ref[36:] = ra_ref[:36]
+    for i in range(3):
+        mb_ref[36 + 9 * i : 44 + 9 * i] = ra_ref[12 * i : 12 * i + 8]
+        mb_ref[44 + 9 * i] = ra_ref[12 * i + 8 + 3 * pz]
 
 
 def march(nz, ny, at, own_ref, ye_ref, mate_ref, far_ref, far2_ref, g0_ref, dpre_ref,
@@ -224,9 +227,12 @@
     place(8 + 4 * pz, mine)
     place(12 - 4 * pz, piece(mate_ref, 0))
     place(16 * pz + 4 - 4 * pz, piece(far_ref, 0))
-    place(16 * pz + 4 * pz, piece(far_ref, 36))
     place(16 - 16 * pz + 4 * pz, piece(far2_ref, 0))
-    place(16 - 16 * pz + 4 - 4 * pz, piece(far2_ref, 36))
+
+    def beyond(i, f, k):
+        return far_ref[44 + 9 * i if f == 2 else 36 + 9 * i + 4 * f + k]
+
+    place(16 * pz + 4 * pz, beyond)
 
     dd[0, 0] = jnp.zeros((24, X), f32)
     rows_in = inside(iy * BY - 8, (24, X), ny)
@@ -432,11 +438,9 @@
     part = keep + even(give, "gz")
     for axis, unit in (("gy", 1), ("gy", 4), ("gz", 8), ("gz", 2)):
         sets = groups(lax.axis_size(axis), unit)
-        if len(sets[0]) > 1 and unit == 8:
+        if len(sets[0]) > 1:
             copies = jnp.broadcast_to(part[None], (len(sets[0]),) + part.shape)
             part = jnp.sum(lax.all_to_all(copies, axis, 0, 0, axis_index_groups=sets), axis=0)
-        elif len(sets[0]) > 1:
-            part = jnp.sum(lax.all_gather(part, axis, axis_index_groups=sets), axis=0)
     other = even(part, "gz")
     return jnp.where(core == 0, part, other), jnp.where(core == 0, other, part)
 
@@ -485,10 +489,10 @@
         widen, [shape((84, 8, X), SENT), shape((48, 8, X), SENT), shape((BZ, 12, C, X))]
     )(at, fe, slope2, ge, go)
     ha = even(fa, "gz")
-    hb = odd(call(relay, shape((72, 8, X), SENT))(None, fa, ha), "gz")
+    hb = odd(call(relay, shape((63, 8, X), SENT))(at, fa, ha), "gz")
     hb, fs = lax.optimization_barrier((hb, fs))
     hs = odd(fs, "gz")
-    hc = even(hb, "gz")
+    hc = even(hb[:36], "gz")
 
     plane = (24, 24, X)
     dpre = call(

time: 151 us -> 146 us (0.967)
  starting transfers between devices: 57.1 us -> 52.5 us
  blocking collectives: 57.6 us -> 54.7 us
  waiting for transfers between devices: 13 us -> 14.7 us
    all_gather x3 -> x0, blocking collectives: 46 us -> none  [total_of(): part = jnp.sum(lax.all_gather(part, axis, axis_index_groups=sets), axis=0)]
    all_to_all x1 -> x4, blocking collectives: 11.6 us -> 54.7 us  [total_of(): lax.all_to_all(copies, axis, 0, 0, axis_index_groups=sets)]
    ppermute x7, starting transfers between devices: 37.2 us -> 33.4 us  [even(): return lax.ppermute(value, axis, [(i, i ^ 1) for i in range(n)])]
  transfers between devices with their start and end apart: 12 -> 12, of which waited for: 7 -> 8; matrix products, arithmetic and copies ran while one was open for 0% -> 0% of each run, Pallas kernels for 4% -> 4%
where the time goes in v6:
time: 146 us; the launch traced here: 145 us
  blocking collectives  54.7 us (37%)
  starting transfers between devices  52.5 us (36%)
  Pallas kernels  19.6 us (13%)
  waiting for transfers between devices  14.7 us (10%)
  local copies, waits for them, and re-layouts  2.84 us (2%)
    all_to_all x4, blocking collectives, total_of(): lax.all_to_all(copies, axis, 0, 0, axis_index_groups=sets)  54.7 us
    ppermute x7, starting transfers between devices, even(): return lax.ppermute(value, axis, [(i, i ^ 1) for i in range(n)])  33.4 us
    pallas_call x9, Pallas kernels, run(): pl.pallas_call(kernel, out_shape=outs, in_specs=specs, out_specs=[vmem] *...  19.6 us
    ppermute x5, starting transfers between devices, odd(): return lax.ppermute(value, axis, pairs + [(j, i) for i, j in pairs])  19 us
    ppermute x5, waiting for transfers between devices, odd(): return lax.ppermute(value, axis, pairs + [(j, i) for i, j in pairs])  8.51 us
    ppermute x7, waiting for transfers between devices, even(): return lax.ppermute(value, axis, [(i, i ^ 1) for i in range(n)])  6.21 us
  transfers between devices with their start and end apart: 12, of which 8 were waited for; matrix products, arithmetic and copies ran while one was open for 0% of the time, Pallas kernels for 4%

profile of v6, /device:TPU:1, one launch (start us, length us, event | category | flops | bytes accessed | tf_op | source)
XLA Modules:
  0.0 145.3 jit_solution(6947026406393744709)
XLA Ops:
  0.6 0.0 copy-start.3
  0.7 0.1 pad_add_fusion.at.refs_0_
  0.7 0.6 copy-done.3
  1.4 0.0 copy-start
  1.4 0.9 copy-done
  2.3 0.6 shard_map.93
  2.9 3.9 %collective-permute-start = (bf16[9,16,128]{2,1,0:T(8,128)(2,1)S(1)}, bf16[9,16,128]{2,1,0:T(8,128)(2,1)S(1)}, u32[]{:S(2)}, u32[]{:S(2)}) collective-permute-start(bf16[9,16,128]{2,1,0:T(8,128)(2,1)S(1)} %get-tuple-element.37), channel_id=1, source_target_pairs={{0,1},{1,0},{2,3},{3,2},{4,5},{5,4},{6,7},{7,6},{8,9},{9,8},{10,11... | collective-permute-start | bytes 110600 | tf_op jit(solution)/shard_map/ppermute | solution.py:419
  6.8 0.7 collective-permute-start.1
  7.5 0.7 collective-permute-done.re_ref
  8.2 0.0 collective-permute-done.1.ro_ref
  8.2 0.6 shard_map.94
  8.7 9.3 %collective-permute-start.2 = (bf16[27,16,128]{2,1,0:T(8,128)(2,1)S(1)}, bf16[27,16,128]{2,1,0:T(8,128)(2,1)S(1)}, u32[]{:S(2)}, u32[]{:S(2)}) collective-permute-start(bf16[27,16,128]{2,1,0:T(8,128)(2,1)S(1)} %get-tuple-element.41), channel_id=1, source_target_pairs={{0,16},{16,0},{32,48},{48,32},{64,80},{80,64},{96,112},{112,96},{1... | collective-permute-start | bytes 331784 | tf_op jit(solution)/shard_map/ppermute | solution.py:419
  18.1 3.4 %collective-permute-start.3 = (bf16[27,16,128]{2,1,0:T(8,128)(2,1)S(1)}, bf16[27,16,128]{2,1,0:T(8,128)(2,1)S(1)}, u32[]{:S(2)}, u32[]{:S(2)}) collective-permute-start(bf16[27,16,128]{2,1,0:T(8,128)(2,1)S(1)} %get-tuple-element.42), channel_id=1, source_target_pairs={{16,32},{48,64},{80,96},{112,128},{144,160},{176,192},{208,224},{2... | collective-permute-start | bytes 331784 | tf_op jit(solution)/shard_map/ppermute | solution.py:425
  21.5 0.0 copy-start.5
  21.5 0.0 copy-done.4
  21.5 0.0 copy-done.1
  21.5 0.0 copy-done.2
  21.5 0.6 copy-done.5
  22.1 0.4 shard_map.95
  22.5 0.0 collective-permute-done.2.refs_3_
  22.5 5.5 %collective-permute-done.3.refs_4_ = bf16[27,16,128]{2,1,0:T(8,128)(2,1)S(1)} collective-permute-done((bf16[27,16,128]{2,1,0:T(8,128)(2,1)S(1)}, bf16[27,16,128]{2,1,0:T(8,128)(2,1)S(1)}, u32[]{:S(2)}, u32[]{:S(2)}) %collective-permute-start.3) | collective-permute-done | bytes 110624 | tf_op jit(solution)/shard_map/ppermute | solution.py:425
  28.1 4.0 %shard_map.96 = (bf16[6,10,3,16,128]{4,3,2,1,0:T(8,128)(2,1)S(1)}, bf16[6,10,3,16,128]{4,3,2,1,0:T(8,128)(2,1)S(1)}, f32[6,10,16,128]{3,2,1,0:T(8,128)S(1)}, f32...) custom-call(s32[4]{0:T(128)S(1)} %pad_add_fusion.at.refs_0_, ...), custom_call_target="tpu_custom_call" | custom-call | bytes 548880 | tf_op jit(solution)/shard_map/pallas_call | solution.py:400
  32.0 6.8 %collective-permute-start.4 = (bf16[28,8,128]{2,1,0:T(8,128)(2,1)S(1)}, bf16[28,8,128]{2,1,0:T(8,128)(2,1)S(1)}, u32[]{:S(2)}, u32[]{:S(2)}) collective-permute-start(bf16[28,8,128]{2,1,0:T(8,128)(2,1)S(1)} %get-tuple-element.48.me_ref), channel_id=1, source_target_pairs={{0,1},{1,0},{2,3},{3,2},{4,5},{5,4},{6,7},{7,6},{8,9},{9,8},{10,11... | collective-permute-start | bytes 172040 | tf_op jit(solution)/shard_map/ppermute | solution.py:419
  38.8 0.7 collective-permute-start.5
  39.5 0.9 collective-permute-done.4.re_ref
  40.3 0.0 collective-permute-done.5.ro_ref
  40.3 1.2 shard_map.97
  41.6 1.9 %collective-permute-start.6 = (bf16[84,8,128]{2,1,0:T(8,128)(2,1)S(1)}, bf16[84,8,128]{2,1,0:T(8,128)(2,1)S(1)}, u32[]{:S(2)}, u32[]{:S(2)}) collective-permute-start(bf16[84,8,128]{2,1,0:T(8,128)(2,1)S(1)} %get-tuple-element.51.ma_ref.refs_2_), channel_id=1, source_target_pairs={{0,16},{16,0},{32,48},{48,32},{64,80},{80,64},{96,112},{112,96},{1... | collective-permute-start | bytes 516104 | tf_op jit(solution)/shard_map/ppermute | solution.py:419
  43.5 1.4 collective-permute-done.6.ra_ref.refs_3_
  44.9 0.5 shard_map.98
  45.4 7.2 %collective-permute-start.7 = (bf16[63,8,128]{2,1,0:T(8,128)(2,1)S(1)}, bf16[63,8,128]{2,1,0:T(8,128)(2,1)S(1)}, u32[]{:S(2)}, u32[]{:S(2)}) collective-permute-start(bf16[63,8,128]{2,1,0:T(8,128)(2,1)S(1)} %shard_map.98), channel_id=1, source_target_pairs={{16,32},{48,64},{80,96},{112,128},{144,160},{176,192},{208,224},{2... | collective-permute-start | bytes 387080 | tf_op jit(solution)/shard_map/ppermute | solution.py:425
  52.6 3.0 %collective-permute-done.7.refs_4_ = bf16[63,8,128]{2,1,0:T(8,128)(2,1)S(1)} collective-permute-done((bf16[63,8,128]{2,1,0:T(8,128)(2,1)S(1)}, bf16[63,8,128]{2,1,0:T(8,128)(2,1)S(1)}, u32[]{:S(2)}, u32[]{:S(2)}) %collective-permute-start.7) | collective-permute-done | bytes 129056 | tf_op jit(solution)/shard_map/ppermute | solution.py:425
  55.6 7.2 %collective-permute-start.9 = (bf16[48,8,128]{2,1,0:T(8,128)(2,1)}, bf16[48,8,128]{2,1,0:T(8,128)(2,1)S(1)}, u32[]{:S(2)}, u32[]{:S(2)}) collective-permute-start(bf16[48,8,128]{2,1,0:T(8,128)(2,1)} %get-tuple-element.56), channel_id=1, source_target_pairs={{16,32},{48,64},{80,96},{112,128},{144,160},{176,192},{208,224},{2... | collective-permute-start | bytes 294920 | tf_op jit(solution)/shard_map/ppermute | solution.py:425
  62.8 0.6 slice.3
  63.4 1.9 %collective-permute-start.8 = (bf16[36,8,128]{2,1,0:T(8,128)(2,1)}, bf16[36,8,128]{2,1,0:T(8,128)(2,1)S(1)}, u32[]{:S(2)}, u32[]{:S(2)}) collective-permute-start(bf16[36,8,128]{2,1,0:T(8,128)(2,1)} %slice.3), channel_id=1, source_target_pairs={{0,16},{16,0},{32,48},{48,32},{64,80},{80,64},{96,112},{112,96},{1... | collective-permute-start | bytes 221192 | tf_op jit(solution)/shard_map/ppermute | solution.py:419
  65.3 1.4 collective-permute-done.8.refs_5_
  66.8 5.0 %shard_map.99.dpre_ref = f32[8,16,128]{2,1,0:T(8,128)S(1)} custom-call(s32[4]{0:T(128)S(1)} %pad_add_fusion.at.refs_0_, f32[3,4,8,128]{3,2,1,0:T(8,128)S(1)} %get-tuple-element.47.refs_1_, bf16[84,8,128]{2,1,0:T(8,128)(2,1)S(1)} %get-tuple-element.51.ma_ref.refs_2_, bf16[84,8,128]{2,1,0:T(8,128)(2,1)S(1)} %collective-permute-done.6.ra_ref.refs_3_, ...), custom_call_target="tpu_custom_call" | custom-call | bytes 661520 | tf_op jit(solution)/shard_map/pallas_call | solution.py:400
  71.8 0.0 collective-permute-done.9.rb_ref
  71.8 6.1 %shard_map.100 = (bf16[16,4,8,128]{3,2,1,0:T(8,128)(2,1)}, f32[2,32,256]{2,1,0:T(8,128)S(1)}) custom-call(s32[4]{0:T(128)S(1)} %pad_add_fusion.at.refs_0_, f32[8,16,128]{2,1,0:T(8,128)S(1)} %shard_map.99.dpre_ref, f32[4,8,16,128]{3,2,1,0:T(8,128)S(1)} %get-tuple-element.49.slope2_ref, bf16[4,12,16,128]{3,2,1,0:T(8,128)(2,1)S(1)} %get-tuple-element.55.s2y_ref, ...), custom_call_target="tpu_custom_call" | custom-call | bytes 3104784 | tf_op jit(solution)/shard_map/pallas_call | solution.py:400
  78.0 2.1 %collective-permute-start.10 = (f32[32,256]{1,0:T(8,128)S(1)}, f32[32,256]{1,0:T(8,128)S(1)}, u32[]{:S(2)}, u32[]{:S(2)}) collective-permute-start(f32[32,256]{1,0:T(8,128)S(1)} %dynamic-slice_bitcast_fusion), channel_id=1, source_target_pairs={{0,16},{16,0},{32,48},{48,32},{64,80},{80,64},{96,112},{112,96},{1... | collective-permute-start | bytes 98312 | tf_op jit(solution)/shard_map/ppermute | solution.py:419
  80.0 1.0 collective-permute-done.10
  81.1 13.9 %all_to_all.20 = f32[4,32,256]{2,1,0:T(8,128)S(1)} all-to-all(f32[4,32,256]{2,1,0:T(8,128)S(1)} %broadcast_in_dim.8), channel_id=1, replica_groups={{0,1,2,3},{4,5,6,7},{8,9,10,11},{12,13,14,15},{16,17,18,19},{20,21,22,2..., dimensions={0} | all-to-all | bytes 262144 | tf_op jit(solution)/shard_map/all_to_all | solution.py:443
  95.0 10.8 %all_to_all.21 = f32[4,32,256]{2,1,0:T(8,128)S(1)} all-to-all(f32[4,32,256]{2,1,0:T(8,128)S(1)} %broadcast_in_dim.9), channel_id=1, replica_groups={{0,4,8,12},{1,5,9,13},{2,6,10,14},{3,7,11,15},{16,20,24,28},{17,21,25,2..., dimensions={0} | all-to-all | bytes 262144 | tf_op jit(solution)/shard_map/all_to_all | solution.py:443
  105.8 12.3 %all_to_all.22 = f32[4,32,256]{2,1,0:T(8,128)S(1)} all-to-all(f32[4,32,256]{2,1,0:T(8,128)S(1)} %broadcast_in_dim.10), channel_id=1, replica_groups={{0,128,256,384},{16,144,272,400},{32,160,288,416},{48,176,304,432},{64,..., dimensions={0} | all-to-all | bytes 262144 | tf_op jit(solution)/shard_map/all_to_all | solution.py:443
  118.2 17.7 %all_to_all.23 = f32[4,32,256]{2,1,0:T(8,128)S(1)} all-to-all(f32[4,32,256]{2,1,0:T(8,128)S(1)} %broadcast_in_dim.11), channel_id=1, replica_groups={{0,32,64,96},{16,48,80,112},{128,160,192,224},{144,176,208,240},{256,28..., dimensions={0} | all-to-all | bytes 262144 | tf_op jit(solution)/shard_map/all_to_all | solution.py:443
  135.9 7.6 %collective-permute-start.11 = (f32[32,256]{1,0:T(8,128)S(1)}, f32[32,256]{1,0:T(8,128)S(1)}, u32[]{:S(2)}, u32[]{:S(2)}) collective-permute-start(f32[32,256]{1,0:T(8,128)S(1)} %reduce_sum.39), channel_id=1, source_target_pairs={{0,16},{16,0},{32,48},{48,32},{64,80},{80,64},{96,112},{112,96},{1... | collective-permute-start | bytes 98312 | tf_op jit(solution)/shard_map/ppermute | solution.py:419
  143.4 0.8 collective-permute-done.11
  144.3 1.1 shard_map.101
  (14 shorter events, 0.1 us)
Async XLA Ops:
  0.6 0.7 copy-start.3
  1.4 0.9 copy-start
  2.3 19.2 %copy-start.4 = (s32[4,8,128]{2,1,0:T(8,128)S(1)}, s32[4,8,128]{2,1,0:T(8,128)}, u32[]{:S(2)}) copy-start(s32[4,8,128]{2,1,0:T(8,128)} %lab_ref.1) | copy-start | bytes 49156
  2.9 5.3 %collective-permute-start = (bf16[9,16,128]{2,1,0:T(8,128)(2,1)S(1)}, bf16[9,16,128]{2,1,0:T(8,128)(2,1)S(1)}, u32[]{:S(2)}, u32[]{:S(2)}) collective-permute-start(bf16[9,16,128]{2,1,0:T(8,128)(2,1)S(1)} %get-tuple-element.37), channel_id=1, source_target_pairs={{0,1},{1,0},{2,3},{3,2},{4,5},{5,4},{6,7},{7,6},{8,9},{9,8},{10,11... | collective-permute-start | bytes 110600 | tf_op jit(solution)/shard_map/ppermute | solution.py:419
  6.8 1.3 collective-permute-start.1
  8.2 13.3 %copy-start.1 = (bf16[16,16,3,3,3]{1,0,4,3,2:T(8,128)(2,1)S(1)}, bf16[16,16,3,3,3]{1,0,4,3,2:T(8,128)(2,1)}, u32[]{:S(2)}) copy-start(bf16[16,16,3,3,3]{1,0,4,3,2:T(8,128)(2,1)} %param.9) | copy-start | bytes 41476
  8.2 13.3 %copy-start.2 = (bf16[16,16,3,3,3]{1,0,4,3,2:T(8,128)(2,1)S(1)}, bf16[16,16,3,3,3]{1,0,4,3,2:T(8,128)(2,1)}, u32[]{:S(2)}) copy-start(bf16[16,16,3,3,3]{1,0,4,3,2:T(8,128)(2,1)} %param.10) | copy-start | bytes 41476
  8.7 13.8 %collective-permute-start.2 = (bf16[27,16,128]{2,1,0:T(8,128)(2,1)S(1)}, bf16[27,16,128]{2,1,0:T(8,128)(2,1)S(1)}, u32[]{:S(2)}, u32[]{:S(2)}) collective-permute-start(bf16[27,16,128]{2,1,0:T(8,128)(2,1)S(1)} %get-tuple-element.41), channel_id=1, source_target_pairs={{0,16},{16,0},{32,48},{48,32},{64,80},{80,64},{96,112},{112,96},{1... | collective-permute-start | bytes 331784 | tf_op jit(solution)/shard_map/ppermute | solution.py:419
  18.1 10.0 %collective-permute-start.3 = (bf16[27,16,128]{2,1,0:T(8,128)(2,1)S(1)}, bf16[27,16,128]{2,1,0:T(8,128)(2,1)S(1)}, u32[]{:S(2)}, u32[]{:S(2)}) collective-permute-start(bf16[27,16,128]{2,1,0:T(8,128)(2,1)S(1)} %get-tuple-element.42), channel_id=1, source_target_pairs={{16,32},{48,64},{80,96},{112,128},{144,160},{176,192},{208,224},{2... | collective-permute-start | bytes 331784 | tf_op jit(solution)/shard_map/ppermute | solution.py:425
  21.5 0.7 copy-start.5
  32.0 8.3 %collective-permute-start.4 = (bf16[28,8,128]{2,1,0:T(8,128)(2,1)S(1)}, bf16[28,8,128]{2,1,0:T(8,128)(2,1)S(1)}, u32[]{:S(2)}, u32[]{:S(2)}) collective-permute-start(bf16[28,8,128]{2,1,0:T(8,128)(2,1)S(1)} %get-tuple-element.48.me_ref), channel_id=1, source_target_pairs={{0,1},{1,0},{2,3},{3,2},{4,5},{5,4},{6,7},{7,6},{8,9},{9,8},{10,11... | collective-permute-start | bytes 172040 | tf_op jit(solution)/shard_map/ppermute | solution.py:419
  38.8 1.6 %collective-permute-start.5 = (bf16[28,8,128]{2,1,0:T(8,128)(2,1)S(1)}, bf16[28,8,128]{2,1,0:T(8,128)(2,1)S(1)}, u32[]{:S(2)}, u32[]{:S(2)}) collective-permute-start(bf16[28,8,128]{2,1,0:T(8,128)(2,1)S(1)} %get-tuple-element.50), channel_id=1, source_target_pairs={{1,2},{3,4},{5,6},{7,8},{9,10},{11,12},{13,14},{2,1},{4,3},{6,5},{... | collective-permute-start | bytes 172040 | tf_op jit(solution)/shard_map/ppermute | solution.py:425
  41.6 3.3 %collective-permute-start.6 = (bf16[84,8,128]{2,1,0:T(8,128)(2,1)S(1)}, bf16[84,8,128]{2,1,0:T(8,128)(2,1)S(1)}, u32[]{:S(2)}, u32[]{:S(2)}) collective-permute-start(bf16[84,8,128]{2,1,0:T(8,128)(2,1)S(1)} %get-tuple-element.51.ma_ref.refs_2_), channel_id=1, source_target_pairs={{0,16},{16,0},{32,48},{48,32},{64,80},{80,64},{96,112},{112,96},{1... | collective-permute-start | bytes 516104 | tf_op jit(solution)/shard_map/ppermute | solution.py:419
  45.4 10.2 %collective-permute-start.7 = (bf16[63,8,128]{2,1,0:T(8,128)(2,1)S(1)}, bf16[63,8,128]{2,1,0:T(8,128)(2,1)S(1)}, u32[]{:S(2)}, u32[]{:S(2)}) collective-permute-start(bf16[63,8,128]{2,1,0:T(8,128)(2,1)S(1)} %shard_map.98), channel_id=1, source_target_pairs={{16,32},{48,64},{80,96},{112,128},{144,160},{176,192},{208,224},{2... | collective-permute-start | bytes 387080 | tf_op jit(solution)/shard_map/ppermute | solution.py:425
  55.6 16.2 %collective-permute-start.9 = (bf16[48,8,128]{2,1,0:T(8,128)(2,1)}, bf16[48,8,128]{2,1,0:T(8,128)(2,1)S(1)}, u32[]{:S(2)}, u32[]{:S(2)}) collective-permute-start(bf16[48,8,128]{2,1,0:T(8,128)(2,1)} %get-tuple-element.56), channel_id=1, source_target_pairs={{16,32},{48,64},{80,96},{112,128},{144,160},{176,192},{208,224},{2... | collective-permute-start | bytes 294920 | tf_op jit(solution)/shard_map/ppermute | solution.py:425
  63.4 3.4 %collective-permute-start.8 = (bf16[36,8,128]{2,1,0:T(8,128)(2,1)}, bf16[36,8,128]{2,1,0:T(8,128)(2,1)S(1)}, u32[]{:S(2)}, u32[]{:S(2)}) collective-permute-start(bf16[36,8,128]{2,1,0:T(8,128)(2,1)} %slice.3), channel_id=1, source_target_pairs={{0,16},{16,0},{32,48},{48,32},{64,80},{80,64},{96,112},{112,96},{1... | collective-permute-start | bytes 221192 | tf_op jit(solution)/shard_map/ppermute | solution.py:419
  78.0 3.1 %collective-permute-start.10 = (f32[32,256]{1,0:T(8,128)S(1)}, f32[32,256]{1,0:T(8,128)S(1)}, u32[]{:S(2)}, u32[]{:S(2)}) collective-permute-start(f32[32,256]{1,0:T(8,128)S(1)} %dynamic-slice_bitcast_fusion), channel_id=1, source_target_pairs={{0,16},{16,0},{32,48},{48,32},{64,80},{80,64},{96,112},{112,96},{1... | collective-permute-start | bytes 98312 | tf_op jit(solution)/shard_map/ppermute | solution.py:419
  135.9 8.4 %collective-permute-start.11 = (f32[32,256]{1,0:T(8,128)S(1)}, f32[32,256]{1,0:T(8,128)S(1)}, u32[]{:S(2)}, u32[]{:S(2)}) collective-permute-start(f32[32,256]{1,0:T(8,128)S(1)} %reduce_sum.39), channel_id=1, source_target_pairs={{0,16},{16,0},{32,48},{48,32},{64,80},{80,64},{96,112},{112,96},{1... | collective-permute-start | bytes 98312 | tf_op jit(solution)/shard_map/ppermute | solution.py:419

commit v7 on v6

--- a/solution.py
+++ b/solution.py
@@ -134,7 +134,7 @@
             hx_ref[z, y : y + 2, 2] = up.astype(bf16)
         return carry
 
-    lax.fori_loop(0, BZ + 2, first, 0)
+    lax.fori_loop(0, BZ + 2, first, 0, unroll=2)
     sw = sw_ref[...]
 
     def second(z, carry):
@@ -149,7 +149,7 @@
         own_ref[0, z] = jnp.tanh(jnp.concatenate(rows, axis=0))
         return carry
 
-    lax.fori_loop(0, BZ, second, 0)
+    lax.fori_loop(0, BZ, second, 0, unroll=2)
 
     for k in range(BZ):
         p_ref[3 + k] = sy_ref[k]
@@ -339,7 +339,7 @@
             ex_ref[z, y : y + 2, 2] = up.astype(bf16)
         return carry
 
-    lax.fori_loop(0, BZ + 2, hidden, 0)
+    lax.fori_loop(0, BZ + 2, hidden, 0, unroll=2)
 
     def features(z, carry):
         rows = []
@@ -350,7 +350,7 @@
         df_ref[:, z] = jnp.transpose(plane, (1, 0, 2)).astype(bf16)
         return carry
 
-    lax.fori_loop(0, BZ, features, 0)
+    lax.fori_loop(0, BZ, features, 0, unroll=2)
 
     nt = (((1,), (1,)), ((), ()))
 
@@ -370,9 +370,11 @@
     g1, g2, gs = lax.fori_loop(0, BZ, weights, (zero, zero, jnp.zeros((C, X), f32)))
     grad_ref[...] = jnp.zeros_like(grad_ref)
     for i, g in enumerate((g1, g2)):
-        grad_ref[i, :C] = g[:, :256]
-        grad_ref[i, C:, : TAPS - 256] = g[:, 256:]
-    grad_ref[0, C : C + 1, TAPS - 256 : TAPS - 240] = jnp.sum(jnp.transpose(gs), axis=0, keepdims=True)
+        for k in range(3):
+            grad_ref[i, C * k : C * k + C] = g[:, X * k : X * k + X]
+        grad_ref[i, 48:, :48] = g[:8, 3 * X :]
+        grad_ref[i, 48:, 64:112] = g[8:, 3 * X :]
+    grad_ref[0, 48:49, 48:64] = jnp.sum(jnp.transpose(gs), axis=0, keepdims=True)
 
 
 def finish(a_ref, b_ref, first_ref, second_ref, speed_ref):
@@ -381,11 +383,15 @@
     count = 54.0 * C * C + C
     factor = 1.0 / jnp.maximum(jnp.sqrt(jnp.full((1, 1), total)) / jnp.sqrt(f32(count)), 1.0)
     a, b = a * factor, b * factor
-    for t in range(27):
-        row, lane = C * (t // 16), C * (t % 16)
-        first_ref[t] = a[row : row + C, lane : lane + C]
-        second_ref[t] = b[row : row + C, lane : lane + C]
-    speed_ref[...] = a[C : C + 1, TAPS - 256 : TAPS - 240]
+    for out, g in ((first_ref, a), (second_ref, b)):
+        for t in range(27):
+            row, lane = C * (t // 8), C * (t % 8)
+            if t < 24:
+                out[t] = g[row : row + C, lane : lane + C]
+            else:
+                out[t, :8] = g[48:, lane : lane + C]
+                out[t, 8:] = g[48:, 64 + lane : 64 + lane + C]
+    speed_ref[...] = a[48:49, 48:64]
 
 
 def call(kernel, outs, scratch=(), flops=0):
@@ -439,8 +445,10 @@
     for axis, unit in (("gy", 1), ("gy", 4), ("gz", 8), ("gz", 2)):
         sets = groups(lax.axis_size(axis), unit)
         if len(sets[0]) > 1:
-            copies = jnp.broadcast_to(part[None], (len(sets[0]),) + part.shape)
-            part = jnp.sum(lax.all_to_all(copies, axis, 0, 0, axis_index_groups=sets), axis=0)
+            sent = part.astype(bf16) if unit == 2 else part
+            copies = jnp.broadcast_to(sent[None], (len(sets[0]),) + part.shape)
+            got = lax.all_to_all(copies, axis, 0, 0, axis_index_groups=sets)
+            part = jnp.sum(got.astype(f32), axis=0)
     other = even(part, "gz")
     return jnp.where(core == 0, part, other), jnp.where(core == 0, other, part)
 
@@ -492,7 +500,7 @@
     hb = odd(call(relay, shape((63, 8, X), SENT))(at, fa, ha), "gz")
     hb, fs = lax.optimization_barrier((hb, fs))
     hs = odd(fs, "gz")
-    hc = even(hb[:36], "gz")
+    hc = even(hb, "gz")
 
     plane = (24, 24, X)
     dpre = call(
@@ -514,7 +522,7 @@
 
     d_features, grad = call(
         backward,
-        [shape((C, BZ, BY, X)), shape((2, 2 * C, 256), f32)],
+        [shape((C, BZ, BY, X)), shape((2, 56, X), f32)],
         [pltpu.VMEM((8, 12, 3, C, X), bf16), pltpu.VMEM((6, 10, 3, C, X), bf16)],
     )(at, dpre, slope2, s2y, ha, hs, sw, hx, fx, slope1, top, w1b, w2b)
 

time: 146 us -> 144 us (0.986)
  Pallas kernels: 19.6 us -> 17.6 us
  waiting for transfers between devices: 14.7 us -> 12.8 us
    pallas_call x9, Pallas kernels: 19.6 us -> 17.6 us  [run(): pl.pallas_call(kernel, out_shape=outs, in_specs=specs, out_specs=[vmem] *...]
    unnamed x12 -> x20, local copies, waits for them, and re-layouts: 2.16 us -> 3.43 us
  transfers between devices with their start and end apart: 12 -> 12, of which waited for: 8 -> 7; matrix products, arithmetic and copies ran while one was open for 0% -> 0% of each run, Pallas kernels for 4% -> 4%
where the time goes in v7:
time: 144 us; the launch traced here: 143 us
  blocking collectives  54.6 us (38%)
  starting transfers between devices  53.5 us (37%)
  Pallas kernels  17.6 us (12%)
  waiting for transfers between devices  12.8 us (9%)
  local copies, waits for them, and re-layouts  3.47 us (2%)
    all_to_all x4, blocking collectives, total_of(): got = lax.all_to_all(copies, axis, 0, 0, axis_index_groups=sets)  54.6 us
    ppermute x7, starting transfers between devices, even(): return lax.ppermute(value, axis, [(i, i ^ 1) for i in range(n)])  33.7 us
    ppermute x5, starting transfers between devices, odd(): return lax.ppermute(value, axis, pairs + [(j, i) for i, j in pairs])  19.8 us
    pallas_call x9, Pallas kernels, run(): pl.pallas_call(kernel, out_shape=outs, in_specs=specs, out_specs=[vmem] *...  17.6 us
    ppermute x5, waiting for transfers between devices, odd(): return lax.ppermute(value, axis, pairs + [(j, i) for i, j in pairs])  7.9 us
    ppermute x7, waiting for transfers between devices, even(): return lax.ppermute(value, axis, [(i, i ^ 1) for i in range(n)])  4.91 us
    unnamed x20, local copies, waits for them, and re-layouts  3.43 us
  transfers between devices with their start and end apart: 12, of which 7 were waited for; matrix products, arithmetic and copies ran while one was open for 0% of the time, Pallas kernels for 4%

profile of v7, /device:TPU:1, one launch (start us, length us, event | category | flops | bytes accessed | tf_op | source)
XLA Modules:
  0.0 143.1 jit_solution(633898214037735924)
XLA Ops:
  0.6 0.0 copy-start.3
  0.7 0.1 pad_add_fusion.at.refs_0_
  0.7 0.6 copy-done.3
  1.4 0.9 copy-done
  2.3 0.6 shard_map.93
  2.9 3.9 %collective-permute-start = (bf16[9,16,128]{2,1,0:T(8,128)(2,1)S(1)}, bf16[9,16,128]{2,1,0:T(8,128)(2,1)S(1)}, u32[]{:S(2)}, u32[]{:S(2)}) collective-permute-start(bf16[9,16,128]{2,1,0:T(8,128)(2,1)S(1)} %get-tuple-element.37), channel_id=1, source_target_pairs={{0,1},{1,0},{2,3},{3,2},{4,5},{5,4},{6,7},{7,6},{8,9},{9,8},{10,11... | collective-permute-start | bytes 110600 | tf_op jit(solution)/shard_map/ppermute | solution.py:425
  6.8 0.7 collective-permute-start.1
  7.5 0.7 collective-permute-done.re_ref
  8.2 0.0 collective-permute-done.1.ro_ref
  8.2 0.6 shard_map.94
  8.7 9.3 %collective-permute-start.2 = (bf16[27,16,128]{2,1,0:T(8,128)(2,1)S(1)}, bf16[27,16,128]{2,1,0:T(8,128)(2,1)S(1)}, u32[]{:S(2)}, u32[]{:S(2)}) collective-permute-start(bf16[27,16,128]{2,1,0:T(8,128)(2,1)S(1)} %get-tuple-element.41), channel_id=1, source_target_pairs={{0,16},{16,0},{32,48},{48,32},{64,80},{80,64},{96,112},{112,96},{1... | collective-permute-start | bytes 331784 | tf_op jit(solution)/shard_map/ppermute | solution.py:425
  18.1 3.4 %collective-permute-start.3 = (bf16[27,16,128]{2,1,0:T(8,128)(2,1)S(1)}, bf16[27,16,128]{2,1,0:T(8,128)(2,1)S(1)}, u32[]{:S(2)}, u32[]{:S(2)}) collective-permute-start(bf16[27,16,128]{2,1,0:T(8,128)(2,1)S(1)} %get-tuple-element.42), channel_id=1, source_target_pairs={{16,32},{48,64},{80,96},{112,128},{144,160},{176,192},{208,224},{2... | collective-permute-start | bytes 331784 | tf_op jit(solution)/shard_map/ppermute | solution.py:431
  21.5 0.0 copy-start.9
  21.5 0.0 copy-done.8
  21.5 0.6 copy-done.9
  22.1 0.4 shard_map.95
  22.5 0.0 copy-start.4
  22.5 0.6 copy-done.4
  23.2 0.0 collective-permute-done.2.refs_3_
  23.2 4.9 %collective-permute-done.3.refs_4_ = bf16[27,16,128]{2,1,0:T(8,128)(2,1)S(1)} collective-permute-done((bf16[27,16,128]{2,1,0:T(8,128)(2,1)S(1)}, bf16[27,16,128]{2,1,0:T(8,128)(2,1)S(1)}, u32[]{:S(2)}, u32[]{:S(2)}) %collective-permute-start.3) | collective-permute-done | bytes 110624 | tf_op jit(solution)/shard_map/ppermute | solution.py:431
  28.1 3.0 %shard_map.96 = (bf16[6,10,3,16,128]{4,3,2,1,0:T(8,128)(2,1)S(1)}, bf16[6,10,3,16,128]{4,3,2,1,0:T(8,128)(2,1)S(1)}, f32[6,10,16,128]{3,2,1,0:T(8,128)S(1)}, f32...) custom-call(s32[4]{0:T(128)S(1)} %pad_add_fusion.at.refs_0_, ...), custom_call_target="tpu_custom_call" | custom-call | bytes 548880 | tf_op jit(solution)/shard_map/pallas_call | solution.py:406
  31.0 6.8 %collective-permute-start.4 = (bf16[28,8,128]{2,1,0:T(8,128)(2,1)S(1)}, bf16[28,8,128]{2,1,0:T(8,128)(2,1)S(1)}, u32[]{:S(2)}, u32[]{:S(2)}) collective-permute-start(bf16[28,8,128]{2,1,0:T(8,128)(2,1)S(1)} %get-tuple-element.48.me_ref), channel_id=1, source_target_pairs={{0,1},{1,0},{2,3},{3,2},{4,5},{5,4},{6,7},{7,6},{8,9},{9,8},{10,11... | collective-permute-start | bytes 172040 | tf_op jit(solution)/shard_map/ppermute | solution.py:425
  37.8 0.7 collective-permute-start.5
  38.5 0.9 collective-permute-done.4.re_ref
  39.3 0.0 collective-permute-done.5.ro_ref
  39.4 1.2 shard_map.97
  40.6 1.9 %collective-permute-start.6 = (bf16[84,8,128]{2,1,0:T(8,128)(2,1)S(1)}, bf16[84,8,128]{2,1,0:T(8,128)(2,1)S(1)}, u32[]{:S(2)}, u32[]{:S(2)}) collective-permute-start(bf16[84,8,128]{2,1,0:T(8,128)(2,1)S(1)} %get-tuple-element.51.ma_ref.refs_2_), channel_id=1, source_target_pairs={{0,16},{16,0},{32,48},{48,32},{64,80},{80,64},{96,112},{112,96},{1... | collective-permute-start | bytes 516104 | tf_op jit(solution)/shard_map/ppermute | solution.py:425
  42.5 1.4 collective-permute-done.6.ra_ref.refs_3_
  43.9 0.6 shard_map.98
  44.4 7.2 %collective-permute-start.7 = (bf16[63,8,128]{2,1,0:T(8,128)(2,1)S(1)}, bf16[63,8,128]{2,1,0:T(8,128)(2,1)S(1)}, u32[]{:S(2)}, u32[]{:S(2)}) collective-permute-start(bf16[63,8,128]{2,1,0:T(8,128)(2,1)S(1)} %shard_map.98), channel_id=1, source_target_pairs={{16,32},{48,64},{80,96},{112,128},{144,160},{176,192},{208,224},{2... | collective-permute-start | bytes 387080 | tf_op jit(solution)/shard_map/ppermute | solution.py:431
  51.6 3.0 %collective-permute-done.7.refs_4_ = bf16[63,8,128]{2,1,0:T(8,128)(2,1)S(1)} collective-permute-done((bf16[63,8,128]{2,1,0:T(8,128)(2,1)S(1)}, bf16[63,8,128]{2,1,0:T(8,128)(2,1)S(1)}, u32[]{:S(2)}, u32[]{:S(2)}) %collective-permute-start.7) | collective-permute-done | bytes 129056 | tf_op jit(solution)/shard_map/ppermute | solution.py:431
  54.6 1.9 %collective-permute-start.8 = (bf16[63,8,128]{2,1,0:T(8,128)(2,1)S(1)}, bf16[63,8,128]{2,1,0:T(8,128)(2,1)S(1)}, u32[]{:S(2)}, u32[]{:S(2)}) collective-permute-start(bf16[63,8,128]{2,1,0:T(8,128)(2,1)S(1)} %collective-permute-done.7.refs_4_), channel_id=1, source_target_pairs={{0,16},{16,0},{32,48},{48,32},{64,80},{80,64},{96,112},{112,96},{1... | collective-permute-start | bytes 387080 | tf_op jit(solution)/shard_map/ppermute | solution.py:425
  56.5 7.9 %collective-permute-start.9 = (bf16[48,8,128]{2,1,0:T(8,128)(2,1)}, bf16[48,8,128]{2,1,0:T(8,128)(2,1)S(1)}, u32[]{:S(2)}, u32[]{:S(2)}) collective-permute-start(bf16[48,8,128]{2,1,0:T(8,128)(2,1)} %get-tuple-element.56), channel_id=1, source_target_pairs={{16,32},{48,64},{80,96},{112,128},{144,160},{176,192},{208,224},{2... | collective-permute-start | bytes 294920 | tf_op jit(solution)/shard_map/ppermute | solution.py:431
  64.5 0.0 collective-permute-done.8.refs_5_
  64.5 0.0 copy-start.7
  64.5 0.6 copy-done.7
  65.2 5.0 %shard_map.99.dpre_ref = f32[8,16,128]{2,1,0:T(8,128)S(1)} custom-call(s32[4]{0:T(128)S(1)} %copy-done.7, f32[3,4,8,128]{3,2,1,0:T(8,128)S(1)} %get-tuple-element.47.refs_1_, bf16[84,8,128]{2,1,0:T(8,128)(2,1)S(1)} %get-tuple-element.51.ma_ref.refs_2_, bf16[84,8,128]{2,1,0:T(8,128)(2,1)S(1)} %collective-permute-done.6.ra_ref.refs_3_, ...), custom_call_target="tpu_custom_call" | custom-call | bytes 716816 | tf_op jit(solution)/shard_map/pallas_call | solution.py:406
  70.2 0.0 collective-permute-done.9.rb_ref
  70.2 5.2 %shard_map.100 = (bf16[16,4,8,128]{3,2,1,0:T(8,128)(2,1)}, f32[2,56,128]{2,1,0:T(8,128)S(1)}) custom-call(s32[4]{0:T(128)S(1)} %copy-done.7, f32[8,16,128]{2,1,0:T(8,128)S(1)} %shard_map.99.dpre_ref, f32[4,8,16,128]{3,2,1,0:T(8,128)S(1)} %get-tuple-element.49.slope2_ref, bf16[4,12,16,128]{3,2,1,0:T(8,128)(2,1)S(1)} %get-tuple-element.55.s2y_ref, ...), custom_call_target="tpu_custom_call" | custom-call | bytes 3104784 | tf_op jit(solution)/shard_map/pallas_call | solution.py:406
  75.4 1.9 %collective-permute-start.10 = (f32[56,128]{1,0:T(8,128)S(1)}, f32[56,128]{1,0:T(8,128)S(1)}, u32[]{:S(2)}, u32[]{:S(2)}) collective-permute-start(f32[56,128]{1,0:T(8,128)S(1)} %dynamic-slice_bitcast_fusion), channel_id=1, source_target_pairs={{0,16},{16,0},{32,48},{48,32},{64,80},{80,64},{96,112},{112,96},{1... | collective-permute-start | bytes 86024 | tf_op jit(solution)/shard_map/ppermute | solution.py:425
  77.3 1.2 collective-permute-done.10
  78.5 17.7 %all_to_all.20 = f32[4,56,128]{2,1,0:T(8,128)S(1)} all-to-all(f32[4,56,128]{2,1,0:T(8,128)S(1)} %broadcast_in_dim.8), channel_id=1, replica_groups={{0,1,2,3},{4,5,6,7},{8,9,10,11},{12,13,14,15},{16,17,18,19},{20,21,22,2..., dimensions={0} | all-to-all | bytes 229376 | tf_op jit(solution)/shard_map/all_to_all | solution.py:450
  96.3 7.1 %all_to_all.21 = f32[4,56,128]{2,1,0:T(8,128)S(1)} all-to-all(f32[4,56,128]{2,1,0:T(8,128)S(1)} %broadcast_in_dim.9), channel_id=1, replica_groups={{0,4,8,12},{1,5,9,13},{2,6,10,14},{3,7,11,15},{16,20,24,28},{17,21,25,2..., dimensions={0} | all-to-all | bytes 229376 | tf_op jit(solution)/shard_map/all_to_all | solution.py:450
  103.4 11.2 %all_to_all.22 = f32[4,56,128]{2,1,0:T(8,128)S(1)} all-to-all(f32[4,56,128]{2,1,0:T(8,128)S(1)} %broadcast_in_dim.10), channel_id=1, replica_groups={{0,128,256,384},{16,144,272,400},{32,160,288,416},{48,176,304,432},{64,..., dimensions={0} | all-to-all | bytes 229376 | tf_op jit(solution)/shard_map/all_to_all | solution.py:450
  114.6 18.6 %all_to_all.23 = bf16[4,56,128]{2,1,0:T(8,128)(2,1)S(1)} all-to-all(bf16[4,56,128]{2,1,0:T(8,128)(2,1)S(1)} %broadcast_in_dim.11), channel_id=1, replica_groups={{0,32,64,96},{16,48,80,112},{128,160,192,224},{144,176,208,240},{256,28..., dimensions={0} | all-to-all | bytes 114688 | tf_op jit(solution)/shard_map/all_to_all | solution.py:450
  133.3 8.0 %collective-permute-start.11 = (f32[56,128]{1,0:T(8,128)S(1)}, f32[56,128]{1,0:T(8,128)S(1)}, u32[]{:S(2)}, u32[]{:S(2)}) collective-permute-start(f32[56,128]{1,0:T(8,128)S(1)} %convert_reduce_fusion), channel_id=1, source_target_pairs={{0,16},{16,0},{32,48},{48,32},{64,80},{80,64},{96,112},{112,96},{1... | collective-permute-start | bytes 86024 | tf_op jit(solution)/shard_map/ppermute | solution.py:425
  141.2 0.8 collective-permute-done.11
  142.1 1.0 shard_map.101
  (21 shorter events, 0.1 us)
Async XLA Ops:
  0.6 0.7 copy-start.3
  1.4 0.9 copy-start
  2.3 41.6 %copy-start.6 = (s32[4]{0:T(128)}, s32[4]{0:T(128)S(1)}, u32[]{:S(2)}) copy-start(s32[4]{0:T(128)S(1)} %pad_add_fusion.at.refs_0_) | copy-start | bytes 52
  2.3 19.2 %copy-start.8 = (s32[4,8,128]{2,1,0:T(8,128)S(1)}, s32[4,8,128]{2,1,0:T(8,128)}, u32[]{:S(2)}) copy-start(s32[4,8,128]{2,1,0:T(8,128)} %lab_ref.1) | copy-start | bytes 49156
  2.9 5.3 %collective-permute-start = (bf16[9,16,128]{2,1,0:T(8,128)(2,1)S(1)}, bf16[9,16,128]{2,1,0:T(8,128)(2,1)S(1)}, u32[]{:S(2)}, u32[]{:S(2)}) collective-permute-start(bf16[9,16,128]{2,1,0:T(8,128)(2,1)S(1)} %get-tuple-element.37), channel_id=1, source_target_pairs={{0,1},{1,0},{2,3},{3,2},{4,5},{5,4},{6,7},{7,6},{8,9},{9,8},{10,11... | collective-permute-start | bytes 110600 | tf_op jit(solution)/shard_map/ppermute | solution.py:425
  6.8 1.3 collective-permute-start.1
  8.2 13.3 %copy-start.1 = (bf16[16,16,3,3,3]{1,0,4,3,2:T(8,128)(2,1)S(1)}, bf16[16,16,3,3,3]{1,0,4,3,2:T(8,128)(2,1)}, u32[]{:S(2)}) copy-start(bf16[16,16,3,3,3]{1,0,4,3,2:T(8,128)(2,1)} %param.9) | copy-start | bytes 41476
  8.2 13.3 %copy-start.2 = (bf16[16,16,3,3,3]{1,0,4,3,2:T(8,128)(2,1)S(1)}, bf16[16,16,3,3,3]{1,0,4,3,2:T(8,128)(2,1)}, u32[]{:S(2)}) copy-start(bf16[16,16,3,3,3]{1,0,4,3,2:T(8,128)(2,1)} %param.10) | copy-start | bytes 41476
  8.7 14.4 %collective-permute-start.2 = (bf16[27,16,128]{2,1,0:T(8,128)(2,1)S(1)}, bf16[27,16,128]{2,1,0:T(8,128)(2,1)S(1)}, u32[]{:S(2)}, u32[]{:S(2)}) collective-permute-start(bf16[27,16,128]{2,1,0:T(8,128)(2,1)S(1)} %get-tuple-element.41), channel_id=1, source_target_pairs={{0,16},{16,0},{32,48},{48,32},{64,80},{80,64},{96,112},{112,96},{1... | collective-permute-start | bytes 331784 | tf_op jit(solution)/shard_map/ppermute | solution.py:425
  18.1 10.0 %collective-permute-start.3 = (bf16[27,16,128]{2,1,0:T(8,128)(2,1)S(1)}, bf16[27,16,128]{2,1,0:T(8,128)(2,1)S(1)}, u32[]{:S(2)}, u32[]{:S(2)}) collective-permute-start(bf16[27,16,128]{2,1,0:T(8,128)(2,1)S(1)} %get-tuple-element.42), channel_id=1, source_target_pairs={{16,32},{48,64},{80,96},{112,128},{144,160},{176,192},{208,224},{2... | collective-permute-start | bytes 331784 | tf_op jit(solution)/shard_map/ppermute | solution.py:431
  21.5 0.7 copy-start.9
  22.5 0.6 copy-start.4
  31.0 8.3 %collective-permute-start.4 = (bf16[28,8,128]{2,1,0:T(8,128)(2,1)S(1)}, bf16[28,8,128]{2,1,0:T(8,128)(2,1)S(1)}, u32[]{:S(2)}, u32[]{:S(2)}) collective-permute-start(bf16[28,8,128]{2,1,0:T(8,128)(2,1)S(1)} %get-tuple-element.48.me_ref), channel_id=1, source_target_pairs={{0,1},{1,0},{2,3},{3,2},{4,5},{5,4},{6,7},{7,6},{8,9},{9,8},{10,11... | collective-permute-start | bytes 172040 | tf_op jit(solution)/shard_map/ppermute | solution.py:425
  37.8 1.6 %collective-permute-start.5 = (bf16[28,8,128]{2,1,0:T(8,128)(2,1)S(1)}, bf16[28,8,128]{2,1,0:T(8,128)(2,1)S(1)}, u32[]{:S(2)}, u32[]{:S(2)}) collective-permute-start(bf16[28,8,128]{2,1,0:T(8,128)(2,1)S(1)} %get-tuple-element.50), channel_id=1, source_target_pairs={{1,2},{3,4},{5,6},{7,8},{9,10},{11,12},{13,14},{2,1},{4,3},{6,5},{... | collective-permute-start | bytes 172040 | tf_op jit(solution)/shard_map/ppermute | solution.py:431
  40.6 3.3 %collective-permute-start.6 = (bf16[84,8,128]{2,1,0:T(8,128)(2,1)S(1)}, bf16[84,8,128]{2,1,0:T(8,128)(2,1)S(1)}, u32[]{:S(2)}, u32[]{:S(2)}) collective-permute-start(bf16[84,8,128]{2,1,0:T(8,128)(2,1)S(1)} %get-tuple-element.51.ma_ref.refs_2_), channel_id=1, source_target_pairs={{0,16},{16,0},{32,48},{48,32},{64,80},{80,64},{96,112},{112,96},{1... | collective-permute-start | bytes 516104 | tf_op jit(solution)/shard_map/ppermute | solution.py:425
  44.4 10.2 %collective-permute-start.7 = (bf16[63,8,128]{2,1,0:T(8,128)(2,1)S(1)}, bf16[63,8,128]{2,1,0:T(8,128)(2,1)S(1)}, u32[]{:S(2)}, u32[]{:S(2)}) collective-permute-start(bf16[63,8,128]{2,1,0:T(8,128)(2,1)S(1)} %shard_map.98), channel_id=1, source_target_pairs={{16,32},{48,64},{80,96},{112,128},{144,160},{176,192},{208,224},{2... | collective-permute-start | bytes 387080 | tf_op jit(solution)/shard_map/ppermute | solution.py:431
  54.6 9.9 %collective-permute-start.8 = (bf16[63,8,128]{2,1,0:T(8,128)(2,1)S(1)}, bf16[63,8,128]{2,1,0:T(8,128)(2,1)S(1)}, u32[]{:S(2)}, u32[]{:S(2)}) collective-permute-start(bf16[63,8,128]{2,1,0:T(8,128)(2,1)S(1)} %collective-permute-done.7.refs_4_), channel_id=1, source_target_pairs={{0,16},{16,0},{32,48},{48,32},{64,80},{80,64},{96,112},{112,96},{1... | collective-permute-start | bytes 387080 | tf_op jit(solution)/shard_map/ppermute | solution.py:425
  56.5 13.7 %collective-permute-start.9 = (bf16[48,8,128]{2,1,0:T(8,128)(2,1)}, bf16[48,8,128]{2,1,0:T(8,128)(2,1)S(1)}, u32[]{:S(2)}, u32[]{:S(2)}) collective-permute-start(bf16[48,8,128]{2,1,0:T(8,128)(2,1)} %get-tuple-element.56), channel_id=1, source_target_pairs={{16,32},{48,64},{80,96},{112,128},{144,160},{176,192},{208,224},{2... | collective-permute-start | bytes 294920 | tf_op jit(solution)/shard_map/ppermute | solution.py:431
  64.5 0.7 copy-start.7
  65.2 5.0 %copy-start.5 = (bf16[32,576]{1,0:T(8,128)(2,1)S(1)}, bf16[32,576]{1,0:T(8,128)(2,1)}, u32[]{:S(2)}) copy-start(bf16[32,576]{1,0:T(8,128)(2,1)} %copy-done.4) | copy-start | bytes 110596
  75.4 3.1 %collective-permute-start.10 = (f32[56,128]{1,0:T(8,128)S(1)}, f32[56,128]{1,0:T(8,128)S(1)}, u32[]{:S(2)}, u32[]{:S(2)}) collective-permute-start(f32[56,128]{1,0:T(8,128)S(1)} %dynamic-slice_bitcast_fusion), channel_id=1, source_target_pairs={{0,16},{16,0},{32,48},{48,32},{64,80},{80,64},{96,112},{112,96},{1... | collective-permute-start | bytes 86024 | tf_op jit(solution)/shard_map/ppermute | solution.py:425
  133.3 8.8 %collective-permute-start.11 = (f32[56,128]{1,0:T(8,128)S(1)}, f32[56,128]{1,0:T(8,128)S(1)}, u32[]{:S(2)}, u32[]{:S(2)}) collective-permute-start(f32[56,128]{1,0:T(8,128)S(1)} %convert_reduce_fusion), channel_id=1, source_target_pairs={{0,16},{16,0},{32,48},{48,32},{64,80},{80,64},{96,112},{112,96},{1... | collective-permute-start | bytes 86024 | tf_op jit(solution)/shard_map/ppermute | solution.py:425

commit v8 on v7

--- a/solution.py
+++ b/solution.py
@@ -4,7 +4,6 @@
 from jax.experimental import pallas as pl
 from jax.experimental.pallas import tpu as pltpu
 from jax.sharding import PartitionSpec as P
-
 
 C = 16
 BZ = 4
@@ -206,7 +205,7 @@
 
 def march(nz, ny, at, own_ref, ye_ref, mate_ref, far_ref, far2_ref, g0_ref, dpre_ref,
           sp, lab, ph, w_s, dz_s, dy_s, dx_s, ag_s, ds, dd):
-    iz, iy, pz = at[0], at[1], at[2]
+    iz, iy, pz, py = at[0], at[1], at[2], at[3]
     base = 4 * pz
 
     def place(start, block):
@@ -250,12 +249,13 @@
             ly, uy = pltpu.roll(centre, 1, 0), pltpu.roll(centre, 23, 0)
             lx, ux = sides(centre)
             dz, dy, dx = (uz - lz) * 0.5, (uy - ly) * 0.5, (ux - lx) * 0.5
-            g = jnp.sqrt(dz * dz + dy * dy + dx * dx + FLOOR)
+            square = dz * dz + dy * dy + dx * dx + FLOOR
+            root = lax.rsqrt(square)
             lap = uz + lz + uy + ly + ux + lx - 6.0 * centre
             speed = sp[z]
-            ag = A * g
+            ag = A * square * root
             new = jnp.where(within(z), centre + speed * ag + (A * 0.5) * lap, 0.0)
-            w_s[t - 1, z] = (A * 0.5) * speed / g
+            w_s[t - 1, z] = (A * 0.5) * speed * root
             dz_s[t - 1, z] = dz
             dy_s[t - 1, z] = dy
             dx_s[t - 1, z] = dx
@@ -303,7 +303,7 @@
     pz = at[2]
     sw = sw_ref[...]
 
-    def second(z, slope):
+    def second(z, k, slope):
         for y in range(BY + 4):
             d = dpre_ref[z, 2 + y : 3 + y, :]
             value = (sw * d * slope(y))[None]
@@ -317,14 +317,12 @@
             if 2 <= y < 2 + BY:
                 return slope2_ref[k, y - 2]
             return s2y_ref[k, y].astype(f32)
-
-        second(2 + k, own)
+        second(2 + k, k, own)
     for k in range(2):
         for ref, first, z in ((ra_ref, 36, 6 - 6 * pz), (rb_ref, 0, 6 * pz)):
             def far(y, ref=ref, first=first + 24 * k):
                 return ref[first + 2 * y : first + 2 * y + 2].astype(f32).reshape(C, X)
-
-            second(z + k, far)
+            second(z + k, k, far)
 
     w2 = w2_ref[...]
     w1 = w1_ref[...]
@@ -445,10 +443,8 @@
     for axis, unit in (("gy", 1), ("gy", 4), ("gz", 8), ("gz", 2)):
         sets = groups(lax.axis_size(axis), unit)
         if len(sets[0]) > 1:
-            sent = part.astype(bf16) if unit == 2 else part
-            copies = jnp.broadcast_to(sent[None], (len(sets[0]),) + part.shape)
-            got = lax.all_to_all(copies, axis, 0, 0, axis_index_groups=sets)
-            part = jnp.sum(got.astype(f32), axis=0)
+            copies = jnp.broadcast_to(part[None], (len(sets[0]),) + part.shape)
+            part = jnp.sum(lax.all_to_all(copies, axis, 0, 0, axis_index_groups=sets), axis=0)
     other = even(part, "gz")
     return jnp.where(core == 0, part, other), jnp.where(core == 0, other, part)
 
@@ -499,8 +495,8 @@
     ha = even(fa, "gz")
     hb = odd(call(relay, shape((63, 8, X), SENT))(at, fa, ha), "gz")
     hb, fs = lax.optimization_barrier((hb, fs))
+    hc = even(hb, "gz")
     hs = odd(fs, "gz")
-    hc = even(hb, "gz")
 
     plane = (24, 24, X)
     dpre = call(
@@ -538,7 +534,6 @@
 def solution(mesh):
     in_specs = (P(None, "gz", "gy", None), P("gz", "gy", None), P("gz", "gy", None), P(), P(), P())
     out_specs = (P(None, "gz", "gy", None), P(), P(), P())
-
     return jax.shard_map(
         on_device, mesh=mesh, in_specs=in_specs, out_specs=out_specs, check_vma=False
     )

time: 144 us -> 144 us (level)
  no operation moved by 1% of the time
where the time goes in v8:
time: 144 us; the launch traced here: 143 us
  blocking collectives  55 us (38%)
  starting transfers between devices  53.4 us (37%)
  Pallas kernels  17.5 us (12%)
  waiting for transfers between devices  12.8 us (9%)
  local copies, waits for them, and re-layouts  3.47 us (2%)
    all_to_all x4, blocking collectives, total_of(): lax.all_to_all(copies, axis, 0, 0, axis_index_groups=sets)  55 us
    ppermute x7, starting transfers between devices, even(): return lax.ppermute(value, axis, [(i, i ^ 1) for i in range(n)])  33.6 us
    ppermute x5, starting transfers between devices, odd(): return lax.ppermute(value, axis, pairs + [(j, i) for i, j in pairs])  19.8 us
    pallas_call x9, Pallas kernels, run(): pl.pallas_call(kernel, out_shape=outs, in_specs=specs, out_specs=[vmem] *...  17.5 us
    ppermute x5, waiting for transfers between devices, odd(): return lax.ppermute(value, axis, pairs + [(j, i) for i, j in pairs])  7.9 us
    ppermute x7, waiting for transfers between devices, even(): return lax.ppermute(value, axis, [(i, i ^ 1) for i in range(n)])  4.91 us
    unnamed x20, local copies, waits for them, and re-layouts  3.43 us
  transfers between devices with their start and end apart: 12, of which 7 were waited for; matrix products, arithmetic and copies ran while one was open for 0% of the time, Pallas kernels for 4%

profile of v8, /device:TPU:1, one launch (start us, length us, event | category | flops | bytes accessed | tf_op | source)
XLA Modules:
  0.0 143.3 jit_solution(2669181141316851103)
XLA Ops:
  0.7 0.1 pad_add_fusion.at.refs_0_
  0.7 0.6 copy-done.3
  1.4 0.9 copy-done
  2.3 0.6 shard_map.93
  2.9 3.9 %collective-permute-start = (bf16[9,16,128]{2,1,0:T(8,128)(2,1)S(1)}, bf16[9,16,128]{2,1,0:T(8,128)(2,1)S(1)}, u32[]{:S(2)}, u32[]{:S(2)}) collective-permute-start(bf16[9,16,128]{2,1,0:T(8,128)(2,1)S(1)} %get-tuple-element.37), channel_id=1, source_target_pairs={{0,1},{1,0},{2,3},{3,2},{4,5},{5,4},{6,7},{7,6},{8,9},{9,8},{10,11... | collective-permute-start | bytes 110600 | tf_op jit(solution)/shard_map/ppermute | solution.py:423
  6.8 0.7 collective-permute-start.1
  7.5 0.7 collective-permute-done.re_ref
  8.2 0.0 collective-permute-done.1.ro_ref
  8.2 0.6 shard_map.94
  8.7 9.3 %collective-permute-start.2 = (bf16[27,16,128]{2,1,0:T(8,128)(2,1)S(1)}, bf16[27,16,128]{2,1,0:T(8,128)(2,1)S(1)}, u32[]{:S(2)}, u32[]{:S(2)}) collective-permute-start(bf16[27,16,128]{2,1,0:T(8,128)(2,1)S(1)} %get-tuple-element.41), channel_id=1, source_target_pairs={{0,16},{16,0},{32,48},{48,32},{64,80},{80,64},{96,112},{112,96},{1... | collective-permute-start | bytes 331784 | tf_op jit(solution)/shard_map/ppermute | solution.py:423
  18.1 3.4 %collective-permute-start.3 = (bf16[27,16,128]{2,1,0:T(8,128)(2,1)S(1)}, bf16[27,16,128]{2,1,0:T(8,128)(2,1)S(1)}, u32[]{:S(2)}, u32[]{:S(2)}) collective-permute-start(bf16[27,16,128]{2,1,0:T(8,128)(2,1)S(1)} %get-tuple-element.42), channel_id=1, source_target_pairs={{16,32},{48,64},{80,96},{112,128},{144,160},{176,192},{208,224},{2... | collective-permute-start | bytes 331784 | tf_op jit(solution)/shard_map/ppermute | solution.py:429
  21.5 0.0 copy-start.9
  21.5 0.0 copy-done.8
  21.5 0.0 copy-done.1
  21.5 0.6 copy-done.9
  22.1 0.4 shard_map.95
  22.5 0.0 copy-start.4
  22.5 0.6 copy-done.4
  23.2 0.0 collective-permute-done.2.refs_3_
  23.2 4.9 %collective-permute-done.3.refs_4_ = bf16[27,16,128]{2,1,0:T(8,128)(2,1)S(1)} collective-permute-done((bf16[27,16,128]{2,1,0:T(8,128)(2,1)S(1)}, bf16[27,16,128]{2,1,0:T(8,128)(2,1)S(1)}, u32[]{:S(2)}, u32[]{:S(2)}) %collective-permute-start.3) | collective-permute-done | bytes 110624 | tf_op jit(solution)/shard_map/ppermute | solution.py:429
  28.1 3.0 %shard_map.96 = (bf16[6,10,3,16,128]{4,3,2,1,0:T(8,128)(2,1)S(1)}, bf16[6,10,3,16,128]{4,3,2,1,0:T(8,128)(2,1)S(1)}, f32[6,10,16,128]{3,2,1,0:T(8,128)S(1)}, f32...) custom-call(s32[4]{0:T(128)S(1)} %pad_add_fusion.at.refs_0_, ...), custom_call_target="tpu_custom_call" | custom-call | bytes 548880 | tf_op jit(solution)/shard_map/pallas_call | solution.py:404
  31.0 6.8 %collective-permute-start.4 = (bf16[28,8,128]{2,1,0:T(8,128)(2,1)S(1)}, bf16[28,8,128]{2,1,0:T(8,128)(2,1)S(1)}, u32[]{:S(2)}, u32[]{:S(2)}) collective-permute-start(bf16[28,8,128]{2,1,0:T(8,128)(2,1)S(1)} %get-tuple-element.48.me_ref), channel_id=1, source_target_pairs={{0,1},{1,0},{2,3},{3,2},{4,5},{5,4},{6,7},{7,6},{8,9},{9,8},{10,11... | collective-permute-start | bytes 172040 | tf_op jit(solution)/shard_map/ppermute | solution.py:423
  37.8 0.7 collective-permute-start.5
  38.5 0.9 collective-permute-done.4.re_ref
  39.3 0.0 collective-permute-done.5.ro_ref
  39.4 1.2 shard_map.97
  40.6 1.9 %collective-permute-start.6 = (bf16[84,8,128]{2,1,0:T(8,128)(2,1)S(1)}, bf16[84,8,128]{2,1,0:T(8,128)(2,1)S(1)}, u32[]{:S(2)}, u32[]{:S(2)}) collective-permute-start(bf16[84,8,128]{2,1,0:T(8,128)(2,1)S(1)} %get-tuple-element.51.ma_ref.refs_2_), channel_id=1, source_target_pairs={{0,16},{16,0},{32,48},{48,32},{64,80},{80,64},{96,112},{112,96},{1... | collective-permute-start | bytes 516104 | tf_op jit(solution)/shard_map/ppermute | solution.py:423
  42.5 1.4 collective-permute-done.6.ra_ref.refs_3_
  43.9 0.6 shard_map.98
  44.4 7.2 %collective-permute-start.7 = (bf16[63,8,128]{2,1,0:T(8,128)(2,1)S(1)}, bf16[63,8,128]{2,1,0:T(8,128)(2,1)S(1)}, u32[]{:S(2)}, u32[]{:S(2)}) collective-permute-start(bf16[63,8,128]{2,1,0:T(8,128)(2,1)S(1)} %shard_map.98), channel_id=1, source_target_pairs={{16,32},{48,64},{80,96},{112,128},{144,160},{176,192},{208,224},{2... | collective-permute-start | bytes 387080 | tf_op jit(solution)/shard_map/ppermute | solution.py:429
  51.6 3.0 %collective-permute-done.7.refs_4_ = bf16[63,8,128]{2,1,0:T(8,128)(2,1)S(1)} collective-permute-done((bf16[63,8,128]{2,1,0:T(8,128)(2,1)S(1)}, bf16[63,8,128]{2,1,0:T(8,128)(2,1)S(1)}, u32[]{:S(2)}, u32[]{:S(2)}) %collective-permute-start.7) | collective-permute-done | bytes 129056 | tf_op jit(solution)/shard_map/ppermute | solution.py:429
  54.6 1.9 %collective-permute-start.8 = (bf16[63,8,128]{2,1,0:T(8,128)(2,1)S(1)}, bf16[63,8,128]{2,1,0:T(8,128)(2,1)S(1)}, u32[]{:S(2)}, u32[]{:S(2)}) collective-permute-start(bf16[63,8,128]{2,1,0:T(8,128)(2,1)S(1)} %collective-permute-done.7.refs_4_), channel_id=1, source_target_pairs={{0,16},{16,0},{32,48},{48,32},{64,80},{80,64},{96,112},{112,96},{1... | collective-permute-start | bytes 387080 | tf_op jit(solution)/shard_map/ppermute | solution.py:423
  56.5 7.9 %collective-permute-start.9 = (bf16[48,8,128]{2,1,0:T(8,128)(2,1)}, bf16[48,8,128]{2,1,0:T(8,128)(2,1)S(1)}, u32[]{:S(2)}, u32[]{:S(2)}) collective-permute-start(bf16[48,8,128]{2,1,0:T(8,128)(2,1)} %get-tuple-element.56), channel_id=1, source_target_pairs={{16,32},{48,64},{80,96},{112,128},{144,160},{176,192},{208,224},{2... | collective-permute-start | bytes 294920 | tf_op jit(solution)/shard_map/ppermute | solution.py:429
  64.5 0.0 collective-permute-done.8.refs_5_
  64.5 0.0 copy-start.7
  64.5 0.6 copy-done.7
  65.2 4.9 %shard_map.99.dpre_ref = f32[8,16,128]{2,1,0:T(8,128)S(1)} custom-call(s32[4]{0:T(128)S(1)} %copy-done.7, f32[3,4,8,128]{3,2,1,0:T(8,128)S(1)} %get-tuple-element.47.refs_1_, bf16[84,8,128]{2,1,0:T(8,128)(2,1)S(1)} %get-tuple-element.51.ma_ref.refs_2_, bf16[84,8,128]{2,1,0:T(8,128)(2,1)S(1)} %collective-permute-done.6.ra_ref.refs_3_, ...), custom_call_target="tpu_custom_call" | custom-call | bytes 716816 | tf_op jit(solution)/shard_map/pallas_call | solution.py:404
  70.1 0.0 collective-permute-done.9.rb_ref
  70.1 5.2 %shard_map.100 = (bf16[16,4,8,128]{3,2,1,0:T(8,128)(2,1)}, f32[2,56,128]{2,1,0:T(8,128)S(1)}) custom-call(s32[4]{0:T(128)S(1)} %copy-done.7, f32[8,16,128]{2,1,0:T(8,128)S(1)} %shard_map.99.dpre_ref, f32[4,8,16,128]{3,2,1,0:T(8,128)S(1)} %get-tuple-element.49.slope2_ref, bf16[4,12,16,128]{3,2,1,0:T(8,128)(2,1)S(1)} %get-tuple-element.55.s2y_ref, ...), custom_call_target="tpu_custom_call" | custom-call | bytes 3104784 | tf_op jit(solution)/shard_map/pallas_call | solution.py:404
  75.3 1.9 %collective-permute-start.10 = (f32[56,128]{1,0:T(8,128)S(1)}, f32[56,128]{1,0:T(8,128)S(1)}, u32[]{:S(2)}, u32[]{:S(2)}) collective-permute-start(f32[56,128]{1,0:T(8,128)S(1)} %dynamic-slice_bitcast_fusion), channel_id=1, source_target_pairs={{0,16},{16,0},{32,48},{48,32},{64,80},{80,64},{96,112},{112,96},{1... | collective-permute-start | bytes 86024 | tf_op jit(solution)/shard_map/ppermute | solution.py:423
  77.2 1.2 collective-permute-done.10
  78.4 17.7 %all_to_all.20 = f32[4,56,128]{2,1,0:T(8,128)S(1)} all-to-all(f32[4,56,128]{2,1,0:T(8,128)S(1)} %broadcast_in_dim.8), channel_id=1, replica_groups={{0,1,2,3},{4,5,6,7},{8,9,10,11},{12,13,14,15},{16,17,18,19},{20,21,22,2..., dimensions={0} | all-to-all | bytes 229376 | tf_op jit(solution)/shard_map/all_to_all | solution.py:447
  96.1 7.1 %all_to_all.21 = f32[4,56,128]{2,1,0:T(8,128)S(1)} all-to-all(f32[4,56,128]{2,1,0:T(8,128)S(1)} %broadcast_in_dim.9), channel_id=1, replica_groups={{0,4,8,12},{1,5,9,13},{2,6,10,14},{3,7,11,15},{16,20,24,28},{17,21,25,2..., dimensions={0} | all-to-all | bytes 229376 | tf_op jit(solution)/shard_map/all_to_all | solution.py:447
  103.3 11.2 %all_to_all.22 = f32[4,56,128]{2,1,0:T(8,128)S(1)} all-to-all(f32[4,56,128]{2,1,0:T(8,128)S(1)} %broadcast_in_dim.10), channel_id=1, replica_groups={{0,128,256,384},{16,144,272,400},{32,160,288,416},{48,176,304,432},{64,..., dimensions={0} | all-to-all | bytes 229376 | tf_op jit(solution)/shard_map/all_to_all | solution.py:447
  114.5 19.0 %all_to_all.23 = f32[4,56,128]{2,1,0:T(8,128)S(1)} all-to-all(f32[4,56,128]{2,1,0:T(8,128)S(1)} %broadcast_in_dim.11), channel_id=1, replica_groups={{0,32,64,96},{16,48,80,112},{128,160,192,224},{144,176,208,240},{256,28..., dimensions={0} | all-to-all | bytes 229376 | tf_op jit(solution)/shard_map/all_to_all | solution.py:447
  133.5 7.9 %collective-permute-start.11 = (f32[56,128]{1,0:T(8,128)S(1)}, f32[56,128]{1,0:T(8,128)S(1)}, u32[]{:S(2)}, u32[]{:S(2)}) collective-permute-start(f32[56,128]{1,0:T(8,128)S(1)} %reduce_sum.39), channel_id=1, source_target_pairs={{0,16},{16,0},{32,48},{48,32},{64,80},{80,64},{96,112},{112,96},{1... | collective-permute-start | bytes 86024 | tf_op jit(solution)/shard_map/ppermute | solution.py:423
  141.4 0.8 collective-permute-done.11
  142.3 1.0 shard_map.101
  (21 shorter events, 0.1 us)
Async XLA Ops:
  0.6 0.7 copy-start.3
  1.4 0.9 copy-start
  2.3 41.6 %copy-start.6 = (s32[4]{0:T(128)}, s32[4]{0:T(128)S(1)}, u32[]{:S(2)}) copy-start(s32[4]{0:T(128)S(1)} %pad_add_fusion.at.refs_0_) | copy-start | bytes 52
  2.3 19.2 %copy-start.8 = (s32[4,8,128]{2,1,0:T(8,128)S(1)}, s32[4,8,128]{2,1,0:T(8,128)}, u32[]{:S(2)}) copy-start(s32[4,8,128]{2,1,0:T(8,128)} %lab_ref.1) | copy-start | bytes 49156
  2.9 5.3 %collective-permute-start = (bf16[9,16,128]{2,1,0:T(8,128)(2,1)S(1)}, bf16[9,16,128]{2,1,0:T(8,128)(2,1)S(1)}, u32[]{:S(2)}, u32[]{:S(2)}) collective-permute-start(bf16[9,16,128]{2,1,0:T(8,128)(2,1)S(1)} %get-tuple-element.37), channel_id=1, source_target_pairs={{0,1},{1,0},{2,3},{3,2},{4,5},{5,4},{6,7},{7,6},{8,9},{9,8},{10,11... | collective-permute-start | bytes 110600 | tf_op jit(solution)/shard_map/ppermute | solution.py:423
  6.8 1.3 collective-permute-start.1
  8.2 13.3 %copy-start.1 = (bf16[16,16,3,3,3]{1,0,4,3,2:T(8,128)(2,1)S(1)}, bf16[16,16,3,3,3]{1,0,4,3,2:T(8,128)(2,1)}, u32[]{:S(2)}) copy-start(bf16[16,16,3,3,3]{1,0,4,3,2:T(8,128)(2,1)} %param.9) | copy-start | bytes 41476
  8.2 13.3 %copy-start.2 = (bf16[16,16,3,3,3]{1,0,4,3,2:T(8,128)(2,1)S(1)}, bf16[16,16,3,3,3]{1,0,4,3,2:T(8,128)(2,1)}, u32[]{:S(2)}) copy-start(bf16[16,16,3,3,3]{1,0,4,3,2:T(8,128)(2,1)} %param.10) | copy-start | bytes 41476
  8.7 14.4 %collective-permute-start.2 = (bf16[27,16,128]{2,1,0:T(8,128)(2,1)S(1)}, bf16[27,16,128]{2,1,0:T(8,128)(2,1)S(1)}, u32[]{:S(2)}, u32[]{:S(2)}) collective-permute-start(bf16[27,16,128]{2,1,0:T(8,128)(2,1)S(1)} %get-tuple-element.41), channel_id=1, source_target_pairs={{0,16},{16,0},{32,48},{48,32},{64,80},{80,64},{96,112},{112,96},{1... | collective-permute-start | bytes 331784 | tf_op jit(solution)/shard_map/ppermute | solution.py:423
  18.1 10.0 %collective-permute-start.3 = (bf16[27,16,128]{2,1,0:T(8,128)(2,1)S(1)}, bf16[27,16,128]{2,1,0:T(8,128)(2,1)S(1)}, u32[]{:S(2)}, u32[]{:S(2)}) collective-permute-start(bf16[27,16,128]{2,1,0:T(8,128)(2,1)S(1)} %get-tuple-element.42), channel_id=1, source_target_pairs={{16,32},{48,64},{80,96},{112,128},{144,160},{176,192},{208,224},{2... | collective-permute-start | bytes 331784 | tf_op jit(solution)/shard_map/ppermute | solution.py:429
  21.5 0.7 copy-start.9
  22.5 0.6 copy-start.4
  31.0 8.3 %collective-permute-start.4 = (bf16[28,8,128]{2,1,0:T(8,128)(2,1)S(1)}, bf16[28,8,128]{2,1,0:T(8,128)(2,1)S(1)}, u32[]{:S(2)}, u32[]{:S(2)}) collective-permute-start(bf16[28,8,128]{2,1,0:T(8,128)(2,1)S(1)} %get-tuple-element.48.me_ref), channel_id=1, source_target_pairs={{0,1},{1,0},{2,3},{3,2},{4,5},{5,4},{6,7},{7,6},{8,9},{9,8},{10,11... | collective-permute-start | bytes 172040 | tf_op jit(solution)/shard_map/ppermute | solution.py:423
  37.8 1.6 %collective-permute-start.5 = (bf16[28,8,128]{2,1,0:T(8,128)(2,1)S(1)}, bf16[28,8,128]{2,1,0:T(8,128)(2,1)S(1)}, u32[]{:S(2)}, u32[]{:S(2)}) collective-permute-start(bf16[28,8,128]{2,1,0:T(8,128)(2,1)S(1)} %get-tuple-element.50), channel_id=1, source_target_pairs={{1,2},{3,4},{5,6},{7,8},{9,10},{11,12},{13,14},{2,1},{4,3},{6,5},{... | collective-permute-start | bytes 172040 | tf_op jit(solution)/shard_map/ppermute | solution.py:429
  40.6 3.3 %collective-permute-start.6 = (bf16[84,8,128]{2,1,0:T(8,128)(2,1)S(1)}, bf16[84,8,128]{2,1,0:T(8,128)(2,1)S(1)}, u32[]{:S(2)}, u32[]{:S(2)}) collective-permute-start(bf16[84,8,128]{2,1,0:T(8,128)(2,1)S(1)} %get-tuple-element.51.ma_ref.refs_2_), channel_id=1, source_target_pairs={{0,16},{16,0},{32,48},{48,32},{64,80},{80,64},{96,112},{112,96},{1... | collective-permute-start | bytes 516104 | tf_op jit(solution)/shard_map/ppermute | solution.py:423
  44.4 10.2 %collective-permute-start.7 = (bf16[63,8,128]{2,1,0:T(8,128)(2,1)S(1)}, bf16[63,8,128]{2,1,0:T(8,128)(2,1)S(1)}, u32[]{:S(2)}, u32[]{:S(2)}) collective-permute-start(bf16[63,8,128]{2,1,0:T(8,128)(2,1)S(1)} %shard_map.98), channel_id=1, source_target_pairs={{16,32},{48,64},{80,96},{112,128},{144,160},{176,192},{208,224},{2... | collective-permute-start | bytes 387080 | tf_op jit(solution)/shard_map/ppermute | solution.py:429
  54.6 9.9 %collective-permute-start.8 = (bf16[63,8,128]{2,1,0:T(8,128)(2,1)S(1)}, bf16[63,8,128]{2,1,0:T(8,128)(2,1)S(1)}, u32[]{:S(2)}, u32[]{:S(2)}) collective-permute-start(bf16[63,8,128]{2,1,0:T(8,128)(2,1)S(1)} %collective-permute-done.7.refs_4_), channel_id=1, source_target_pairs={{0,16},{16,0},{32,48},{48,32},{64,80},{80,64},{96,112},{112,96},{1... | collective-permute-start | bytes 387080 | tf_op jit(solution)/shard_map/ppermute | solution.py:423
  56.5 13.5 %collective-permute-start.9 = (bf16[48,8,128]{2,1,0:T(8,128)(2,1)}, bf16[48,8,128]{2,1,0:T(8,128)(2,1)S(1)}, u32[]{:S(2)}, u32[]{:S(2)}) collective-permute-start(bf16[48,8,128]{2,1,0:T(8,128)(2,1)} %get-tuple-element.56), channel_id=1, source_target_pairs={{16,32},{48,64},{80,96},{112,128},{144,160},{176,192},{208,224},{2... | collective-permute-start | bytes 294920 | tf_op jit(solution)/shard_map/ppermute | solution.py:429
  64.5 0.7 copy-start.7
  65.2 4.9 %copy-start.5 = (bf16[32,576]{1,0:T(8,128)(2,1)S(1)}, bf16[32,576]{1,0:T(8,128)(2,1)}, u32[]{:S(2)}) copy-start(bf16[32,576]{1,0:T(8,128)(2,1)} %copy-done.4) | copy-start | bytes 110596
  75.3 3.1 %collective-permute-start.10 = (f32[56,128]{1,0:T(8,128)S(1)}, f32[56,128]{1,0:T(8,128)S(1)}, u32[]{:S(2)}, u32[]{:S(2)}) collective-permute-start(f32[56,128]{1,0:T(8,128)S(1)} %dynamic-slice_bitcast_fusion), channel_id=1, source_target_pairs={{0,16},{16,0},{32,48},{48,32},{64,80},{80,64},{96,112},{112,96},{1... | collective-permute-start | bytes 86024 | tf_op jit(solution)/shard_map/ppermute | solution.py:423
  133.5 8.7 %collective-permute-start.11 = (f32[56,128]{1,0:T(8,128)S(1)}, f32[56,128]{1,0:T(8,128)S(1)}, u32[]{:S(2)}, u32[]{:S(2)}) collective-permute-start(f32[56,128]{1,0:T(8,128)S(1)} %reduce_sum.39), channel_id=1, source_target_pairs={{0,16},{16,0},{32,48},{48,32},{64,80},{80,64},{96,112},{112,96},{1... | collective-permute-start | bytes 86024 | tf_op jit(solution)/shard_map/ppermute | solution.py:423

commit v9 on v8

--- a/solution.py
+++ b/solution.py
@@ -4,6 +4,7 @@
 from jax.experimental import pallas as pl
 from jax.experimental.pallas import tpu as pltpu
 from jax.sharding import PartitionSpec as P
+
 
 C = 16
 BZ = 4
@@ -205,7 +206,7 @@
 
 def march(nz, ny, at, own_ref, ye_ref, mate_ref, far_ref, far2_ref, g0_ref, dpre_ref,
           sp, lab, ph, w_s, dz_s, dy_s, dx_s, ag_s, ds, dd):
-    iz, iy, pz, py = at[0], at[1], at[2], at[3]
+    iz, iy, pz = at[0], at[1], at[2]
     base = 4 * pz
 
     def place(start, block):
@@ -303,7 +304,7 @@
     pz = at[2]
     sw = sw_ref[...]
 
-    def second(z, k, slope):
+    def second(z, slope):
         for y in range(BY + 4):
             d = dpre_ref[z, 2 + y : 3 + y, :]
             value = (sw * d * slope(y))[None]
@@ -317,12 +318,14 @@
             if 2 <= y < 2 + BY:
                 return slope2_ref[k, y - 2]
             return s2y_ref[k, y].astype(f32)
-        second(2 + k, k, own)
+
+        second(2 + k, own)
     for k in range(2):
         for ref, first, z in ((ra_ref, 36, 6 - 6 * pz), (rb_ref, 0, 6 * pz)):
             def far(y, ref=ref, first=first + 24 * k):
                 return ref[first + 2 * y : first + 2 * y + 2].astype(f32).reshape(C, X)
-            second(z + k, k, far)
+
+            second(z + k, far)
 
     w2 = w2_ref[...]
     w1 = w1_ref[...]
@@ -493,10 +496,10 @@
         widen, [shape((84, 8, X), SENT), shape((48, 8, X), SENT), shape((BZ, 12, C, X))]
     )(at, fe, slope2, ge, go)
     ha = even(fa, "gz")
-    hb = odd(call(relay, shape((63, 8, X), SENT))(at, fa, ha), "gz")
-    hb, fs = lax.optimization_barrier((hb, fs))
+    fb = call(relay, shape((63, 8, X), SENT))(at, fa, ha)
+    hb = odd(fb, "gz")
+    hs = odd(fs, "gz")
     hc = even(hb, "gz")
-    hs = odd(fs, "gz")
 
     plane = (24, 24, X)
     dpre = call(
@@ -534,6 +537,7 @@
 def solution(mesh):
     in_specs = (P(None, "gz", "gy", None), P("gz", "gy", None), P("gz", "gy", None), P(), P(), P())
     out_specs = (P(None, "gz", "gy", None), P(), P(), P())
+
     return jax.shard_map(
         on_device, mesh=mesh, in_specs=in_specs, out_specs=out_specs, check_vma=False
     )

time: 144 us -> 144 us (level)
  no operation moved by 1% of the time
where the time goes in v9:
time: 144 us; the launch traced here: 143 us
  blocking collectives  55 us (38%)
  starting transfers between devices  53.4 us (37%)
  Pallas kernels  17.5 us (12%)
  waiting for transfers between devices  12.8 us (9%)
  local copies, waits for them, and re-layouts  3.47 us (2%)
    all_to_all x4, blocking collectives, total_of(): lax.all_to_all(copies, axis, 0, 0, axis_index_groups=sets)  55 us
    ppermute x7, starting transfers between devices, even(): return lax.ppermute(value, axis, [(i, i ^ 1) for i in range(n)])  33.6 us
    ppermute x5, starting transfers between devices, odd(): return lax.ppermute(value, axis, pairs + [(j, i) for i, j in pairs])  19.8 us
    pallas_call x9, Pallas kernels, run(): pl.pallas_call(kernel, out_shape=outs, in_specs=specs, out_specs=[vmem] *...  17.5 us
    ppermute x5, waiting for transfers between devices, odd(): return lax.ppermute(value, axis, pairs + [(j, i) for i, j in pairs])  7.9 us
    ppermute x7, waiting for transfers between devices, even(): return lax.ppermute(value, axis, [(i, i ^ 1) for i in range(n)])  4.91 us
    unnamed x20, local copies, waits for them, and re-layouts  3.43 us
  transfers between devices with their start and end apart: 12, of which 7 were waited for; matrix products, arithmetic and copies ran while one was open for 0% of the time, Pallas kernels for 4%

profile of v9, /device:TPU:1, one launch (start us, length us, event | category | flops | bytes accessed | tf_op | source)
XLA Modules:
  0.0 143.3 jit_solution(2669181141316851103)
XLA Ops:
  0.6 0.0 copy-start.3
  0.7 0.1 pad_add_fusion.at.refs_0_
  0.7 0.6 copy-done.3
  1.4 0.9 copy-done
  2.3 0.6 shard_map.93
  2.9 3.9 %collective-permute-start = (bf16[9,16,128]{2,1,0:T(8,128)(2,1)S(1)}, bf16[9,16,128]{2,1,0:T(8,128)(2,1)S(1)}, u32[]{:S(2)}, u32[]{:S(2)}) collective-permute-start(bf16[9,16,128]{2,1,0:T(8,128)(2,1)S(1)} %get-tuple-element.35), channel_id=1, source_target_pairs={{0,1},{1,0},{2,3},{3,2},{4,5},{5,4},{6,7},{7,6},{8,9},{9,8},{10,11... | collective-permute-start | bytes 110600 | tf_op jit(solution)/shard_map/ppermute | solution.py:426
  6.8 0.7 collective-permute-start.1
  7.5 0.7 collective-permute-done.re_ref
  8.2 0.0 collective-permute-done.1.ro_ref
  8.2 0.6 shard_map.94
  8.7 9.3 %collective-permute-start.2 = (bf16[27,16,128]{2,1,0:T(8,128)(2,1)S(1)}, bf16[27,16,128]{2,1,0:T(8,128)(2,1)S(1)}, u32[]{:S(2)}, u32[]{:S(2)}) collective-permute-start(bf16[27,16,128]{2,1,0:T(8,128)(2,1)S(1)} %get-tuple-element.39), channel_id=1, source_target_pairs={{0,16},{16,0},{32,48},{48,32},{64,80},{80,64},{96,112},{112,96},{1... | collective-permute-start | bytes 331784 | tf_op jit(solution)/shard_map/ppermute | solution.py:426
  18.1 3.4 %collective-permute-start.3 = (bf16[27,16,128]{2,1,0:T(8,128)(2,1)S(1)}, bf16[27,16,128]{2,1,0:T(8,128)(2,1)S(1)}, u32[]{:S(2)}, u32[]{:S(2)}) collective-permute-start(bf16[27,16,128]{2,1,0:T(8,128)(2,1)S(1)} %get-tuple-element.40), channel_id=1, source_target_pairs={{16,32},{48,64},{80,96},{112,128},{144,160},{176,192},{208,224},{2... | collective-permute-start | bytes 331784 | tf_op jit(solution)/shard_map/ppermute | solution.py:432
  21.5 0.0 copy-start.9
  21.5 0.0 copy-done.8
  21.5 0.6 copy-done.9
  22.1 0.4 shard_map.95
  22.5 0.0 copy-start.4
  22.5 0.6 copy-done.4
  23.2 0.0 collective-permute-done.2.refs_3_
  23.2 4.9 %collective-permute-done.3.refs_4_ = bf16[27,16,128]{2,1,0:T(8,128)(2,1)S(1)} collective-permute-done((bf16[27,16,128]{2,1,0:T(8,128)(2,1)S(1)}, bf16[27,16,128]{2,1,0:T(8,128)(2,1)S(1)}, u32[]{:S(2)}, u32[]{:S(2)}) %collective-permute-start.3) | collective-permute-done | bytes 110624 | tf_op jit(solution)/shard_map/ppermute | solution.py:432
  28.1 3.0 %shard_map.96 = (bf16[6,10,3,16,128]{4,3,2,1,0:T(8,128)(2,1)S(1)}, bf16[6,10,3,16,128]{4,3,2,1,0:T(8,128)(2,1)S(1)}, f32[6,10,16,128]{3,2,1,0:T(8,128)S(1)}, f32...) custom-call(s32[4]{0:T(128)S(1)} %pad_add_fusion.at.refs_0_, ...), custom_call_target="tpu_custom_call" | custom-call | bytes 548880 | tf_op jit(solution)/shard_map/pallas_call | solution.py:407
  31.0 6.8 %collective-permute-start.4 = (bf16[28,8,128]{2,1,0:T(8,128)(2,1)S(1)}, bf16[28,8,128]{2,1,0:T(8,128)(2,1)S(1)}, u32[]{:S(2)}, u32[]{:S(2)}) collective-permute-start(bf16[28,8,128]{2,1,0:T(8,128)(2,1)S(1)} %get-tuple-element.46.me_ref), channel_id=1, source_target_pairs={{0,1},{1,0},{2,3},{3,2},{4,5},{5,4},{6,7},{7,6},{8,9},{9,8},{10,11... | collective-permute-start | bytes 172040 | tf_op jit(solution)/shard_map/ppermute | solution.py:426
  37.8 0.7 collective-permute-start.5
  38.5 0.9 collective-permute-done.4.re_ref
  39.3 0.0 collective-permute-done.5.ro_ref
  39.4 1.2 shard_map.97
  40.6 1.9 %collective-permute-start.6 = (bf16[84,8,128]{2,1,0:T(8,128)(2,1)S(1)}, bf16[84,8,128]{2,1,0:T(8,128)(2,1)S(1)}, u32[]{:S(2)}, u32[]{:S(2)}) collective-permute-start(bf16[84,8,128]{2,1,0:T(8,128)(2,1)S(1)} %get-tuple-element.49.ma_ref.refs_2_), channel_id=1, source_target_pairs={{0,16},{16,0},{32,48},{48,32},{64,80},{80,64},{96,112},{112,96},{1... | collective-permute-start | bytes 516104 | tf_op jit(solution)/shard_map/ppermute | solution.py:426
  42.5 1.4 collective-permute-done.6.ra_ref.refs_3_
  43.9 0.6 shard_map.98
  44.4 7.2 %collective-permute-start.7 = (bf16[63,8,128]{2,1,0:T(8,128)(2,1)S(1)}, bf16[63,8,128]{2,1,0:T(8,128)(2,1)S(1)}, u32[]{:S(2)}, u32[]{:S(2)}) collective-permute-start(bf16[63,8,128]{2,1,0:T(8,128)(2,1)S(1)} %shard_map.98), channel_id=1, source_target_pairs={{16,32},{48,64},{80,96},{112,128},{144,160},{176,192},{208,224},{2... | collective-permute-start | bytes 387080 | tf_op jit(solution)/shard_map/ppermute | solution.py:432
  51.6 3.0 %collective-permute-done.7.refs_4_ = bf16[63,8,128]{2,1,0:T(8,128)(2,1)S(1)} collective-permute-done((bf16[63,8,128]{2,1,0:T(8,128)(2,1)S(1)}, bf16[63,8,128]{2,1,0:T(8,128)(2,1)S(1)}, u32[]{:S(2)}, u32[]{:S(2)}) %collective-permute-start.7) | collective-permute-done | bytes 129056 | tf_op jit(solution)/shard_map/ppermute | solution.py:432
  54.6 1.9 %collective-permute-start.8 = (bf16[63,8,128]{2,1,0:T(8,128)(2,1)S(1)}, bf16[63,8,128]{2,1,0:T(8,128)(2,1)S(1)}, u32[]{:S(2)}, u32[]{:S(2)}) collective-permute-start(bf16[63,8,128]{2,1,0:T(8,128)(2,1)S(1)} %collective-permute-done.7.refs_4_), channel_id=1, source_target_pairs={{0,16},{16,0},{32,48},{48,32},{64,80},{80,64},{96,112},{112,96},{1... | collective-permute-start | bytes 387080 | tf_op jit(solution)/shard_map/ppermute | solution.py:426
  56.5 7.9 %collective-permute-start.9 = (bf16[48,8,128]{2,1,0:T(8,128)(2,1)}, bf16[48,8,128]{2,1,0:T(8,128)(2,1)S(1)}, u32[]{:S(2)}, u32[]{:S(2)}) collective-permute-start(bf16[48,8,128]{2,1,0:T(8,128)(2,1)} %get-tuple-element.52), channel_id=1, source_target_pairs={{16,32},{48,64},{80,96},{112,128},{144,160},{176,192},{208,224},{2... | collective-permute-start | bytes 294920 | tf_op jit(solution)/shard_map/ppermute | solution.py:432
  64.5 0.0 collective-permute-done.8.refs_5_
  64.5 0.0 copy-start.7
  64.5 0.6 copy-done.7
  65.2 4.9 %shard_map.99.dpre_ref = f32[8,16,128]{2,1,0:T(8,128)S(1)} custom-call(s32[4]{0:T(128)S(1)} %copy-done.7, f32[3,4,8,128]{3,2,1,0:T(8,128)S(1)} %get-tuple-element.45.refs_1_, bf16[84,8,128]{2,1,0:T(8,128)(2,1)S(1)} %get-tuple-element.49.ma_ref.refs_2_, bf16[84,8,128]{2,1,0:T(8,128)(2,1)S(1)} %collective-permute-done.6.ra_ref.refs_3_, ...), custom_call_target="tpu_custom_call" | custom-call | bytes 716816 | tf_op jit(solution)/shard_map/pallas_call | solution.py:407
  70.1 0.0 collective-permute-done.9.rb_ref
  70.1 5.2 %shard_map.100 = (bf16[16,4,8,128]{3,2,1,0:T(8,128)(2,1)}, f32[2,56,128]{2,1,0:T(8,128)S(1)}) custom-call(s32[4]{0:T(128)S(1)} %copy-done.7, f32[8,16,128]{2,1,0:T(8,128)S(1)} %shard_map.99.dpre_ref, f32[4,8,16,128]{3,2,1,0:T(8,128)S(1)} %get-tuple-element.47.slope2_ref, bf16[4,12,16,128]{3,2,1,0:T(8,128)(2,1)S(1)} %get-tuple-element.51.s2y_ref, ...), custom_call_target="tpu_custom_call" | custom-call | bytes 3104784 | tf_op jit(solution)/shard_map/pallas_call | solution.py:407
  75.3 1.9 %collective-permute-start.10 = (f32[56,128]{1,0:T(8,128)S(1)}, f32[56,128]{1,0:T(8,128)S(1)}, u32[]{:S(2)}, u32[]{:S(2)}) collective-permute-start(f32[56,128]{1,0:T(8,128)S(1)} %dynamic-slice_bitcast_fusion), channel_id=1, source_target_pairs={{0,16},{16,0},{32,48},{48,32},{64,80},{80,64},{96,112},{112,96},{1... | collective-permute-start | bytes 86024 | tf_op jit(solution)/shard_map/ppermute | solution.py:426
  77.2 1.2 collective-permute-done.10
  78.4 17.7 %all_to_all.20 = f32[4,56,128]{2,1,0:T(8,128)S(1)} all-to-all(f32[4,56,128]{2,1,0:T(8,128)S(1)} %broadcast_in_dim.8), channel_id=1, replica_groups={{0,1,2,3},{4,5,6,7},{8,9,10,11},{12,13,14,15},{16,17,18,19},{20,21,22,2..., dimensions={0} | all-to-all | bytes 229376 | tf_op jit(solution)/shard_map/all_to_all | solution.py:450
  96.1 7.1 %all_to_all.21 = f32[4,56,128]{2,1,0:T(8,128)S(1)} all-to-all(f32[4,56,128]{2,1,0:T(8,128)S(1)} %broadcast_in_dim.9), channel_id=1, replica_groups={{0,4,8,12},{1,5,9,13},{2,6,10,14},{3,7,11,15},{16,20,24,28},{17,21,25,2..., dimensions={0} | all-to-all | bytes 229376 | tf_op jit(solution)/shard_map/all_to_all | solution.py:450
  103.3 11.2 %all_to_all.22 = f32[4,56,128]{2,1,0:T(8,128)S(1)} all-to-all(f32[4,56,128]{2,1,0:T(8,128)S(1)} %broadcast_in_dim.10), channel_id=1, replica_groups={{0,128,256,384},{16,144,272,400},{32,160,288,416},{48,176,304,432},{64,..., dimensions={0} | all-to-all | bytes 229376 | tf_op jit(solution)/shard_map/all_to_all | solution.py:450
  114.5 19.0 %all_to_all.23 = f32[4,56,128]{2,1,0:T(8,128)S(1)} all-to-all(f32[4,56,128]{2,1,0:T(8,128)S(1)} %broadcast_in_dim.11), channel_id=1, replica_groups={{0,32,64,96},{16,48,80,112},{128,160,192,224},{144,176,208,240},{256,28..., dimensions={0} | all-to-all | bytes 229376 | tf_op jit(solution)/shard_map/all_to_all | solution.py:450
  133.5 7.9 %collective-permute-start.11 = (f32[56,128]{1,0:T(8,128)S(1)}, f32[56,128]{1,0:T(8,128)S(1)}, u32[]{:S(2)}, u32[]{:S(2)}) collective-permute-start(f32[56,128]{1,0:T(8,128)S(1)} %reduce_sum.39), channel_id=1, source_target_pairs={{0,16},{16,0},{32,48},{48,32},{64,80},{80,64},{96,112},{112,96},{1... | collective-permute-start | bytes 86024 | tf_op jit(solution)/shard_map/ppermute | solution.py:426
  141.4 0.8 collective-permute-done.11
  142.3 1.0 shard_map.101
  (21 shorter events, 0.1 us)
Async XLA Ops:
  0.6 0.7 copy-start.3
  1.4 0.9 copy-start
  2.3 41.6 %copy-start.6 = (s32[4]{0:T(128)}, s32[4]{0:T(128)S(1)}, u32[]{:S(2)}) copy-start(s32[4]{0:T(128)S(1)} %pad_add_fusion.at.refs_0_) | copy-start | bytes 52
  2.3 19.2 %copy-start.8 = (s32[4,8,128]{2,1,0:T(8,128)S(1)}, s32[4,8,128]{2,1,0:T(8,128)}, u32[]{:S(2)}) copy-start(s32[4,8,128]{2,1,0:T(8,128)} %lab_ref.1) | copy-start | bytes 49156
  2.9 5.3 %collective-permute-start = (bf16[9,16,128]{2,1,0:T(8,128)(2,1)S(1)}, bf16[9,16,128]{2,1,0:T(8,128)(2,1)S(1)}, u32[]{:S(2)}, u32[]{:S(2)}) collective-permute-start(bf16[9,16,128]{2,1,0:T(8,128)(2,1)S(1)} %get-tuple-element.35), channel_id=1, source_target_pairs={{0,1},{1,0},{2,3},{3,2},{4,5},{5,4},{6,7},{7,6},{8,9},{9,8},{10,11... | collective-permute-start | bytes 110600 | tf_op jit(solution)/shard_map/ppermute | solution.py:426
  6.8 1.3 collective-permute-start.1
  8.2 13.3 %copy-start.1 = (bf16[16,16,3,3,3]{1,0,4,3,2:T(8,128)(2,1)S(1)}, bf16[16,16,3,3,3]{1,0,4,3,2:T(8,128)(2,1)}, u32[]{:S(2)}) copy-start(bf16[16,16,3,3,3]{1,0,4,3,2:T(8,128)(2,1)} %param.9) | copy-start | bytes 41476
  8.2 13.3 %copy-start.2 = (bf16[16,16,3,3,3]{1,0,4,3,2:T(8,128)(2,1)S(1)}, bf16[16,16,3,3,3]{1,0,4,3,2:T(8,128)(2,1)}, u32[]{:S(2)}) copy-start(bf16[16,16,3,3,3]{1,0,4,3,2:T(8,128)(2,1)} %param.10) | copy-start | bytes 41476
  8.7 14.4 %collective-permute-start.2 = (bf16[27,16,128]{2,1,0:T(8,128)(2,1)S(1)}, bf16[27,16,128]{2,1,0:T(8,128)(2,1)S(1)}, u32[]{:S(2)}, u32[]{:S(2)}) collective-permute-start(bf16[27,16,128]{2,1,0:T(8,128)(2,1)S(1)} %get-tuple-element.39), channel_id=1, source_target_pairs={{0,16},{16,0},{32,48},{48,32},{64,80},{80,64},{96,112},{112,96},{1... | collective-permute-start | bytes 331784 | tf_op jit(solution)/shard_map/ppermute | solution.py:426
  18.1 10.0 %collective-permute-start.3 = (bf16[27,16,128]{2,1,0:T(8,128)(2,1)S(1)}, bf16[27,16,128]{2,1,0:T(8,128)(2,1)S(1)}, u32[]{:S(2)}, u32[]{:S(2)}) collective-permute-start(bf16[27,16,128]{2,1,0:T(8,128)(2,1)S(1)} %get-tuple-element.40), channel_id=1, source_target_pairs={{16,32},{48,64},{80,96},{112,128},{144,160},{176,192},{208,224},{2... | collective-permute-start | bytes 331784 | tf_op jit(solution)/shard_map/ppermute | solution.py:432
  21.5 0.7 copy-start.9
  22.5 0.6 copy-start.4
  31.0 8.3 %collective-permute-start.4 = (bf16[28,8,128]{2,1,0:T(8,128)(2,1)S(1)}, bf16[28,8,128]{2,1,0:T(8,128)(2,1)S(1)}, u32[]{:S(2)}, u32[]{:S(2)}) collective-permute-start(bf16[28,8,128]{2,1,0:T(8,128)(2,1)S(1)} %get-tuple-element.46.me_ref), channel_id=1, source_target_pairs={{0,1},{1,0},{2,3},{3,2},{4,5},{5,4},{6,7},{7,6},{8,9},{9,8},{10,11... | collective-permute-start | bytes 172040 | tf_op jit(solution)/shard_map/ppermute | solution.py:426
  37.8 1.6 %collective-permute-start.5 = (bf16[28,8,128]{2,1,0:T(8,128)(2,1)S(1)}, bf16[28,8,128]{2,1,0:T(8,128)(2,1)S(1)}, u32[]{:S(2)}, u32[]{:S(2)}) collective-permute-start(bf16[28,8,128]{2,1,0:T(8,128)(2,1)S(1)} %get-tuple-element.48), channel_id=1, source_target_pairs={{1,2},{3,4},{5,6},{7,8},{9,10},{11,12},{13,14},{2,1},{4,3},{6,5},{... | collective-permute-start | bytes 172040 | tf_op jit(solution)/shard_map/ppermute | solution.py:432
  40.6 3.3 %collective-permute-start.6 = (bf16[84,8,128]{2,1,0:T(8,128)(2,1)S(1)}, bf16[84,8,128]{2,1,0:T(8,128)(2,1)S(1)}, u32[]{:S(2)}, u32[]{:S(2)}) collective-permute-start(bf16[84,8,128]{2,1,0:T(8,128)(2,1)S(1)} %get-tuple-element.49.ma_ref.refs_2_), channel_id=1, source_target_pairs={{0,16},{16,0},{32,48},{48,32},{64,80},{80,64},{96,112},{112,96},{1... | collective-permute-start | bytes 516104 | tf_op jit(solution)/shard_map/ppermute | solution.py:426
  44.4 10.2 %collective-permute-start.7 = (bf16[63,8,128]{2,1,0:T(8,128)(2,1)S(1)}, bf16[63,8,128]{2,1,0:T(8,128)(2,1)S(1)}, u32[]{:S(2)}, u32[]{:S(2)}) collective-permute-start(bf16[63,8,128]{2,1,0:T(8,128)(2,1)S(1)} %shard_map.98), channel_id=1, source_target_pairs={{16,32},{48,64},{80,96},{112,128},{144,160},{176,192},{208,224},{2... | collective-permute-start | bytes 387080 | tf_op jit(solution)/shard_map/ppermute | solution.py:432
  54.6 9.9 %collective-permute-start.8 = (bf16[63,8,128]{2,1,0:T(8,128)(2,1)S(1)}, bf16[63,8,128]{2,1,0:T(8,128)(2,1)S(1)}, u32[]{:S(2)}, u32[]{:S(2)}) collective-permute-start(bf16[63,8,128]{2,1,0:T(8,128)(2,1)S(1)} %collective-permute-done.7.refs_4_), channel_id=1, source_target_pairs={{0,16},{16,0},{32,48},{48,32},{64,80},{80,64},{96,112},{112,96},{1... | collective-permute-start | bytes 387080 | tf_op jit(solution)/shard_map/ppermute | solution.py:426
  56.5 13.5 %collective-permute-start.9 = (bf16[48,8,128]{2,1,0:T(8,128)(2,1)}, bf16[48,8,128]{2,1,0:T(8,128)(2,1)S(1)}, u32[]{:S(2)}, u32[]{:S(2)}) collective-permute-start(bf16[48,8,128]{2,1,0:T(8,128)(2,1)} %get-tuple-element.52), channel_id=1, source_target_pairs={{16,32},{48,64},{80,96},{112,128},{144,160},{176,192},{208,224},{2... | collective-permute-start | bytes 294920 | tf_op jit(solution)/shard_map/ppermute | solution.py:432
  64.5 0.7 copy-start.7
  65.2 4.9 %copy-start.5 = (bf16[32,576]{1,0:T(8,128)(2,1)S(1)}, bf16[32,576]{1,0:T(8,128)(2,1)}, u32[]{:S(2)}) copy-start(bf16[32,576]{1,0:T(8,128)(2,1)} %copy-done.4) | copy-start | bytes 110596
  75.3 3.1 %collective-permute-start.10 = (f32[56,128]{1,0:T(8,128)S(1)}, f32[56,128]{1,0:T(8,128)S(1)}, u32[]{:S(2)}, u32[]{:S(2)}) collective-permute-start(f32[56,128]{1,0:T(8,128)S(1)} %dynamic-slice_bitcast_fusion), channel_id=1, source_target_pairs={{0,16},{16,0},{32,48},{48,32},{64,80},{80,64},{96,112},{112,96},{1... | collective-permute-start | bytes 86024 | tf_op jit(solution)/shard_map/ppermute | solution.py:426
  133.5 8.7 %collective-permute-start.11 = (f32[56,128]{1,0:T(8,128)S(1)}, f32[56,128]{1,0:T(8,128)S(1)}, u32[]{:S(2)}, u32[]{:S(2)}) collective-permute-start(f32[56,128]{1,0:T(8,128)S(1)} %reduce_sum.39), channel_id=1, source_target_pairs={{0,16},{16,0},{32,48},{48,32},{64,80},{80,64},{96,112},{112,96},{1... | collective-permute-start | bytes 86024 | tf_op jit(solution)/shard_map/ppermute | solution.py:426

commit v10 on v9

--- a/solution.py
+++ b/solution.py
@@ -179,21 +179,24 @@
             ref[12 + 4 * z : 16 + 4 * z] = slope2_ref[z, pl.ds(start, 2)].reshape(4, 8, X).astype(SENT)
 
 
-def widen(at, me_ref, slope2_ref, re_ref, ro_ref, ma_ref, mb_ref, s2y_ref):
-    pz, py = at[2], at[3]
+def widen(at, me_ref, re_ref, ro_ref, ma_ref):
+    py = at[3]
     ma_ref[12:24] = me_ref[:12]
     ma_ref[pl.ds(24 - 24 * py, 12)] = re_ref[:12]
     ma_ref[pl.ds(24 * py, 12)] = ro_ref[:12]
+
+
+def spread(at, slope2_ref, re_ref, ro_ref, ma_ref, mb_ref, s2y_ref):
+    pz, py = at[2], at[3]
     for z in range(BZ):
         s2y_ref[z, 2 : 2 + BY] = slope2_ref[z].astype(bf16)
         for ref, start in ((re_ref, 10 - 10 * py), (ro_ref, 10 * py)):
             rows = ref[12 + 4 * z : 16 + 4 * z].astype(f32).reshape(2, C, X)
             s2y_ref[z, pl.ds(start, 2)] = rows.astype(bf16)
     for k in range(2):
-        rows = s2y_ref[2 - 2 * pz + k].astype(f32).reshape(24, 8, X)
-        ma_ref[36 + 24 * k : 60 + 24 * k] = rows.astype(SENT)
-        rows = s2y_ref[2 * pz + k].astype(f32).reshape(24, 8, X)
-        mb_ref[24 * k : 24 + 24 * k] = rows.astype(SENT)
+        for ref, start in ((ma_ref, 2 - 2 * pz), (mb_ref, 2 * pz)):
+            rows = s2y_ref[start + k].astype(f32).reshape(24, 8, X)
+            ref[24 * k : 24 + 24 * k] = rows.astype(SENT)
 
 
 def relay(at, ma_ref, ra_ref, mb_ref):
@@ -321,7 +324,7 @@
 
         second(2 + k, own)
     for k in range(2):
-        for ref, first, z in ((ra_ref, 36, 6 - 6 * pz), (rb_ref, 0, 6 * pz)):
+        for ref, first, z in ((ra_ref, 0, 6 - 6 * pz), (rb_ref, 0, 6 * pz)):
             def far(y, ref=ref, first=first + 24 * k):
                 return ref[first + 2 * y : first + 2 * y + 2].astype(f32).reshape(C, X)
 
@@ -492,13 +495,15 @@
 
     go = odd(fo, "gy")
     ge = even(fe, "gy")
-    fa, fs, s2y = call(
-        widen, [shape((84, 8, X), SENT), shape((48, 8, X), SENT), shape((BZ, 12, C, X))]
-    )(at, fe, slope2, ge, go)
+    fa = call(widen, shape((36, 8, X), SENT))(at, fe, ge, go)
     ha = even(fa, "gz")
+    ms, fs, s2y = call(
+        spread, [shape((48, 8, X), SENT), shape((48, 8, X), SENT), shape((BZ, 12, C, X))]
+    )(at, slope2, ge, go)
     fb = call(relay, shape((63, 8, X), SENT))(at, fa, ha)
     hb = odd(fb, "gz")
     hs = odd(fs, "gz")
+    hm = even(ms, "gz")
     hc = even(hb, "gz")
 
     plane = (24, 24, X)
@@ -523,7 +528,7 @@
         backward,
         [shape((C, BZ, BY, X)), shape((2, 56, X), f32)],
         [pltpu.VMEM((8, 12, 3, C, X), bf16), pltpu.VMEM((6, 10, 3, C, X), bf16)],
-    )(at, dpre, slope2, s2y, ha, hs, sw, hx, fx, slope1, top, w1b, w2b)
+    )(at, dpre, slope2, s2y, hm, hs, sw, hx, fx, slope1, top, w1b, w2b)
 
     a, b = total_of(grad, iz)
     tap_major = shape((27, C, C), f32)

time: 144 us -> 147 us (1.021)
  starting transfers between devices: 53.4 us -> 55.4 us
    ppermute x7 -> x8, starting transfers between devices: 33.6 us -> 36 us  [even(): return lax.ppermute(value, axis, [(i, i ^ 1) for i in range(n)])]
    unnamed x20 -> x12, local copies, waits for them, and re-layouts: 3.43 us -> 2.16 us
    pallas_call x9 -> x10, Pallas kernels: 17.5 us -> 18.1 us  [run(): pl.pallas_call(kernel, out_shape=outs, in_specs=specs, out_specs=[vmem] *...]
    ppermute x7 -> x8, waiting for transfers between devices: 4.91 us -> 4.77 us  [even(): return lax.ppermute(value, axis, [(i, i ^ 1) for i in range(n)])]
  transfers between devices with their start and end apart: 12 -> 13, of which waited for: 7 -> 7; matrix products, arithmetic and copies ran while one was open for 0% -> 0% of each run, Pallas kernels for 4% -> 5%
where the time goes in v10:
time: 147 us; the launch traced here: 146 us
  blocking collectives  56 us (38%)
  starting transfers between devices  55.4 us (38%)
  Pallas kernels  18.1 us (12%)
  waiting for transfers between devices  13.3 us (9%)
  local copies, waits for them, and re-layouts  2.2 us (1%)
    all_to_all x4, blocking collectives, total_of(): lax.all_to_all(copies, axis, 0, 0, axis_index_groups=sets)  56 us
    ppermute x8, starting transfers between devices, even(): return lax.ppermute(value, axis, [(i, i ^ 1) for i in range(n)])  36 us
    ppermute x5, starting transfers between devices, odd(): return lax.ppermute(value, axis, pairs + [(j, i) for i, j in pairs])  19.3 us
    pallas_call x10, Pallas kernels, run(): pl.pallas_call(kernel, out_shape=outs, in_specs=specs, out_specs=[vmem] *...  18.1 us
    ppermute x5, waiting for transfers between devices, odd(): return lax.ppermute(value, axis, pairs + [(j, i) for i, j in pairs])  8.5 us
    ppermute x8, waiting for transfers between devices, even(): return lax.ppermute(value, axis, [(i, i ^ 1) for i in range(n)])  4.77 us
  transfers between devices with their start and end apart: 13, of which 7 were waited for; matrix products, arithmetic and copies ran while one was open for 0% of the time, Pallas kernels for 5%

profile of v10, /device:TPU:1, one launch (start us, length us, event | category | flops | bytes accessed | tf_op | source)
XLA Modules:
  0.0 145.9 jit_solution(18141075939442750617)
XLA Ops:
  0.6 0.0 copy-start.3
  0.7 0.1 pad_add_fusion.at.refs_0_
  0.7 0.6 copy-done.3
  1.4 0.9 copy-done
  2.3 0.6 shard_map.93
  2.9 3.9 %collective-permute-start = (bf16[9,16,128]{2,1,0:T(8,128)(2,1)S(1)}, bf16[9,16,128]{2,1,0:T(8,128)(2,1)S(1)}, u32[]{:S(2)}, u32[]{:S(2)}) collective-permute-start(bf16[9,16,128]{2,1,0:T(8,128)(2,1)S(1)} %get-tuple-element.35), channel_id=1, source_target_pairs={{0,1},{1,0},{2,3},{3,2},{4,5},{5,4},{6,7},{7,6},{8,9},{9,8},{10,11... | collective-permute-start | bytes 110600 | tf_op jit(solution)/shard_map/ppermute | solution.py:429
  6.8 0.7 collective-permute-start.1
  7.5 0.7 collective-permute-done.re_ref
  8.2 0.0 collective-permute-done.1.ro_ref
  8.2 0.6 shard_map.94
  8.7 9.3 %collective-permute-start.2 = (bf16[27,16,128]{2,1,0:T(8,128)(2,1)S(1)}, bf16[27,16,128]{2,1,0:T(8,128)(2,1)S(1)}, u32[]{:S(2)}, u32[]{:S(2)}) collective-permute-start(bf16[27,16,128]{2,1,0:T(8,128)(2,1)S(1)} %get-tuple-element.39), channel_id=1, source_target_pairs={{0,16},{16,0},{32,48},{48,32},{64,80},{80,64},{96,112},{112,96},{1... | collective-permute-start | bytes 331784 | tf_op jit(solution)/shard_map/ppermute | solution.py:429
  18.1 3.4 %collective-permute-start.3 = (bf16[27,16,128]{2,1,0:T(8,128)(2,1)S(1)}, bf16[27,16,128]{2,1,0:T(8,128)(2,1)S(1)}, u32[]{:S(2)}, u32[]{:S(2)}) collective-permute-start(bf16[27,16,128]{2,1,0:T(8,128)(2,1)S(1)} %get-tuple-element.40), channel_id=1, source_target_pairs={{16,32},{48,64},{80,96},{112,128},{144,160},{176,192},{208,224},{2... | collective-permute-start | bytes 331784 | tf_op jit(solution)/shard_map/ppermute | solution.py:435
  21.5 0.0 copy-start.5
  21.5 0.0 copy-done.4
  21.5 0.0 copy-done.1
  21.5 0.6 copy-done.5
  22.1 0.4 shard_map.95
  22.5 0.0 collective-permute-done.2.refs_3_
  22.5 5.5 %collective-permute-done.3.refs_4_ = bf16[27,16,128]{2,1,0:T(8,128)(2,1)S(1)} collective-permute-done((bf16[27,16,128]{2,1,0:T(8,128)(2,1)S(1)}, bf16[27,16,128]{2,1,0:T(8,128)(2,1)S(1)}, u32[]{:S(2)}, u32[]{:S(2)}) %collective-permute-start.3) | collective-permute-done | bytes 110624 | tf_op jit(solution)/shard_map/ppermute | solution.py:435
  28.1 3.0 %shard_map.96 = (bf16[6,10,3,16,128]{4,3,2,1,0:T(8,128)(2,1)S(1)}, bf16[6,10,3,16,128]{4,3,2,1,0:T(8,128)(2,1)S(1)}, f32[6,10,16,128]{3,2,1,0:T(8,128)S(1)}, f32...) custom-call(s32[4]{0:T(128)S(1)} %pad_add_fusion.at.refs_0_, ...), custom_call_target="tpu_custom_call" | custom-call | bytes 548880 | tf_op jit(solution)/shard_map/pallas_call | solution.py:410
  31.0 6.8 %collective-permute-start.4 = (bf16[28,8,128]{2,1,0:T(8,128)(2,1)S(1)}, bf16[28,8,128]{2,1,0:T(8,128)(2,1)S(1)}, u32[]{:S(2)}, u32[]{:S(2)}) collective-permute-start(bf16[28,8,128]{2,1,0:T(8,128)(2,1)S(1)} %get-tuple-element.46.me_ref), channel_id=1, source_target_pairs={{0,1},{1,0},{2,3},{3,2},{4,5},{5,4},{6,7},{7,6},{8,9},{9,8},{10,11... | collective-permute-start | bytes 172040 | tf_op jit(solution)/shard_map/ppermute | solution.py:429
  37.8 0.7 collective-permute-start.5
  38.5 0.9 collective-permute-done.4.re_ref
  39.3 0.0 collective-permute-done.5.ro_ref
  39.3 0.6 shard_map.97.ma_ref.refs_2_
  39.9 1.9 %collective-permute-start.6 = (bf16[36,8,128]{2,1,0:T(8,128)(2,1)S(1)}, bf16[36,8,128]{2,1,0:T(8,128)(2,1)S(1)}, u32[]{:S(2)}, u32[]{:S(2)}) collective-permute-start(bf16[36,8,128]{2,1,0:T(8,128)(2,1)S(1)} %shard_map.97.ma_ref.refs_2_), channel_id=1, source_target_pairs={{0,16},{16,0},{32,48},{48,32},{64,80},{80,64},{96,112},{112,96},{1... | collective-permute-start | bytes 221192 | tf_op jit(solution)/shard_map/ppermute | solution.py:429
  41.8 1.2 collective-permute-done.6.ra_ref.refs_3_
  43.1 0.5 shard_map.98
  43.6 7.2 %collective-permute-start.7 = (bf16[63,8,128]{2,1,0:T(8,128)(2,1)S(1)}, bf16[63,8,128]{2,1,0:T(8,128)(2,1)S(1)}, u32[]{:S(2)}, u32[]{:S(2)}) collective-permute-start(bf16[63,8,128]{2,1,0:T(8,128)(2,1)S(1)} %shard_map.98), channel_id=1, source_target_pairs={{16,32},{48,64},{80,96},{112,128},{144,160},{176,192},{208,224},{2... | collective-permute-start | bytes 387080 | tf_op jit(solution)/shard_map/ppermute | solution.py:435
  50.8 3.0 %collective-permute-done.7.refs_4_ = bf16[63,8,128]{2,1,0:T(8,128)(2,1)S(1)} collective-permute-done((bf16[63,8,128]{2,1,0:T(8,128)(2,1)S(1)}, bf16[63,8,128]{2,1,0:T(8,128)(2,1)S(1)}, u32[]{:S(2)}, u32[]{:S(2)}) %collective-permute-start.7) | collective-permute-done | bytes 129056 | tf_op jit(solution)/shard_map/ppermute | solution.py:435
  53.8 1.9 %collective-permute-start.8 = (bf16[63,8,128]{2,1,0:T(8,128)(2,1)S(1)}, bf16[63,8,128]{2,1,0:T(8,128)(2,1)S(1)}, u32[]{:S(2)}, u32[]{:S(2)}) collective-permute-start(bf16[63,8,128]{2,1,0:T(8,128)(2,1)S(1)} %collective-permute-done.7.refs_4_), channel_id=1, source_target_pairs={{0,16},{16,0},{32,48},{48,32},{64,80},{80,64},{96,112},{112,96},{1... | collective-permute-start | bytes 387080 | tf_op jit(solution)/shard_map/ppermute | solution.py:429
  55.7 1.3 shard_map.100
  57.0 2.4 %collective-permute-start.9 = (bf16[48,8,128]{2,1,0:T(8,128)(2,1)}, bf16[48,8,128]{2,1,0:T(8,128)(2,1)S(1)}, u32[]{:S(2)}, u32[]{:S(2)}) collective-permute-start(bf16[48,8,128]{2,1,0:T(8,128)(2,1)} %get-tuple-element.51), channel_id=1, source_target_pairs={{0,16},{16,0},{32,48},{48,32},{64,80},{80,64},{96,112},{112,96},{1... | collective-permute-start | bytes 294920 | tf_op jit(solution)/shard_map/ppermute | solution.py:429
  59.4 7.5 %collective-permute-start.10 = (bf16[48,8,128]{2,1,0:T(8,128)(2,1)}, bf16[48,8,128]{2,1,0:T(8,128)(2,1)S(1)}, u32[]{:S(2)}, u32[]{:S(2)}) collective-permute-start(bf16[48,8,128]{2,1,0:T(8,128)(2,1)} %get-tuple-element.52), channel_id=1, source_target_pairs={{16,32},{48,64},{80,96},{112,128},{144,160},{176,192},{208,224},{2... | collective-permute-start | bytes 294920 | tf_op jit(solution)/shard_map/ppermute | solution.py:435
  66.9 0.0 collective-permute-done.8.refs_5_
  66.9 4.9 %shard_map.99.dpre_ref = f32[8,16,128]{2,1,0:T(8,128)S(1)} custom-call(s32[4]{0:T(128)S(1)} %pad_add_fusion.at.refs_0_, f32[3,4,8,128]{3,2,1,0:T(8,128)S(1)} %get-tuple-element.45.refs_1_, bf16[36,8,128]{2,1,0:T(8,128)(2,1)S(1)} %shard_map.97.ma_ref.refs_2_, bf16[36,8,128]{2,1,0:T(8,128)(2,1)S(1)} %collective-permute-done.6.ra_ref.refs_3_, ...), custom_call_target="tpu_custom_call" | custom-call | bytes 520208 | tf_op jit(solution)/shard_map/pallas_call | solution.py:410
  71.8 0.0 collective-permute-done.9.ra_ref
  71.8 0.0 collective-permute-done.10.rb_ref
  71.8 5.2 %shard_map.101 = (bf16[16,4,8,128]{3,2,1,0:T(8,128)(2,1)}, f32[2,56,128]{2,1,0:T(8,128)S(1)}) custom-call(s32[4]{0:T(128)S(1)} %pad_add_fusion.at.refs_0_, f32[8,16,128]{2,1,0:T(8,128)S(1)} %shard_map.99.dpre_ref, f32[4,8,16,128]{3,2,1,0:T(8,128)S(1)} %get-tuple-element.49.slope2_ref, bf16[4,12,16,128]{3,2,1,0:T(8,128)(2,1)S(1)} %get-tuple-element.50.s2y_ref, ...), custom_call_target="tpu_custom_call" | custom-call | bytes 3031056 | tf_op jit(solution)/shard_map/pallas_call | solution.py:410
  77.0 1.9 %collective-permute-start.11 = (f32[56,128]{1,0:T(8,128)S(1)}, f32[56,128]{1,0:T(8,128)S(1)}, u32[]{:S(2)}, u32[]{:S(2)}) collective-permute-start(f32[56,128]{1,0:T(8,128)S(1)} %dynamic-slice_bitcast_fusion), channel_id=1, source_target_pairs={{0,16},{16,0},{32,48},{48,32},{64,80},{80,64},{96,112},{112,96},{1... | collective-permute-start | bytes 86024 | tf_op jit(solution)/shard_map/ppermute | solution.py:429
  78.9 1.2 collective-permute-done.11
  80.1 17.7 %all_to_all.20 = f32[4,56,128]{2,1,0:T(8,128)S(1)} all-to-all(f32[4,56,128]{2,1,0:T(8,128)S(1)} %broadcast_in_dim.8), channel_id=1, replica_groups={{0,1,2,3},{4,5,6,7},{8,9,10,11},{12,13,14,15},{16,17,18,19},{20,21,22,2..., dimensions={0} | all-to-all | bytes 229376 | tf_op jit(solution)/shard_map/all_to_all | solution.py:453
  97.9 7.1 %all_to_all.21 = f32[4,56,128]{2,1,0:T(8,128)S(1)} all-to-all(f32[4,56,128]{2,1,0:T(8,128)S(1)} %broadcast_in_dim.9), channel_id=1, replica_groups={{0,4,8,12},{1,5,9,13},{2,6,10,14},{3,7,11,15},{16,20,24,28},{17,21,25,2..., dimensions={0} | all-to-all | bytes 229376 | tf_op jit(solution)/shard_map/all_to_all | solution.py:453
  105.0 11.6 %all_to_all.22 = f32[4,56,128]{2,1,0:T(8,128)S(1)} all-to-all(f32[4,56,128]{2,1,0:T(8,128)S(1)} %broadcast_in_dim.10), channel_id=1, replica_groups={{0,128,256,384},{16,144,272,400},{32,160,288,416},{48,176,304,432},{64,..., dimensions={0} | all-to-all | bytes 229376 | tf_op jit(solution)/shard_map/all_to_all | solution.py:453
  116.7 19.5 %all_to_all.23 = f32[4,56,128]{2,1,0:T(8,128)S(1)} all-to-all(f32[4,56,128]{2,1,0:T(8,128)S(1)} %broadcast_in_dim.11), channel_id=1, replica_groups={{0,32,64,96},{16,48,80,112},{128,160,192,224},{144,176,208,240},{256,28..., dimensions={0} | all-to-all | bytes 229376 | tf_op jit(solution)/shard_map/all_to_all | solution.py:453
  136.2 7.9 %collective-permute-start.12 = (f32[56,128]{1,0:T(8,128)S(1)}, f32[56,128]{1,0:T(8,128)S(1)}, u32[]{:S(2)}, u32[]{:S(2)}) collective-permute-start(f32[56,128]{1,0:T(8,128)S(1)} %reduce_sum.39), channel_id=1, source_target_pairs={{0,16},{16,0},{32,48},{48,32},{64,80},{80,64},{96,112},{112,96},{1... | collective-permute-start | bytes 86024 | tf_op jit(solution)/shard_map/ppermute | solution.py:429
  144.0 0.8 collective-permute-done.12
  144.9 1.0 shard_map.102
  (16 shorter events, 0.1 us)
Async XLA Ops:
  0.6 0.7 copy-start.3
  1.4 0.9 copy-start
  2.3 19.2 %copy-start.4 = (s32[4,8,128]{2,1,0:T(8,128)S(1)}, s32[4,8,128]{2,1,0:T(8,128)}, u32[]{:S(2)}) copy-start(s32[4,8,128]{2,1,0:T(8,128)} %lab_ref.1) | copy-start | bytes 49156
  2.9 5.3 %collective-permute-start = (bf16[9,16,128]{2,1,0:T(8,128)(2,1)S(1)}, bf16[9,16,128]{2,1,0:T(8,128)(2,1)S(1)}, u32[]{:S(2)}, u32[]{:S(2)}) collective-permute-start(bf16[9,16,128]{2,1,0:T(8,128)(2,1)S(1)} %get-tuple-element.35), channel_id=1, source_target_pairs={{0,1},{1,0},{2,3},{3,2},{4,5},{5,4},{6,7},{7,6},{8,9},{9,8},{10,11... | collective-permute-start | bytes 110600 | tf_op jit(solution)/shard_map/ppermute | solution.py:429
  6.8 1.3 collective-permute-start.1
  8.2 13.3 %copy-start.1 = (bf16[16,16,3,3,3]{1,0,4,3,2:T(8,128)(2,1)S(1)}, bf16[16,16,3,3,3]{1,0,4,3,2:T(8,128)(2,1)}, u32[]{:S(2)}) copy-start(bf16[16,16,3,3,3]{1,0,4,3,2:T(8,128)(2,1)} %param.9) | copy-start | bytes 41476
  8.2 13.3 %copy-start.2 = (bf16[16,16,3,3,3]{1,0,4,3,2:T(8,128)(2,1)S(1)}, bf16[16,16,3,3,3]{1,0,4,3,2:T(8,128)(2,1)}, u32[]{:S(2)}) copy-start(bf16[16,16,3,3,3]{1,0,4,3,2:T(8,128)(2,1)} %param.10) | copy-start | bytes 41476
  8.7 13.8 %collective-permute-start.2 = (bf16[27,16,128]{2,1,0:T(8,128)(2,1)S(1)}, bf16[27,16,128]{2,1,0:T(8,128)(2,1)S(1)}, u32[]{:S(2)}, u32[]{:S(2)}) collective-permute-start(bf16[27,16,128]{2,1,0:T(8,128)(2,1)S(1)} %get-tuple-element.39), channel_id=1, source_target_pairs={{0,16},{16,0},{32,48},{48,32},{64,80},{80,64},{96,112},{112,96},{1... | collective-permute-start | bytes 331784 | tf_op jit(solution)/shard_map/ppermute | solution.py:429
  18.1 10.0 %collective-permute-start.3 = (bf16[27,16,128]{2,1,0:T(8,128)(2,1)S(1)}, bf16[27,16,128]{2,1,0:T(8,128)(2,1)S(1)}, u32[]{:S(2)}, u32[]{:S(2)}) collective-permute-start(bf16[27,16,128]{2,1,0:T(8,128)(2,1)S(1)} %get-tuple-element.40), channel_id=1, source_target_pairs={{16,32},{48,64},{80,96},{112,128},{144,160},{176,192},{208,224},{2... | collective-permute-start | bytes 331784 | tf_op jit(solution)/shard_map/ppermute | solution.py:435
  21.5 0.7 copy-start.5
  31.0 8.3 %collective-permute-start.4 = (bf16[28,8,128]{2,1,0:T(8,128)(2,1)S(1)}, bf16[28,8,128]{2,1,0:T(8,128)(2,1)S(1)}, u32[]{:S(2)}, u32[]{:S(2)}) collective-permute-start(bf16[28,8,128]{2,1,0:T(8,128)(2,1)S(1)} %get-tuple-element.46.me_ref), channel_id=1, source_target_pairs={{0,1},{1,0},{2,3},{3,2},{4,5},{5,4},{6,7},{7,6},{8,9},{9,8},{10,11... | collective-permute-start | bytes 172040 | tf_op jit(solution)/shard_map/ppermute | solution.py:429
  37.8 1.6 %collective-permute-start.5 = (bf16[28,8,128]{2,1,0:T(8,128)(2,1)S(1)}, bf16[28,8,128]{2,1,0:T(8,128)(2,1)S(1)}, u32[]{:S(2)}, u32[]{:S(2)}) collective-permute-start(bf16[28,8,128]{2,1,0:T(8,128)(2,1)S(1)} %get-tuple-element.47), channel_id=1, source_target_pairs={{1,2},{3,4},{5,6},{7,8},{9,10},{11,12},{13,14},{2,1},{4,3},{6,5},{... | collective-permute-start | bytes 172040 | tf_op jit(solution)/shard_map/ppermute | solution.py:435
  39.9 3.2 %collective-permute-start.6 = (bf16[36,8,128]{2,1,0:T(8,128)(2,1)S(1)}, bf16[36,8,128]{2,1,0:T(8,128)(2,1)S(1)}, u32[]{:S(2)}, u32[]{:S(2)}) collective-permute-start(bf16[36,8,128]{2,1,0:T(8,128)(2,1)S(1)} %shard_map.97.ma_ref.refs_2_), channel_id=1, source_target_pairs={{0,16},{16,0},{32,48},{48,32},{64,80},{80,64},{96,112},{112,96},{1... | collective-permute-start | bytes 221192 | tf_op jit(solution)/shard_map/ppermute | solution.py:429
  43.6 10.2 %collective-permute-start.7 = (bf16[63,8,128]{2,1,0:T(8,128)(2,1)S(1)}, bf16[63,8,128]{2,1,0:T(8,128)(2,1)S(1)}, u32[]{:S(2)}, u32[]{:S(2)}) collective-permute-start(bf16[63,8,128]{2,1,0:T(8,128)(2,1)S(1)} %shard_map.98), channel_id=1, source_target_pairs={{16,32},{48,64},{80,96},{112,128},{144,160},{176,192},{208,224},{2... | collective-permute-start | bytes 387080 | tf_op jit(solution)/shard_map/ppermute | solution.py:435
  53.8 13.1 %collective-permute-start.8 = (bf16[63,8,128]{2,1,0:T(8,128)(2,1)S(1)}, bf16[63,8,128]{2,1,0:T(8,128)(2,1)S(1)}, u32[]{:S(2)}, u32[]{:S(2)}) collective-permute-start(bf16[63,8,128]{2,1,0:T(8,128)(2,1)S(1)} %collective-permute-done.7.refs_4_), channel_id=1, source_target_pairs={{0,16},{16,0},{32,48},{48,32},{64,80},{80,64},{96,112},{112,96},{1... | collective-permute-start | bytes 387080 | tf_op jit(solution)/shard_map/ppermute | solution.py:429
  57.0 14.8 %collective-permute-start.9 = (bf16[48,8,128]{2,1,0:T(8,128)(2,1)}, bf16[48,8,128]{2,1,0:T(8,128)(2,1)S(1)}, u32[]{:S(2)}, u32[]{:S(2)}) collective-permute-start(bf16[48,8,128]{2,1,0:T(8,128)(2,1)} %get-tuple-element.51), channel_id=1, source_target_pairs={{0,16},{16,0},{32,48},{48,32},{64,80},{80,64},{96,112},{112,96},{1... | collective-permute-start | bytes 294920 | tf_op jit(solution)/shard_map/ppermute | solution.py:429
  59.4 12.4 %collective-permute-start.10 = (bf16[48,8,128]{2,1,0:T(8,128)(2,1)}, bf16[48,8,128]{2,1,0:T(8,128)(2,1)S(1)}, u32[]{:S(2)}, u32[]{:S(2)}) collective-permute-start(bf16[48,8,128]{2,1,0:T(8,128)(2,1)} %get-tuple-element.52), channel_id=1, source_target_pairs={{16,32},{48,64},{80,96},{112,128},{144,160},{176,192},{208,224},{2... | collective-permute-start | bytes 294920 | tf_op jit(solution)/shard_map/ppermute | solution.py:435
  77.0 3.1 %collective-permute-start.11 = (f32[56,128]{1,0:T(8,128)S(1)}, f32[56,128]{1,0:T(8,128)S(1)}, u32[]{:S(2)}, u32[]{:S(2)}) collective-permute-start(f32[56,128]{1,0:T(8,128)S(1)} %dynamic-slice_bitcast_fusion), channel_id=1, source_target_pairs={{0,16},{16,0},{32,48},{48,32},{64,80},{80,64},{96,112},{112,96},{1... | collective-permute-start | bytes 86024 | tf_op jit(solution)/shard_map/ppermute | solution.py:429
  136.2 8.7 %collective-permute-start.12 = (f32[56,128]{1,0:T(8,128)S(1)}, f32[56,128]{1,0:T(8,128)S(1)}, u32[]{:S(2)}, u32[]{:S(2)}) collective-permute-start(f32[56,128]{1,0:T(8,128)S(1)} %reduce_sum.39), channel_id=1, source_target_pairs={{0,16},{16,0},{32,48},{48,32},{64,80},{80,64},{96,112},{112,96},{1... | collective-permute-start | bytes 86024 | tf_op jit(solution)/shard_map/ppermute | solution.py:429

commit v11 on v10

--- a/solution.py
+++ b/solution.py
@@ -134,7 +134,7 @@
             hx_ref[z, y : y + 2, 2] = up.astype(bf16)
         return carry
 
-    lax.fori_loop(0, BZ + 2, first, 0, unroll=2)
+    lax.fori_loop(0, BZ + 2, first, 0, unroll=3)
     sw = sw_ref[...]
 
     def second(z, carry):
@@ -149,7 +149,7 @@
         own_ref[0, z] = jnp.tanh(jnp.concatenate(rows, axis=0))
         return carry
 
-    lax.fori_loop(0, BZ, second, 0, unroll=2)
+    lax.fori_loop(0, BZ, second, 0, unroll=4)
 
     for k in range(BZ):
         p_ref[3 + k] = sy_ref[k]
@@ -343,7 +343,7 @@
             ex_ref[z, y : y + 2, 2] = up.astype(bf16)
         return carry
 
-    lax.fori_loop(0, BZ + 2, hidden, 0, unroll=2)
+    lax.fori_loop(0, BZ + 2, hidden, 0, unroll=3)
 
     def features(z, carry):
         rows = []
@@ -354,7 +354,7 @@
         df_ref[:, z] = jnp.transpose(plane, (1, 0, 2)).astype(bf16)
         return carry
 
-    lax.fori_loop(0, BZ, features, 0, unroll=2)
+    lax.fori_loop(0, BZ, features, 0, unroll=4)
 
     nt = (((1,), (1,)), ((), ()))
 
@@ -371,7 +371,7 @@
         return g1, g2, gs
 
     zero = jnp.zeros((C, TAPS), f32)
-    g1, g2, gs = lax.fori_loop(0, BZ, weights, (zero, zero, jnp.zeros((C, X), f32)))
+    g1, g2, gs = lax.fori_loop(0, BZ, weights, (zero, zero, jnp.zeros((C, X), f32)), unroll=2)
     grad_ref[...] = jnp.zeros_like(grad_ref)
     for i, g in enumerate((g1, g2)):
         for k in range(3):

time: 147 us -> 145 us (0.986)
  no operation moved by 1% of the time
where the time goes in v11:
time: 145 us
  blocking collectives  56 us (39%)
  starting transfers between devices  55.4 us (38%)
  Pallas kernels  16.9 us (12%)
  waiting for transfers between devices  13.3 us (9%)
  local copies, waits for them, and re-layouts  2.2 us (2%)
    all_to_all x4, blocking collectives, total_of(): lax.all_to_all(copies, axis, 0, 0, axis_index_groups=sets)  56 us
    ppermute x8, starting transfers between devices, even(): return lax.ppermute(value, axis, [(i, i ^ 1) for i in range(n)])  36 us
    ppermute x5, starting transfers between devices, odd(): return lax.ppermute(value, axis, pairs + [(j, i) for i, j in pairs])  19.3 us
    pallas_call x10, Pallas kernels, run(): pl.pallas_call(kernel, out_shape=outs, in_specs=specs, out_specs=[vmem] *...  16.9 us
    ppermute x5, waiting for transfers between devices, odd(): return lax.ppermute(value, axis, pairs + [(j, i) for i, j in pairs])  8.49 us
    ppermute x8, waiting for transfers between devices, even(): return lax.ppermute(value, axis, [(i, i ^ 1) for i in range(n)])  4.77 us
  transfers between devices with their start and end apart: 13, of which 7 were waited for; matrix products, arithmetic and copies ran while one was open for 0% of the time, Pallas kernels for 5%

profile of v11, /device:TPU:1, one launch (start us, length us, event | category | flops | bytes accessed | tf_op | source)
XLA Modules:
  0.0 144.8 jit_solution(7143296902870886921)
XLA Ops:
  0.6 0.0 copy-start.3
  0.7 0.1 pad_add_fusion.at.refs_0_
  0.7 0.6 copy-done.3
  1.4 0.9 copy-done
  2.3 0.6 shard_map.93
  2.9 3.9 %collective-permute-start = (bf16[9,16,128]{2,1,0:T(8,128)(2,1)S(1)}, bf16[9,16,128]{2,1,0:T(8,128)(2,1)S(1)}, u32[]{:S(2)}, u32[]{:S(2)}) collective-permute-start(bf16[9,16,128]{2,1,0:T(8,128)(2,1)S(1)} %get-tuple-element.35), channel_id=1, source_target_pairs={{0,1},{1,0},{2,3},{3,2},{4,5},{5,4},{6,7},{7,6},{8,9},{9,8},{10,11... | collective-permute-start | bytes 110600 | tf_op jit(solution)/shard_map/ppermute | solution.py:429
  6.8 0.7 collective-permute-start.1
  7.5 0.7 collective-permute-done.re_ref
  8.2 0.0 collective-permute-done.1.ro_ref
  8.2 0.6 shard_map.94
  8.7 9.3 %collective-permute-start.2 = (bf16[27,16,128]{2,1,0:T(8,128)(2,1)S(1)}, bf16[27,16,128]{2,1,0:T(8,128)(2,1)S(1)}, u32[]{:S(2)}, u32[]{:S(2)}) collective-permute-start(bf16[27,16,128]{2,1,0:T(8,128)(2,1)S(1)} %get-tuple-element.39), channel_id=1, source_target_pairs={{0,16},{16,0},{32,48},{48,32},{64,80},{80,64},{96,112},{112,96},{1... | collective-permute-start | bytes 331784 | tf_op jit(solution)/shard_map/ppermute | solution.py:429
  18.1 3.4 %collective-permute-start.3 = (bf16[27,16,128]{2,1,0:T(8,128)(2,1)S(1)}, bf16[27,16,128]{2,1,0:T(8,128)(2,1)S(1)}, u32[]{:S(2)}, u32[]{:S(2)}) collective-permute-start(bf16[27,16,128]{2,1,0:T(8,128)(2,1)S(1)} %get-tuple-element.40), channel_id=1, source_target_pairs={{16,32},{48,64},{80,96},{112,128},{144,160},{176,192},{208,224},{2... | collective-permute-start | bytes 331784 | tf_op jit(solution)/shard_map/ppermute | solution.py:435
  21.5 0.0 copy-start.5
  21.5 0.0 copy-done.4
  21.5 0.0 copy-done.1
  21.5 0.6 copy-done.5
  22.1 0.4 shard_map.95
  22.5 0.0 collective-permute-done.2.refs_3_
  22.5 5.5 %collective-permute-done.3.refs_4_ = bf16[27,16,128]{2,1,0:T(8,128)(2,1)S(1)} collective-permute-done((bf16[27,16,128]{2,1,0:T(8,128)(2,1)S(1)}, bf16[27,16,128]{2,1,0:T(8,128)(2,1)S(1)}, u32[]{:S(2)}, u32[]{:S(2)}) %collective-permute-start.3) | collective-permute-done | bytes 110624 | tf_op jit(solution)/shard_map/ppermute | solution.py:435
  28.1 2.5 %shard_map.96 = (bf16[6,10,3,16,128]{4,3,2,1,0:T(8,128)(2,1)S(1)}, bf16[6,10,3,16,128]{4,3,2,1,0:T(8,128)(2,1)S(1)}, f32[6,10,16,128]{3,2,1,0:T(8,128)S(1)}, f32...) custom-call(s32[4]{0:T(128)S(1)} %pad_add_fusion.at.refs_0_, ...), custom_call_target="tpu_custom_call" | custom-call | bytes 548880 | tf_op jit(solution)/shard_map/pallas_call | solution.py:410
  30.5 6.8 %collective-permute-start.4 = (bf16[28,8,128]{2,1,0:T(8,128)(2,1)S(1)}, bf16[28,8,128]{2,1,0:T(8,128)(2,1)S(1)}, u32[]{:S(2)}, u32[]{:S(2)}) collective-permute-start(bf16[28,8,128]{2,1,0:T(8,128)(2,1)S(1)} %get-tuple-element.46.me_ref), channel_id=1, source_target_pairs={{0,1},{1,0},{2,3},{3,2},{4,5},{5,4},{6,7},{7,6},{8,9},{9,8},{10,11... | collective-permute-start | bytes 172040 | tf_op jit(solution)/shard_map/ppermute | solution.py:429
  37.3 0.7 collective-permute-start.5
  37.9 0.9 collective-permute-done.4.re_ref
  38.8 0.0 collective-permute-done.5.ro_ref
  38.8 0.6 shard_map.97.ma_ref.refs_2_
  39.4 1.9 %collective-permute-start.6 = (bf16[36,8,128]{2,1,0:T(8,128)(2,1)S(1)}, bf16[36,8,128]{2,1,0:T(8,128)(2,1)S(1)}, u32[]{:S(2)}, u32[]{:S(2)}) collective-permute-start(bf16[36,8,128]{2,1,0:T(8,128)(2,1)S(1)} %shard_map.97.ma_ref.refs_2_), channel_id=1, source_target_pairs={{0,16},{16,0},{32,48},{48,32},{64,80},{80,64},{96,112},{112,96},{1... | collective-permute-start | bytes 221192 | tf_op jit(solution)/shard_map/ppermute | solution.py:429
  41.3 1.2 collective-permute-done.6.ra_ref.refs_3_
  42.6 0.5 shard_map.98
  43.1 7.2 %collective-permute-start.7 = (bf16[63,8,128]{2,1,0:T(8,128)(2,1)S(1)}, bf16[63,8,128]{2,1,0:T(8,128)(2,1)S(1)}, u32[]{:S(2)}, u32[]{:S(2)}) collective-permute-start(bf16[63,8,128]{2,1,0:T(8,128)(2,1)S(1)} %shard_map.98), channel_id=1, source_target_pairs={{16,32},{48,64},{80,96},{112,128},{144,160},{176,192},{208,224},{2... | collective-permute-start | bytes 387080 | tf_op jit(solution)/shard_map/ppermute | solution.py:435
  50.3 3.0 %collective-permute-done.7.refs_4_ = bf16[63,8,128]{2,1,0:T(8,128)(2,1)S(1)} collective-permute-done((bf16[63,8,128]{2,1,0:T(8,128)(2,1)S(1)}, bf16[63,8,128]{2,1,0:T(8,128)(2,1)S(1)}, u32[]{:S(2)}, u32[]{:S(2)}) %collective-permute-start.7) | collective-permute-done | bytes 129056 | tf_op jit(solution)/shard_map/ppermute | solution.py:435
  53.3 1.9 %collective-permute-start.8 = (bf16[63,8,128]{2,1,0:T(8,128)(2,1)S(1)}, bf16[63,8,128]{2,1,0:T(8,128)(2,1)S(1)}, u32[]{:S(2)}, u32[]{:S(2)}) collective-permute-start(bf16[63,8,128]{2,1,0:T(8,128)(2,1)S(1)} %collective-permute-done.7.refs_4_), channel_id=1, source_target_pairs={{0,16},{16,0},{32,48},{48,32},{64,80},{80,64},{96,112},{112,96},{1... | collective-permute-start | bytes 387080 | tf_op jit(solution)/shard_map/ppermute | solution.py:429
  55.2 1.3 shard_map.100
  56.5 2.4 %collective-permute-start.9 = (bf16[48,8,128]{2,1,0:T(8,128)(2,1)}, bf16[48,8,128]{2,1,0:T(8,128)(2,1)S(1)}, u32[]{:S(2)}, u32[]{:S(2)}) collective-permute-start(bf16[48,8,128]{2,1,0:T(8,128)(2,1)} %get-tuple-element.51), channel_id=1, source_target_pairs={{0,16},{16,0},{32,48},{48,32},{64,80},{80,64},{96,112},{112,96},{1... | collective-permute-start | bytes 294920 | tf_op jit(solution)/shard_map/ppermute | solution.py:429
  58.9 7.5 %collective-permute-start.10 = (bf16[48,8,128]{2,1,0:T(8,128)(2,1)}, bf16[48,8,128]{2,1,0:T(8,128)(2,1)S(1)}, u32[]{:S(2)}, u32[]{:S(2)}) collective-permute-start(bf16[48,8,128]{2,1,0:T(8,128)(2,1)} %get-tuple-element.52), channel_id=1, source_target_pairs={{16,32},{48,64},{80,96},{112,128},{144,160},{176,192},{208,224},{2... | collective-permute-start | bytes 294920 | tf_op jit(solution)/shard_map/ppermute | solution.py:435
  66.3 0.0 collective-permute-done.8.refs_5_
  66.4 4.9 %shard_map.99.dpre_ref = f32[8,16,128]{2,1,0:T(8,128)S(1)} custom-call(s32[4]{0:T(128)S(1)} %pad_add_fusion.at.refs_0_, f32[3,4,8,128]{3,2,1,0:T(8,128)S(1)} %get-tuple-element.45.refs_1_, bf16[36,8,128]{2,1,0:T(8,128)(2,1)S(1)} %shard_map.97.ma_ref.refs_2_, bf16[36,8,128]{2,1,0:T(8,128)(2,1)S(1)} %collective-permute-done.6.ra_ref.refs_3_, ...), custom_call_target="tpu_custom_call" | custom-call | bytes 520208 | tf_op jit(solution)/shard_map/pallas_call | solution.py:410
  71.2 0.0 collective-permute-done.9.ra_ref
  71.3 0.0 collective-permute-done.10.rb_ref
  71.3 4.6 %shard_map.101 = (bf16[16,4,8,128]{3,2,1,0:T(8,128)(2,1)}, f32[2,56,128]{2,1,0:T(8,128)S(1)}) custom-call(s32[4]{0:T(128)S(1)} %pad_add_fusion.at.refs_0_, f32[8,16,128]{2,1,0:T(8,128)S(1)} %shard_map.99.dpre_ref, f32[4,8,16,128]{3,2,1,0:T(8,128)S(1)} %get-tuple-element.49.slope2_ref, bf16[4,12,16,128]{3,2,1,0:T(8,128)(2,1)S(1)} %get-tuple-element.50.s2y_ref, ...), custom_call_target="tpu_custom_call" | custom-call | bytes 3031056 | tf_op jit(solution)/shard_map/pallas_call | solution.py:410
  75.9 1.9 %collective-permute-start.11 = (f32[56,128]{1,0:T(8,128)S(1)}, f32[56,128]{1,0:T(8,128)S(1)}, u32[]{:S(2)}, u32[]{:S(2)}) collective-permute-start(f32[56,128]{1,0:T(8,128)S(1)} %dynamic-slice_bitcast_fusion), channel_id=1, source_target_pairs={{0,16},{16,0},{32,48},{48,32},{64,80},{80,64},{96,112},{112,96},{1... | collective-permute-start | bytes 86024 | tf_op jit(solution)/shard_map/ppermute | solution.py:429
  77.8 1.2 collective-permute-done.11
  79.0 17.7 %all_to_all.20 = f32[4,56,128]{2,1,0:T(8,128)S(1)} all-to-all(f32[4,56,128]{2,1,0:T(8,128)S(1)} %broadcast_in_dim.8), channel_id=1, replica_groups={{0,1,2,3},{4,5,6,7},{8,9,10,11},{12,13,14,15},{16,17,18,19},{20,21,22,2..., dimensions={0} | all-to-all | bytes 229376 | tf_op jit(solution)/shard_map/all_to_all | solution.py:453
  96.7 7.1 %all_to_all.21 = f32[4,56,128]{2,1,0:T(8,128)S(1)} all-to-all(f32[4,56,128]{2,1,0:T(8,128)S(1)} %broadcast_in_dim.9), channel_id=1, replica_groups={{0,4,8,12},{1,5,9,13},{2,6,10,14},{3,7,11,15},{16,20,24,28},{17,21,25,2..., dimensions={0} | all-to-all | bytes 229376 | tf_op jit(solution)/shard_map/all_to_all | solution.py:453
  103.9 11.6 %all_to_all.22 = f32[4,56,128]{2,1,0:T(8,128)S(1)} all-to-all(f32[4,56,128]{2,1,0:T(8,128)S(1)} %broadcast_in_dim.10), channel_id=1, replica_groups={{0,128,256,384},{16,144,272,400},{32,160,288,416},{48,176,304,432},{64,..., dimensions={0} | all-to-all | bytes 229376 | tf_op jit(solution)/shard_map/all_to_all | solution.py:453
  115.5 19.5 %all_to_all.23 = f32[4,56,128]{2,1,0:T(8,128)S(1)} all-to-all(f32[4,56,128]{2,1,0:T(8,128)S(1)} %broadcast_in_dim.11), channel_id=1, replica_groups={{0,32,64,96},{16,48,80,112},{128,160,192,224},{144,176,208,240},{256,28..., dimensions={0} | all-to-all | bytes 229376 | tf_op jit(solution)/shard_map/all_to_all | solution.py:453
  135.0 7.9 %collective-permute-start.12 = (f32[56,128]{1,0:T(8,128)S(1)}, f32[56,128]{1,0:T(8,128)S(1)}, u32[]{:S(2)}, u32[]{:S(2)}) collective-permute-start(f32[56,128]{1,0:T(8,128)S(1)} %reduce_sum.39), channel_id=1, source_target_pairs={{0,16},{16,0},{32,48},{48,32},{64,80},{80,64},{96,112},{112,96},{1... | collective-permute-start | bytes 86024 | tf_op jit(solution)/shard_map/ppermute | solution.py:429
  142.9 0.8 collective-permute-done.12
  143.8 1.0 shard_map.102
  (16 shorter events, 0.1 us)
Async XLA Ops:
  0.6 0.7 copy-start.3
  1.4 0.9 copy-start
  2.3 19.2 %copy-start.4 = (s32[4,8,128]{2,1,0:T(8,128)S(1)}, s32[4,8,128]{2,1,0:T(8,128)}, u32[]{:S(2)}) copy-start(s32[4,8,128]{2,1,0:T(8,128)} %lab_ref.1) | copy-start | bytes 49156
  2.9 5.3 %collective-permute-start = (bf16[9,16,128]{2,1,0:T(8,128)(2,1)S(1)}, bf16[9,16,128]{2,1,0:T(8,128)(2,1)S(1)}, u32[]{:S(2)}, u32[]{:S(2)}) collective-permute-start(bf16[9,16,128]{2,1,0:T(8,128)(2,1)S(1)} %get-tuple-element.35), channel_id=1, source_target_pairs={{0,1},{1,0},{2,3},{3,2},{4,5},{5,4},{6,7},{7,6},{8,9},{9,8},{10,11... | collective-permute-start | bytes 110600 | tf_op jit(solution)/shard_map/ppermute | solution.py:429
  6.8 1.3 collective-permute-start.1
  8.2 13.3 %copy-start.1 = (bf16[16,16,3,3,3]{1,0,4,3,2:T(8,128)(2,1)S(1)}, bf16[16,16,3,3,3]{1,0,4,3,2:T(8,128)(2,1)}, u32[]{:S(2)}) copy-start(bf16[16,16,3,3,3]{1,0,4,3,2:T(8,128)(2,1)} %param.9) | copy-start | bytes 41476
  8.2 13.3 %copy-start.2 = (bf16[16,16,3,3,3]{1,0,4,3,2:T(8,128)(2,1)S(1)}, bf16[16,16,3,3,3]{1,0,4,3,2:T(8,128)(2,1)}, u32[]{:S(2)}) copy-start(bf16[16,16,3,3,3]{1,0,4,3,2:T(8,128)(2,1)} %param.10) | copy-start | bytes 41476
  8.7 13.8 %collective-permute-start.2 = (bf16[27,16,128]{2,1,0:T(8,128)(2,1)S(1)}, bf16[27,16,128]{2,1,0:T(8,128)(2,1)S(1)}, u32[]{:S(2)}, u32[]{:S(2)}) collective-permute-start(bf16[27,16,128]{2,1,0:T(8,128)(2,1)S(1)} %get-tuple-element.39), channel_id=1, source_target_pairs={{0,16},{16,0},{32,48},{48,32},{64,80},{80,64},{96,112},{112,96},{1... | collective-permute-start | bytes 331784 | tf_op jit(solution)/shard_map/ppermute | solution.py:429
  18.1 10.0 %collective-permute-start.3 = (bf16[27,16,128]{2,1,0:T(8,128)(2,1)S(1)}, bf16[27,16,128]{2,1,0:T(8,128)(2,1)S(1)}, u32[]{:S(2)}, u32[]{:S(2)}) collective-permute-start(bf16[27,16,128]{2,1,0:T(8,128)(2,1)S(1)} %get-tuple-element.40), channel_id=1, source_target_pairs={{16,32},{48,64},{80,96},{112,128},{144,160},{176,192},{208,224},{2... | collective-permute-start | bytes 331784 | tf_op jit(solution)/shard_map/ppermute | solution.py:435
  21.5 0.7 copy-start.5
  30.5 8.3 %collective-permute-start.4 = (bf16[28,8,128]{2,1,0:T(8,128)(2,1)S(1)}, bf16[28,8,128]{2,1,0:T(8,128)(2,1)S(1)}, u32[]{:S(2)}, u32[]{:S(2)}) collective-permute-start(bf16[28,8,128]{2,1,0:T(8,128)(2,1)S(1)} %get-tuple-element.46.me_ref), channel_id=1, source_target_pairs={{0,1},{1,0},{2,3},{3,2},{4,5},{5,4},{6,7},{7,6},{8,9},{9,8},{10,11... | collective-permute-start | bytes 172040 | tf_op jit(solution)/shard_map/ppermute | solution.py:429
  37.3 1.6 %collective-permute-start.5 = (bf16[28,8,128]{2,1,0:T(8,128)(2,1)S(1)}, bf16[28,8,128]{2,1,0:T(8,128)(2,1)S(1)}, u32[]{:S(2)}, u32[]{:S(2)}) collective-permute-start(bf16[28,8,128]{2,1,0:T(8,128)(2,1)S(1)} %get-tuple-element.47), channel_id=1, source_target_pairs={{1,2},{3,4},{5,6},{7,8},{9,10},{11,12},{13,14},{2,1},{4,3},{6,5},{... | collective-permute-start | bytes 172040 | tf_op jit(solution)/shard_map/ppermute | solution.py:435
  39.4 3.2 %collective-permute-start.6 = (bf16[36,8,128]{2,1,0:T(8,128)(2,1)S(1)}, bf16[36,8,128]{2,1,0:T(8,128)(2,1)S(1)}, u32[]{:S(2)}, u32[]{:S(2)}) collective-permute-start(bf16[36,8,128]{2,1,0:T(8,128)(2,1)S(1)} %shard_map.97.ma_ref.refs_2_), channel_id=1, source_target_pairs={{0,16},{16,0},{32,48},{48,32},{64,80},{80,64},{96,112},{112,96},{1... | collective-permute-start | bytes 221192 | tf_op jit(solution)/shard_map/ppermute | solution.py:429
  43.1 10.2 %collective-permute-start.7 = (bf16[63,8,128]{2,1,0:T(8,128)(2,1)S(1)}, bf16[63,8,128]{2,1,0:T(8,128)(2,1)S(1)}, u32[]{:S(2)}, u32[]{:S(2)}) collective-permute-start(bf16[63,8,128]{2,1,0:T(8,128)(2,1)S(1)} %shard_map.98), channel_id=1, source_target_pairs={{16,32},{48,64},{80,96},{112,128},{144,160},{176,192},{208,224},{2... | collective-permute-start | bytes 387080 | tf_op jit(solution)/shard_map/ppermute | solution.py:435
  53.3 13.1 %collective-permute-start.8 = (bf16[63,8,128]{2,1,0:T(8,128)(2,1)S(1)}, bf16[63,8,128]{2,1,0:T(8,128)(2,1)S(1)}, u32[]{:S(2)}, u32[]{:S(2)}) collective-permute-start(bf16[63,8,128]{2,1,0:T(8,128)(2,1)S(1)} %collective-permute-done.7.refs_4_), channel_id=1, source_target_pairs={{0,16},{16,0},{32,48},{48,32},{64,80},{80,64},{96,112},{112,96},{1... | collective-permute-start | bytes 387080 | tf_op jit(solution)/shard_map/ppermute | solution.py:429
  56.5 14.8 %collective-permute-start.9 = (bf16[48,8,128]{2,1,0:T(8,128)(2,1)}, bf16[48,8,128]{2,1,0:T(8,128)(2,1)S(1)}, u32[]{:S(2)}, u32[]{:S(2)}) collective-permute-start(bf16[48,8,128]{2,1,0:T(8,128)(2,1)} %get-tuple-element.51), channel_id=1, source_target_pairs={{0,16},{16,0},{32,48},{48,32},{64,80},{80,64},{96,112},{112,96},{1... | collective-permute-start | bytes 294920 | tf_op jit(solution)/shard_map/ppermute | solution.py:429
  58.9 12.4 %collective-permute-start.10 = (bf16[48,8,128]{2,1,0:T(8,128)(2,1)}, bf16[48,8,128]{2,1,0:T(8,128)(2,1)S(1)}, u32[]{:S(2)}, u32[]{:S(2)}) collective-permute-start(bf16[48,8,128]{2,1,0:T(8,128)(2,1)} %get-tuple-element.52), channel_id=1, source_target_pairs={{16,32},{48,64},{80,96},{112,128},{144,160},{176,192},{208,224},{2... | collective-permute-start | bytes 294920 | tf_op jit(solution)/shard_map/ppermute | solution.py:435
  75.9 3.1 %collective-permute-start.11 = (f32[56,128]{1,0:T(8,128)S(1)}, f32[56,128]{1,0:T(8,128)S(1)}, u32[]{:S(2)}, u32[]{:S(2)}) collective-permute-start(f32[56,128]{1,0:T(8,128)S(1)} %dynamic-slice_bitcast_fusion), channel_id=1, source_target_pairs={{0,16},{16,0},{32,48},{48,32},{64,80},{80,64},{96,112},{112,96},{1... | collective-permute-start | bytes 86024 | tf_op jit(solution)/shard_map/ppermute | solution.py:429
  135.0 8.7 %collective-permute-start.12 = (f32[56,128]{1,0:T(8,128)S(1)}, f32[56,128]{1,0:T(8,128)S(1)}, u32[]{:S(2)}, u32[]{:S(2)}) collective-permute-start(f32[56,128]{1,0:T(8,128)S(1)} %reduce_sum.39), channel_id=1, source_target_pairs={{0,16},{16,0},{32,48},{48,32},{64,80},{80,64},{96,112},{112,96},{1... | collective-permute-start | bytes 86024 | tf_op jit(solution)/shard_map/ppermute | solution.py:429
